TPU v7x, 32 devices: a whole 2x2x4 slice. The times are simulated.
32 devices in a mesh: rep: 8 (over z, y), shard: 4 (over x, core).
Axes of the slice: x: 2, y: 2, z: 4, core: 2. Of those that a mesh axis runs over, the one named last changes fastest.
Arguments:
- tokens: bfloat16 [8192, 2048], P(('rep', 'shard')), may hold values from -6 to 6
- w_query: bfloat16 [2048, 2048], P('shard'), may hold values from -0.125 to 0.125
- w_key: bfloat16 [2048, 2048], P('shard'), may hold values from -0.125 to 0.125
- w_value: bfloat16 [2048, 2048], P('shard'), may hold values from -0.125 to 0.125
- w_out: bfloat16 [2048, 2048], P('shard'), may hold values from -0.75 to 0.75
- w_router: bfloat16 [2048, 16], P('shard'), may hold values from -0.0625 to 0.0625
- norm_attn: bfloat16 [2048], P('shard'), may hold values from 0.5 to 1.5
- norm_ffn: bfloat16 [2048], P('shard'), may hold values from 0.5 to 1.5
- norm_query: bfloat16 [128], P('shard'), may hold values from 0.099609375 to 1.8984375
- norm_key: bfloat16 [128], P('shard'), may hold values from 0.099609375 to 1.8984375
- w_gate: bfloat16 [16, 2048, 1024], P('rep', 'shard'), may hold values from -0.125 to 0.125
- w_up: bfloat16 [16, 2048, 1024], P('rep', 'shard'), may hold values from -0.125 to 0.125
- w_down: bfloat16 [16, 1024, 2048], P('rep', 'shard'), may hold values from -0.75 to 0.75
- segments: int32 [8, 1024], P('rep'), may hold values from 0 to 3, never falling along the last dimension, each value on 1 to 800 neighbouring positions
- routes: int32 [8192, 8], P(('rep', 'shard')), may hold values from 0 to 15, all different within a row; in each aligned block of 256 rows (0 to 255, 256 to 511, ...) at most 144 rows name the same one
- cotangent: bfloat16 [8192, 2048], P(('rep', 'shard')), may hold values from -6 to 6
Outputs:
- output: bfloat16 [8192, 2048], P(('rep', 'shard'))
- tokens_grad: bfloat16 [8192, 2048], P(('rep', 'shard'))
- w_query_grad: float32 [2048, 2048], P('shard')
- w_key_grad: float32 [2048, 2048], P('shard')
- w_value_grad: float32 [2048, 2048], P('shard')
- w_out_grad: float32 [2048, 2048], P('shard')
- w_router_grad: float32 [2048, 16], P('shard')
- norm_attn_grad: float32 [2048], P('shard')
- norm_ffn_grad: float32 [2048], P('shard')
- norm_query_grad: float32 [128], P('shard')
- norm_key_grad: float32 [128], P('shard')
- w_gate_grad: float32 [16, 2048, 1024], P('rep', 'shard')
- w_up_grad: float32 [16, 2048, 1024], P('rep', 'shard')
- w_down_grad: float32 [16, 1024, 2048], P('rep', 'shard')
Inputs may be any that keep to these rules, and one draw needn't show every extreme that they name: `segments`: segment numbers never fall along a sequence; each segment holds 1 to 800 positions, one exactly 800. `routes`: each token names 8 different experts. Among the 256 tokens of one device no expert is named more than 144 times, and in every draw some expert is named exactly 144 times by the tokens of some device.
All inputs are finite; a program needn't handle non-finite values.
Results may differ from a plain program's by a relative error of at most 0.025.
Values may be sent and summed in bfloat16 or wider, within the bound.
No kernel may reach another device: no remote copies, remote signals or barrier semaphores. Data moves between devices by JAX's collectives and lax.ppermute only.
A program may use at most 384 MiB of HBM per device.

v0:
```python
import jax
import jax.numpy as jnp
from jax import lax
from jax.sharding import PartitionSpec as P

HEADS = 16
HD = 128
TOP = 8


EPSILON = 1e-05
THETA = 50000.0
MASKED = -1e30


def rms_scale(values):
    return lax.rsqrt(jnp.mean(values * values, axis=-1, keepdims=True) + EPSILON)


def norm_back(grad, normed, scale):
    return scale * (grad - normed * jnp.mean(grad * normed, axis=-1, keepdims=True))


def rope_tables(start, count, width):
    position = (start + jnp.arange(count, dtype=jnp.int32)).astype(jnp.float32)
    inverse = THETA ** (-jnp.arange(width // 2, dtype=jnp.float32) * 2.0 / width)
    angles = position[:, None] * inverse[None, :]
    angles = jnp.concatenate([angles, angles], axis=-1)
    return (jnp.cos(angles)[:, None, :], jnp.sin(angles)[:, None, :])


def rotate(values, cosine, sine):
    half = values.shape[-1] // 2
    turned = jnp.concatenate([-values[..., half:], values[..., :half]], axis=-1)
    return values * cosine + turned * sine


def rotate_back(grad, cosine, sine):
    half = grad.shape[-1] // 2
    scaled = grad * sine
    turned = jnp.concatenate([scaled[..., half:], -scaled[..., :half]], axis=-1)
    return grad * cosine + turned


def slot_numbers(route_rows, experts):
    flat_routes = route_rows.reshape(-1)
    onehot = (flat_routes[:, None] == jnp.arange(experts, dtype=jnp.int32)[None, :]).astype(
        jnp.int32
    )
    before = jnp.cumsum(onehot, axis=0) - onehot
    return jnp.sum(before * onehot, axis=1)


def on_device(
    tokens,
    w_query,
    w_key,
    w_value,
    w_out,
    w_router,
    norm_attn,
    norm_ffn,
    norm_query,
    norm_key,
    w_gate,
    w_up,
    w_down,
    segments,
    routes,
    cotangent,
):
    owned = (
        w_query,
        w_key,
        w_value,
        w_out,
        w_router,
        norm_attn,
        norm_ffn,
        norm_query,
        norm_key,
        w_gate,
        w_up,
        w_down,
    )
    gathered = (
        lax.all_gather(owned[0], "shard", axis=0, tiled=True),
        lax.all_gather(owned[1], "shard", axis=0, tiled=True),
        lax.all_gather(owned[2], "shard", axis=0, tiled=True),
        lax.all_gather(owned[3], "shard", axis=0, tiled=True),
        lax.all_gather(owned[4], "shard", axis=0, tiled=True),
        lax.all_gather(owned[5], "shard", axis=0, tiled=True),
        lax.all_gather(owned[6], "shard", axis=0, tiled=True),
        lax.all_gather(owned[7], "shard", axis=0, tiled=True),
        lax.all_gather(owned[8], "shard", axis=0, tiled=True),
        lax.all_gather(owned[9], "shard", axis=1, tiled=True),
        lax.all_gather(owned[10], "shard", axis=1, tiled=True),
        lax.all_gather(owned[11], "shard", axis=1, tiled=True),
    )
    full_query, full_key, full_value, full_out, full_router = (
        gathered[0],
        gathered[1],
        gathered[2],
        gathered[3],
        gathered[4],
    )
    gain_attn = gathered[5].astype(jnp.float32)
    gain_ffn = gathered[6].astype(jnp.float32)
    gain_query = gathered[7].astype(jnp.float32)
    gain_key = gathered[8].astype(jnp.float32)
    full_gate, full_up, full_down = (gathered[9], gathered[10], gathered[11])
    rows_count = tokens.shape[0]
    width = tokens.shape[1]
    experts = w_router.shape[1]
    local_experts = w_gate.shape[0]
    rep_count = lax.axis_size("rep")
    shard_count = lax.axis_size("shard")
    position = lax.axis_index("shard")
    capacity = max(2, rows_count * TOP * 9 // (8 * experts))
    length = rows_count * shard_count
    score_scale = HD ** (-0.5)
    tokens_f = tokens.astype(jnp.float32)
    scale_in = rms_scale(tokens_f)
    normed_in = tokens_f * scale_in
    input_b = (normed_in * gain_attn).astype(jnp.bfloat16)
    query_raw = jnp.dot(input_b, full_query, preferred_element_type=jnp.float32)
    key_raw = jnp.dot(input_b, full_key, preferred_element_type=jnp.float32)
    value_b = jnp.dot(input_b, full_value, preferred_element_type=jnp.float32).astype(jnp.bfloat16)
    cosine, sine = rope_tables(position * rows_count, rows_count, HD)

    def head_norm(raw, gain):
        shaped = raw.reshape(rows_count, HEADS, HD)
        scale = rms_scale(shaped)
        normed = shaped * scale
        return (normed, scale, rotate(normed * gain, cosine, sine).astype(jnp.bfloat16))

    query_norm, query_scale, query_b = head_norm(query_raw, gain_query)
    key_norm, key_scale, key_b = head_norm(key_raw, gain_key)
    key_all, value_all = (
        lax.all_gather(key_b.reshape(rows_count, HEADS * HD), "shard", axis=0, tiled=True),
        lax.all_gather(value_b, "shard", axis=0, tiled=True),
    )
    key_all = key_all.reshape(length, HEADS, HD)
    value_all = value_all.reshape(length, HEADS, HD)
    segment_all = segments[0]
    segment_own = lax.dynamic_slice_in_dim(segment_all, position * rows_count, rows_count)
    same = segment_own[:, None] == segment_all[None, :]

    def scores_of():
        raw_scores = (
            jnp.einsum("ihd,jhd->hij", query_b, key_all, preferred_element_type=jnp.float32)
            * score_scale
        )
        return jnp.where(same[None, :, :], raw_scores, MASKED)

    scores = scores_of()
    row_max = jnp.max(scores, axis=-1, keepdims=True)
    shifted = jnp.exp(scores - row_max)
    row_total = jnp.sum(shifted, axis=-1, keepdims=True)
    log_total = row_max + jnp.log(row_total)
    attn_probs = (shifted / row_total).astype(jnp.bfloat16)
    attended = jnp.einsum("hij,jhd->ihd", attn_probs, value_all, preferred_element_type=jnp.float32)
    mixed_b = attended.reshape(rows_count, HEADS * HD).astype(jnp.bfloat16)
    hidden_state = tokens_f + jnp.dot(mixed_b, full_out, preferred_element_type=jnp.float32)
    scale_mid = rms_scale(hidden_state)
    normed_mid = hidden_state * scale_mid
    mid_b = (normed_mid * gain_ffn).astype(jnp.bfloat16)
    logits = jnp.dot(mid_b, full_router, preferred_element_type=jnp.float32)
    logit_exp = jnp.exp(logits - jnp.max(logits, axis=-1, keepdims=True))
    router_probs = logit_exp / jnp.sum(logit_exp, axis=-1, keepdims=True)
    route_hits = routes[:, :, None] == jnp.arange(experts, dtype=jnp.int32)[None, None, :]
    chosen = jnp.sum(jnp.where(route_hits, router_probs[:, None, :], 0.0), axis=-1)
    chosen_total = jnp.sum(chosen, axis=1, keepdims=True)
    gates = chosen / chosen_total
    slot = slot_numbers(routes, experts)
    place = routes.reshape(-1) * capacity + slot
    pair_table = (
        jnp.full((experts * capacity,), rows_count * TOP, jnp.int32)
        .at[place]
        .set(jnp.arange(rows_count * TOP, dtype=jnp.int32))
    )
    token_table = pair_table // TOP
    padded_mid = jnp.concatenate([mid_b, jnp.zeros((1, width), jnp.bfloat16)], axis=0)
    sending = padded_mid[token_table].reshape(rep_count, local_experts, capacity, width)
    expert_rows = lax.all_to_all(sending, "rep", split_axis=0, concat_axis=2, tiled=True)[0]
    gate_pre = jnp.einsum(
        "jnd,jdf->jnf", expert_rows, full_gate, preferred_element_type=jnp.float32
    )
    up_pre = jnp.einsum("jnd,jdf->jnf", expert_rows, full_up, preferred_element_type=jnp.float32)
    activated = gate_pre / (1.0 + jnp.exp(-gate_pre))
    hidden_b = (activated * up_pre).astype(jnp.bfloat16)
    expert_out = jnp.einsum(
        "jnf,jfd->jnd", hidden_b, full_down, preferred_element_type=jnp.float32
    ).astype(jnp.bfloat16)
    returned = lax.all_to_all(
        expert_out[None], "rep", split_axis=2, concat_axis=0, tiled=True
    ).reshape(experts * capacity, width)
    picked = returned[place].reshape(rows_count, TOP, width).astype(jnp.float32)
    output = (hidden_state + jnp.sum(gates[:, :, None] * picked, axis=1)).astype(jnp.bfloat16)
    gathered = (
        lax.all_gather(owned[0], "shard", axis=0, tiled=True),
        lax.all_gather(owned[1], "shard", axis=0, tiled=True),
        lax.all_gather(owned[2], "shard", axis=0, tiled=True),
        lax.all_gather(owned[3], "shard", axis=0, tiled=True),
        lax.all_gather(owned[4], "shard", axis=0, tiled=True),
        lax.all_gather(owned[5], "shard", axis=0, tiled=True),
        lax.all_gather(owned[6], "shard", axis=0, tiled=True),
        lax.all_gather(owned[7], "shard", axis=0, tiled=True),
        lax.all_gather(owned[8], "shard", axis=0, tiled=True),
        lax.all_gather(owned[9], "shard", axis=1, tiled=True),
        lax.all_gather(owned[10], "shard", axis=1, tiled=True),
        lax.all_gather(owned[11], "shard", axis=1, tiled=True),
    )
    full_query, full_key, full_value, full_out, full_router = (
        gathered[0],
        gathered[1],
        gathered[2],
        gathered[3],
        gathered[4],
    )
    full_gate, full_up, full_down = (gathered[9], gathered[10], gathered[11])
    grad_out = cotangent.astype(jnp.float32)
    grad_picked = (gates[:, :, None] * grad_out[:, None, :]).astype(jnp.bfloat16)
    grad_gates = jnp.sum(grad_out[:, None, :] * picked, axis=-1)
    padded_grad = jnp.concatenate(
        [grad_picked.reshape(rows_count * TOP, width), jnp.zeros((1, width), jnp.bfloat16)], axis=0
    )
    grad_sending = padded_grad[pair_table].reshape(rep_count, local_experts, capacity, width)
    grad_expert_out = lax.all_to_all(grad_sending, "rep", split_axis=0, concat_axis=2, tiled=True)[
        0
    ]
    grad_hidden = jnp.einsum(
        "jnd,jfd->jnf", grad_expert_out, full_down, preferred_element_type=jnp.float32
    )
    grad_down = jnp.einsum(
        "jnf,jnd->jfd", hidden_b, grad_expert_out, preferred_element_type=jnp.float32
    )
    sigmoid_gate = 1.0 / (1.0 + jnp.exp(-gate_pre))
    grad_gate_pre = (
        grad_hidden * up_pre * sigmoid_gate * (1.0 + gate_pre * (1.0 - sigmoid_gate))
    ).astype(jnp.bfloat16)
    grad_up_pre = (grad_hidden * activated).astype(jnp.bfloat16)
    grad_gate = jnp.einsum(
        "jnd,jnf->jdf", expert_rows, grad_gate_pre, preferred_element_type=jnp.float32
    )
    grad_up = jnp.einsum(
        "jnd,jnf->jdf", expert_rows, grad_up_pre, preferred_element_type=jnp.float32
    )
    grad_rows_in = jnp.einsum(
        "jnf,jdf->jnd", grad_gate_pre, full_gate, preferred_element_type=jnp.float32
    )
    grad_rows_in = (
        grad_rows_in
        + jnp.einsum("jnf,jdf->jnd", grad_up_pre, full_up, preferred_element_type=jnp.float32)
    ).astype(jnp.bfloat16)
    grad_returned = lax.all_to_all(
        grad_rows_in[None], "rep", split_axis=2, concat_axis=0, tiled=True
    ).reshape(experts * capacity, width)
    grad_mid_moe = jnp.sum(
        grad_returned[place].reshape(rows_count, TOP, width).astype(jnp.float32), axis=1
    )
    expert_sums = (
        lax.psum_scatter(
            grad_gate.astype(jnp.bfloat16), "shard", scatter_dimension=1, tiled=True
        ).astype(jnp.float32),
        lax.psum_scatter(
            grad_up.astype(jnp.bfloat16), "shard", scatter_dimension=1, tiled=True
        ).astype(jnp.float32),
        lax.psum_scatter(
            grad_down.astype(jnp.bfloat16), "shard", scatter_dimension=1, tiled=True
        ).astype(jnp.float32),
    )
    grad_chosen = (grad_gates - jnp.sum(grad_gates * gates, axis=1, keepdims=True)) / chosen_total
    grad_probs = jnp.sum(jnp.where(route_hits, grad_chosen[:, :, None], 0.0), axis=1)
    grad_logits = (
        router_probs * (grad_probs - jnp.sum(router_probs * grad_probs, axis=1, keepdims=True))
    ).astype(jnp.bfloat16)
    grad_mid = grad_mid_moe + jnp.einsum(
        "te,de->td", grad_logits, full_router, preferred_element_type=jnp.float32
    )
    grad_gain_ffn = jnp.sum(grad_mid * normed_mid, axis=0)
    grad_state = grad_out + norm_back(grad_mid * gain_ffn, normed_mid, scale_mid)
    grad_state_b = grad_state.astype(jnp.bfloat16)
    grad_mixed = jnp.einsum("td,id->ti", grad_state_b, full_out, preferred_element_type=jnp.float32)
    grad_mixed = grad_mixed.astype(jnp.bfloat16).reshape(rows_count, HEADS, HD)
    again_probs = jnp.exp(scores_of() - log_total)
    grad_probs_attn = jnp.einsum(
        "ihd,jhd->hij", grad_mixed, value_all, preferred_element_type=jnp.float32
    )
    grad_value_all = jnp.einsum(
        "hij,ihd->jhd",
        again_probs.astype(jnp.bfloat16),
        grad_mixed,
        preferred_element_type=jnp.float32,
    )
    grad_scores = (
        again_probs
        * (grad_probs_attn - jnp.sum(again_probs * grad_probs_attn, axis=-1, keepdims=True))
    ).astype(jnp.bfloat16)
    grad_query = (
        jnp.einsum("hij,jhd->ihd", grad_scores, key_all, preferred_element_type=jnp.float32)
        * score_scale
    )
    grad_key_all = (
        jnp.einsum("hij,ihd->jhd", grad_scores, query_b, preferred_element_type=jnp.float32)
        * score_scale
    )
    grad_key_own, grad_value_own = (
        lax.psum_scatter(
            grad_key_all.reshape(length, HEADS * HD).astype(jnp.bfloat16),
            "shard",
            scatter_dimension=0,
            tiled=True,
        ).astype(jnp.float32),
        lax.psum_scatter(
            grad_value_all.reshape(length, HEADS * HD).astype(jnp.bfloat16),
            "shard",
            scatter_dimension=0,
            tiled=True,
        ).astype(jnp.float32),
    )

    def head_back(grad_rot, normed, scale, gain):
        grad_normed = rotate_back(grad_rot, cosine, sine)
        grad_gain = jnp.sum(grad_normed * normed, axis=(0, 1))
        grad_raw = norm_back(grad_normed * gain, normed, scale)
        return (grad_raw.reshape(rows_count, HEADS * HD).astype(jnp.bfloat16), grad_gain)

    grad_query_raw, grad_gain_query = head_back(grad_query, query_norm, query_scale, gain_query)
    grad_key_raw, grad_gain_key = head_back(
        grad_key_own.reshape(rows_count, HEADS, HD), key_norm, key_scale, gain_key
    )
    grad_value_raw = grad_value_own.astype(jnp.bfloat16)
    grad_input = jnp.einsum(
        "ti,di->td", grad_query_raw, full_query, preferred_element_type=jnp.float32
    )
    grad_input = grad_input + jnp.einsum(
        "ti,di->td", grad_key_raw, full_key, preferred_element_type=jnp.float32
    )
    grad_input = grad_input + jnp.einsum(
        "ti,di->td", grad_value_raw, full_value, preferred_element_type=jnp.float32
    )
    grad_gain_attn = jnp.sum(grad_input * normed_in, axis=0)
    tokens_grad = (grad_state + norm_back(grad_input * gain_attn, normed_in, scale_in)).astype(
        jnp.bfloat16
    )
    grad_wq = jnp.einsum("td,ti->di", input_b, grad_query_raw, preferred_element_type=jnp.float32)
    grad_wk = jnp.einsum("td,ti->di", input_b, grad_key_raw, preferred_element_type=jnp.float32)
    grad_wv = jnp.einsum("td,ti->di", input_b, grad_value_raw, preferred_element_type=jnp.float32)
    grad_out_proj = jnp.einsum(
        "ti,td->id", mixed_b, grad_state_b, preferred_element_type=jnp.float32
    )
    grad_router = jnp.einsum("td,te->de", mid_b, grad_logits, preferred_element_type=jnp.float32)
    layer_parts = (
        lax.psum_scatter(
            grad_wq.astype(jnp.bfloat16), "shard", scatter_dimension=0, tiled=True
        ).astype(jnp.float32),
        lax.psum_scatter(
            grad_wk.astype(jnp.bfloat16), "shard", scatter_dimension=0, tiled=True
        ).astype(jnp.float32),
        lax.psum_scatter(
            grad_wv.astype(jnp.bfloat16), "shard", scatter_dimension=0, tiled=True
        ).astype(jnp.float32),
        lax.psum_scatter(
            grad_out_proj.astype(jnp.bfloat16), "shard", scatter_dimension=0, tiled=True
        ).astype(jnp.float32),
        lax.psum_scatter(
            grad_router.astype(jnp.bfloat16), "shard", scatter_dimension=0, tiled=True
        ).astype(jnp.float32),
        lax.psum_scatter(
            grad_gain_attn.astype(jnp.bfloat16), "shard", scatter_dimension=0, tiled=True
        ).astype(jnp.float32),
        lax.psum_scatter(
            grad_gain_ffn.astype(jnp.bfloat16), "shard", scatter_dimension=0, tiled=True
        ).astype(jnp.float32),
        lax.psum_scatter(
            grad_gain_query.astype(jnp.bfloat16), "shard", scatter_dimension=0, tiled=True
        ).astype(jnp.float32),
        lax.psum_scatter(
            grad_gain_key.astype(jnp.bfloat16), "shard", scatter_dimension=0, tiled=True
        ).astype(jnp.float32),
    )
    part_query, part_key, part_value, part_out, part_router = (
        layer_parts[0],
        layer_parts[1],
        layer_parts[2],
        layer_parts[3],
        layer_parts[4],
    )
    part_attn, part_ffn, part_hquery, part_hkey = (
        layer_parts[5],
        layer_parts[6],
        layer_parts[7],
        layer_parts[8],
    )
    layer_sums = (
        lax.psum(part_query.astype(jnp.bfloat16), "rep").astype(jnp.float32),
        lax.psum(part_key.astype(jnp.bfloat16), "rep").astype(jnp.float32),
        lax.psum(part_value.astype(jnp.bfloat16), "rep").astype(jnp.float32),
        lax.psum(part_out.astype(jnp.bfloat16), "rep").astype(jnp.float32),
        lax.psum(part_router.astype(jnp.bfloat16), "rep").astype(jnp.float32),
        lax.psum(part_attn.astype(jnp.bfloat16), "rep").astype(jnp.float32),
        lax.psum(part_ffn.astype(jnp.bfloat16), "rep").astype(jnp.float32),
        lax.psum(part_hquery.astype(jnp.bfloat16), "rep").astype(jnp.float32),
        lax.psum(part_hkey.astype(jnp.bfloat16), "rep").astype(jnp.float32),
    )
    return (
        output,
        tokens_grad,
        layer_sums[0],
        layer_sums[1],
        layer_sums[2],
        layer_sums[3],
        layer_sums[4],
        layer_sums[5],
        layer_sums[6],
        layer_sums[7],
        layer_sums[8],
        expert_sums[0],
        expert_sums[1],
        expert_sums[2],
    )


def solution(mesh):
    return jax.shard_map(
        on_device,
        mesh=mesh,
        in_specs=(
            P(("rep", "shard"), None),
            P("shard", None),
            P("shard", None),
            P("shard", None),
            P("shard", None),
            P("shard", None),
            P("shard"),
            P("shard"),
            P("shard"),
            P("shard"),
            P("rep", "shard", None),
            P("rep", "shard", None),
            P("rep", "shard", None),
            P("rep", None),
            P(("rep", "shard"), None),
            P(("rep", "shard"), None),
        ),
        out_specs=(
            P(("rep", "shard"), None),
            P(("rep", "shard"), None),
            P("shard", None),
            P("shard", None),
            P("shard", None),
            P("shard", None),
            P("shard", None),
            P("shard"),
            P("shard"),
            P("shard"),
            P("shard"),
            P("rep", "shard", None),
            P("rep", "shard", None),
            P("rep", "shard", None),
        ),
        check_vma=False,
    )
```

profile of v0, /device:TPU:0, one launch (start us, length us, event | category | flops | bytes accessed | tf_op | source)
XLA Modules:
  0.0 2282.7 jit_solution(10785380320242982940)
XLA Ops:
  11.3 8.3 all-reduce.11
  29.0 41.7 %all-gather.18.cloned.1.call-done = bf16[2048,2048]{1,0:T(8,128)(2,1)} async-done(((bf16[512,2048]{1,0:T(8,128)(2,1)}), bf16[2048,2048]{1,0:T(8,128)(2,1)}) %all-gather.18.cloned.1.call-update) | async-done | bytes 8388624 | tf_op jit(solution)/shard_map/all_gather | solution.py:88
  70.7 5.8 fusion.57
  83.3 47.3 %all-gather.16.cloned.1.call-done = bf16[2048,2048]{1,0:T(8,128)(2,1)} async-done(((bf16[512,2048]{1,0:T(8,128)(2,1)}), bf16[2048,2048]{1,0:T(8,128)(2,1)}) %all-gather.16.cloned.1.call-update) | async-done | bytes 8388624 | tf_op jit(solution)/shard_map/all_gather | solution.py:87
  130.6 5.8 convolution_bitcast_fusion
  159.1 31.3 %all-gather.12.cloned.1.call-done = bf16[2048,2048]{1,0:T(8,128)(2,1)} async-done(((bf16[512,2048]{1,0:T(8,128)(2,1)}), bf16[2048,2048]{1,0:T(8,128)(2,1)}) %all-gather.12.cloned.1.call-update) | async-done | bytes 8388624 | tf_op jit(solution)/shard_map/all_gather | solution.py:89
  190.4 6.7 convolution_convert_fusion.9
  209.0 8.1 scatter_custom_fusion
  217.4 9.6 all-gather.20.cloned.1.call-done
  227.0 6.4 copy.270
  238.8 5.8 copy-done
  248.2 15.2 all-gather.14.cloned.1.call-done
  263.5 9.9 fusion.37
  273.3 49.8 %all-gather.22.cloned.1.call-done = bf16[2048,2048]{1,0:T(8,128)(2,1)} async-done(((bf16[512,2048]{1,0:T(8,128)(2,1)}), bf16[2048,2048]{1,0:T(8,128)(2,1)}) %all-gather.22.cloned.1.call-update) | async-done | bytes 8388624 | tf_op jit(solution)/shard_map/all_gather | solution.py:90
  323.2 5.8 multiply_reduce_fusion.7
  330.7 9.8 gather_fusion
  349.1 5.7 all_gather.60
  361.0 8.6 concatenate.35
  369.6 22.8 gather_fusion.2
  392.4 159.8 %all-to-all-done = bf16[8,2,144,2048]{3,2,1,0:T(8,128)(2,1)} async-done(((bf16[8,2,144,2048]{3,2,1,0:T(8,128)(2,1)}), bf16[8,2,144,2048]{3,2,1,0:T(8,128)(2,1)}, u32[]{:S(2)}, u32[]{:S(2)}) %all-to-all-start) | async-done | bytes 9437216 | tf_op jit(solution)/shard_map/all_to_all | solution.py:185
  557.9 9.6 copy.239
  567.5 194.8 %all-to-all-done.2 = bf16[8,2,144,2048]{3,2,1,0:T(8,128)(2,1)} async-done(((bf16[8,2,144,2048]{3,2,1,0:T(8,128)(2,1)}), bf16[8,2,144,2048]{3,2,1,0:T(8,128)(2,1)}, u32[]{:S(2)}, u32[]{:S(2)}) %all-to-all-start.2) | async-done | bytes 9437216 | tf_op jit(solution)/shard_map/all_to_all | solution.py:229
  762.3 9.3 copy.243
  771.6 17.3 fusion.67
  788.9 17.2 fusion.66
  806.1 22.7 multiply_convert_fusion.1
  828.8 14.4 fusion.6
  843.2 27.9 %copy.240 = bf16[1,2,1152,2048]{3,1,0,2:T(2,128)(2,1)} copy(bf16[1,2,1152,2048]{3,2,1,0:T(8,128)(2,1)S(1)} %fusion.6) | data formatting | bytes 18874368 | tf_op jit(solution)/shard_map/broadcast_in_dim | solution.py:196
  876.2 17.4 fusion.68
  893.5 18.6 fusion.7
  912.1 18.2 copy.244
  930.3 150.2 %all-to-all-done.1 = bf16[1,2,1152,2048]{3,1,0,2:T(2,128)(2,1)} async-done(((bf16[1,2,1152,2048]{3,1,0,2:T(2,128)(2,1)}), bf16[1,2,1152,2048]{3,1,0,2:T(2,128)(2,1)}, u32[]{:S(2)}, u32[]{:S(2)}) %all-to-all-start.1) | async-done | bytes 9437216 | tf_op jit(solution)/shard_map/all_to_all | solution.py:195
  1086.1 11.7 copy.241
  1097.9 21.5 gather_fusion.1
  1119.5 9.5 fusion.1
  1129.2 161.1 %all-to-all-done.3 = bf16[1,2,1152,2048]{3,1,0,2:T(2,128)(2,1)} async-done(((bf16[1,2,1152,2048]{3,1,0,2:T(2,128)(2,1)}), bf16[1,2,1152,2048]{3,1,0,2:T(2,128)(2,1)}, u32[]{:S(2)}, u32[]{:S(2)}) %all-to-all-start.3) | async-done | bytes 9437216 | tf_op jit(solution)/shard_map/all_to_all | solution.py:256
  1290.3 11.8 copy.245
  1302.0 21.4 gather_fusion.3
  1323.5 11.5 convert_reduce_fusion
  1344.2 8.7 fusion.21
  1353.4 14.7 multiply_reduce_fusion
  1368.1 12.6 multiply_convert_fusion
  1385.3 6.4 copy.267
  1393.6 5.6 convolution_convert_fusion.1
  1400.1 7.7 bitcast_multiply_fusion.2
  1412.4 5.9 convolution_convert_fusion.4
  1418.4 7.1 convolution_convert_fusion.2
  1425.9 18.0 reduce-scatter.11.cloned.1.call-done
  1455.0 8.1 multiply_reduce_fusion.1
  1464.1 5.8 convolution_convert_fusion.3
  1470.0 17.8 convolution_convert_fusion.5
  1488.3 17.3 convolution_convert_fusion.6
  1505.7 17.2 convolution_convert_fusion.7
  1526.0 66.5 %reduce-scatter.15.cloned.1.call-done = bf16[512,2048]{1,0:T(8,128)(2,1)} async-done(((bf16[2048,2048]{1,0:T(8,128)(2,1)}), bf16[512,2048]{1,0:T(8,128)(2,1)}) %reduce-scatter.15.cloned.1.call-update) | async-done | bytes 2097168 | tf_op jit(solution)/shard_map/reduce_scatter | solution.py:355
  1592.5 74.1 %reduce-scatter.19.cloned.1.call-done = bf16[512,2048]{1,0:T(8,128)(2,1)} async-done(((bf16[2048,2048]{1,0:T(8,128)(2,1)}), bf16[512,2048]{1,0:T(8,128)(2,1)}) %reduce-scatter.19.cloned.1.call-update) | async-done | bytes 2097168 | tf_op jit(solution)/shard_map/reduce_scatter | solution.py:361
  1666.6 74.4 %reduce-scatter.17.cloned.1.call-done = bf16[512,2048]{1,0:T(8,128)(2,1)} async-done(((bf16[2048,2048]{1,0:T(8,128)(2,1)}), bf16[512,2048]{1,0:T(8,128)(2,1)}) %reduce-scatter.17.cloned.1.call-update) | async-done | bytes 2097168 | tf_op jit(solution)/shard_map/reduce_scatter | solution.py:358
  1742.3 7.4 fusion.69
  1749.8 65.4 %reduce-scatter.29.cloned.1.call-done = bf16[2,256,2048]{2,1,0:T(8,128)(2,1)} async-done(((bf16[2,1024,2048]{2,1,0:T(8,128)(2,1)}), bf16[2,256,2048]{2,1,0:T(8,128)(2,1)}) %reduce-scatter.29.cloned.1.call-update) | async-done | bytes 2097168 | tf_op jit(solution)/shard_map/reduce_scatter | solution.py:269
  1819.3 70.2 %reduce-scatter.27.cloned.1.call-done = bf16[2,512,1024]{2,1,0:T(8,128)(2,1)} async-done(((bf16[2,2048,1024]{2,1,0:T(8,128)(2,1)}), bf16[2,512,1024]{2,1,0:T(8,128)(2,1)}) %reduce-scatter.27.cloned.1.call-update) | async-done | bytes 2097168 | tf_op jit(solution)/shard_map/reduce_scatter | solution.py:266
  1893.6 70.1 %reduce-scatter.25.cloned.1.call-done = bf16[2,512,1024]{2,1,0:T(8,128)(2,1)} async-done(((bf16[2,2048,1024]{2,1,0:T(8,128)(2,1)}), bf16[2,512,1024]{2,1,0:T(8,128)(2,1)}) %reduce-scatter.25.cloned.1.call-update) | async-done | bytes 2097168 | tf_op jit(solution)/shard_map/reduce_scatter | solution.py:263
  1968.0 6.5 convolution_add_fusion.2
  1978.7 6.1 all-reduce.10
  1986.4 38.4 %all-reduce.8 = (bf16[512,16]{0,1:T(8,128)(2,1)S(1)}, bf16[512]{0:T(512)(128)(2,1)S(1)}, bf16[512]{0:T(512)(128)(2,1)S(1)}, bf16[32]{0:T(256)(128)(2,1)S(1)}, bf16[32]{0:T(256)(128)(2,1)S(1)}) all-reduce(bf16[512,16]{0,1:T(8,128)(2,1)} %reduce-scatter.23.cloned.1.call-done, ...), channel_id=1, replica_groups=mesh['rep'=8,'shard'=4] {'rep'}, use_global_device_ids=true, to_apply=%region_36.37 | all-reduce | flops 9280 | bytes 37120 | tf_op jit(solution)/shard_map/psum | solution.py:401
  2030.8 233.0 %all-reduce.14.cloned.1.call-done = (bf16[512,2048]{1,0:T(8,128)(2,1)}, bf16[512,2048]{1,0:T(8,128)(2,1)}, bf16[512,2048]{1,0:T(8,128)(2,1)}, bf16[512,2048]{1,0:T(8,128)(2,1)}) async-done(((bf16[512,2048]{1,0:T(8,128)(2,1)}, bf16[512,2048]{1,0:T(8,128)(2,1)}, bf16[512,2048]{1,0:T(8,128)(2,1)}, bf16[512,2048]{1,0:T(8,128)(2,1)}), (bf16[512,2048]{1,0:T(8,128)(2,1)}, bf16[512,2048]{1,0:T(8,128)(2,1)}, ...) | async-done | bytes 8388624 | tf_op jit(solution)/shard_map/psum | solution.py:397
  (352 shorter events, 169.5 us)
Async XLA Ops:
  7.2 12.9 copy-start.83
  7.2 63.4 %all-gather.18.cloned.1.call-start = ((), (), s32[]{:S(2)}) async-start(), calls=%async_computation.17 | async-start | bytes 10485760 | tf_op jit(solution)/shard_map/all_gather | solution.py:88
  8.0 122.6 %all-gather.16.cloned.1.call-start = ((), (), s32[]{:S(2)}) async-start(), calls=%async_computation.16 | async-start | bytes 10485760 | tf_op jit(solution)/shard_map/all_gather | solution.py:87
  8.7 19.9 copy-start.2
  8.7 181.7 %all-gather.12.cloned.1.call-start = ((), (), s32[]{:S(2)}) async-start(), calls=%async_computation.14 | async-start | bytes 10485760 | tf_op jit(solution)/shard_map/all_gather | solution.py:89
  9.5 217.5 %all-gather.20.cloned.1.call-start = ((), (), s32[]{:S(2)}) async-start(), calls=%async_computation.18 | async-start | bytes 5242880 | tf_op jit(solution)/shard_map/all_gather | solution.py:140
  20.1 56.3 %copy-start.80 = (f32[128]{0:T(128)}, f32[128]{0:T(128)S(1)}, u32[]{:S(2)}) copy-start(f32[128]{0:T(128)S(1)} %convert_element_type.245) | copy-start | bytes 1540
  25.3 165.1 %copy-start.36 = (f32[4,1,512]{2,1,0:T(1,128)}, f32[4,1,512]{2,1,0:T(1,128)S(1)}, u32[]{:S(2)}) copy-start(f32[4,1,512]{2,1,0:T(1,128)S(1)} %convert_element_type.309) | copy-start | bytes 24580
  26.6 121.1 %copy-start.26 = (f32[256,128]{0,1:T(8,128)}, f32[256,128]{0,1:T(8,128)S(1)}, u32[]{:S(2)}) copy-start(f32[256,128]{0,1:T(8,128)S(1)} %get-tuple-element.64) | copy-start | bytes 393220
  26.6 121.1 %copy-start.31 = (f32[256,128]{0,1:T(8,128)}, f32[256,128]{0,1:T(8,128)S(1)}, u32[]{:S(2)}) copy-start(f32[256,128]{0,1:T(8,128)S(1)} %get-tuple-element.63) | copy-start | bytes 393220
  28.9 47.5 %copy-start.62 = (f32[256]{0:T(256)}, f32[256]{0:T(256)S(1)}, u32[]{:S(2)}) copy-start(f32[256]{0:T(256)S(1)} %add_rsqrt_fusion.3) | copy-start | bytes 3076
  28.9 124.4 %copy-start.54 = (f32[2048]{0:T(1024)}, f32[2048]{0:T(1024)S(1)}, u32[]{:S(2)}) copy-start(f32[2048]{0:T(1024)S(1)} %broadcast_bitcast_fusion) | copy-start | bytes 24580
  153.4 37.1 %copy-start.63 = (f32[256]{0:T(256)S(1)}, f32[256]{0:T(256)}, u32[]{:S(2)}) copy-start(f32[256]{0:T(256)} %copy-done.62) | copy-start | bytes 3076
  158.8 39.0 %copy-start.52 = (s32[256,8]{0,1:T(8,128)S(1)}, s32[256,8]{0,1:T(8,128)}, u32[]{:S(2)}) copy-start(s32[256,8]{0,1:T(8,128)} %param.30) | copy-start | bytes 24580
  158.8 39.3 %copy-start.84 = (bf16[512]{0:T(512)(128)(2,1)S(1)}, bf16[512]{0:T(512)(128)(2,1)}, u32[]{:S(2)}) copy-start(bf16[512]{0:T(512)(128)(2,1)} %param.23) | copy-start | bytes 3076
  158.9 104.6 %all-gather.14.cloned.1.call-start = ((), (), s32[]{:S(2)}) async-start(), calls=%async_computation.15 | async-start | bytes 5242880 | tf_op jit(solution)/shard_map/all_gather | solution.py:141
  197.2 19.9 copy-start.79
  197.2 126.0 %all-gather.22.cloned.1.call-start = ((), (), s32[]{:S(2)}) async-start(), calls=%async_computation.19 | async-start | bytes 10485760 | tf_op jit(solution)/shard_map/all_gather | solution.py:90
  203.3 125.7 %copy-start.50 = (f32[4,1,512]{2,1,0:T(1,128)}, f32[4,1,512]{2,1,0:T(1,128)S(1)}, u32[]{:S(2)}) copy-start(f32[4,1,512]{2,1,0:T(1,128)S(1)} %convert_element_type.310) | copy-start | bytes 24580
  217.4 16.0 copy-start.16
  238.8 24.6 %copy-start.48 = (f32[16,256]{1,0:T(8,128)}, f32[16,256]{1,0:T(8,128)S(1)}, u32[]{:S(2)}) copy-start(f32[16,256]{1,0:T(8,128)S(1)} %get-tuple-element.69) | copy-start | bytes 49156
  248.2 25.1 %copy-start.60 = (f32[16,256]{1,0:T(8,128)}, f32[16,256]{1,0:T(8,128)S(1)}, u32[]{:S(2)}) copy-start(f32[16,256]{1,0:T(8,128)S(1)} %fusion.3) | copy-start | bytes 49156
  273.3 55.7 %copy-start.20 = (bf16[16,128,256]{2,1,0:T(8,128)(2,1)}, bf16[16,128,256]{2,1,0:T(8,128)(2,1)S(1)}, u32[]{:S(2)}) copy-start(bf16[16,128,256]{2,1,0:T(8,128)(2,1)S(1)} %fusion.37) | copy-start | bytes 3145732
  330.6 24.1 %copy-start.15 = (bf16[256,2048]{1,0:T(8,128)(2,1)}, bf16[256,2048]{1,0:T(8,128)(2,1)S(1)}, u32[]{:S(2)}) copy-start(bf16[256,2048]{1,0:T(8,128)(2,1)S(1)} %multiply_convert_fusion.6) | copy-start | bytes 3145732
  340.6 211.6 %all-to-all-start = ((bf16[8,2,144,2048]{3,2,1,0:T(8,128)(2,1)}), bf16[8,2,144,2048]{3,2,1,0:T(8,128)(2,1)}, u32[]{:S(2)}, u32[]{:S(2)}) async-start(bf16[8,2,144,2048]{3,2,1,0:T(8,128)(2,1)} %bitcast.168), calls=%async_computation | async-start | bytes 18874368 | tf_op jit(solution)/shard_map/all_to_all | solution.py:185
  346.1 425.5 %all-gather.26.cloned.1.call-start = ((), (), s32[]{:S(2)}) async-start(), calls=%async_computation.21 | async-start | bytes 10485760 | tf_op jit(solution)/shard_map/all_gather | solution.py:97
  346.8 442.0 %all-gather.24.cloned.1.call-start = ((), (), s32[]{:S(2)}) async-start(), calls=%async_computation.20 | async-start | bytes 10485760 | tf_op jit(solution)/shard_map/all_gather | solution.py:96
  349.1 11.9 copy-start.11
  355.1 14.4 copy-start.67
  355.2 14.4 copy-start.73
  552.2 210.2 %all-to-all-start.2 = ((bf16[8,2,144,2048]{3,2,1,0:T(8,128)(2,1)}), bf16[8,2,144,2048]{3,2,1,0:T(8,128)(2,1)}, u32[]{:S(2)}, u32[]{:S(2)}) async-start(bf16[8,2,144,2048]{3,2,1,0:T(8,128)(2,1)} %bitcast.169), calls=%async_computation.2 | async-start | bytes 18874368 | tf_op jit(solution)/shard_map/all_to_all | solution.py:229
  557.2 248.9 %all-gather.28.cloned.1.call-start = ((), (), s32[]{:S(2)}) async-start(), calls=%async_computation.22 | async-start | bytes 10485760 | tf_op jit(solution)/shard_map/all_gather | solution.py:98
  871.1 209.4 %all-to-all-start.1 = ((bf16[1,2,1152,2048]{3,1,0,2:T(2,128)(2,1)}), bf16[1,2,1152,2048]{3,1,0,2:T(2,128)(2,1)}, u32[]{:S(2)}, u32[]{:S(2)}) async-start(bf16[1,2,1152,2048]{3,1,0,2:T(2,128)(2,1)} %copy.240), calls=%async_computation.1 | async-start | bytes 18874368 | tf_op jit(solution)/shard_map/all_to_all | solution.py:195
  930.3 155.7 %copy-start.66 = (s32[2048,1]{0,1:T(1,128)S(1)}, s32[2048,1]{0,1:T(1,128)}, u32[]{:S(2)}) copy-start(s32[2048,1]{0,1:T(1,128)} %copy-done.65) | copy-start | bytes 24580
  930.3 155.8 %copy-start.49 = (f32[16,256]{1,0:T(8,128)S(1)}, f32[16,256]{1,0:T(8,128)}, u32[]{:S(2)}) copy-start(f32[16,256]{1,0:T(8,128)} %copy-done.48) | copy-start | bytes 49156
  930.3 155.8 %copy-start.61 = (f32[16,256]{1,0:T(8,128)S(1)}, f32[16,256]{1,0:T(8,128)}, u32[]{:S(2)}) copy-start(f32[16,256]{1,0:T(8,128)} %copy-done.60) | copy-start | bytes 49156
  1080.6 209.7 %all-to-all-start.3 = ((bf16[1,2,1152,2048]{3,1,0,2:T(2,128)(2,1)}), bf16[1,2,1152,2048]{3,1,0,2:T(2,128)(2,1)}, u32[]{:S(2)}, u32[]{:S(2)}) async-start(bf16[1,2,1152,2048]{3,1,0,2:T(2,128)(2,1)} %copy.244), calls=%async_computation.3 | async-start | bytes 18874368 | tf_op jit(solution)/shard_map/all_to_all | solution.py:256
  1085.6 332.8 %reduce-scatter.13.cloned.1.call-start = ((), (), s32[]{:S(2)}) async-start(), calls=%async_computation.24 | async-start | bytes 5242880 | tf_op jit(solution)/shard_map/reduce_scatter | solution.py:315
  1097.9 21.5 copy-start.12
  1097.9 21.5 copy-start.34
  1119.4 9.6 copy-start.59
  1119.4 9.6 copy-start.53
  1119.4 9.7 copy-start.45
  1119.4 9.7 copy-start.68
  1119.4 9.7 copy-start.74
  1129.2 205.8 %copy-start.56 = (bf16[256,16]{0,1:T(8,128)(2,1)}, bf16[256,16]{0,1:T(8,128)(2,1)S(1)}, u32[]{:S(2)}) copy-start(bf16[256,16]{0,1:T(8,128)(2,1)S(1)} %multiply_convert_fusion.7) | copy-start | bytes 24580
  1323.5 11.5 copy-start.7
  1323.5 11.5 copy-start.39
  1323.5 11.5 copy-start.51
  1323.5 11.5 copy-start.70
  1323.5 14.6 copy-start.22
  1352.9 90.9 %reduce-scatter.11.cloned.1.call-start = ((), (), s32[]{:S(2)}) async-start(), calls=%async_computation.23 | async-start | bytes 5242880 | tf_op jit(solution)/shard_map/reduce_scatter | solution.py:309
  1368.1 12.6 copy-start.17
  1391.8 134.2 %reduce-scatter.21.cloned.1.call-start = ((), (), s32[]{:S(2)}) async-start(), calls=%async_computation.28 | async-start | bytes 10485760 | tf_op jit(solution)/shard_map/reduce_scatter | solution.py:364
  1399.2 193.3 %reduce-scatter.15.cloned.1.call-start = ((), (), s32[]{:S(2)}) async-start(), calls=%async_computation.25 | async-start | bytes 10485760 | tf_op jit(solution)/shard_map/reduce_scatter | solution.py:355
  1418.4 248.3 %reduce-scatter.19.cloned.1.call-start = ((), (), s32[]{:S(2)}) async-start(), calls=%async_computation.27 | async-start | bytes 10485760 | tf_op jit(solution)/shard_map/reduce_scatter | solution.py:361
  1425.6 20.8 copy-start.32
  1425.6 315.4 %reduce-scatter.17.cloned.1.call-start = ((), (), s32[]{:S(2)}) async-start(), calls=%async_computation.26 | async-start | bytes 10485760 | tf_op jit(solution)/shard_map/reduce_scatter | solution.py:358
  1469.9 345.3 %reduce-scatter.29.cloned.1.call-start = ((), (), s32[]{:S(2)}) async-start(), calls=%async_computation.32 | async-start | bytes 10485760 | tf_op jit(solution)/shard_map/reduce_scatter | solution.py:269
  1487.8 401.7 %reduce-scatter.27.cloned.1.call-start = ((), (), s32[]{:S(2)}) async-start(), calls=%async_computation.31 | async-start | bytes 10485760 | tf_op jit(solution)/shard_map/reduce_scatter | solution.py:266
  1505.7 458.1 %reduce-scatter.25.cloned.1.call-start = ((), (), s32[]{:S(2)}) async-start(), calls=%async_computation.30 | async-start | bytes 10485760 | tf_op jit(solution)/shard_map/reduce_scatter | solution.py:263
  1522.9 463.5 %reduce-scatter.23.cloned.1.call-start = ((), (), s32[]{:S(2)}) async-start(), calls=%async_computation.29 | async-start | bytes 81920 | tf_op jit(solution)/shard_map/reduce_scatter | solution.py:367
  1525.7 738.1 %all-reduce.14.cloned.1.call-start = ((), (), s32[]{:S(2)}) async-start(), calls=%async_computation.33 | async-start | bytes 16777216 | tf_op jit(solution)/shard_map/psum | solution.py:397
  1963.8 10.8 slice-start.2
  (51 other events, 150.5 us)
Sparse Core Ops, SparseCore 0:
  9.6 60.9 all-gather.17
  72.2 58.2 all-gather.15
  132.1 58.2 all-gather.11
  192.4 34.4 all-gather.19
  228.9 34.4 all-gather.13
  264.9 58.2 all-gather.21
  348.5 58.7 all-gather.25
  408.8 58.2 all-gather.23
  559.6 58.6 all-gather.27
  1353.0 42.9 reduce-scatter.12
  1399.3 44.5 reduce-scatter.10
  1446.3 71.6 reduce-scatter.20
  1520.7 71.7 reduce-scatter.14
  1594.9 71.6 reduce-scatter.18
  1669.3 71.7 reduce-scatter.16
  1743.5 71.6 reduce-scatter.28
  1817.8 71.7 reduce-scatter.26
  1892.0 71.7 reduce-scatter.24
  1966.9 19.4 reduce-scatter.22
  1990.8 272.9 all-reduce.13
where the time goes:
time: 2290 us; the launch traced here: 2280 us
  waiting for transfers between devices  1540 us (67%)
  matrix products  285 us (12%)
  local copies, waits for them, and re-layouts  236 us (10%)
  other arithmetic  113 us (5%)
  blocking collectives  68.8 us (3%)
  starting transfers between devices  23.4 us (1%)
    psum x1, waiting for transfers between devices, on_device(): lax.psum(part_query.astype(jnp.bfloat16), 'rep').astype(jnp.float32)  233 us
    all_to_all x1, waiting for transfers between devices, on_device(): lax.all_to_all(grad_sending, 'rep', split_axis=0, concat_axis=2, tiled=True)  195 us
    all_to_all x1, waiting for transfers between devices, on_device(): lax.all_to_all(grad_rows_in[None], 'rep', split_axis=2, concat_axis=0, ti...  161 us
    all_to_all x1, waiting for transfers between devices, on_device(): lax.all_to_all(sending, 'rep', split_axis=0, concat_axis=2, tiled=True)[0]  160 us
    all_to_all x1, waiting for transfers between devices, on_device(): lax.all_to_all(expert_out[None], 'rep', split_axis=2, concat_axis=0, tile...  150 us
    reduce_scatter x1, waiting for transfers between devices, on_device(): lax.psum_scatter(grad_wk.astype(jnp.bfloat16), 'shard', scatter_dimension...  74.4 us
    reduce_scatter x1, waiting for transfers between devices, on_device(): lax.psum_scatter(grad_wv.astype(jnp.bfloat16), 'shard', scatter_dimension...  74.1 us
    reduce_scatter x1, waiting for transfers between devices, on_device(): lax.psum_scatter(grad_up.astype(jnp.bfloat16), 'shard', scatter_dimension...  70.2 us
  transfers between devices with their start and end apart: 24, of which 19 were waited for; matrix products, arithmetic and copies ran while one was open for 20% of the time, Pallas kernels for 0%

commit v1 on v0

v1 whole, which is shorter than its diff:
```python
import functools

import jax
import jax.numpy as jnp
from jax import lax
from jax.experimental import pallas as pl
from jax.experimental.pallas import tpu as pltpu
from jax.sharding import PartitionSpec as P

HEADS = 16
HD = 128
TOP = 8

EPSILON = 1e-05
THETA = 50000.0
MASKED = -1e30
BF = jnp.bfloat16
F32 = jnp.float32
QCHUNK = 256


def rms_scale(values):
    return lax.rsqrt(jnp.mean(values * values, axis=-1, keepdims=True) + EPSILON)


def norm_back(grad, normed, scale):
    return scale * (grad - normed * jnp.mean(grad * normed, axis=-1, keepdims=True))


def dot_t(left, right):
    return lax.dot_general(left, right, (((1,), (1,)), ((), ())), preferred_element_type=F32)


def t_dot(left, right):
    return lax.dot_general(left, right, (((0,), (0,)), ((), ())), preferred_element_type=F32)


def attend_forward(q_ref, k_ref, v_ref, cos_ref, sin_ref, gq_ref, gk_ref, segc_ref, segr_ref, o_ref, kb_ref):
    length = q_ref.shape[0]
    k_raw = k_ref[...]
    k_gained = k_raw * rms_scale(k_raw) * gk_ref[...]
    kb_ref[...] = (
        k_gained * cos_ref[...] + pltpu.roll(k_gained, HD // 2, 1) * sin_ref[...]
    ).astype(BF)

    def step(i, carry):
        rows = pl.ds(pl.multiple_of(i * QCHUNK, QCHUNK), QCHUNK)
        q_raw = q_ref[rows, :]
        gained = q_raw * rms_scale(q_raw) * gq_ref[...]
        qb = (gained * cos_ref[rows, :] + pltpu.roll(gained, HD // 2, 1) * sin_ref[rows, :]).astype(BF)
        scores = dot_t(qb, kb_ref[...]) * (HD**-0.5)
        scores = jnp.where(segc_ref[rows, :] == segr_ref[...], scores, MASKED)
        shifted = jnp.exp(scores - jnp.max(scores, axis=-1, keepdims=True))
        total = jnp.sum(shifted, axis=-1, keepdims=True)
        probs = (shifted * (1.0 / total)).astype(BF)
        o_ref[rows, :] = jnp.dot(probs, v_ref[...], preferred_element_type=F32).astype(BF)
        return carry

    lax.fori_loop(0, length // QCHUNK, step, 0)


def attend_backward(
    q_ref,
    k_ref,
    v_ref,
    do_ref,
    cos_ref,
    sin_ref,
    gq_ref,
    gk_ref,
    segc_ref,
    segr_ref,
    dq_ref,
    dk_ref,
    dv_ref,
    gains_ref,
    kb_ref,
    dk_acc,
    dv_acc,
):
    length = q_ref.shape[0]
    scale = HD**-0.5

    @pl.when(pl.program_id(0) == 0)
    def _():
        gains_ref[...] = jnp.zeros_like(gains_ref)

    k_raw = k_ref[...]
    k_scale = rms_scale(k_raw)
    k_norm = k_raw * k_scale
    k_gained = k_norm * gk_ref[...]
    kb_ref[...] = (
        k_gained * cos_ref[...] + pltpu.roll(k_gained, HD // 2, 1) * sin_ref[...]
    ).astype(BF)
    dk_acc[...] = jnp.zeros_like(dk_acc)
    dv_acc[...] = jnp.zeros_like(dv_acc)

    def step(i, carry):
        rows = pl.ds(pl.multiple_of(i * QCHUNK, QCHUNK), QCHUNK)
        cosine, sine = cos_ref[rows, :], sin_ref[rows, :]
        q_raw = q_ref[rows, :]
        q_scale = rms_scale(q_raw)
        q_norm = q_raw * q_scale
        gained = q_norm * gq_ref[...]
        qb = (gained * cosine + pltpu.roll(gained, HD // 2, 1) * sine).astype(BF)
        scores = dot_t(qb, kb_ref[...]) * scale
        scores = jnp.where(segc_ref[rows, :] == segr_ref[...], scores, MASKED)
        shifted = jnp.exp(scores - jnp.max(scores, axis=-1, keepdims=True))
        total = jnp.sum(shifted, axis=-1, keepdims=True)
        probs = shifted * (1.0 / total)
        grad_o = do_ref[rows, :]
        grad_probs = dot_t(grad_o, v_ref[...])
        dv_acc[...] += t_dot(probs.astype(BF), grad_o)
        weighted = probs * grad_probs
        grad_scores = (weighted - probs * jnp.sum(weighted, axis=-1, keepdims=True)).astype(BF)
        dk_acc[...] += t_dot(grad_scores, qb)
        grad_q = jnp.dot(grad_scores, kb_ref[...], preferred_element_type=F32) * scale
        eq = grad_q * cosine - pltpu.roll(grad_q, HD // 2, 1) * sine
        gains_ref[0:1, :] += jnp.sum(eq * q_norm, axis=0, keepdims=True)
        dq_ref[rows, :] = norm_back(eq * gq_ref[...], q_norm, q_scale).astype(BF)
        return carry

    lax.fori_loop(0, length // QCHUNK, step, 0)
    grad_k = dk_acc[...] * scale
    ek = grad_k * cos_ref[...] - pltpu.roll(grad_k, HD // 2, 1) * sin_ref[...]
    k_raw = k_ref[...]
    k_scale = rms_scale(k_raw)
    k_norm = k_raw * k_scale
    gains_ref[1:2, :] += jnp.sum(ek * k_norm, axis=0, keepdims=True)
    dk_ref[...] = norm_back(ek * gk_ref[...], k_norm, k_scale).astype(BF)
    dv_ref[...] = dv_acc[...].astype(BF)


def attention_specs(length):
    head = pl.BlockSpec((length, HD), lambda h: (0, h))
    table = pl.BlockSpec((length, HD), lambda h: (0, 0))
    gain = pl.BlockSpec((1, HD), lambda h: (0, 0))
    column = pl.BlockSpec((length, 1), lambda h: (0, 0))
    row = pl.BlockSpec((1, length), lambda h: (0, 0))
    return head, table, gain, column, row


def attention_forward(query, key, value, cosine, sine, gain_q, gain_k, seg_column, seg_row):
    length, width = query.shape
    head, table, gain, column, row = attention_specs(length)
    heads = width // HD
    return pl.pallas_call(
        attend_forward,
        grid=(heads,),
        in_specs=[head, head, head, table, table, gain, gain, column, row],
        out_specs=head,
        out_shape=jax.ShapeDtypeStruct((length, width), BF),
        scratch_shapes=[pltpu.VMEM((length, HD), BF)],
        compiler_params=pltpu.CompilerParams(vmem_limit_bytes=40 << 20),
        cost_estimate=pl.CostEstimate(
            flops=4 * heads * length * length * HD * 4,
            bytes_accessed=length * width * 12,
            transcendentals=heads * length * length,
        ),
    )(query, key, value, cosine, sine, gain_q, gain_k, seg_column, seg_row)


def attention_backward(query, key, value, grad_o, cosine, sine, gain_q, gain_k, seg_column, seg_row):
    length, width = query.shape
    head, table, gain, column, row = attention_specs(length)
    heads = width // HD
    out = jax.ShapeDtypeStruct((length, width), BF)
    return pl.pallas_call(
        attend_backward,
        grid=(heads,),
        in_specs=[head, head, head, head, table, table, gain, gain, column, row],
        out_specs=[head, head, head, pl.BlockSpec((8, HD), lambda h: (0, 0))],
        out_shape=[out, out, out, jax.ShapeDtypeStruct((8, HD), F32)],
        scratch_shapes=[
            pltpu.VMEM((length, HD), BF),
            pltpu.VMEM((length, HD), F32),
            pltpu.VMEM((length, HD), F32),
        ],
        compiler_params=pltpu.CompilerParams(vmem_limit_bytes=48 << 20),
        cost_estimate=pl.CostEstimate(
            flops=10 * heads * length * length * HD * 4,
            bytes_accessed=length * width * 18,
            transcendentals=heads * length * length,
        ),
    )(query, key, value, grad_o, cosine, sine, gain_q, gain_k, seg_column, seg_row)


def pick_rows(slots_ref, x_ref, out_ref):
    experts, capacity = out_ref.shape[0], out_ref.shape[2]
    count = x_ref.shape[1]
    for j in range(experts):
        wanted = lax.broadcasted_iota(jnp.int32, (capacity, count), 0)
        hot = (wanted == slots_ref[0, j : j + 1, :]).astype(BF)
        out_ref[j, 0] = jnp.dot(hot, x_ref[0], preferred_element_type=F32).astype(BF)


def pick_scaled(slots_ref, gates_ref, x_ref, out_ref):
    experts, capacity = out_ref.shape[0], out_ref.shape[2]
    count = x_ref.shape[1]
    for j in range(experts):
        wanted = lax.broadcasted_iota(jnp.int32, (capacity, count), 0)
        hot = wanted == slots_ref[0, j : j + 1, :]
        gate = jnp.sum(jnp.where(hot, gates_ref[0, j : j + 1, :], 0.0), axis=1, keepdims=True)
        rows = jnp.dot(hot.astype(BF), x_ref[0], preferred_element_type=F32)
        out_ref[j, 0] = (rows * gate).astype(BF)


def pick(slots, x, capacity, gates=None):
    blocks, count, width = x.shape
    experts = slots.shape[1]
    small = pl.BlockSpec((1, experts, count), lambda b: (b, 0, 0))
    specs = [small] + ([small] if gates is not None else [])
    operands = (slots,) + ((gates,) if gates is not None else ())
    return pl.pallas_call(
        pick_rows if gates is None else pick_scaled,
        grid=(blocks,),
        in_specs=specs + [pl.BlockSpec((1, count, width), lambda b: (b, 0, 0))],
        out_specs=pl.BlockSpec((experts, 1, capacity, width), lambda b: (0, b, 0, 0)),
        out_shape=jax.ShapeDtypeStruct((experts, blocks, capacity, width), BF),
        compiler_params=pltpu.CompilerParams(vmem_limit_bytes=40 << 20),
        cost_estimate=pl.CostEstimate(
            flops=2 * blocks * experts * capacity * count * width,
            bytes_accessed=2 * blocks * width * (count + experts * capacity),
            transcendentals=0,
        ),
    )(*operands, x)


def merge_results(slots_ref, gates_ref, rows_ref, grad_ref, out_ref, dgate_ref):
    experts, capacity = rows_ref.shape[0], rows_ref.shape[2]
    count = out_ref.shape[1]
    grad = grad_ref[0].astype(F32)
    total = None
    dgates = []
    for j in range(experts):
        place = lax.broadcasted_iota(jnp.int32, (count, capacity), 1)
        hot = (place == slots_ref[0, :, j : j + 1]).astype(BF)
        rows = jnp.dot(hot, rows_ref[j, 0], preferred_element_type=F32)
        dgates.append(jnp.sum(rows * grad, axis=1, keepdims=True))
        gated = rows * gates_ref[0, :, j : j + 1]
        total = gated if total is None else total + gated
    out_ref[0] = total.astype(BF)
    dgate_ref[0] = jnp.concatenate(dgates, axis=1)


def merge_rows(slots_ref, rows_ref, out_ref):
    experts, capacity = rows_ref.shape[0], rows_ref.shape[2]
    count = out_ref.shape[1]
    total = None
    for j in range(experts):
        place = lax.broadcasted_iota(jnp.int32, (count, capacity), 1)
        hot = (place == slots_ref[0, :, j : j + 1]).astype(BF)
        rows = jnp.dot(hot, rows_ref[j, 0], preferred_element_type=F32)
        total = rows if total is None else total + rows
    out_ref[0] = total.astype(BF)


def merge(slots, rows, gates=None, grad=None):
    experts, blocks, capacity, width = rows.shape
    count = slots.shape[1]
    small = pl.BlockSpec((1, count, experts), lambda b: (b, 0, 0))
    row_spec = pl.BlockSpec((experts, 1, capacity, width), lambda b: (0, b, 0, 0))
    token_spec = pl.BlockSpec((1, count, width), lambda b: (b, 0, 0))
    token_shape = jax.ShapeDtypeStruct((blocks, count, width), BF)
    cost = pl.CostEstimate(
        flops=2 * blocks * experts * capacity * count * width,
        bytes_accessed=2 * blocks * width * (2 * count + experts * capacity),
        transcendentals=0,
    )
    params = pltpu.CompilerParams(vmem_limit_bytes=40 << 20)
    if gates is None:
        return pl.pallas_call(
            merge_rows,
            grid=(blocks,),
            in_specs=[small, row_spec],
            out_specs=token_spec,
            out_shape=token_shape,
            compiler_params=params,
            cost_estimate=cost,
        )(slots, rows)
    return pl.pallas_call(
        merge_results,
        grid=(blocks,),
        in_specs=[small, small, row_spec, token_spec],
        out_specs=[token_spec, small],
        out_shape=[token_shape, jax.ShapeDtypeStruct((blocks, count, experts), F32)],
        compiler_params=params,
        cost_estimate=cost,
    )(slots, gates, rows, grad)


def swap_core(value):
    return lax.ppermute(value, "shard", [(i, i ^ 1) for i in range(4)])


def swap_x(value):
    return lax.ppermute(value, "shard", [(i, i ^ 2) for i in range(4)])


def shard_order(position):
    return [position, position ^ 1, position ^ 2, position ^ 3]


def shard_gather(value):
    far = swap_x(value)
    near = swap_core(value)
    return [value, near, far, swap_core(far)]


def shard_reduce(blocks):
    far = blocks[2].astype(F32) + swap_core(blocks[3].astype(BF)).astype(F32)
    far = swap_x(far.astype(BF))
    near = blocks[0].astype(F32) + swap_core(blocks[1].astype(BF)).astype(F32)
    return near + far.astype(F32)


def ring_next(count):
    return [(z * 2 + y, ((z + 1) % (count // 2)) * 2 + y) for z in range(count // 2) for y in range(2)]


def swap_y(value, count):
    return lax.ppermute(value, "rep", [(i, i ^ 1) for i in range(count)])


def turn_z(value, count):
    return lax.ppermute(value, "rep", ring_next(count))


def rep_order(rep, count):
    planes = count // 2
    z, y = rep // 2, rep % 2
    return [((z + planes - k) % planes) * 2 + (y ^ w) for k in range(planes) for w in range(2)]


def rep_gather(value, count):
    blocks = []
    held = value
    for k in range(count // 2):
        if k > 0:
            held = turn_z(held, count)
        blocks += [held, swap_y(held, count)]
    return blocks


def rep_reduce(blocks, count):
    planes = count // 2

    def pair(k):
        return blocks[2 * k].astype(F32) + swap_y(blocks[2 * k + 1].astype(BF), count).astype(F32)

    total = pair(1)
    for k in list(range(2, planes)) + [0]:
        total = turn_z(total.astype(BF), count).astype(F32) + pair(k)
    return total


def on_device(
    tokens,
    w_query,
    w_key,
    w_value,
    w_out,
    w_router,
    norm_attn,
    norm_ffn,
    norm_query,
    norm_key,
    w_gate,
    w_up,
    w_down,
    segments,
    routes,
    cotangent,
):
    rows_count, width = tokens.shape
    experts = w_router.shape[1]
    local_experts = w_gate.shape[0]
    rep_count = lax.axis_size("rep")
    shard_count = lax.axis_size("shard")
    position = lax.axis_index("shard")
    rep = lax.axis_index("rep")
    head_width = HEADS * HD // shard_count
    length = rows_count * shard_count
    capacity = max(2, rows_count * TOP * 9 // (8 * experts))
    capacity = -(-capacity // 16) * 16
    rows = w_query.shape[0]

    gains = jnp.concatenate([norm_attn, norm_ffn, norm_query, norm_key])
    gains = lax.all_gather(gains, "shard", axis=0, tiled=False)
    gain_attn = gains[:, :rows].reshape(-1).astype(F32)
    gain_ffn = gains[:, rows : 2 * rows].reshape(-1).astype(F32)
    tail = gains[:, 2 * rows :].reshape(shard_count, 2, -1)
    gain_query = tail[:, 0].reshape(1, HD).astype(F32)
    gain_key = tail[:, 1].reshape(1, HD).astype(F32)
    full_router = lax.all_gather(w_router, "shard", axis=0, tiled=True)

    tokens_f = tokens.astype(F32)
    scale_in = rms_scale(tokens_f)
    normed_in = tokens_f * scale_in
    input_own = (normed_in * gain_attn).astype(BF)
    input_b = jnp.concatenate(shard_gather(input_own), axis=0)

    def columns(weight):
        return lax.all_to_all(weight, "shard", split_axis=1, concat_axis=0, tiled=True)

    cols_query, cols_key, cols_value = columns(w_query), columns(w_key), columns(w_value)

    full_gate = lax.all_gather(w_gate, "shard", axis=1, tiled=True)
    full_up = lax.all_gather(w_up, "shard", axis=1, tiled=True)
    full_down = lax.all_gather(w_down, "shard", axis=1, tiled=True)
    grad_blocks = jnp.stack(rep_gather(cotangent, rep_count))

    order = jnp.stack(rep_order(rep, rep_count))
    route_all = lax.all_gather(routes, "rep", axis=0, tiled=False)[order]
    expert_ids = jnp.arange(experts, dtype=jnp.int32)
    named_all = jnp.any(route_all[:, :, :, None] == expert_ids, axis=2)
    mine = lambda a: lax.dynamic_slice_in_dim(a, rep * local_experts, local_experts, axis=2)
    named_mine = mine(named_all)
    before = jnp.tril(jnp.ones((rows_count, rows_count), BF), -1)
    slot_mine = jnp.einsum("ts,bsj->btj", before, named_mine.astype(BF), preferred_element_type=F32)
    slot_tokens = jnp.where(named_mine, slot_mine.astype(jnp.int32), -1)
    slot_lanes = jnp.swapaxes(slot_tokens, 1, 2)

    query_raw = jnp.dot(input_b, cols_query, preferred_element_type=F32)
    key_raw = jnp.dot(input_b, cols_key, preferred_element_type=F32)
    value_b = jnp.dot(input_b, cols_value, preferred_element_type=F32).astype(BF)
    order_in = shard_order(position)
    places = jnp.concatenate([p * rows_count + jnp.arange(rows_count, dtype=jnp.int32) for p in order_in])
    inverse = THETA ** (-jnp.arange(HD // 2, dtype=F32) * 2.0 / HD)
    angles = places.astype(F32)[:, None] * inverse[None, :]
    cosine, sine = jnp.cos(angles), jnp.sin(angles)
    cosine = jnp.concatenate([cosine, cosine], axis=-1)
    sine = jnp.concatenate([-sine, sine], axis=-1)
    segment_all = jnp.concatenate(
        [lax.dynamic_slice_in_dim(segments[0], p * rows_count, rows_count) for p in order_in]
    )
    attn_args = (cosine, sine, gain_query, gain_key, segment_all[:, None], segment_all[None, :])
    mixed_b = attention_forward(query_raw, key_raw, value_b, *attn_args)
    projected = jnp.dot(mixed_b, w_out, preferred_element_type=F32).astype(BF)
    projected = projected.reshape(shard_count, rows_count, width)
    hidden_state = tokens_f + shard_reduce([projected[i] for i in range(shard_count)])

    scale_mid = rms_scale(hidden_state)
    normed_mid = hidden_state * scale_mid
    mid_b = (normed_mid * gain_ffn).astype(BF)
    mid_blocks = jnp.stack(rep_gather(mid_b, rep_count))

    def router(inputs):
        logits = jnp.einsum("...d,de->...e", inputs, full_router, preferred_element_type=F32)
        exps = jnp.exp(logits - jnp.max(logits, axis=-1, keepdims=True))
        return exps / jnp.sum(exps, axis=-1, keepdims=True)

    probs_all = router(mid_blocks)
    chosen_all = jnp.where(named_all, probs_all, 0.0)
    gates_all = chosen_all / jnp.sum(chosen_all, axis=-1, keepdims=True)
    gate_tokens = mine(gates_all)
    gate_lanes = jnp.swapaxes(gate_tokens, 1, 2)

    expert_rows = pick(slot_lanes, mid_blocks, capacity)
    grad_rows = pick(slot_lanes, grad_blocks, capacity, gate_lanes)
    count = rep_count * capacity
    expert_rows = expert_rows.reshape(local_experts, count, width)
    grad_rows = grad_rows.reshape(local_experts, count, width)
    results, grad_ins, kept = [], [], []
    for j in range(local_experts):
        x = expert_rows[j]
        gate_pre = jnp.dot(x, full_gate[j], preferred_element_type=F32)
        up_pre = jnp.dot(x, full_up[j], preferred_element_type=F32)
        sigmoid = 1.0 / (1.0 + jnp.exp(-gate_pre))
        activated = gate_pre * sigmoid
        hidden_b = (activated * up_pre).astype(BF)
        results.append(jnp.dot(hidden_b, full_down[j], preferred_element_type=F32).astype(BF))
        grad_hidden = dot_t(grad_rows[j], full_down[j])
        grad_gate_pre = (
            grad_hidden * up_pre * sigmoid * (1.0 + gate_pre * (1.0 - sigmoid))
        ).astype(BF)
        grad_up_pre = (grad_hidden * activated).astype(BF)
        grad_in = dot_t(grad_gate_pre, full_gate[j]) + dot_t(grad_up_pre, full_up[j])
        grad_ins.append(grad_in.astype(BF))
        kept.append((x, hidden_b, grad_rows[j], grad_gate_pre, grad_up_pre))
    shape = (local_experts, rep_count, capacity, width)
    grad_parts = merge(slot_tokens, jnp.stack(grad_ins).reshape(shape))
    result_parts, dgate_parts = merge(
        slot_tokens, jnp.stack(results).reshape(shape), gate_tokens, grad_blocks
    )
    grad_mid_moe = rep_reduce([grad_parts[i] for i in range(rep_count)], rep_count)
    expert_sum = rep_reduce([result_parts[i] for i in range(rep_count)], rep_count)
    output = (hidden_state + expert_sum).astype(BF)

    def owned_part(parts):
        return lax.psum_scatter(
            jnp.stack(parts), "shard", scatter_dimension=1, tiled=True
        ).astype(F32)

    grad_gate = owned_part([t_dot(x, dg).astype(BF) for x, _, _, dg, _ in kept])
    grad_up = owned_part([t_dot(x, du).astype(BF) for x, _, _, _, du in kept])
    grad_down = owned_part([t_dot(h, dy).astype(BF) for _, h, dy, _, _ in kept])

    inverse_order = jnp.zeros((rep_count,), jnp.int32).at[order].set(
        jnp.arange(rep_count, dtype=jnp.int32)
    )
    dgates = lax.all_to_all(
        jnp.swapaxes(dgate_parts, 1, 2)[inverse_order], "rep", split_axis=0, concat_axis=0, tiled=True
    )
    dgates = dgates.reshape(experts, rows_count).T
    named_own = jnp.any(routes[:, :, None] == expert_ids, axis=1)
    probs_own = router(mid_b)
    chosen_total = jnp.sum(jnp.where(named_own, probs_own, 0.0), axis=1, keepdims=True)
    gates_own = jnp.where(named_own, probs_own, 0.0) / chosen_total
    grad_probs = jnp.where(
        named_own, dgates - jnp.sum(dgates * gates_own, axis=1, keepdims=True), 0.0
    ) / chosen_total
    grad_logits = (
        probs_own * (grad_probs - jnp.sum(probs_own * grad_probs, axis=1, keepdims=True))
    ).astype(BF)
    grad_mid = grad_mid_moe + dot_t(grad_logits, full_router)
    grad_gain_ffn = jnp.sum(grad_mid * normed_mid, axis=0)
    grad_router = t_dot(mid_b, grad_logits)
    grad_out = cotangent.astype(F32)
    grad_state = grad_out + norm_back(grad_mid * gain_ffn, normed_mid, scale_mid)
    grad_state_b = grad_state.astype(BF)

    grad_state_all = jnp.concatenate(shard_gather(grad_state_b), axis=0)
    grad_mixed = dot_t(grad_state_all, w_out).astype(BF)
    grad_out_proj = t_dot(mixed_b, grad_state_all)
    grad_query_raw, grad_key_raw, grad_value_raw, grad_head_gains = attention_backward(
        query_raw, key_raw, value_b, grad_mixed, *attn_args
    )
    grad_input = (
        dot_t(grad_query_raw, cols_query)
        + dot_t(grad_key_raw, cols_key)
        + dot_t(grad_value_raw, cols_value)
    ).astype(BF)
    grad_input = grad_input.reshape(shard_count, rows_count, width)
    grad_input = shard_reduce([grad_input[i] for i in range(shard_count)])
    grad_gain_attn = jnp.sum(grad_input * normed_in, axis=0)
    tokens_grad = (grad_state + norm_back(grad_input * gain_attn, normed_in, scale_in)).astype(BF)

    part = rows // rep_count

    def spread(grad):
        view = grad.astype(BF).reshape(shard_count, rep_count, part, -1)
        return [
            lax.dynamic_index_in_dim(view, r, axis=1, keepdims=False) for r in rep_order(rep, rep_count)
        ]

    def collected(part_sum):
        whole = jnp.stack(rep_gather(part_sum, rep_count))[inverse_order]
        return whole.reshape(rows, -1).astype(F32)

    def summed_columns(grad):
        mine_part = rep_reduce(spread(grad), rep_count).astype(BF)
        mine_part = lax.all_to_all(mine_part, "shard", split_axis=0, concat_axis=0, tiled=True)
        mine_part = jnp.swapaxes(mine_part, 0, 1).reshape(part, -1)
        return collected(mine_part)

    view = grad_out_proj.astype(BF).reshape(rep_count, part, width)
    out_part = rep_reduce(
        [lax.dynamic_index_in_dim(view, r, axis=0, keepdims=False) for r in rep_order(rep, rep_count)],
        rep_count,
    ).astype(BF)
    sum_out = collected(out_part)
    sum_query = summed_columns(t_dot(input_b, grad_query_raw))
    sum_key = summed_columns(t_dot(input_b, grad_key_raw))
    sum_value = summed_columns(t_dot(input_b, grad_value_raw))

    first = jnp.concatenate([grad_router.reshape(-1), grad_gain_ffn])
    first = lax.psum(first, ("rep", "shard"))
    second = jnp.concatenate([grad_gain_attn, grad_head_gains[0], grad_head_gains[1]])
    second = lax.psum(second, ("rep", "shard"))

    def own_slice(vector, start, size):
        piece = size // shard_count
        return lax.dynamic_slice_in_dim(vector, start + position * piece, piece)

    sum_router = own_slice(first, 0, width * experts).reshape(rows, experts)
    sum_ffn = own_slice(first, width * experts, width)
    sum_attn = own_slice(second, 0, width)
    sum_hquery = own_slice(second, width, HD)
    sum_hkey = own_slice(second, width + HD, HD)
    return (
        output,
        tokens_grad,
        sum_query,
        sum_key,
        sum_value,
        sum_out,
        sum_router,
        sum_attn,
        sum_ffn,
        sum_hquery,
        sum_hkey,
        grad_gate,
        grad_up,
        grad_down,
    )


def solution(mesh):
    return jax.shard_map(
        on_device,
        mesh=mesh,
        in_specs=(
            P(("rep", "shard"), None),
            P("shard", None),
            P("shard", None),
            P("shard", None),
            P("shard", None),
            P("shard", None),
            P("shard"),
            P("shard"),
            P("shard"),
            P("shard"),
            P("rep", "shard", None),
            P("rep", "shard", None),
            P("rep", "shard", None),
            P("rep", None),
            P(("rep", "shard"), None),
            P(("rep", "shard"), None),
        ),
        out_specs=(
            P(("rep", "shard"), None),
            P(("rep", "shard"), None),
            P("shard", None),
            P("shard", None),
            P("shard", None),
            P("shard", None),
            P("shard", None),
            P("shard"),
            P("shard"),
            P("shard"),
            P("shard"),
            P("rep", "shard", None),
            P("rep", "shard", None),
            P("rep", "shard", None),
        ),
        check_vma=False,
    )
```

time: 2290 us -> 1380 us (0.60)
  waiting for transfers between devices: 1540 us -> 481 us
  starting transfers between devices: 23.4 us -> 123 us
  local copies, waits for them, and re-layouts: 236 us -> 143 us
  Pallas kernels: 0 us -> 90.8 us
  blocking collectives: 68.8 us -> 159 us
  matrix products: 285 us -> 242 us
    all_to_all x4 -> x7, waiting for transfers between devices: 666 us -> 45.7 us  [the longest x3 29.7 us: columns(): lax.all_to_all(weight, 'shard', split_axis=1, concat_axis=0, tiled=True)]
    reduce_scatter x10 -> x3, waiting for transfers between devices: 440 us -> 0.01 us  [owned_part(): lax.psum_scatter(jnp.stack(parts), 'shard', scatter_dimension=1, tiled=True)]
    ppermute x0 -> x96, waiting for transfers between devices: none -> 423 us  [the longest x48 237 us: swap_y(): return lax.ppermute(value, 'rep', [(i, i ^ 1) for i in range(count)])]
    psum x1, waiting for transfers between devices: 233 us -> 11.2 us  [on_device(): first = lax.psum(first, ('rep', 'shard'))]
    all_gather x9 -> x3, waiting for transfers between devices: 195 us -> 0.01 us  [the longest x1 0.01 us: on_device(): full_gate = lax.all_gather(w_gate, 'shard', axis=1, tiled=True)]
    ppermute x0 -> x96, starting transfers between devices: none -> 95.2 us  [the longest x48 54.7 us: swap_y(): return lax.ppermute(value, 'rep', [(i, i ^ 1) for i in range(count)])]
    pallas_call x0 -> x6, Pallas kernels: none -> 90.8 us  [the longest x1 33.3 us: attention_backward(): pl.pallas_call(attend_backward, grid=(heads,), in_specs=[head, head, head...]
    gather x4 -> x7, local copies, waits for them, and re-layouts: 75.5 us -> 17.8 us  [the longest x4 14.4 us: collected(): whole = jnp.stack(rep_gather(part_sum, rep_count))[inverse_order]]
  transfers between devices with their start and end apart: 24 -> 110, of which waited for: 19 -> 59; matrix products, arithmetic and copies ran while one was open for 20% -> 30% of each run, Pallas kernels for 0% -> 6%
where the time goes in v1:
time: 1380 us; the launch traced here: 1370 us
  waiting for transfers between devices  481 us (35%)
  matrix products  242 us (18%)
  blocking collectives  159 us (12%)
  local copies, waits for them, and re-layouts  143 us (10%)
  starting transfers between devices  123 us (9%)
  other arithmetic  118 us (9%)
  Pallas kernels  90.8 us (7%)
  between operations  16.8 us (1%)
    ppermute x48, waiting for transfers between devices, swap_y(): return lax.ppermute(value, 'rep', [(i, i ^ 1) for i in range(count)])  237 us
    ppermute x36, waiting for transfers between devices, turn_z(): return lax.ppermute(value, 'rep', ring_next(count))  171 us
    dot_general x11, matrix products, dot_t(): lax.dot_general(left, right, (((1,), (1,)), ((), ())), preferred_element_...  92.9 us
    dot_general x11, matrix products, t_dot(): lax.dot_general(left, right, (((0,), (0,)), ((), ())), preferred_element_...  74.2 us
    unnamed x252, local copies, waits for them, and re-layouts  63.1 us
    ppermute x48, starting transfers between devices, swap_y(): return lax.ppermute(value, 'rep', [(i, i ^ 1) for i in range(count)])  54.7 us
    unnamed x1, blocking collectives  50.4 us
    all_gather x1, blocking collectives, on_device(): route_all = lax.all_gather(routes, 'rep', axis=0, tiled=False)[order]  45.2 us
  transfers between devices with their start and end apart: 110, of which 59 were waited for; matrix products, arithmetic and copies ran while one was open for 30% of the time, Pallas kernels for 6%

profile of v1, /device:TPU:0, one launch (start us, length us, event | category | flops | bytes accessed | tf_op | source)
XLA Modules:
  0.0 1373.8 jit_solution(9340463205094328129)
XLA Ops:
  18.8 50.4 %all-reduce = bf16[4352]{0:T(1024)(128)(2,1)S(1)} all-reduce(bf16[4352]{0:T(1024)(128)(2,1)S(1)} %dynamic-update-slice), channel_id=2, replica_groups=mesh['rep'=8,'shard'=4] {'shard'}, use_global_device_ids=true, to_apply=%add | all-reduce | flops 4352 | bytes 17408
  90.8 45.2 %all-gather.1 = s32[2048,8]{0,1:T(8,128)S(1)} all-gather(s32[256,8]{0,1:T(8,128)S(1)} %copy-done.64), channel_id=3, replica_groups=mesh['rep'=8,'shard'=4] {'rep'}, dimensions={0}, use_global_device_ids=true | all-gather | bytes 73728 | tf_op jit(solution)/shard_map/all_gather | solution.py:414
  142.4 14.7 %collective-permute-done.1 = bf16[256,2048]{1,0:T(8,128)(2,1)} collective-permute-done((bf16[256,2048]{1,0:T(8,128)(2,1)}, bf16[256,2048]{1,0:T(8,128)(2,1)}, u32[]{:S(2)}, u32[]{:S(2)}) %collective-permute-start.1) | collective-permute-done | bytes 1048608 | tf_op jit(solution)/shard_map/ppermute | solution.py:297
  171.4 29.7 %all-to-all-done = bf16[512,4,512]{0,2,1:T(8,128)(2,1)} async-done(((bf16[512,4,512]{0,2,1:T(8,128)(2,1)}), bf16[512,4,512]{0,2,1:T(8,128)(2,1)}, u32[]{:S(2)}, u32[]{:S(2)}) %all-to-all-start) | async-done | bytes 2097184 | tf_op jit(solution)/shard_map/all_to_all | solution.py:404
  222.9 18.7 %shard_map.263 = bf16[1024,512]{1,0:T(8,128)(2,1)S(1)} custom-call(f32[1024,512]{1,0:T(8,128)S(1)} %fusion.99.q_ref, f32[1024,512]{1,0:T(8,128)S(1)} %fusion.98.k_ref, bf16[1024,512]{1,0:T(8,128)(2,1)S(1)} %convolution_convert_fusion.8.v_ref, f32[1024,128]{1,0:T(8,128)S(1)} %copy-done.9, f32[1024,128]{1,0:T(8,128)S(1)} %pad_maximum_fusion.10.sin_ref, ...), custom_call_target="tpu_custom_call" | custom-call | flops 8589934592 | bytes 6291456 | tf_op jit(solution)/shard_map/pallas_call | solution.py:147
  247.3 14.3 %collective-permute-start.16 = (bf16[256,2048]{1,0:T(8,128)(2,1)}, bf16[256,2048]{1,0:T(8,128)(2,1)}, u32[]{:S(2)}, u32[]{:S(2)}) collective-permute-start(bf16[256,2048]{1,0:T(8,128)(2,1)} %collective-permute-done.14), channel_id=1, source_target_pairs={{0,8},{4,12},{8,16},{12,20},{16,24},{20,28},{24,0},{28,4},{1,9},{5... | collective-permute-start | bytes 3145736 | tf_op jit(solution)/shard_map/ppermute | solution.py:326
  264.4 25.5 %all_gather.28 = bf16[2048,16]{0,1:T(8,128)(2,1)S(1)} all-gather(bf16[512,16]{0,1:T(8,128)(2,1)S(1)} %copy-done.69), channel_id=1, replica_groups=mesh['rep'=8,'shard'=4] {'shard'}, dimensions={0}, use_global_device_ids=true | all-gather | bytes 81920 | tf_op jit(solution)/shard_map/all_gather | solution.py:395
  304.1 11.9 collective-permute-done.15
  326.2 12.4 collective-permute-done.17
  347.4 13.6 collective-permute-done.19
  364.2 7.5 collective-permute-done.9
  371.7 11.8 collective-permute-done.6
  387.1 18.8 %collective-permute-done.8 = bf16[256,2048]{1,0:T(8,128)(2,1)S(1)} collective-permute-done((bf16[256,2048]{1,0:T(8,128)(2,1)S(1)}, bf16[256,2048]{1,0:T(8,128)(2,1)S(1)}, u32[]{:S(2)}, u32[]{:S(2)}) %collective-permute-start.8) | collective-permute-done | bytes 1048608 | tf_op jit(solution)/shard_map/ppermute | solution.py:322
  409.7 18.8 %collective-permute-done.10 = bf16[256,2048]{1,0:T(8,128)(2,1)S(1)} collective-permute-done((bf16[256,2048]{1,0:T(8,128)(2,1)S(1)}, bf16[256,2048]{1,0:T(8,128)(2,1)S(1)}, u32[]{:S(2)}, u32[]{:S(2)}) %collective-permute-start.10) | collective-permute-done | bytes 1048608 | tf_op jit(solution)/shard_map/ppermute | solution.py:322
  430.6 19.7 %collective-permute-done.12 = bf16[256,2048]{1,0:T(8,128)(2,1)S(1)} collective-permute-done((bf16[256,2048]{1,0:T(8,128)(2,1)S(1)}, bf16[256,2048]{1,0:T(8,128)(2,1)S(1)}, u32[]{:S(2)}, u32[]{:S(2)}) %collective-permute-start.12) | collective-permute-done | bytes 1048608 | tf_op jit(solution)/shard_map/ppermute | solution.py:322
  458.5 10.8 shard_map.264
  479.4 9.3 fusion.102
  488.6 9.3 fusion.103
  497.9 9.7 fusion.4
  507.6 9.9 fusion.5
  517.4 6.8 fusion.8
  531.0 13.8 %multiply_convert_fusion.2 = (bf16[1152,1024]{1,0:T(8,128)(2,1)S(1)}, bf16[1152,1024]{1,0:T(8,128)(2,1)S(1)}, bf16[1152,1024]{1,0:T(8,128)(2,1)}) fusion(f32[1152,1024]{1,0:T(8,128)} %fusion.4, f32[1152,1024]{1,0:T(8,128)} %fusion.5, bf16[1152,2048]{1,0:T(8,128)(2,1)} %bitcast.453, bf16[2,1024,2048]{2,1,0:T(8,128)(2,1)} %all-gather.10.cloned.1.call-done), kind=kOutput, calls=%fused_computation.20 | convolution fusion | flops 4849532928 | bytes 25427968 | tf_op jit(solution)/shard_map/dot_general | solution.py:31
  544.8 11.4 fusion.3
  556.1 14.3 %multiply_convert_fusion = (bf16[1152,1024]{1,0:T(8,128)(2,1)}, bf16[1152,1024]{1,0:T(8,128)(2,1)}, bf16[1152,1024]{1,0:T(8,128)(2,1)}) fusion(f32[1152,1024]{1,0:T(8,128)} %fusion.8, f32[1152,1024]{1,0:T(8,128)} %fusion.9, bf16[1152,2048]{1,0:T(8,128)(2,1)} %bitcast.451, bf16[2,1024,2048]{2,1,0:T(8,128)(2,1)} %all-gather.10.cloned.1.call-done), kind=kOutput, calls=%fused_computation.18 | convolution fusion | flops 4849532928 | bytes 25427968 | tf_op jit(solution)/shard_map/dot_general | solution.py:31
  570.5 9.3 fusion.7
  579.8 9.5 add_convert_fusion.1
  589.3 8.6 add_convert_fusion
  597.9 8.2 pad_maximum_fusion.1.rows_ref
  606.2 9.1 shard_map.267
  621.2 9.0 convolution_convert_fusion.1
  630.2 13.1 collective-permute-done.27
  646.3 7.0 convolution_convert_fusion
  653.2 8.2 pad_maximum_fusion.rows_ref
  662.7 12.3 shard_map.265
  691.3 9.6 convert_bitcast_fusion.1
  700.9 12.1 collective-permute-done.30
  716.2 9.7 convert_bitcast_fusion
  729.5 9.6 collective-permute-done.32
  744.4 7.6 pad_maximum_fusion.4
  752.1 8.9 convert_bitcast_fusion.3
  761.0 9.6 convert_bitcast_fusion.2
  783.4 24.6 %collective-permute-done.20 = bf16[256,2048]{1,0:T(8,128)(2,1)} collective-permute-done((bf16[256,2048]{1,0:T(8,128)(2,1)}, bf16[256,2048]{1,0:T(8,128)(2,1)}, u32[]{:S(2)}, u32[]{:S(2)}) %collective-permute-start.20) | collective-permute-done | bytes 1048608 | tf_op jit(solution)/shard_map/ppermute | solution.py:322
  813.8 8.5 convert_bitcast_fusion.5
  823.7 6.9 collective-permute-done.22
  833.9 7.4 convert_bitcast_fusion.4
  853.8 11.2 all-reduce.3.cloned.1.call-done
  873.8 33.3 %shard_map.268 = (bf16[1024,512]{1,0:T(8,128)(2,1)S(1)}, bf16[1024,512]{1,0:T(8,128)(2,1)S(1)}, bf16[1024,512]{1,0:T(8,128)(2,1)S(1)}, f32[8,128]{1,0:T(8,128)S(1)}) custom-call(f32[1024,512]{1,0:T(8,128)} %copy-done.21, f32[1024,512]{1,0:T(8,128)} %copy-done.20, bf16[1024,512]{1,0:T(8,128)(2,1)S(1)} %copy-done.23, ...), custom_call_target="tpu_custom_call" | custom-call | flops 21474836480 | bytes 9437184 | tf_op jit(solution)/shard_map/pallas_call | solution.py:168
  918.4 8.6 add_convert_fusion.2
  958.3 8.6 collective-permute-done.54
  1031.0 15.6 %collective-permute-done.88 = bf16[64,2048]{1,0:T(8,128)(2,1)} collective-permute-done((bf16[64,2048]{1,0:T(8,128)(2,1)}, bf16[64,2048]{1,0:T(8,128)(2,1)}, u32[]{:S(2)}, u32[]{:S(2)}) %collective-permute-start.88) | collective-permute-done | bytes 262176 | tf_op jit(solution)/shard_map/ppermute | solution.py:322
  1069.9 8.0 all-to-all-done.5
  1082.5 8.0 all-to-all-done.4
  1102.8 7.8 collective-permute-done.76
  1117.8 7.4 collective-permute-done.62
  1132.4 7.4 collective-permute-done.48
  1147.1 7.7 collective-permute-done.92
  1161.9 7.7 collective-permute-done.78
  1178.1 10.0 collective-permute-done.64
  1197.1 8.6 collective-permute-done.50
  1213.0 7.4 collective-permute-done.94
  1227.5 7.4 collective-permute-done.80
  1242.0 7.4 collective-permute-done.66
  1257.3 7.4 collective-permute-done.52
  1290.1 37.7 %psum.15 = f32[2304]{0:T(1024)S(1)} all-reduce(f32[2304]{0:T(1024)S(1)} %pad_maximum_fusion.12), channel_id=1, replica_groups=mesh['rep'=8,'shard'=4] {'rep','shard'}, use_global_device_ids=true, to_apply=%region_18.19 | all-reduce | flops 2304 | bytes 18432 | tf_op jit(solution)/shard_map/psum | solution.py:570
  (598 shorter events, 523.0 us)
Async XLA Ops:
  7.2 490.7 %all-gather.6.cloned.1.call-start = ((), (), s32[]{:S(2)}) async-start(), calls=%async_computation.10 | async-start | bytes 10485760 | tf_op jit(solution)/shard_map/all_gather | solution.py:408
  7.9 499.6 %all-gather.8.cloned.1.call-start = ((), (), s32[]{:S(2)}) async-start(), calls=%async_computation.11 | async-start | bytes 10485760 | tf_op jit(solution)/shard_map/all_gather | solution.py:409
  12.7 60.7 %all-to-all-start.1 = ((bf16[512,4,512]{0,2,1:T(8,128)(2,1)}), bf16[512,4,512]{0,2,1:T(8,128)(2,1)}, u32[]{:S(2)}, u32[]{:S(2)}) async-start(bf16[512,4,512]{0,2,1:T(8,128)(2,1)} %bitcast.440), calls=%async_computation.1 | async-start | bytes 4194304 | tf_op jit(solution)/shard_map/all_to_all | solution.py:404
  73.3 63.5 %all-to-all-start.2 = ((bf16[512,4,512]{0,2,1:T(8,128)(2,1)}), bf16[512,4,512]{0,2,1:T(8,128)(2,1)}, u32[]{:S(2)}, u32[]{:S(2)}) async-start(bf16[512,4,512]{0,2,1:T(8,128)(2,1)} %bitcast.438), calls=%async_computation.2 | async-start | bytes 4194304 | tf_op jit(solution)/shard_map/all_to_all | solution.py:404
  77.8 453.2 %all-gather.10.cloned.1.call-start = ((), (), s32[]{:S(2)}) async-start(), calls=%async_computation.12 | async-start | bytes 10485760 | tf_op jit(solution)/shard_map/all_gather | solution.py:410
  79.5 77.6 %collective-permute-start.1 = (bf16[256,2048]{1,0:T(8,128)(2,1)}, bf16[256,2048]{1,0:T(8,128)(2,1)}, u32[]{:S(2)}, u32[]{:S(2)}) collective-permute-start(bf16[256,2048]{1,0:T(8,128)(2,1)} %fusion.15), channel_id=1, source_target_pairs={{0,2},{1,3},{2,0},{3,1},{4,6},{5,7},{6,4},{7,5},{8,10},{9,11},{10,... | collective-permute-start | bytes 3145736 | tf_op jit(solution)/shard_map/ppermute | solution.py:297
  82.2 123.0 %collective-permute-start = (bf16[256,2048]{1,0:T(8,128)(2,1)}, bf16[256,2048]{1,0:T(8,128)(2,1)}, u32[]{:S(2)}, u32[]{:S(2)}) collective-permute-start(bf16[256,2048]{1,0:T(8,128)(2,1)} %fusion.15), channel_id=1, source_target_pairs={{0,1},{1,0},{2,3},{3,2},{4,5},{5,4},{6,7},{7,6},{8,9},{9,8},{10,11... | collective-permute-start | bytes 3145736 | tf_op jit(solution)/shard_map/ppermute | solution.py:293
  82.2 165.0 %collective-permute-start.14 = (bf16[256,2048]{1,0:T(8,128)(2,1)}, bf16[256,2048]{1,0:T(8,128)(2,1)}, u32[]{:S(2)}, u32[]{:S(2)}) collective-permute-start(bf16[256,2048]{1,0:T(8,128)(2,1)} %param.31), channel_id=1, source_target_pairs={{0,8},{4,12},{8,16},{12,20},{16,24},{20,28},{24,0},{28,4},{1,9},{5... | collective-permute-start | bytes 3145736 | tf_op jit(solution)/shard_map/ppermute | solution.py:326
  85.2 206.3 %collective-permute-start.13 = (bf16[256,2048]{1,0:T(8,128)(2,1)}, bf16[256,2048]{1,0:T(8,128)(2,1)}, u32[]{:S(2)}, u32[]{:S(2)}) collective-permute-start(bf16[256,2048]{1,0:T(8,128)(2,1)} %param.31), channel_id=1, source_target_pairs={{0,4},{4,0},{8,12},{12,8},{16,20},{20,16},{24,28},{28,24},{1,5},{5... | collective-permute-start | bytes 3145736 | tf_op jit(solution)/shard_map/ppermute | solution.py:322
  136.8 64.3 %all-to-all-start = ((bf16[512,4,512]{0,2,1:T(8,128)(2,1)}), bf16[512,4,512]{0,2,1:T(8,128)(2,1)}, u32[]{:S(2)}, u32[]{:S(2)}) async-start(bf16[512,4,512]{0,2,1:T(8,128)(2,1)} %bitcast.439), calls=%async_computation | async-start | bytes 4194304 | tf_op jit(solution)/shard_map/all_to_all | solution.py:404
  157.1 48.2 %collective-permute-start.2 = (bf16[256,2048]{1,0:T(8,128)(2,1)}, bf16[256,2048]{1,0:T(8,128)(2,1)}, u32[]{:S(2)}, u32[]{:S(2)}) collective-permute-start(bf16[256,2048]{1,0:T(8,128)(2,1)} %collective-permute-done.1), channel_id=1, source_target_pairs={{0,1},{1,0},{2,3},{3,2},{4,5},{5,4},{6,7},{7,6},{8,9},{9,8},{10,11... | collective-permute-start | bytes 3145736 | tf_op jit(solution)/shard_map/ppermute | solution.py:293
  247.3 48.8 %collective-permute-start.16 = (bf16[256,2048]{1,0:T(8,128)(2,1)}, bf16[256,2048]{1,0:T(8,128)(2,1)}, u32[]{:S(2)}, u32[]{:S(2)}) collective-permute-start(bf16[256,2048]{1,0:T(8,128)(2,1)} %collective-permute-done.14), channel_id=1, source_target_pairs={{0,8},{4,12},{8,16},{12,20},{16,24},{20,28},{24,0},{28,4},{1,9},{5... | collective-permute-start | bytes 3145736 | tf_op jit(solution)/shard_map/ppermute | solution.py:326
  261.5 36.7 %collective-permute-start.3 = (bf16[256,2048]{1,0:T(8,128)(2,1)}, bf16[256,2048]{1,0:T(8,128)(2,1)}, u32[]{:S(2)}, u32[]{:S(2)}) collective-permute-start(bf16[256,2048]{1,0:T(8,128)(2,1)} %get-tuple-element.129), channel_id=1, source_target_pairs={{0,1},{1,0},{2,3},{3,2},{4,5},{5,4},{6,7},{7,6},{8,9},{9,8},{10,11... | collective-permute-start | bytes 3145736 | tf_op jit(solution)/shard_map/ppermute | solution.py:293
  262.9 35.3 %collective-permute-start.5 = (bf16[256,2048]{1,0:T(8,128)(2,1)}, bf16[256,2048]{1,0:T(8,128)(2,1)}, u32[]{:S(2)}, u32[]{:S(2)}) collective-permute-start(bf16[256,2048]{1,0:T(8,128)(2,1)} %add_convert_fusion.4), channel_id=1, source_target_pairs={{0,2},{1,3},{2,0},{3,1},{4,6},{5,7},{6,4},{7,5},{8,10},{9,11},{10,... | collective-permute-start | bytes 3145736 | tf_op jit(solution)/shard_map/ppermute | solution.py:297
  289.9 26.2 %collective-permute-start.15 = (bf16[256,2048]{1,0:T(8,128)(2,1)}, bf16[256,2048]{1,0:T(8,128)(2,1)S(1)}, u32[]{:S(2)}, u32[]{:S(2)}) collective-permute-start(bf16[256,2048]{1,0:T(8,128)(2,1)} %collective-permute-done.14), channel_id=1, source_target_pairs={{0,4},{4,0},{8,12},{12,8},{16,20},{20,16},{24,28},{28,24},{1,5},{5... | collective-permute-start | bytes 3145736 | tf_op jit(solution)/shard_map/ppermute | solution.py:322
  296.1 42.5 %collective-permute-start.17 = (bf16[256,2048]{1,0:T(8,128)(2,1)}, bf16[256,2048]{1,0:T(8,128)(2,1)S(1)}, u32[]{:S(2)}, u32[]{:S(2)}) collective-permute-start(bf16[256,2048]{1,0:T(8,128)(2,1)} %collective-permute-done.16), channel_id=1, source_target_pairs={{0,4},{4,0},{8,12},{12,8},{16,20},{20,16},{24,28},{28,24},{1,5},{5... | collective-permute-start | bytes 3145736 | tf_op jit(solution)/shard_map/ppermute | solution.py:322
  296.6 28.1 %collective-permute-start.18 = (bf16[256,2048]{1,0:T(8,128)(2,1)}, bf16[256,2048]{1,0:T(8,128)(2,1)S(1)}, u32[]{:S(2)}, u32[]{:S(2)}) collective-permute-start(bf16[256,2048]{1,0:T(8,128)(2,1)} %collective-permute-done.16), channel_id=1, source_target_pairs={{0,8},{4,12},{8,16},{12,20},{16,24},{20,28},{24,0},{28,4},{1,9},{5... | collective-permute-start | bytes 3145736 | tf_op jit(solution)/shard_map/ppermute | solution.py:326
  302.5 43.4 %collective-permute-start.7 = (bf16[256,2048]{1,0:T(8,128)(2,1)S(1)}, bf16[256,2048]{1,0:T(8,128)(2,1)S(1)}, u32[]{:S(2)}, u32[]{:S(2)}) collective-permute-start(bf16[256,2048]{1,0:T(8,128)(2,1)S(1)} %get-tuple-element.106), channel_id=1, source_target_pairs={{0,8},{4,12},{8,16},{12,20},{16,24},{20,28},{24,0},{28,4},{1,9},{5... | collective-permute-start | bytes 3145736 | tf_op jit(solution)/shard_map/ppermute | solution.py:326
  324.6 36.4 %collective-permute-start.19 = (bf16[256,2048]{1,0:T(8,128)(2,1)S(1)}, bf16[256,2048]{1,0:T(8,128)(2,1)S(1)}, u32[]{:S(2)}, u32[]{:S(2)}) collective-permute-start(bf16[256,2048]{1,0:T(8,128)(2,1)S(1)} %collective-permute-done.18), channel_id=1, source_target_pairs={{0,4},{4,0},{8,12},{12,8},{16,20},{20,16},{24,28},{28,24},{1,5},{5... | collective-permute-start | bytes 3145736 | tf_op jit(solution)/shard_map/ppermute | solution.py:322
  339.6 43.9 %collective-permute-start.6 = (bf16[256,2048]{1,0:T(8,128)(2,1)S(1)}, bf16[256,2048]{1,0:T(8,128)(2,1)S(1)}, u32[]{:S(2)}, u32[]{:S(2)}) collective-permute-start(bf16[256,2048]{1,0:T(8,128)(2,1)S(1)} %get-tuple-element.106), channel_id=1, source_target_pairs={{0,4},{4,0},{8,12},{12,8},{16,20},{20,16},{24,28},{28,24},{1,5},{5... | collective-permute-start | bytes 3145736 | tf_op jit(solution)/shard_map/ppermute | solution.py:322
  345.9 25.8 %collective-permute-start.9 = (bf16[256,2048]{1,0:T(8,128)(2,1)S(1)}, bf16[256,2048]{1,0:T(8,128)(2,1)S(1)}, u32[]{:S(2)}, u32[]{:S(2)}) collective-permute-start(bf16[256,2048]{1,0:T(8,128)(2,1)S(1)} %collective-permute-done.7), channel_id=1, source_target_pairs={{0,8},{4,12},{8,16},{12,20},{16,24},{20,28},{24,0},{28,4},{1,9},{5... | collective-permute-start | bytes 3145736 | tf_op jit(solution)/shard_map/ppermute | solution.py:326
  362.1 43.9 %collective-permute-start.8 = (bf16[256,2048]{1,0:T(8,128)(2,1)S(1)}, bf16[256,2048]{1,0:T(8,128)(2,1)S(1)}, u32[]{:S(2)}, u32[]{:S(2)}) collective-permute-start(bf16[256,2048]{1,0:T(8,128)(2,1)S(1)} %collective-permute-done.7), channel_id=1, source_target_pairs={{0,4},{4,0},{8,12},{12,8},{16,20},{20,16},{24,28},{28,24},{1,5},{5... | collective-permute-start | bytes 3145736 | tf_op jit(solution)/shard_map/ppermute | solution.py:322
  371.7 35.4 %collective-permute-start.11 = (bf16[256,2048]{1,0:T(8,128)(2,1)S(1)}, bf16[256,2048]{1,0:T(8,128)(2,1)S(1)}, u32[]{:S(2)}, u32[]{:S(2)}) collective-permute-start(bf16[256,2048]{1,0:T(8,128)(2,1)S(1)} %collective-permute-done.9), channel_id=1, source_target_pairs={{0,8},{4,12},{8,16},{12,20},{16,24},{20,28},{24,0},{28,4},{1,9},{5... | collective-permute-start | bytes 3145736 | tf_op jit(solution)/shard_map/ppermute | solution.py:326
  384.5 43.9 %collective-permute-start.10 = (bf16[256,2048]{1,0:T(8,128)(2,1)S(1)}, bf16[256,2048]{1,0:T(8,128)(2,1)S(1)}, u32[]{:S(2)}, u32[]{:S(2)}) collective-permute-start(bf16[256,2048]{1,0:T(8,128)(2,1)S(1)} %collective-permute-done.9), channel_id=1, source_target_pairs={{0,4},{4,0},{8,12},{12,8},{16,20},{20,16},{24,28},{28,24},{1,5},{5... | collective-permute-start | bytes 3145736 | tf_op jit(solution)/shard_map/ppermute | solution.py:322
  407.0 43.3 %collective-permute-start.12 = (bf16[256,2048]{1,0:T(8,128)(2,1)S(1)}, bf16[256,2048]{1,0:T(8,128)(2,1)S(1)}, u32[]{:S(2)}, u32[]{:S(2)}) collective-permute-start(bf16[256,2048]{1,0:T(8,128)(2,1)S(1)} %collective-permute-done.11), channel_id=1, source_target_pairs={{0,4},{4,0},{8,12},{12,8},{16,20},{20,16},{24,28},{28,24},{1,5},{5... | collective-permute-start | bytes 3145736 | tf_op jit(solution)/shard_map/ppermute | solution.py:322
  617.2 26.1 %collective-permute-start.27 = (bf16[256,2048]{1,0:T(8,128)(2,1)S(1)}, bf16[256,2048]{1,0:T(8,128)(2,1)S(1)}, u32[]{:S(2)}, u32[]{:S(2)}) collective-permute-start(bf16[256,2048]{1,0:T(8,128)(2,1)S(1)} %get-tuple-element.119), channel_id=1, source_target_pairs={{0,4},{4,0},{8,12},{12,8},{16,20},{20,16},{24,28},{28,24},{1,5},{5... | collective-permute-start | bytes 3145736 | tf_op jit(solution)/shard_map/ppermute | solution.py:322
  618.7 68.0 %collective-permute-start.29 = (bf16[256,2048]{1,0:T(8,128)(2,1)}, bf16[256,2048]{1,0:T(8,128)(2,1)}, u32[]{:S(2)}, u32[]{:S(2)}) collective-permute-start(bf16[256,2048]{1,0:T(8,128)(2,1)} %get-tuple-element.122), channel_id=1, source_target_pairs={{0,4},{4,0},{8,12},{12,8},{16,20},{20,16},{24,28},{28,24},{1,5},{5... | collective-permute-start | bytes 3145736 | tf_op jit(solution)/shard_map/ppermute | solution.py:322
  619.2 81.7 %collective-permute-start.31 = (bf16[256,2048]{1,0:T(8,128)(2,1)}, bf16[256,2048]{1,0:T(8,128)(2,1)}, u32[]{:S(2)}, u32[]{:S(2)}) collective-permute-start(bf16[256,2048]{1,0:T(8,128)(2,1)} %get-tuple-element.121), channel_id=1, source_target_pairs={{0,4},{4,0},{8,12},{12,8},{16,20},{20,16},{24,28},{28,24},{1,5},{5... | collective-permute-start | bytes 3145736 | tf_op jit(solution)/shard_map/ppermute | solution.py:322
  620.7 108.8 %collective-permute-start.33 = (bf16[256,2048]{1,0:T(8,128)(2,1)}, bf16[256,2048]{1,0:T(8,128)(2,1)}, u32[]{:S(2)}, u32[]{:S(2)}) collective-permute-start(bf16[256,2048]{1,0:T(8,128)(2,1)} %get-tuple-element.120), channel_id=1, source_target_pairs={{0,4},{4,0},{8,12},{12,8},{16,20},{20,16},{24,28},{28,24},{1,5},{5... | collective-permute-start | bytes 3145736 | tf_op jit(solution)/shard_map/ppermute | solution.py:322
  644.6 42.1 %collective-permute-start.28 = (bf16[256,2048]{1,0:T(8,128)(2,1)}, bf16[256,2048]{1,0:T(8,128)(2,1)}, u32[]{:S(2)}, u32[]{:S(2)}) collective-permute-start(bf16[256,2048]{1,0:T(8,128)(2,1)} %fusion.29), channel_id=1, source_target_pairs={{0,8},{4,12},{8,16},{12,20},{16,24},{20,28},{24,0},{28,4},{1,9},{5... | collective-permute-start | bytes 3145736 | tf_op jit(solution)/shard_map/ppermute | solution.py:326
  682.2 43.6 %all-to-all-start.3 = ((f32[8,2,256]{2,1,0:T(2,128)}), f32[8,2,256]{2,1,0:T(2,128)S(1)}, u32[]{:S(2)}, u32[]{:S(2)}) async-start(f32[8,2,256]{2,1,0:T(2,128)} %copy.212), calls=%async_computation.3 | async-start | bytes 32768 | tf_op jit(solution)/shard_map/all_to_all | solution.py:502
  686.7 178.4 %all-reduce.3.cloned.1.call-start = ((), (), s32[]{:S(2)}) async-start(), calls=%async_computation.13 | async-start | bytes 278528 | tf_op jit(solution)/shard_map/psum | solution.py:568
  689.3 23.7 %collective-permute-start.30 = (bf16[256,2048]{1,0:T(8,128)(2,1)S(1)}, bf16[256,2048]{1,0:T(8,128)(2,1)S(1)}, u32[]{:S(2)}, u32[]{:S(2)}) collective-permute-start(bf16[256,2048]{1,0:T(8,128)(2,1)S(1)} %fusion.28), channel_id=1, source_target_pairs={{0,8},{4,12},{8,16},{12,20},{16,24},{20,28},{24,0},{28,4},{1,9},{5... | collective-permute-start | bytes 3145736 | tf_op jit(solution)/shard_map/ppermute | solution.py:326
  716.1 23.0 %collective-permute-start.32 = (bf16[256,2048]{1,0:T(8,128)(2,1)}, bf16[256,2048]{1,0:T(8,128)(2,1)}, u32[]{:S(2)}, u32[]{:S(2)}) collective-permute-start(bf16[256,2048]{1,0:T(8,128)(2,1)} %fusion.26), channel_id=1, source_target_pairs={{0,8},{4,12},{8,16},{12,20},{16,24},{20,28},{24,0},{28,4},{1,9},{5... | collective-permute-start | bytes 3145736 | tf_op jit(solution)/shard_map/ppermute | solution.py:326
  744.4 610.2 %reduce-scatter.8.cloned.1.call-start = ((), (), s32[]{:S(2)}) async-start(), calls=%async_computation.16 | async-start | bytes 10485760 | tf_op jit(solution)/shard_map/reduce_scatter | solution.py:491
  752.1 606.6 %reduce-scatter.6.cloned.1.call-start = ((), (), s32[]{:S(2)}) async-start(), calls=%async_computation.15 | async-start | bytes 10485760 | tf_op jit(solution)/shard_map/reduce_scatter | solution.py:491
  776.9 585.8 %reduce-scatter.4.cloned.1.call-start = ((), (), s32[]{:S(2)}) async-start(), calls=%async_computation.14 | async-start | bytes 10485760 | tf_op jit(solution)/shard_map/reduce_scatter | solution.py:491
  781.4 26.6 %collective-permute-start.20 = (bf16[256,2048]{1,0:T(8,128)(2,1)}, bf16[256,2048]{1,0:T(8,128)(2,1)}, u32[]{:S(2)}, u32[]{:S(2)}) collective-permute-start(bf16[256,2048]{1,0:T(8,128)(2,1)} %get-tuple-element.123), channel_id=1, source_target_pairs={{0,4},{4,0},{8,12},{12,8},{16,20},{20,16},{24,28},{28,24},{1,5},{5... | collective-permute-start | bytes 3145736 | tf_op jit(solution)/shard_map/ppermute | solution.py:322
  782.8 47.8 %collective-permute-start.22 = (bf16[256,2048]{1,0:T(8,128)(2,1)}, bf16[256,2048]{1,0:T(8,128)(2,1)S(1)}, u32[]{:S(2)}, u32[]{:S(2)}) collective-permute-start(bf16[256,2048]{1,0:T(8,128)(2,1)} %get-tuple-element.126), channel_id=1, source_target_pairs={{0,4},{4,0},{8,12},{12,8},{16,20},{20,16},{24,28},{28,24},{1,5},{5... | collective-permute-start | bytes 3145736 | tf_op jit(solution)/shard_map/ppermute | solution.py:322
  810.0 20.7 %collective-permute-start.21 = (bf16[256,2048]{1,0:T(8,128)(2,1)S(1)}, bf16[256,2048]{1,0:T(8,128)(2,1)S(1)}, u32[]{:S(2)}, u32[]{:S(2)}) collective-permute-start(bf16[256,2048]{1,0:T(8,128)(2,1)S(1)} %fusion.37), channel_id=1, source_target_pairs={{0,8},{4,12},{8,16},{12,20},{16,24},{20,28},{24,0},{28,4},{1,9},{5... | collective-permute-start | bytes 3145736 | tf_op jit(solution)/shard_map/ppermute | solution.py:326
  813.4 20.0 %collective-permute-start.35 = (bf16[256,2048]{1,0:T(8,128)(2,1)}, bf16[256,2048]{1,0:T(8,128)(2,1)}, u32[]{:S(2)}, u32[]{:S(2)}) collective-permute-start(bf16[256,2048]{1,0:T(8,128)(2,1)} %fusion.97), channel_id=1, source_target_pairs={{0,2},{1,3},{2,0},{3,1},{4,6},{5,7},{6,4},{7,5},{8,10},{9,11},{10,... | collective-permute-start | bytes 3145736 | tf_op jit(solution)/shard_map/ppermute | solution.py:297
  822.3 25.2 %collective-permute-start.24 = (bf16[256,2048]{1,0:T(8,128)(2,1)}, bf16[256,2048]{1,0:T(8,128)(2,1)}, u32[]{:S(2)}, u32[]{:S(2)}) collective-permute-start(bf16[256,2048]{1,0:T(8,128)(2,1)} %get-tuple-element.125), channel_id=1, source_target_pairs={{0,4},{4,0},{8,12},{12,8},{16,20},{20,16},{24,28},{28,24},{1,5},{5... | collective-permute-start | bytes 3145736 | tf_op jit(solution)/shard_map/ppermute | solution.py:322
  833.4 17.0 %collective-permute-start.23 = (bf16[256,2048]{1,0:T(8,128)(2,1)}, bf16[256,2048]{1,0:T(8,128)(2,1)}, u32[]{:S(2)}, u32[]{:S(2)}) collective-permute-start(bf16[256,2048]{1,0:T(8,128)(2,1)} %fusion.36), channel_id=1, source_target_pairs={{0,8},{4,12},{8,16},{12,20},{16,24},{20,28},{24,0},{28,4},{1,9},{5... | collective-permute-start | bytes 3145736 | tf_op jit(solution)/shard_map/ppermute | solution.py:326
  833.4 34.7 %collective-permute-start.34 = (bf16[256,2048]{1,0:T(8,128)(2,1)}, bf16[256,2048]{1,0:T(8,128)(2,1)}, u32[]{:S(2)}, u32[]{:S(2)}) collective-permute-start(bf16[256,2048]{1,0:T(8,128)(2,1)} %fusion.97), channel_id=1, source_target_pairs={{0,1},{1,0},{2,3},{3,2},{4,5},{5,4},{6,7},{7,6},{8,9},{9,8},{10,11... | collective-permute-start | bytes 3145736 | tf_op jit(solution)/shard_map/ppermute | solution.py:293
  833.4 34.7 %collective-permute-start.36 = (bf16[256,2048]{1,0:T(8,128)(2,1)}, bf16[256,2048]{1,0:T(8,128)(2,1)}, u32[]{:S(2)}, u32[]{:S(2)}) collective-permute-start(bf16[256,2048]{1,0:T(8,128)(2,1)} %collective-permute-done.35), channel_id=1, source_target_pairs={{0,1},{1,0},{2,3},{3,2},{4,5},{5,4},{6,7},{7,6},{8,9},{9,8},{10,11... | collective-permute-start | bytes 3145736 | tf_op jit(solution)/shard_map/ppermute | solution.py:293
  928.6 99.5 %collective-permute-start.38 = (bf16[256,2048]{1,0:T(8,128)(2,1)}, bf16[256,2048]{1,0:T(8,128)(2,1)S(1)}, u32[]{:S(2)}, u32[]{:S(2)}) collective-permute-start(bf16[256,2048]{1,0:T(8,128)(2,1)} %get-tuple-element.128), channel_id=1, source_target_pairs={{0,1},{1,0},{2,3},{3,2},{4,5},{5,4},{6,7},{7,6},{8,9},{9,8},{10,11... | collective-permute-start | bytes 3145736 | tf_op jit(solution)/shard_map/ppermute | solution.py:293
  935.3 20.8 %collective-permute-start.82 = (bf16[64,2048]{1,0:T(8,128)(2,1)S(1)}, bf16[64,2048]{1,0:T(8,128)(2,1)S(1)}, u32[]{:S(2)}, u32[]{:S(2)}) collective-permute-start(bf16[64,2048]{1,0:T(8,128)(2,1)S(1)} %get-tuple-element.131), channel_id=1, source_target_pairs={{0,4},{4,0},{8,12},{12,8},{16,20},{20,16},{24,28},{28,24},{1,5},{5... | collective-permute-start | bytes 786440 | tf_op jit(solution)/shard_map/ppermute | solution.py:322
  937.0 37.3 %collective-permute-start.84 = (bf16[64,2048]{1,0:T(8,128)(2,1)S(1)}, bf16[64,2048]{1,0:T(8,128)(2,1)S(1)}, u32[]{:S(2)}, u32[]{:S(2)}) collective-permute-start(bf16[64,2048]{1,0:T(8,128)(2,1)S(1)} %get-tuple-element.134), channel_id=1, source_target_pairs={{0,4},{4,0},{8,12},{12,8},{16,20},{20,16},{24,28},{28,24},{1,5},{5... | collective-permute-start | bytes 786440 | tf_op jit(solution)/shard_map/ppermute | solution.py:322
  943.8 33.3 %collective-permute-start.70 = (bf16[4,64,512]{2,1,0:T(8,128)(2,1)S(1)}, bf16[4,64,512]{2,1,0:T(8,128)(2,1)S(1)}, u32[]{:S(2)}, u32[]{:S(2)}) collective-permute-start(bf16[4,64,512]{2,1,0:T(8,128)(2,1)S(1)} %get-tuple-element.137), channel_id=1, source_target_pairs={{0,4},{4,0},{8,12},{12,8},{16,20},{20,16},{24,28},{28,24},{1,5},{5... | collective-permute-start | bytes 786440 | tf_op jit(solution)/shard_map/ppermute | solution.py:322
  1014.6 267.4 %collective-permute-start.26 = (bf16[256,2048]{1,0:T(8,128)(2,1)}, bf16[256,2048]{1,0:T(8,128)(2,1)}, u32[]{:S(2)}, u32[]{:S(2)}) collective-permute-start(bf16[256,2048]{1,0:T(8,128)(2,1)} %get-tuple-element.124), channel_id=1, source_target_pairs={{0,4},{4,0},{8,12},{12,8},{16,20},{20,16},{24,28},{28,24},{1,5},{5... | collective-permute-start | bytes 3145736 | tf_op jit(solution)/shard_map/ppermute | solution.py:322
  1019.4 27.2 %collective-permute-start.88 = (bf16[64,2048]{1,0:T(8,128)(2,1)}, bf16[64,2048]{1,0:T(8,128)(2,1)}, u32[]{:S(2)}, u32[]{:S(2)}) collective-permute-start(bf16[64,2048]{1,0:T(8,128)(2,1)} %get-tuple-element.132), channel_id=1, source_target_pairs={{0,4},{4,0},{8,12},{12,8},{16,20},{20,16},{24,28},{28,24},{1,5},{5... | collective-permute-start | bytes 786440 | tf_op jit(solution)/shard_map/ppermute | solution.py:322
  1021.4 30.3 %collective-permute-start.60 = (bf16[4,64,512]{2,1,0:T(8,128)(2,1)}, bf16[4,64,512]{2,1,0:T(8,128)(2,1)}, u32[]{:S(2)}, u32[]{:S(2)}) collective-permute-start(bf16[4,64,512]{2,1,0:T(8,128)(2,1)} %get-tuple-element.142), channel_id=1, source_target_pairs={{0,4},{4,0},{8,12},{12,8},{16,20},{20,16},{24,28},{28,24},{1,5},{5... | collective-permute-start | bytes 786440 | tf_op jit(solution)/shard_map/ppermute | solution.py:322
  1023.5 36.2 %collective-permute-start.46 = (bf16[4,64,512]{2,1,0:T(8,128)(2,1)}, bf16[4,64,512]{2,1,0:T(8,128)(2,1)}, u32[]{:S(2)}, u32[]{:S(2)}) collective-permute-start(bf16[4,64,512]{2,1,0:T(8,128)(2,1)} %get-tuple-element.146), channel_id=1, source_target_pairs={{0,4},{4,0},{8,12},{12,8},{16,20},{20,16},{24,28},{28,24},{1,5},{5... | collective-permute-start | bytes 786440 | tf_op jit(solution)/shard_map/ppermute | solution.py:322
  1024.7 40.6 %all-to-all-start.6 = ((bf16[4,64,512]{2,1,0:T(8,128)(2,1)}), bf16[4,64,512]{2,1,0:T(8,128)(2,1)S(1)}, u32[]{:S(2)}, u32[]{:S(2)}) async-start(bf16[4,64,512]{2,1,0:T(8,128)(2,1)} %fusion.49), calls=%async_computation.6 | async-start | bytes 524288 | tf_op jit(solution)/shard_map/all_to_all | solution.py:553
  1028.1 18.5 %collective-permute-start.87 = (bf16[64,2048]{1,0:T(8,128)(2,1)}, bf16[64,2048]{1,0:T(8,128)(2,1)S(1)}, u32[]{:S(2)}, u32[]{:S(2)}) collective-permute-start(bf16[64,2048]{1,0:T(8,128)(2,1)} %fusion.44), channel_id=1, source_target_pairs={{0,8},{4,12},{8,16},{12,20},{16,24},{20,28},{24,0},{28,4},{1,9},{5... | collective-permute-start | bytes 786440 | tf_op jit(solution)/shard_map/ppermute | solution.py:326
  1046.6 16.9 %collective-permute-start.45 = (bf16[4,64,512]{2,1,0:T(8,128)(2,1)}, bf16[4,64,512]{2,1,0:T(8,128)(2,1)S(1)}, u32[]{:S(2)}, u32[]{:S(2)}) collective-permute-start(bf16[4,64,512]{2,1,0:T(8,128)(2,1)} %fusion.65), channel_id=1, source_target_pairs={{0,8},{4,12},{8,16},{12,20},{16,24},{20,28},{24,0},{28,4},{1,9},{5... | collective-permute-start | bytes 786440 | tf_op jit(solution)/shard_map/ppermute | solution.py:326
  1051.6 230.3 %collective-permute-start.25 = (bf16[256,2048]{1,0:T(8,128)(2,1)}, bf16[256,2048]{1,0:T(8,128)(2,1)}, u32[]{:S(2)}, u32[]{:S(2)}) collective-permute-start(bf16[256,2048]{1,0:T(8,128)(2,1)} %fusion.34), channel_id=1, source_target_pairs={{0,8},{4,12},{8,16},{12,20},{16,24},{20,28},{24,0},{28,4},{1,9},{5... | collective-permute-start | bytes 3145736 | tf_op jit(solution)/shard_map/ppermute | solution.py:326
  1057.9 219.2 %collective-permute-start.37 = (bf16[256,2048]{1,0:T(8,128)(2,1)}, bf16[256,2048]{1,0:T(8,128)(2,1)}, u32[]{:S(2)}, u32[]{:S(2)}) collective-permute-start(bf16[256,2048]{1,0:T(8,128)(2,1)} %get-tuple-element.127), channel_id=1, source_target_pairs={{0,1},{1,0},{2,3},{3,2},{4,5},{5,4},{6,7},{7,6},{8,9},{9,8},{10,11... | collective-permute-start | bytes 3145736 | tf_op jit(solution)/shard_map/ppermute | solution.py:293
  1059.7 31.8 %collective-permute-start.89 = (bf16[64,2048]{1,0:T(8,128)(2,1)}, bf16[64,2048]{1,0:T(8,128)(2,1)}, u32[]{:S(2)}, u32[]{:S(2)}) collective-permute-start(bf16[64,2048]{1,0:T(8,128)(2,1)} %get-tuple-element.103), channel_id=1, source_target_pairs={{0,4},{4,0},{8,12},{12,8},{16,20},{20,16},{24,28},{28,24},{1,5},{5... | collective-permute-start | bytes 786440 | tf_op jit(solution)/shard_map/ppermute | solution.py:322
  1063.5 29.9 %collective-permute-start.90 = (bf16[64,2048]{1,0:T(8,128)(2,1)}, bf16[64,2048]{1,0:T(8,128)(2,1)}, u32[]{:S(2)}, u32[]{:S(2)}) collective-permute-start(bf16[64,2048]{1,0:T(8,128)(2,1)} %get-tuple-element.103), channel_id=1, source_target_pairs={{0,8},{4,12},{8,16},{12,20},{16,24},{20,28},{24,0},{28,4},{1,9},{5... | collective-permute-start | bytes 786440 | tf_op jit(solution)/shard_map/ppermute | solution.py:326
  1091.6 185.9 %collective-permute-start.39 = (bf16[256,2048]{1,0:T(8,128)(2,1)}, bf16[256,2048]{1,0:T(8,128)(2,1)}, u32[]{:S(2)}, u32[]{:S(2)}) collective-permute-start(bf16[256,2048]{1,0:T(8,128)(2,1)} %add_convert_fusion.3), channel_id=1, source_target_pairs={{0,2},{1,3},{2,0},{3,1},{4,6},{5,7},{6,4},{7,5},{8,10},{9,11},{10,... | collective-permute-start | bytes 3145736 | tf_op jit(solution)/shard_map/ppermute | solution.py:297
  1271.1 58.0 %collective-permute-start.81 = (bf16[64,2048]{1,0:T(8,128)(2,1)S(1)}, bf16[64,2048]{1,0:T(8,128)(2,1)}, u32[]{:S(2)}, u32[]{:S(2)}) collective-permute-start(bf16[64,2048]{1,0:T(8,128)(2,1)S(1)} %collective-permute-done.80), channel_id=1, source_target_pairs={{0,4},{4,0},{8,12},{12,8},{16,20},{20,16},{24,28},{28,24},{1,5},{5... | collective-permute-start | bytes 786440 | tf_op jit(solution)/shard_map/ppermute | solution.py:322
  1277.0 57.3 %collective-permute-start.67 = (bf16[64,2048]{1,0:T(8,128)(2,1)}, bf16[64,2048]{1,0:T(8,128)(2,1)}, u32[]{:S(2)}, u32[]{:S(2)}) collective-permute-start(bf16[64,2048]{1,0:T(8,128)(2,1)} %copy-done.54), channel_id=1, source_target_pairs={{0,4},{4,0},{8,12},{12,8},{16,20},{20,16},{24,28},{28,24},{1,5},{5... | collective-permute-start | bytes 786440 | tf_op jit(solution)/shard_map/ppermute | solution.py:322
  1277.5 62.1 %collective-permute-start.53 = (bf16[64,2048]{1,0:T(8,128)(2,1)}, bf16[64,2048]{1,0:T(8,128)(2,1)}, u32[]{:S(2)}, u32[]{:S(2)}) collective-permute-start(bf16[64,2048]{1,0:T(8,128)(2,1)} %copy-done.55), channel_id=1, source_target_pairs={{0,4},{4,0},{8,12},{12,8},{16,20},{20,16},{24,28},{28,24},{1,5},{5... | collective-permute-start | bytes 786440 | tf_op jit(solution)/shard_map/ppermute | solution.py:322
  (147 other events, 3119.1 us)
Sparse Core Ops, SparseCore 0:
  9.6 88.0 all-gather.5
  99.2 103.2 all-gather.7
  204.1 58.4 all-gather.9
  744.5 120.5 all-reduce.2
  867.5 74.0 reduce-scatter.7
  944.2 71.7 reduce-scatter.5
  1018.5 77.7 reduce-scatter.3

commit v2 on v1

v2 whole, which is shorter than its diff:
```python
import functools

import jax
import jax.numpy as jnp
from jax import lax
from jax.experimental import pallas as pl
from jax.experimental.pallas import tpu as pltpu
from jax.sharding import PartitionSpec as P

HEADS = 16
HD = 128
TOP = 8

EPSILON = 1e-05
THETA = 50000.0
MASKED = -1e30
BF = jnp.bfloat16
F32 = jnp.float32
QCHUNK = 256


def rms_scale(values):
    return lax.rsqrt(jnp.mean(values * values, axis=-1, keepdims=True) + EPSILON)


def norm_back(grad, normed, scale):
    return scale * (grad - normed * jnp.mean(grad * normed, axis=-1, keepdims=True))


def dot(left, right):
    return jnp.dot(left, right, preferred_element_type=F32)


def dot_t(left, right):
    return lax.dot_general(left, right, (((1,), (1,)), ((), ())), preferred_element_type=F32)


def t_dot(left, right):
    return lax.dot_general(left, right, (((0,), (0,)), ((), ())), preferred_element_type=F32)


def params(mib):
    return pltpu.CompilerParams(vmem_limit_bytes=mib << 20)


def cost(flops, size, transcendentals=0):
    return pl.CostEstimate(
        flops=int(flops), bytes_accessed=int(size), transcendentals=int(transcendentals)
    )


def after(value, *others):
    return lax.optimization_barrier((value,) + others)[0]


def pack_columns(q_ref, k_ref, v_ref, out_ref):
    for h in range(q_ref.shape[1] // HD):
        for m, ref in enumerate((q_ref, k_ref, v_ref)):
            start = (3 * h + m) * HD
            out_ref[0, :, start : start + HD] = ref[:, h * HD : (h + 1) * HD]


def packed_columns(w_query, w_key, w_value, shards):
    rows, width = w_query.shape
    part = width // shards
    spec = pl.BlockSpec((rows, part), lambda s: (0, s))
    return pl.pallas_call(
        pack_columns,
        grid=(shards,),
        in_specs=[spec, spec, spec],
        out_specs=pl.BlockSpec((1, rows, 3 * part), lambda s: (s, 0, 0)),
        out_shape=jax.ShapeDtypeStruct((shards, rows, 3 * part), BF),
        compiler_params=params(32),
        cost_estimate=cost(0, 12 * rows * width),
    )(w_query, w_key, w_value)


def turned(values, cosine, sine):
    return values * cosine + pltpu.roll(values, HD // 2, 1) * sine


def turned_back(grad, cosine, sine):
    return grad * cosine - pltpu.roll(grad, HD // 2, 1) * sine


def weights_of(qb, keys, seg_column, seg_row):
    scores = dot_t(qb, keys) * (HD**-0.5)
    scores = jnp.where(seg_column == seg_row, scores, MASKED)
    shifted = jnp.exp(scores - jnp.max(scores, axis=-1, keepdims=True))
    return shifted * (1.0 / jnp.sum(shifted, axis=-1, keepdims=True))


def attend_forward(qkv_ref, cos_ref, sin_ref, gq_ref, gk_ref, segc_ref, segr_ref, o_ref, kb_ref, vb_ref):
    length = qkv_ref.shape[0]
    k_raw = qkv_ref[:, HD : 2 * HD]
    kb_ref[...] = turned(k_raw * rms_scale(k_raw) * gk_ref[...], cos_ref[...], sin_ref[...]).astype(BF)
    vb_ref[...] = qkv_ref[:, 2 * HD :].astype(BF)

    def step(i, carry):
        rows = pl.ds(pl.multiple_of(i * QCHUNK, QCHUNK), QCHUNK)
        q_raw = qkv_ref[rows, :HD]
        qb = turned(q_raw * rms_scale(q_raw) * gq_ref[...], cos_ref[rows, :], sin_ref[rows, :]).astype(BF)
        probs = weights_of(qb, kb_ref[...], segc_ref[rows, :], segr_ref[...])
        o_ref[rows, :] = dot(probs.astype(BF), vb_ref[...]).astype(BF)
        return carry

    lax.fori_loop(0, length // QCHUNK, step, 0)


def attend_backward(
    qkv_ref,
    do_ref,
    cos_ref,
    sin_ref,
    gq_ref,
    gk_ref,
    segc_ref,
    segr_ref,
    grad_ref,
    gains_ref,
    kb_ref,
    vb_ref,
    dk_acc,
    dv_acc,
):
    length = qkv_ref.shape[0]
    scale = HD**-0.5

    @pl.when(pl.program_id(0) == 0)
    def _():
        gains_ref[...] = jnp.zeros_like(gains_ref)

    k_raw = qkv_ref[:, HD : 2 * HD]
    kb_ref[...] = turned(k_raw * rms_scale(k_raw) * gk_ref[...], cos_ref[...], sin_ref[...]).astype(BF)
    vb_ref[...] = qkv_ref[:, 2 * HD :].astype(BF)
    dk_acc[...] = jnp.zeros_like(dk_acc)
    dv_acc[...] = jnp.zeros_like(dv_acc)

    def step(i, carry):
        rows = pl.ds(pl.multiple_of(i * QCHUNK, QCHUNK), QCHUNK)
        cosine, sine = cos_ref[rows, :], sin_ref[rows, :]
        q_raw = qkv_ref[rows, :HD]
        q_scale = rms_scale(q_raw)
        q_norm = q_raw * q_scale
        qb = turned(q_norm * gq_ref[...], cosine, sine).astype(BF)
        probs = weights_of(qb, kb_ref[...], segc_ref[rows, :], segr_ref[...])
        grad_o = do_ref[rows, :]
        grad_probs = dot_t(grad_o, vb_ref[...])
        dv_acc[...] += t_dot(probs.astype(BF), grad_o)
        weighted = probs * grad_probs
        grad_scores = (weighted - probs * jnp.sum(weighted, axis=-1, keepdims=True)).astype(BF)
        dk_acc[...] += t_dot(grad_scores, qb)
        eq = turned_back(dot(grad_scores, kb_ref[...]) * scale, cosine, sine)
        gains_ref[0:1, :] += jnp.sum(eq * q_norm, axis=0, keepdims=True)
        grad_ref[rows, :HD] = norm_back(eq * gq_ref[...], q_norm, q_scale).astype(BF)
        return carry

    lax.fori_loop(0, length // QCHUNK, step, 0)
    ek = turned_back(dk_acc[...] * scale, cos_ref[...], sin_ref[...])
    k_raw = qkv_ref[:, HD : 2 * HD]
    k_scale = rms_scale(k_raw)
    k_norm = k_raw * k_scale
    gains_ref[1:2, :] += jnp.sum(ek * k_norm, axis=0, keepdims=True)
    grad_ref[:, HD : 2 * HD] = norm_back(ek * gk_ref[...], k_norm, k_scale).astype(BF)
    grad_ref[:, 2 * HD :] = dv_acc[...].astype(BF)


def attention_specs(length):
    table = pl.BlockSpec((length, HD), lambda h: (0, 0))
    gain = pl.BlockSpec((1, HD), lambda h: (0, 0))
    column = pl.BlockSpec((length, 1), lambda h: (0, 0))
    row = pl.BlockSpec((1, length), lambda h: (0, 0))
    return [table, table, gain, gain, column, row]


def attention_forward(qkv, attn_args):
    length = qkv.shape[0]
    heads = qkv.shape[1] // (3 * HD)
    return pl.pallas_call(
        attend_forward,
        grid=(heads,),
        in_specs=[pl.BlockSpec((length, 3 * HD), lambda h: (0, h))] + attention_specs(length),
        out_specs=pl.BlockSpec((length, HD), lambda h: (0, h)),
        out_shape=jax.ShapeDtypeStruct((length, heads * HD), BF),
        scratch_shapes=[pltpu.VMEM((length, HD), BF)] * 2,
        compiler_params=params(40),
        cost_estimate=cost(16 * heads * length * length * HD, qkv.size * 5, heads * length * length),
    )(qkv, *attn_args)


def attention_backward(qkv, grad_o, attn_args):
    length = qkv.shape[0]
    heads = qkv.shape[1] // (3 * HD)
    wide = pl.BlockSpec((length, 3 * HD), lambda h: (0, h))
    return pl.pallas_call(
        attend_backward,
        grid=(heads,),
        in_specs=[wide, pl.BlockSpec((length, HD), lambda h: (0, h))] + attention_specs(length),
        out_specs=[wide, pl.BlockSpec((8, HD), lambda h: (0, 0))],
        out_shape=[
            jax.ShapeDtypeStruct(qkv.shape, BF),
            jax.ShapeDtypeStruct((8, HD), F32),
        ],
        scratch_shapes=[pltpu.VMEM((length, HD), BF)] * 2 + [pltpu.VMEM((length, HD), F32)] * 2,
        compiler_params=params(48),
        cost_estimate=cost(40 * heads * length * length * HD, qkv.size * 7, heads * length * length),
    )(qkv, grad_o, *attn_args)


def pick_rows(has_input, number_ref, slots_ref, named_ref, router_ref, x_ref, grad_ref, *refs):
    rows_ref, grad_rows_ref, gates_ref = refs[2 * has_input :]
    experts, capacity = slots_ref.shape[1], rows_ref.shape[2]
    count = x_ref.shape[0]
    x = x_ref[...]
    named = named_ref[0]
    logits = dot(x, router_ref[...])
    lane = lax.broadcasted_iota(jnp.int32, logits.shape, 1)
    logits = jnp.where(lane < number_ref[2], logits, MASKED)
    exps = jnp.exp(logits - jnp.max(logits, axis=-1, keepdims=True))
    probs = exps / jnp.sum(exps, axis=-1, keepdims=True)
    chosen = jnp.where(named > 0.0, probs, 0.0)
    gates = chosen / jnp.sum(chosen, axis=-1, keepdims=True)
    grad = grad_ref[0].astype(F32)
    wanted = lax.broadcasted_iota(jnp.int32, (capacity, count), 0)
    columns = []
    for j in range(experts):
        gate = jnp.sum(jnp.where(lane == number_ref[1] + j, gates, 0.0), axis=1, keepdims=True)
        hot = (wanted == slots_ref[0, j : j + 1, :]).astype(BF)
        rows_ref[j, 0] = dot(hot, x).astype(BF)
        grad_rows_ref[j, 0] = dot(hot, (grad * gate).astype(BF)).astype(BF)
        columns.append(gate)
    gates_ref[...] = jnp.concatenate(columns, axis=1)


def pick(number, slots, named, router, x, grads, held, place, blocks, capacity):
    count, width = x.shape
    experts = slots.shape[1]
    lanes = router.shape[1]
    shape = jax.ShapeDtypeStruct((experts, blocks, capacity, width), BF)
    whole = pl.BlockSpec(memory_space=pl.ANY)
    out = pl.BlockSpec((experts, 1, capacity, width), lambda i, n: (0, place, 0, 0))
    return pl.pallas_call(
        functools.partial(pick_rows, held is not None),
        grid_spec=pltpu.PrefetchScalarGridSpec(
            num_scalar_prefetch=1,
            grid=(1,),
            in_specs=[
                pl.BlockSpec((1, experts, count), lambda i, n: (n[0], 0, 0)),
                pl.BlockSpec((1, count, lanes), lambda i, n: (n[0], 0, 0)),
                pl.BlockSpec((width, lanes), lambda i, n: (0, 0)),
                pl.BlockSpec((count, width), lambda i, n: (0, 0)),
                pl.BlockSpec((1, count, width), lambda i, n: (n[0], 0, 0)),
            ]
            + [whole, whole] * (held is not None),
            out_specs=[out, out, pl.BlockSpec((count, experts), lambda i, n: (0, 0))],
        ),
        out_shape=[shape, shape, jax.ShapeDtypeStruct((count, experts), F32)],
        input_output_aliases={} if held is None else {6: 0, 7: 1},
        compiler_params=params(40),
        cost_estimate=cost(
            4 * experts * capacity * count * width, 4 * width * (count + experts * capacity)
        ),
    )(number, slots, named, router, x, grads, *(held or ()))


def merge_rows(blocks, ids_ref, slots_ref, *refs):
    experts = slots_ref.shape[2]
    rows_refs, out_refs = refs[:experts], refs[experts:]
    capacity = rows_refs[0].shape[0]
    count = out_refs[0].shape[0]
    place = lax.broadcasted_iota(jnp.int32, (count, capacity), 1)
    total = None
    for j in range(experts):
        hot = (place == slots_ref[0, :, j : j + 1]).astype(BF)
        rows = dot(hot, rows_refs[j][...])
        total = rows if total is None else total + rows
    for i in range(blocks):

        @pl.when(pl.program_id(0) == i)
        def _(i=i):
            out_refs[i][...] = total.astype(BF)


def merge_results(blocks, ids_ref, slots_ref, grad_ref, *refs):
    experts = slots_ref.shape[2]
    gates_refs, refs = refs[:blocks], refs[blocks:]
    rows_refs, out_refs, dgate_ref = refs[:experts], refs[experts:-1], refs[-1]
    capacity = rows_refs[0].shape[0]
    count = out_refs[0].shape[0]
    place = lax.broadcasted_iota(jnp.int32, (count, capacity), 1)
    grad = grad_ref[0].astype(F32)
    gates = gates_refs[0][...]
    for i in range(1, blocks):
        gates = jnp.where(pl.program_id(0) == i, gates_refs[i][...], gates)
    total = None
    dgates = []
    for j in range(experts):
        hot = (place == slots_ref[0, :, j : j + 1]).astype(BF)
        rows = dot(hot, rows_refs[j][...])
        dgates.append(jnp.sum(rows * grad, axis=1, keepdims=True))
        gated = rows * gates[:, j : j + 1]
        total = gated if total is None else total + gated
    dgate_ref[0] = jnp.concatenate(dgates, axis=1)
    for i in range(blocks):

        @pl.when(pl.program_id(0) == i)
        def _(i=i):
            out_refs[i][...] = total.astype(BF)


def merge(ids, slots, rows, gates=None, grads=None):
    blocks = ids.shape[0]
    count, experts = slots.shape[1:]
    capacity = rows[0].shape[0] // blocks
    width = rows[0].shape[1]
    small = pl.BlockSpec((1, count, experts), lambda b, n: (n[b], 0, 0))
    in_specs = [small]
    operands = [slots]
    out_specs = [pl.BlockSpec((count, width), lambda b, n: (0, 0))] * blocks
    out_shape = [jax.ShapeDtypeStruct((count, width), BF)] * blocks
    if gates is not None:
        in_specs += [pl.BlockSpec((1, count, width), lambda b, n: (n[b], 0, 0))]
        in_specs += [pl.BlockSpec((count, experts), lambda b, n: (0, 0))] * blocks
        operands += [grads] + list(gates)
        out_specs = out_specs + [pl.BlockSpec((1, count, experts), lambda b, n: (b, 0, 0))]
        out_shape = out_shape + [jax.ShapeDtypeStruct((blocks, count, experts), F32)]
    in_specs += [pl.BlockSpec((capacity, width), lambda b, n: (b, 0))] * experts
    return pl.pallas_call(
        functools.partial(merge_rows if gates is None else merge_results, blocks),
        grid_spec=pltpu.PrefetchScalarGridSpec(
            num_scalar_prefetch=1, grid=(blocks,), in_specs=in_specs, out_specs=out_specs
        ),
        out_shape=out_shape,
        compiler_params=params(40),
        cost_estimate=cost(
            2 * blocks * experts * capacity * count * width,
            2 * blocks * width * (2 * count + experts * capacity),
        ),
    )(ids, *operands, *rows)


def expert_body(
    sub,
    x_ref,
    dy_ref,
    wg_ref,
    wu_ref,
    wd_ref,
    y_ref,
    dx_ref,
    h_ref,
    dg_ref,
    du_ref,
    y_acc,
    dx_acc,
):
    f = pl.program_id(0)
    last = pl.num_programs(0) - 1

    def step(i, carry):
        r = pl.ds(pl.multiple_of(i * sub, sub), sub)
        x = x_ref[r, :]
        gate = dot(x, wg_ref[...])
        up = dot(x, wu_ref[...])
        sigmoid = 1.0 / (1.0 + jnp.exp(-gate))
        activated = gate * sigmoid
        hidden = (activated * up).astype(BF)
        h_ref[r, :] = hidden
        grad_hidden = dot_t(dy_ref[r, :], wd_ref[...])
        grad_gate = (grad_hidden * up * sigmoid * (1.0 + gate * (1.0 - sigmoid))).astype(BF)
        grad_up = (grad_hidden * activated).astype(BF)
        dg_ref[r, :] = grad_gate
        du_ref[r, :] = grad_up
        y = dot(hidden, wd_ref[...])
        dx = dot_t(grad_gate, wg_ref[...]) + dot_t(grad_up, wu_ref[...])

        @pl.when(f == 0)
        def _():
            y_acc[r, :] = y
            dx_acc[r, :] = dx

        @pl.when((f > 0) & (f < last))
        def _():
            y_acc[r, :] += y
            dx_acc[r, :] += dx

        @pl.when(f == last)
        def _():
            y_ref[r, :] = (y_acc[r, :] + y).astype(BF)
            dx_ref[r, :] = (dx_acc[r, :] + dx).astype(BF)

        return carry

    lax.fori_loop(0, x_ref.shape[0] // sub, step, 0)


def expert(j, x, dy, w_gate, w_up, w_down):
    _, rows, width = x.shape
    hidden = w_gate.shape[2]
    tile = hidden // 2
    rows_in = pl.BlockSpec((None, rows, width), lambda f: (j, 0, 0))
    rows_out = pl.BlockSpec((rows, width), lambda f: (0, 0))
    part = pl.BlockSpec((rows, tile), lambda f: (0, f))
    wide = jax.ShapeDtypeStruct((rows, width), BF)
    thin = jax.ShapeDtypeStruct((rows, hidden), BF)
    return pl.pallas_call(
        functools.partial(expert_body, rows // 2),
        grid=(2,),
        in_specs=[
            rows_in,
            rows_in,
            pl.BlockSpec((None, width, tile), lambda f: (j, 0, f)),
            pl.BlockSpec((None, width, tile), lambda f: (j, 0, f)),
            pl.BlockSpec((None, tile, width), lambda f: (j, f, 0)),
        ],
        out_specs=[rows_out, rows_out, part, part, part],
        out_shape=[wide, wide, thin, thin, thin],
        scratch_shapes=[pltpu.VMEM((rows, width), F32)] * 2,
        compiler_params=params(58),
        cost_estimate=cost(
            12 * rows * width * hidden,
            8 * rows * width + 6 * rows * hidden + 6 * width * hidden,
            rows * hidden,
        ),
    )(x, dy, w_gate, w_up, w_down)


def weight_grads_body(groups, count, *refs):
    left, rights, outs = refs[:groups], refs[groups : groups + groups * count], refs[-count:]
    for n in range(count):
        total = None
        for g in range(groups):
            part = t_dot(left[g][...], rights[n * groups + g][...])
            total = part if total is None else total + part
        outs[n][...] = total.astype(BF)


def weight_grads(lefts, rights, left_index, right_index):
    groups, count = len(lefts), len(rights)

    def tiled(array, index, tile):
        if array.ndim == 3:
            return pl.BlockSpec((None, array.shape[1], tile), lambda d: (index, 0, d))
        return pl.BlockSpec((array.shape[0], tile), lambda d: (0, d))

    def fixed(array, index):
        if array.ndim == 3:
            return pl.BlockSpec((None,) + array.shape[1:], lambda d: (index, 0, 0))
        return pl.BlockSpec(array.shape, lambda d: (0, 0))

    tall = lefts[0].shape[-1]
    wide = rights[0][0].shape[-1]
    tile = 256
    flat = [r for one in rights for r in one]
    total_rows = sum(a.shape[-2] for a in lefts)
    return pl.pallas_call(
        functools.partial(weight_grads_body, groups, count),
        grid=(tall // tile,),
        in_specs=[tiled(a, left_index, tile) for a in lefts] + [fixed(a, right_index) for a in flat],
        out_specs=[pl.BlockSpec((tile, wide), lambda d: (d, 0))] * count,
        out_shape=[jax.ShapeDtypeStruct((tall, wide), BF)] * count,
        compiler_params=params(48),
        cost_estimate=cost(
            2 * count * total_rows * tall * wide,
            2 * total_rows * (tall + count * wide) + 2 * count * tall * wide,
        ),
    )(*lefts, *flat)


def swap_core(value):
    return lax.ppermute(value, "shard", [(i, i ^ 1) for i in range(4)])


def swap_x(value):
    return lax.ppermute(value, "shard", [(i, i ^ 2) for i in range(4)])


def shard_order(position):
    return [position, position ^ 1, position ^ 2, position ^ 3]


def shard_gather(value):
    far = swap_x(value)
    near = swap_core(value)
    return [value, near, far, swap_core(far)]


def shard_reduce(blocks):
    far = blocks[2].astype(F32) + swap_core(blocks[3].astype(BF)).astype(F32)
    far = swap_x(far.astype(BF))
    near = blocks[0].astype(F32) + swap_core(blocks[1].astype(BF)).astype(F32)
    return near + far.astype(F32)


def ring_next(count):
    return [(z * 2 + y, ((z + 1) % (count // 2)) * 2 + y) for z in range(count // 2) for y in range(2)]


def swap_y(value, count):
    return lax.ppermute(value, "rep", [(i, i ^ 1) for i in range(count)])


def turn_z(value, count):
    return lax.ppermute(value, "rep", ring_next(count))


def rep_order(rep, count):
    planes = count // 2
    z, y = rep // 2, rep % 2
    return [((z + planes - k) % planes) * 2 + (y ^ w) for k in range(planes) for w in range(2)]


def rep_gather(value, count):
    blocks = []
    held = value
    for k in range(count // 2):
        if k > 0:
            held = turn_z(held, count)
        blocks += [held, swap_y(held, count)]
    return blocks


def rep_reduce(blocks, count):
    planes = count // 2

    def pair(k):
        return blocks[2 * k].astype(F32) + swap_y(blocks[2 * k + 1].astype(BF), count).astype(F32)

    total = pair(1)
    for k in list(range(2, planes)) + [0]:
        total = turn_z(total.astype(BF), count).astype(F32) + pair(k)
    return total


def write_sums_body(blocks, shards, ids_ref, wq_ref, wk_ref, wv_ref, gain_ref, *refs):
    in_refs, (q_ref, k_ref, v_ref, o_ref, extra_ref) = refs[:blocks], refs[blocks:]
    width = q_ref.shape[1]
    heads = width // HD
    for i in range(blocks):

        @pl.when(pl.program_id(0) == i)
        def _(i=i):
            ref = in_refs[i]
            attn = None
            for m, (out, weight) in enumerate(((q_ref, wq_ref), (k_ref, wk_ref), (v_ref, wv_ref))):
                for h in range(heads):
                    start = (3 * h + m) * HD
                    piece = ref[:, start : start + HD].astype(F32)
                    out[:, h * HD : (h + 1) * HD] = piece
                    term = piece * weight[:, h * HD : (h + 1) * HD].astype(F32)
                    attn = term if attn is None else attn + term
            o_ref[...] = ref[:, 3 * width : 4 * width].astype(F32)
            extra = ref[:, 4 * width :].astype(F32)
            attn = jnp.sum(attn, axis=1, keepdims=True) / gain_ref[...]
            lane = lax.broadcasted_iota(jnp.int32, extra.shape, 1)
            extra_ref[...] = jnp.where(lane == extra.shape[1] - 1, attn, extra)


def write_sums(ids, w_query, w_key, w_value, gain, gathered, shards):
    blocks = len(gathered)
    part, total = gathered[0].shape
    rows, width = w_query.shape
    own = pl.BlockSpec((part, width), lambda b, n: (n[b], 0))
    extra = pl.BlockSpec((part, HD), lambda b, n: (n[b], 0))
    big = jax.ShapeDtypeStruct((rows, width), F32)
    return pl.pallas_call(
        functools.partial(write_sums_body, blocks, shards),
        grid_spec=pltpu.PrefetchScalarGridSpec(
            num_scalar_prefetch=1,
            grid=(blocks,),
            in_specs=[own, own, own, pl.BlockSpec((part, 1), lambda b, n: (n[b], 0))]
            + [pl.BlockSpec((part, total), lambda b, n: (0, 0))] * blocks,
            out_specs=[own, own, own, own, extra],
        ),
        out_shape=[big, big, big, big, jax.ShapeDtypeStruct((rows, HD), F32)],
        compiler_params=params(52),
        cost_estimate=cost(0, rows * width * 30),
    )(ids, w_query, w_key, w_value, gain, *gathered)


def on_device(
    tokens,
    w_query,
    w_key,
    w_value,
    w_out,
    w_router,
    norm_attn,
    norm_ffn,
    norm_query,
    norm_key,
    w_gate,
    w_up,
    w_down,
    segments,
    routes,
    cotangent,
):
    rows_count, width = tokens.shape
    experts = w_router.shape[1]
    local_experts = w_gate.shape[0]
    rep_count = lax.axis_size("rep")
    shard_count = lax.axis_size("shard")
    position = lax.axis_index("shard")
    rep = lax.axis_index("rep")
    length = rows_count * shard_count
    capacity = max(2, rows_count * TOP * 9 // (8 * experts))
    capacity = -(-capacity // 16) * 16
    rows = w_query.shape[0]
    order = rep_order(rep, rep_count)
    order_in = shard_order(position)
    group_size = 4
    groups = [list(range(s, s + group_size)) for s in range(0, rep_count, group_size)]

    token_blocks = shard_gather(tokens)
    packed = packed_columns(w_query, w_key, w_value, shard_count)
    columns = lax.all_to_all(packed, "shard", split_axis=0, concat_axis=0, tiled=True)
    columns = columns.reshape(width, -1)
    routes_b = jnp.pad(routes.astype(BF), ((0, 0), (0, HD - TOP)))
    grads = lax.all_gather(jnp.concatenate([cotangent, routes_b], axis=1), "rep", axis=0, tiled=False)

    small = jnp.concatenate(
        [
            w_router,
            norm_attn[:, None],
            norm_ffn[:, None],
            jnp.pad(norm_query, (0, rows - norm_query.shape[0]))[:, None],
            jnp.pad(norm_key, (0, rows - norm_key.shape[0]))[:, None],
        ],
        axis=1,
    )
    small = jnp.pad(small, ((0, 0), (0, HD - small.shape[1])))
    small = jnp.stack(shard_gather(small))
    order_in_array = jnp.stack(order_in)
    small = jnp.zeros_like(small).at[order_in_array].set(small)
    head_gains = small[:, : norm_query.shape[0], experts + 2 : experts + 4].astype(F32)
    gain_query = head_gains[:, :, 0].reshape(1, HD)
    gain_key = head_gains[:, :, 1].reshape(1, HD)
    small = small.reshape(width, HD)
    gain_attn = small[:, experts].astype(F32)
    gain_ffn = small[:, experts + 1].astype(F32)
    full_router = small[:, :experts]

    full_gate = lax.all_gather(after(w_gate, columns), "shard", axis=1, tiled=True)
    full_up = lax.all_gather(after(w_up, columns), "shard", axis=1, tiled=True)
    full_down = lax.all_gather(after(w_down, columns), "shard", axis=1, tiled=True)

    expert_ids = jnp.arange(experts, dtype=jnp.int32)
    named_all = jnp.any(
        grads[:, :, width : width + TOP].astype(jnp.int32)[:, :, :, None] == expert_ids, axis=2
    )
    first_expert = rep * local_experts
    named_mine = lax.dynamic_slice_in_dim(named_all, first_expert, local_experts, axis=2)
    before = jnp.tril(jnp.ones((rows_count, rows_count), BF), -1)
    slot_mine = jnp.einsum("ts,bsj->btj", before, named_mine.astype(BF), preferred_element_type=F32)
    slot_tokens = jnp.where(named_mine, slot_mine.astype(jnp.int32), -1)
    slot_lanes = jnp.swapaxes(slot_tokens, 1, 2)
    named_lanes = jnp.pad(named_all.astype(F32), ((0, 0), (0, 0), (0, HD - experts)))

    tokens_all = jnp.concatenate(token_blocks, axis=0).astype(F32)
    input_b = (tokens_all * rms_scale(tokens_all) * gain_attn).astype(BF)
    qkv = dot(input_b, columns)
    places = jnp.concatenate([p * rows_count + jnp.arange(rows_count, dtype=jnp.int32) for p in order_in])
    inverse = THETA ** (-jnp.arange(HD // 2, dtype=F32) * 2.0 / HD)
    angles = places.astype(F32)[:, None] * inverse[None, :]
    cosine, sine = jnp.cos(angles), jnp.sin(angles)
    cosine = jnp.concatenate([cosine, cosine], axis=-1)
    sine = jnp.concatenate([-sine, sine], axis=-1)
    segment_all = jnp.concatenate(
        [lax.dynamic_slice_in_dim(segments[0], p * rows_count, rows_count) for p in order_in]
    )
    attn_args = (cosine, sine, gain_query, gain_key, segment_all[:, None], segment_all[None, :])
    mixed_b = attention_forward(qkv, attn_args)
    projected = dot(mixed_b, w_out).astype(BF)
    projected = [projected[i * rows_count : (i + 1) * rows_count] for i in range(shard_count)]
    tokens_f = tokens.astype(F32)
    hidden_state = tokens_f + shard_reduce(projected)

    scale_mid = rms_scale(hidden_state)
    normed_mid = hidden_state * scale_mid
    mid_b = (normed_mid * gain_ffn).astype(BF)
    mid_blocks = rep_gather(mid_b, rep_count)
    router_lanes = jnp.pad(full_router, ((0, 0), (0, HD - experts)))
    expert_rows, grad_rows, kept, result_parts, grad_parts, dgate_parts = [], [], [], [], [], []
    for group in groups:
        held, gates = None, []
        for place, b in enumerate(group):
            number = jnp.stack([order[b], first_expert, jnp.int32(experts)])
            x, dy, gate = pick(
                number,
                slot_lanes,
                named_lanes,
                router_lanes,
                mid_blocks[b],
                grads,
                held,
                place,
                len(group),
                capacity,
            )
            held = (x, dy)
            gates.append(gate)
        x, dy = [a.reshape(local_experts, len(group) * capacity, width) for a in held]
        done = [expert(j, x, dy, full_gate, full_up, full_down) for j in range(local_experts)]
        ids = jnp.stack([order[b] for b in group])
        grad_parts += merge(ids, slot_tokens, [d[1] for d in done])
        *parts, dgate = merge(ids, slot_tokens, [d[0] for d in done], gates, grads)
        result_parts += parts
        dgate_parts.append(dgate)
        expert_rows.append(x)
        grad_rows.append(dy)
        kept.append(done)
    grad_mid_moe = rep_reduce(grad_parts, rep_count)
    expert_sum = rep_reduce(result_parts, rep_count)
    output = (hidden_state + expert_sum).astype(BF)

    def owned_part(grad):
        return lax.psum_scatter(grad, "shard", scatter_dimension=0, tiled=True)

    sums_gate, sums_up, sums_down = [], [], []
    for j in range(local_experts):
        down, = weight_grads([k[j][2] for k in kept], [grad_rows], None, j)
        gate, up = weight_grads(
            expert_rows, [[k[j][3] for k in kept], [k[j][4] for k in kept]], j, None
        )
        sums_down.append(owned_part(down))
        sums_gate.append(owned_part(gate))
        sums_up.append(owned_part(up))
    grad_gate = jnp.stack(sums_gate).astype(F32)
    grad_up = jnp.stack(sums_up).astype(F32)
    grad_down = jnp.stack(sums_down).astype(F32)

    order_array = jnp.stack(order)
    dgates = jnp.swapaxes(jnp.concatenate(dgate_parts), 1, 2)
    dgates = jnp.zeros_like(dgates).at[order_array].set(dgates)
    dgates = lax.all_to_all(dgates, "rep", split_axis=0, concat_axis=0, tiled=True)
    dgates = dgates.reshape(experts, rows_count).T
    named_own = jnp.any(routes[:, :, None] == expert_ids, axis=1)
    logits = dot(mid_b, full_router)
    exps = jnp.exp(logits - jnp.max(logits, axis=-1, keepdims=True))
    probs_own = exps / jnp.sum(exps, axis=-1, keepdims=True)
    chosen_total = jnp.sum(jnp.where(named_own, probs_own, 0.0), axis=1, keepdims=True)
    gates_own = jnp.where(named_own, probs_own, 0.0) / chosen_total
    grad_probs = jnp.where(
        named_own, dgates - jnp.sum(dgates * gates_own, axis=1, keepdims=True), 0.0
    ) / chosen_total
    grad_logits = (
        probs_own * (grad_probs - jnp.sum(probs_own * grad_probs, axis=1, keepdims=True))
    ).astype(BF)
    grad_mid = grad_mid_moe + dot_t(grad_logits, full_router)
    grad_gain_ffn = jnp.sum(grad_mid * normed_mid, axis=0)
    grad_router = t_dot(mid_b, grad_logits)
    grad_out = cotangent.astype(F32)
    grad_state = grad_out + norm_back(grad_mid * gain_ffn, normed_mid, scale_mid)
    grad_state_b = grad_state.astype(BF)

    grad_state_all = jnp.concatenate(shard_gather(grad_state_b), axis=0)
    grad_mixed = dot_t(grad_state_all, w_out).astype(BF)
    grad_out_proj = t_dot(mixed_b, grad_state_all).astype(BF)
    grad_qkv, grad_head_gains = attention_backward(qkv, grad_mixed, attn_args)
    grad_columns = t_dot(input_b, grad_qkv).astype(BF)
    grad_input = dot_t(grad_qkv, columns).astype(BF)
    grad_input = shard_reduce(
        [grad_input[i * rows_count : (i + 1) * rows_count] for i in range(shard_count)]
    )
    normed_in = tokens_f * rms_scale(tokens_f)
    tokens_grad = (
        grad_state + norm_back(grad_input * gain_attn, normed_in, rms_scale(tokens_f))
    ).astype(BF)

    part = rows // rep_count
    piece = HD // shard_count
    head_columns = jnp.pad(
        grad_head_gains[:2].reshape(2, shard_count, piece), ((0, 0), (0, 0), (0, rows - piece))
    ).reshape(2, width)
    extras = jnp.concatenate(
        [grad_router, grad_gain_ffn[:, None], head_columns.T], axis=1
    )
    extras = jnp.pad(extras, ((0, 0), (0, HD - extras.shape[1]))).astype(BF)
    out_columns = jnp.swapaxes(grad_out_proj.reshape(rows, shard_count, -1), 0, 1)
    out_columns = out_columns.reshape(shard_count, rep_count, part, -1)
    column_parts = grad_columns.reshape(shard_count, rep_count, part, -1)
    extra_parts = extras.reshape(shard_count, rep_count, part, -1)
    to_sum = jnp.concatenate([column_parts, extra_parts, out_columns], axis=3)
    to_sum = [lax.dynamic_index_in_dim(to_sum, r, axis=1, keepdims=False) for r in order]
    part_sum = rep_reduce(to_sum, rep_count).astype(BF)
    split = grad_columns.shape[1] + HD
    mine = lax.all_to_all(part_sum[:, :, :split], "shard", split_axis=0, concat_axis=0, tiled=True)
    wide = jnp.swapaxes(mine[:, :, : split - HD], 0, 1).reshape(part, -1)
    extra = jnp.sum(mine[:, :, split - HD :].astype(F32), axis=0).astype(BF)
    out_part = jnp.swapaxes(part_sum[:, :, split:], 0, 1).reshape(part, -1)
    gathered = rep_gather(jnp.concatenate([wide, out_part, extra], axis=1), rep_count)
    sum_query, sum_key, sum_value, sum_out, extra = write_sums(
        order_array,
        w_query,
        w_key,
        w_value,
        norm_attn.astype(F32)[:, None],
        gathered,
        shard_count,
    )
    return (
        output,
        tokens_grad,
        sum_query,
        sum_key,
        sum_value,
        sum_out,
        extra[:, :experts],
        extra[:, HD - 1],
        extra[:, experts],
        extra[:piece, experts + 1],
        extra[:piece, experts + 2],
        grad_gate,
        grad_up,
        grad_down,
    )


def solution(mesh):
    return jax.shard_map(
        on_device,
        mesh=mesh,
        in_specs=(
            P(("rep", "shard"), None),
            P("shard", None),
            P("shard", None),
            P("shard", None),
            P("shard", None),
            P("shard", None),
            P("shard"),
            P("shard"),
            P("shard"),
            P("shard"),
            P("rep", "shard", None),
            P("rep", "shard", None),
            P("rep", "shard", None),
            P("rep", None),
            P(("rep", "shard"), None),
            P(("rep", "shard"), None),
        ),
        out_specs=(
            P(("rep", "shard"), None),
            P(("rep", "shard"), None),
            P("shard", None),
            P("shard", None),
            P("shard", None),
            P("shard", None),
            P("shard", None),
            P("shard"),
            P("shard"),
            P("shard"),
            P("shard"),
            P("rep", "shard", None),
            P("rep", "shard", None),
            P("rep", "shard", None),
        ),
        check_vma=False,
    )
```

time: 1380 us -> 1160 us (0.84)
  matrix products: 242 us -> 47.8 us
  Pallas kernels: 90.8 us -> 276 us
  blocking collectives: 159 us -> 74.9 us
  starting transfers between devices: 123 us -> 41.8 us
  other arithmetic: 118 us -> 83.6 us
  local copies, waits for them, and re-layouts: 143 us -> 113 us
  waiting for transfers between devices: 481 us -> 500 us
    pallas_call x6 -> x24, Pallas kernels: 90.8 us -> 276 us  [the longest x4 99.7 us: expert(): pl.pallas_call(functools.partial(expert_body, rows // 2), grid=(2,), in_s...]
    ppermute x4 -> x5, waiting for transfers between devices: 14.7 us -> 101 us  [swap_x(): return lax.ppermute(value, 'shard', [(i, i ^ 2) for i in range(4)])]
    dot_general x11 -> x3, matrix products: 92.9 us -> 17.6 us  [dot_t(): lax.dot_general(left, right, (((1,), (1,)), ((), ())), preferred_element_...]
    all_to_all x0 -> x1, blocking collectives: none -> 74.9 us  [on_device(): lax.all_to_all(packed, 'shard', split_axis=0, concat_axis=0, tiled=True)]
    all_gather x2 -> x0, blocking collectives: 70.7 us -> none  [the longest x1 45.2 us: on_device(): route_all = lax.all_gather(routes, 'rep', axis=0, tiled=False)[order]]
    dot_general x11 -> x3, matrix products: 74.2 us -> 13.7 us  [t_dot(): lax.dot_general(left, right, (((0,), (0,)), ((), ())), preferred_element_...]
    dot_general x11 -> x3, matrix products: 69.2 us -> 16.3 us  [dot(): return jnp.dot(left, right, preferred_element_type=F32)]
    unnamed x1 -> x0, blocking collectives: 50.4 us -> none
  transfers between devices with their start and end apart: 110 -> 62, of which waited for: 59 -> 26; matrix products, arithmetic and copies ran while one was open for 30% -> 14% of each run, Pallas kernels for 6% -> 17%
where the time goes in v2:
time: 1160 us; the launch traced here: 1150 us
  waiting for transfers between devices  500 us (43%)
  Pallas kernels  276 us (24%)
  local copies, waits for them, and re-layouts  113 us (10%)
  other arithmetic  83.6 us (7%)
  blocking collectives  74.9 us (6%)
  matrix products  47.8 us (4%)
  starting transfers between devices  41.8 us (4%)
  between operations  15.9 us (1%)
    ppermute x20, waiting for transfers between devices, swap_y(): return lax.ppermute(value, 'rep', [(i, i ^ 1) for i in range(count)])  213 us
    ppermute x15, waiting for transfers between devices, turn_z(): return lax.ppermute(value, 'rep', ring_next(count))  167 us
    ppermute x5, waiting for transfers between devices, swap_x(): return lax.ppermute(value, 'shard', [(i, i ^ 2) for i in range(4)])  101 us
    pallas_call x4, Pallas kernels, expert(): pl.pallas_call(functools.partial(expert_body, rows // 2), grid=(2,), in_s...  99.7 us
    unnamed x255, local copies, waits for them, and re-layouts  82.5 us
    all_to_all x1, blocking collectives, on_device(): lax.all_to_all(packed, 'shard', split_axis=0, concat_axis=0, tiled=True)  74.9 us
    pallas_call x4, Pallas kernels, weight_grads(): pl.pallas_call(functools.partial(weight_grads_body, groups, count), grid=...  54.8 us
    pallas_call x1, Pallas kernels, attention_backward(): pl.pallas_call(attend_backward, grid=(heads,), in_specs=[wide, pl.BlockSp...  32.9 us
  transfers between devices with their start and end apart: 62, of which 26 were waited for; matrix products, arithmetic and copies ran while one was open for 14% of the time, Pallas kernels for 17%

profile of v2, /device:TPU:0, one launch (start us, length us, event | category | flops | bytes accessed | tf_op | source)
XLA Modules:
  0.0 1153.2 jit_solution(6679316351635248922)
XLA Ops:
  17.0 74.9 %all_to_all.15 = bf16[4,512,1536]{2,1,0:T(8,128)(2,1)} all-to-all(bf16[4,512,1536]{2,1,0:T(8,128)(2,1)S(1)} %shard_map.263), channel_id=1, replica_groups=mesh['rep'=8,'shard'=4] {'shard'}, dimensions={0} | all-to-all | bytes 12582912 | tf_op jit(solution)/shard_map/all_to_all | solution.py:617
  95.6 3.1 fusion.29
  98.7 20.5 %collective-permute-done.1 = bf16[256,2048]{1,0:T(8,128)(2,1)} collective-permute-done((bf16[256,2048]{1,0:T(8,128)(2,1)}, bf16[256,2048]{1,0:T(8,128)(2,1)}, u32[]{:S(2)}, u32[]{:S(2)}) %collective-permute-start.1) | collective-permute-done | bytes 1048608 | tf_op jit(solution)/shard_map/ppermute | solution.py:475
  137.3 12.2 %fusion.20.qkv_ref = f32[1024,1536]{1,0:T(8,128)S(1)} fusion(bf16[2048,1536]{1,0:T(8,128)(2,1)} %bitcast.179, f32[2048]{0:T(1024)S(1)} %get-tuple-element.267, f32[1024]{0:T(1024)S(1)} %add_rsqrt_fusion, bf16[256,2048]{1,0:T(8,128)(2,1)} %collective-permute-done.2, bf16[256,2048]{1,0:T(8,128)(2,1)} %collective-permute-done.1, ...), kind=kOutput, calls=%fused_computation.60 | convolution fusion | flops 6465519616 | bytes 16789504 | tf_op jit(solution)/shard_map/dot_general | solution.py:31
  149.6 18.6 %shard_map.264 = bf16[1024,512]{1,0:T(8,128)(2,1)S(1)} custom-call(f32[1024,1536]{1,0:T(8,128)S(1)} %fusion.20.qkv_ref, f32[1024,128]{1,0:T(8,128)S(1)} %pad_maximum_fusion.7.cos_ref, f32[1024,128]{1,0:T(8,128)S(1)} %pad_maximum_fusion.8.sin_ref, f32[1,128]{1,0:T(1,128)S(1)} %reshape_squeeze.6.gq_ref, f32[1,128]{1,0:T(1,128)S(1)} %reshape_squeeze.7.gk_ref, ...), custom_call_target="tpu_custom_call" | custom-call | flops 8589934592 | bytes 7864320 | tf_op jit(solution)/shard_map/pallas_call | solution.py:179
  175.2 47.2 %collective-permute-done.8 = bf16[256,2048]{1,0:T(8,128)(2,1)S(1)} collective-permute-done((bf16[256,2048]{1,0:T(8,128)(2,1)S(1)}, bf16[256,2048]{1,0:T(8,128)(2,1)S(1)}, u32[]{:S(2)}, u32[]{:S(2)}) %collective-permute-start.8) | collective-permute-done | bytes 1048608 | tf_op jit(solution)/shard_map/ppermute | solution.py:475
  228.7 25.0 %collective-permute-done.10.x_ref = bf16[256,2048]{1,0:T(8,128)(2,1)S(1)} collective-permute-done((bf16[256,2048]{1,0:T(8,128)(2,1)S(1)}, bf16[256,2048]{1,0:T(8,128)(2,1)S(1)}, u32[]{:S(2)}, u32[]{:S(2)}) %collective-permute-start.10) | collective-permute-done | bytes 1048608 | tf_op jit(solution)/shard_map/ppermute | solution.py:504
  254.0 25.7 %collective-permute-done.14.x_ref = bf16[256,2048]{1,0:T(8,128)(2,1)} collective-permute-done((bf16[256,2048]{1,0:T(8,128)(2,1)S(1)}, bf16[256,2048]{1,0:T(8,128)(2,1)}, u32[]{:S(2)}, u32[]{:S(2)}) %collective-permute-start.14) | collective-permute-done | bytes 1048608 | tf_op jit(solution)/shard_map/ppermute | solution.py:504
  284.7 20.5 %collective-permute-done.16.x_ref = bf16[256,2048]{1,0:T(8,128)(2,1)} collective-permute-done((bf16[256,2048]{1,0:T(8,128)(2,1)}, bf16[256,2048]{1,0:T(8,128)(2,1)}, u32[]{:S(2)}, u32[]{:S(2)}) %collective-permute-start.16) | collective-permute-done | bytes 1048608 | tf_op jit(solution)/shard_map/ppermute | solution.py:504
  319.7 3.3 shard_map.265
  325.8 4.7 shard_map.272
  337.4 3.6 shard_map.266
  341.6 3.3 shard_map.267
  347.0 5.8 collective-permute-done.15.x_ref
  355.1 3.6 shard_map.273
  358.7 3.6 shard_map.274
  366.8 3.8 shard_map.268
  377.7 3.6 shard_map.275
  386.2 24.9 %shard_map.269 = (bf16[576,2048]{1,0:T(8,128)(2,1)}, bf16[576,2048]{1,0:T(8,128)(2,1)}, bf16[576,1024]{1,0:T(8,128)(2,1)}, bf16[576,1024]{1,0:T(8,128)(2,1)}, bf16[576,1024]{1,0:T(8,128)(2,1)}) custom-call(bf16[2,576,2048]{2,1,0:T(8,128)(2,1)} %bitcast.151, bf16[2,576,2048]{2,1,0:T(8,128)(2,1)} %bitcast.155, ...), custom_call_target="tpu_custom_call" | custom-call | flops 14495514624 | bytes 25559040 | tf_op jit(solution)/shard_map/pallas_call | solution.py:406
  411.1 25.0 %shard_map.276 = (bf16[576,2048]{1,0:T(8,128)(2,1)}, bf16[576,2048]{1,0:T(8,128)(2,1)}, bf16[576,1024]{1,0:T(8,128)(2,1)}, bf16[576,1024]{1,0:T(8,128)(2,1)}, bf16[576,1024]{1,0:T(8,128)(2,1)}) custom-call(bf16[2,576,2048]{2,1,0:T(8,128)(2,1)} %bitcast.143, bf16[2,576,2048]{2,1,0:T(8,128)(2,1)} %bitcast.147, ...), custom_call_target="tpu_custom_call" | custom-call | flops 14495514624 | bytes 25559040 | tf_op jit(solution)/shard_map/pallas_call | solution.py:406
  438.6 16.5 %shard_map.283 = (bf16[2048,1024]{1,0:T(8,128)(2,1)}, bf16[2048,1024]{1,0:T(8,128)(2,1)}) custom-call(bf16[2,576,2048]{2,1,0:T(8,128)(2,1)} %bitcast.152, bf16[2,576,2048]{2,1,0:T(8,128)(2,1)} %bitcast.144, bf16[576,1024]{1,0:T(8,128)(2,1)S(1)} %copy-done.86, bf16[576,1024]{1,0:T(8,128)(2,1)S(1)} %copy-done.88, bf16[576,1024]{1,0:T(8,128)(2,1)S(1)} %copy-done.87, ...), custom_call_target="tpu_custom_call" | custom-call | flops 9663676416 | bytes 17825792 | tf_op jit(solution)/shard_map/pallas_call | solution.py:456
  455.6 24.8 %shard_map.270 = (bf16[576,2048]{1,0:T(8,128)(2,1)}, bf16[576,2048]{1,0:T(8,128)(2,1)}, bf16[576,1024]{1,0:T(8,128)(2,1)}, bf16[576,1024]{1,0:T(8,128)(2,1)}, bf16[576,1024]{1,0:T(8,128)(2,1)}) custom-call(bf16[2,576,2048]{2,1,0:T(8,128)(2,1)} %bitcast.153, bf16[2,576,2048]{2,1,0:T(8,128)(2,1)} %bitcast.156, ...), custom_call_target="tpu_custom_call" | custom-call | flops 14495514624 | bytes 25559040 | tf_op jit(solution)/shard_map/pallas_call | solution.py:406
  480.4 25.1 %shard_map.277 = (bf16[576,2048]{1,0:T(8,128)(2,1)}, bf16[576,2048]{1,0:T(8,128)(2,1)}, bf16[576,1024]{1,0:T(8,128)(2,1)}, bf16[576,1024]{1,0:T(8,128)(2,1)}, bf16[576,1024]{1,0:T(8,128)(2,1)}) custom-call(bf16[2,576,2048]{2,1,0:T(8,128)(2,1)} %bitcast.145, bf16[2,576,2048]{2,1,0:T(8,128)(2,1)} %bitcast.148, ...), custom_call_target="tpu_custom_call" | custom-call | flops 14495514624 | bytes 25559040 | tf_op jit(solution)/shard_map/pallas_call | solution.py:406
  508.1 16.5 %shard_map.284 = (bf16[2048,1024]{1,0:T(8,128)(2,1)}, bf16[2048,1024]{1,0:T(8,128)(2,1)}) custom-call(bf16[2,576,2048]{2,1,0:T(8,128)(2,1)} %bitcast.154, bf16[2,576,2048]{2,1,0:T(8,128)(2,1)} %bitcast.146, bf16[576,1024]{1,0:T(8,128)(2,1)S(1)} %copy-done.82, bf16[576,1024]{1,0:T(8,128)(2,1)S(1)} %copy-done.84, bf16[576,1024]{1,0:T(8,128)(2,1)S(1)} %copy-done.83, ...), custom_call_target="tpu_custom_call" | custom-call | flops 9663676416 | bytes 17825792 | tf_op jit(solution)/shard_map/pallas_call | solution.py:456
  529.2 5.0 shard_map.279
  541.8 5.0 shard_map.280
  547.6 16.0 %collective-permute-done.23 = bf16[256,2048]{1,0:T(8,128)(2,1)} collective-permute-done((bf16[256,2048]{1,0:T(8,128)(2,1)}, bf16[256,2048]{1,0:T(8,128)(2,1)}, u32[]{:S(2)}, u32[]{:S(2)}) %collective-permute-start.23) | collective-permute-done | bytes 1048608 | tf_op jit(solution)/shard_map/ppermute | solution.py:500
  566.6 19.4 %collective-permute-done.25 = bf16[256,2048]{1,0:T(8,128)(2,1)S(1)} collective-permute-done((bf16[256,2048]{1,0:T(8,128)(2,1)S(1)}, bf16[256,2048]{1,0:T(8,128)(2,1)S(1)}, u32[]{:S(2)}, u32[]{:S(2)}) %collective-permute-start.25) | collective-permute-done | bytes 1048608 | tf_op jit(solution)/shard_map/ppermute | solution.py:500
  598.4 7.6 shard_map.271
  613.3 3.6 add_convert_fusion.1
  619.6 8.0 shard_map.278
  634.9 5.7 all-to-all-start.1
  640.7 6.5 all-to-all-done.1
  648.9 3.5 multiply_reduce_fusion
  654.1 32.1 %collective-permute-done.31 = bf16[256,2048]{1,0:T(8,128)(2,1)} collective-permute-done((bf16[256,2048]{1,0:T(8,128)(2,1)}, bf16[256,2048]{1,0:T(8,128)(2,1)}, u32[]{:S(2)}, u32[]{:S(2)}) %collective-permute-start.31) | collective-permute-done | bytes 1048608 | tf_op jit(solution)/shard_map/ppermute | solution.py:475
  687.4 10.9 shard_map.285
  699.9 5.1 convolution_convert_fusion.5.do_ref
  705.1 32.9 %shard_map.281 = (bf16[1024,1536]{1,0:T(8,128)(2,1)S(1)}, f32[8,128]{1,0:T(8,128)S(1)}) custom-call(f32[1024,1536]{1,0:T(8,128)} %copy-done.78, bf16[1024,512]{1,0:T(8,128)(2,1)S(1)} %convolution_convert_fusion.5.do_ref, f32[1024,128]{1,0:T(8,128)S(1)} %copy-done.49, f32[1024,128]{1,0:T(8,128)S(1)} %copy-done.47, f32[1,128]{1,0:T(1,128)S(1)} %copy-done.67, ...), custom_call_target="tpu_custom_call" | custom-call | flops 21474836480 | bytes 11010048 | tf_op jit(solution)/shard_map/pallas_call | solution.py:195
  742.0 4.5 convolution_convert_fusion.3
  748.5 8.9 convolution_convert_fusion
  765.0 25.4 %collective-permute-done.36 = bf16[4,64,2176]{2,1,0:T(8,128)(2,1)} collective-permute-done((bf16[4,64,2176]{2,1,0:T(8,128)(2,1)S(1)}, bf16[4,64,2176]{2,1,0:T(8,128)(2,1)}, u32[]{:S(2)}, u32[]{:S(2)}) %collective-permute-start.36) | collective-permute-done | bytes 1114144 | tf_op jit(solution)/shard_map/ppermute | solution.py:500
  795.9 18.4 %collective-permute-done.38 = bf16[4,64,2176]{2,1,0:T(8,128)(2,1)} collective-permute-done((bf16[4,64,2176]{2,1,0:T(8,128)(2,1)}, bf16[4,64,2176]{2,1,0:T(8,128)(2,1)}, u32[]{:S(2)}, u32[]{:S(2)}) %collective-permute-start.38) | collective-permute-done | bytes 1114144 | tf_op jit(solution)/shard_map/ppermute | solution.py:500
  814.3 7.3 collective-permute-done.37
  821.7 3.3 fusion.10
  828.3 10.9 shard_map.286
  843.0 17.7 %collective-permute-done.40 = bf16[4,64,2176]{2,1,0:T(8,128)(2,1)} collective-permute-done((bf16[4,64,2176]{2,1,0:T(8,128)(2,1)}, bf16[4,64,2176]{2,1,0:T(8,128)(2,1)}, u32[]{:S(2)}, u32[]{:S(2)}) %collective-permute-start.40) | collective-permute-done | bytes 1114144 | tf_op jit(solution)/shard_map/ppermute | solution.py:500
  864.2 11.0 convolution_convert_fusion.1
  875.2 53.8 %collective-permute-done.42 = bf16[4,64,2176]{2,1,0:T(8,128)(2,1)S(1)} collective-permute-done((bf16[4,64,2176]{2,1,0:T(8,128)(2,1)S(1)}, bf16[4,64,2176]{2,1,0:T(8,128)(2,1)S(1)}, u32[]{:S(2)}, u32[]{:S(2)}) %collective-permute-start.42) | collective-permute-done | bytes 1114144 | tf_op jit(solution)/shard_map/ppermute | solution.py:500
  931.6 4.2 all-to-all-start.2
  935.8 3.1 fusion.49
  939.5 8.8 all-to-all-done.2
  950.9 3.1 add_convert_fusion.6
  956.3 22.6 %collective-permute-done.44.refs_2_ = bf16[64,8320]{1,0:T(8,128)(2,1)} collective-permute-done((bf16[64,8320]{1,0:T(8,128)(2,1)S(1)}, bf16[64,8320]{1,0:T(8,128)(2,1)}, u32[]{:S(2)}, u32[]{:S(2)}) %collective-permute-start.44) | collective-permute-done | bytes 1064992 | tf_op jit(solution)/shard_map/ppermute | solution.py:504
  982.2 19.2 %collective-permute-done.19 = bf16[256,2048]{1,0:T(8,128)(2,1)} collective-permute-done((bf16[256,2048]{1,0:T(8,128)(2,1)}, bf16[256,2048]{1,0:T(8,128)(2,1)}, u32[]{:S(2)}, u32[]{:S(2)}) %collective-permute-start.19) | collective-permute-done | bytes 1048608 | tf_op jit(solution)/shard_map/ppermute | solution.py:504
  1004.5 19.8 %collective-permute-done.46.refs_4_ = bf16[64,8320]{1,0:T(8,128)(2,1)} collective-permute-done((bf16[64,8320]{1,0:T(8,128)(2,1)}, bf16[64,8320]{1,0:T(8,128)(2,1)}, u32[]{:S(2)}, u32[]{:S(2)}) %collective-permute-start.46) | collective-permute-done | bytes 1064992 | tf_op jit(solution)/shard_map/ppermute | solution.py:504
  1024.4 3.8 maximum_convert_fusion.1
  1028.3 3.8 maximum_convert_fusion
  1032.1 4.0 maximum_convert_fusion.2
  1041.6 26.5 %collective-permute-done.48.refs_6_ = bf16[64,8320]{1,0:T(8,128)(2,1)} collective-permute-done((bf16[64,8320]{1,0:T(8,128)(2,1)}, bf16[64,8320]{1,0:T(8,128)(2,1)}, u32[]{:S(2)}, u32[]{:S(2)}) %collective-permute-start.48) | collective-permute-done | bytes 1064992 | tf_op jit(solution)/shard_map/ppermute | solution.py:504
  1068.8 5.1 fusion.17
  1073.9 14.3 %collective-permute-done.45.refs_3_ = bf16[64,8320]{1,0:T(8,128)(2,1)S(1)} collective-permute-done((bf16[64,8320]{1,0:T(8,128)(2,1)}, bf16[64,8320]{1,0:T(8,128)(2,1)S(1)}, u32[]{:S(2)}, u32[]{:S(2)}) %collective-permute-start.45) | collective-permute-done | bytes 1064992 | tf_op jit(solution)/shard_map/ppermute | solution.py:500
  1088.3 22.8 %collective-permute-done.47.refs_5_ = bf16[64,8320]{1,0:T(8,128)(2,1)S(1)} collective-permute-done((bf16[64,8320]{1,0:T(8,128)(2,1)}, bf16[64,8320]{1,0:T(8,128)(2,1)S(1)}, u32[]{:S(2)}, u32[]{:S(2)}) %collective-permute-start.47) | collective-permute-done | bytes 1064992 | tf_op jit(solution)/shard_map/ppermute | solution.py:500
  1111.1 19.3 %collective-permute-done.49.refs_7_ = bf16[64,8320]{1,0:T(8,128)(2,1)} collective-permute-done((bf16[64,8320]{1,0:T(8,128)(2,1)}, bf16[64,8320]{1,0:T(8,128)(2,1)}, u32[]{:S(2)}, u32[]{:S(2)}) %collective-permute-start.49) | collective-permute-done | bytes 1064992 | tf_op jit(solution)/shard_map/ppermute | solution.py:500
  1130.4 13.5 %shard_map.282 = (f32[512,2048]{1,0:T(8,128)}, f32[512,2048]{1,0:T(8,128)}, f32[512,2048]{1,0:T(8,128)}, f32[512,2048]{1,0:T(8,128)}, f32[512,128]{1,0:T(8,128)S(1)}) custom-call(s32[8]{0:T(128)S(1)} %stack.196.ids_ref, bf16[512,2048]{1,0:T(8,128)(2,1)} %wq_ref.1, bf16[512,2048]{1,0:T(8,128)(2,1)} %wk_ref.1, bf16[512,2048]{1,0:T(8,128)(2,1)} %wv_ref.1, ...), custom_call_target="tpu_custom_call" | custom-call | bytes 31457280 | tf_op jit(solution)/shard_map/pallas_call | solution.py:566
  (475 shorter events, 205.7 us)
Async XLA Ops:
  7.2 161.0 %copy-start = (bf16[512,2048]{1,0:T(8,128)(2,1)S(1)}, bf16[512,2048]{1,0:T(8,128)(2,1)}, u32[]{:S(2)}) copy-start(bf16[512,2048]{1,0:T(8,128)(2,1)} %param.20) | copy-start | bytes 6291460
  7.2 298.9 %all-gather.12.cloned.1.call-start = ((), (), s32[]{:S(2)}) async-start(), calls=%async_computation.18 | async-start | bytes 10027008 | tf_op jit(solution)/shard_map/all_gather | solution.py:620
  10.5 375.7 %all-gather.10.cloned.1.call-start = ((), (), s32[]{:S(2)}) async-start(), calls=%async_computation.11 | async-start | bytes 10485760 | tf_op jit(solution)/shard_map/all_gather | solution.py:646
  91.9 294.3 %all-gather.6.cloned.1.call-start = ((), (), s32[]{:S(2)}) async-start(), calls=%async_computation.9 | async-start | bytes 10485760 | tf_op jit(solution)/shard_map/all_gather | solution.py:644
  92.7 293.5 %all-gather.8.cloned.1.call-start = ((), (), s32[]{:S(2)}) async-start(), calls=%async_computation.10 | async-start | bytes 10485760 | tf_op jit(solution)/shard_map/all_gather | solution.py:645
  92.7 26.4 %collective-permute-start.1 = (bf16[256,2048]{1,0:T(8,128)(2,1)}, bf16[256,2048]{1,0:T(8,128)(2,1)}, u32[]{:S(2)}, u32[]{:S(2)}) collective-permute-start(bf16[256,2048]{1,0:T(8,128)(2,1)} %param.16), channel_id=1, source_target_pairs={{0,2},{1,3},{2,0},{3,1},{4,6},{5,7},{6,4},{7,5},{8,10},{9,11},{10,... | collective-permute-start | bytes 3145736 | tf_op jit(solution)/shard_map/ppermute | solution.py:475
  93.2 27.4 %collective-permute-start.4 = (bf16[512,128]{0,1:T(8,128)(2,1)S(1)}, bf16[512,128]{0,1:T(8,128)(2,1)S(1)}, u32[]{:S(2)}, u32[]{:S(2)}) collective-permute-start(bf16[512,128]{0,1:T(8,128)(2,1)S(1)} %get-tuple-element.289), channel_id=1, source_target_pairs={{0,2},{1,3},{2,0},{3,1},{4,6},{5,7},{6,4},{7,5},{8,10},{9,11},{10,... | collective-permute-start | bytes 393224 | tf_op jit(solution)/shard_map/ppermute | solution.py:475
  95.0 28.1 %collective-permute-start.3 = (bf16[512,128]{0,1:T(8,128)(2,1)S(1)}, bf16[512,128]{0,1:T(8,128)(2,1)}, u32[]{:S(2)}, u32[]{:S(2)}) collective-permute-start(bf16[512,128]{0,1:T(8,128)(2,1)S(1)} %get-tuple-element.289), channel_id=1, source_target_pairs={{0,1},{1,0},{2,3},{3,2},{4,5},{5,4},{6,7},{7,6},{8,9},{9,8},{10,11... | collective-permute-start | bytes 393224 | tf_op jit(solution)/shard_map/ppermute | solution.py:471
  95.0 39.0 %collective-permute-start = (bf16[256,2048]{1,0:T(8,128)(2,1)}, bf16[256,2048]{1,0:T(8,128)(2,1)}, u32[]{:S(2)}, u32[]{:S(2)}) collective-permute-start(bf16[256,2048]{1,0:T(8,128)(2,1)} %param.16), channel_id=1, source_target_pairs={{0,1},{1,0},{2,3},{3,2},{4,5},{5,4},{6,7},{7,6},{8,9},{9,8},{10,11... | collective-permute-start | bytes 3145736 | tf_op jit(solution)/shard_map/ppermute | solution.py:471
  119.2 14.9 %collective-permute-start.2 = (bf16[256,2048]{1,0:T(8,128)(2,1)}, bf16[256,2048]{1,0:T(8,128)(2,1)}, u32[]{:S(2)}, u32[]{:S(2)}) collective-permute-start(bf16[256,2048]{1,0:T(8,128)(2,1)} %collective-permute-done.1), channel_id=1, source_target_pairs={{0,1},{1,0},{2,3},{3,2},{4,5},{5,4},{6,7},{7,6},{8,9},{9,8},{10,11... | collective-permute-start | bytes 3145736 | tf_op jit(solution)/shard_map/ppermute | solution.py:471
  120.6 2.6 collective-permute-start.5
  134.0 91.0 %copy-start.105 = (f32[2048]{0:T(1024)}, f32[2048]{0:T(1024)S(1)}, u32[]{:S(2)}) copy-start(f32[2048]{0:T(1024)S(1)} %get-tuple-element.266) | copy-start | bytes 24580
  136.7 887.7 %reduce-scatter.11.cloned.1.call-start = ((), (), s32[]{:S(2)}) async-start(), calls=%async_computation.14 | async-start | bytes 5242880 | tf_op jit(solution)/shard_map/reduce_scatter | solution.py:718
  170.8 2.9 collective-permute-start.7
  171.4 3.8 collective-permute-start.6
  174.1 48.3 %collective-permute-start.8 = (bf16[256,2048]{1,0:T(8,128)(2,1)S(1)}, bf16[256,2048]{1,0:T(8,128)(2,1)S(1)}, u32[]{:S(2)}, u32[]{:S(2)}) collective-permute-start(bf16[256,2048]{1,0:T(8,128)(2,1)S(1)} %add_convert_fusion.8), channel_id=1, source_target_pairs={{0,2},{1,3},{2,0},{3,1},{4,6},{5,7},{6,4},{7,5},{8,10},{9,11},{10,... | collective-permute-start | bytes 3145736 | tf_op jit(solution)/shard_map/ppermute | solution.py:475
  226.3 27.4 %collective-permute-start.10 = (bf16[256,2048]{1,0:T(8,128)(2,1)S(1)}, bf16[256,2048]{1,0:T(8,128)(2,1)S(1)}, u32[]{:S(2)}, u32[]{:S(2)}) collective-permute-start(bf16[256,2048]{1,0:T(8,128)(2,1)S(1)} %multiply_convert_fusion.x_ref), channel_id=1, source_target_pairs={{0,8},{4,12},{8,16},{12,20},{16,24},{20,28},{24,0},{28,4},{1,9},{5... | collective-permute-start | bytes 3145736 | tf_op jit(solution)/shard_map/ppermute | solution.py:504
  253.7 26.1 %collective-permute-start.14 = (bf16[256,2048]{1,0:T(8,128)(2,1)S(1)}, bf16[256,2048]{1,0:T(8,128)(2,1)}, u32[]{:S(2)}, u32[]{:S(2)}) collective-permute-start(bf16[256,2048]{1,0:T(8,128)(2,1)S(1)} %collective-permute-done.10.x_ref), channel_id=1, source_target_pairs={{0,8},{4,12},{8,16},{12,20},{16,24},{20,28},{24,0},{28,4},{1,9},{5... | collective-permute-start | bytes 3145736 | tf_op jit(solution)/shard_map/ppermute | solution.py:504
  279.7 25.4 %collective-permute-start.16 = (bf16[256,2048]{1,0:T(8,128)(2,1)}, bf16[256,2048]{1,0:T(8,128)(2,1)}, u32[]{:S(2)}, u32[]{:S(2)}) collective-permute-start(bf16[256,2048]{1,0:T(8,128)(2,1)} %collective-permute-done.14.x_ref), channel_id=1, source_target_pairs={{0,8},{4,12},{8,16},{12,20},{16,24},{20,28},{24,0},{28,4},{1,9},{5... | collective-permute-start | bytes 3145736 | tf_op jit(solution)/shard_map/ppermute | solution.py:504
  281.4 51.2 %collective-permute-start.9 = (bf16[256,2048]{1,0:T(8,128)(2,1)}, bf16[256,2048]{1,0:T(8,128)(2,1)}, u32[]{:S(2)}, u32[]{:S(2)}) collective-permute-start(bf16[256,2048]{1,0:T(8,128)(2,1)} %copy-done.16), channel_id=1, source_target_pairs={{0,4},{4,0},{8,12},{12,8},{16,20},{20,16},{24,28},{28,24},{1,5},{5... | collective-permute-start | bytes 3145736 | tf_op jit(solution)/shard_map/ppermute | solution.py:500
  282.7 81.7 %collective-permute-start.11 = (bf16[256,2048]{1,0:T(8,128)(2,1)}, bf16[256,2048]{1,0:T(8,128)(2,1)}, u32[]{:S(2)}, u32[]{:S(2)}) collective-permute-start(bf16[256,2048]{1,0:T(8,128)(2,1)} %copy-done.44), channel_id=1, source_target_pairs={{0,4},{4,0},{8,12},{12,8},{16,20},{20,16},{24,28},{28,24},{1,5},{5... | collective-permute-start | bytes 3145736 | tf_op jit(solution)/shard_map/ppermute | solution.py:500
  283.5 69.3 %collective-permute-start.15 = (bf16[256,2048]{1,0:T(8,128)(2,1)}, bf16[256,2048]{1,0:T(8,128)(2,1)}, u32[]{:S(2)}, u32[]{:S(2)}) collective-permute-start(bf16[256,2048]{1,0:T(8,128)(2,1)} %collective-permute-done.14.x_ref), channel_id=1, source_target_pairs={{0,4},{4,0},{8,12},{12,8},{16,20},{20,16},{24,28},{28,24},{1,5},{5... | collective-permute-start | bytes 3145736 | tf_op jit(solution)/shard_map/ppermute | solution.py:500
  305.2 70.2 %collective-permute-start.17 = (bf16[256,2048]{1,0:T(8,128)(2,1)}, bf16[256,2048]{1,0:T(8,128)(2,1)}, u32[]{:S(2)}, u32[]{:S(2)}) collective-permute-start(bf16[256,2048]{1,0:T(8,128)(2,1)} %collective-permute-done.16.x_ref), channel_id=1, source_target_pairs={{0,4},{4,0},{8,12},{12,8},{16,20},{20,16},{24,28},{28,24},{1,5},{5... | collective-permute-start | bytes 3145736 | tf_op jit(solution)/shard_map/ppermute | solution.py:500
  455.1 569.3 %reduce-scatter.13.cloned.1.call-start = ((), (), s32[]{:S(2)}) async-start(), calls=%async_computation.15 | async-start | bytes 5242880 | tf_op jit(solution)/shard_map/reduce_scatter | solution.py:718
  524.6 503.7 %reduce-scatter.7.cloned.1.call-start = ((), (), s32[]{:S(2)}) async-start(), calls=%async_computation.12 | async-start | bytes 5242880 | tf_op jit(solution)/shard_map/reduce_scatter | solution.py:718
  525.3 502.9 %reduce-scatter.9.cloned.1.call-start = ((), (), s32[]{:S(2)}) async-start(), calls=%async_computation.13 | async-start | bytes 5242880 | tf_op jit(solution)/shard_map/reduce_scatter | solution.py:718
  537.1 26.4 %collective-permute-start.23 = (bf16[256,2048]{1,0:T(8,128)(2,1)}, bf16[256,2048]{1,0:T(8,128)(2,1)}, u32[]{:S(2)}, u32[]{:S(2)}) collective-permute-start(bf16[256,2048]{1,0:T(8,128)(2,1)} %get-tuple-element.132), channel_id=1, source_target_pairs={{0,4},{4,0},{8,12},{12,8},{16,20},{20,16},{24,28},{28,24},{1,5},{5... | collective-permute-start | bytes 3145736 | tf_op jit(solution)/shard_map/ppermute | solution.py:500
  546.7 39.2 %collective-permute-start.25 = (bf16[256,2048]{1,0:T(8,128)(2,1)S(1)}, bf16[256,2048]{1,0:T(8,128)(2,1)S(1)}, u32[]{:S(2)}, u32[]{:S(2)}) collective-permute-start(bf16[256,2048]{1,0:T(8,128)(2,1)S(1)} %get-tuple-element.136), channel_id=1, source_target_pairs={{0,4},{4,0},{8,12},{12,8},{16,20},{20,16},{24,28},{28,24},{1,5},{5... | collective-permute-start | bytes 3145736 | tf_op jit(solution)/shard_map/ppermute | solution.py:500
  565.2 20.7 %collective-permute-start.24 = (bf16[256,2048]{1,0:T(8,128)(2,1)S(1)}, bf16[256,2048]{1,0:T(8,128)(2,1)S(1)}, u32[]{:S(2)}, u32[]{:S(2)}) collective-permute-start(bf16[256,2048]{1,0:T(8,128)(2,1)S(1)} %add_convert_fusion.3), channel_id=1, source_target_pairs={{0,8},{4,12},{8,16},{12,20},{16,24},{20,28},{24,0},{28,4},{1,9},{5... | collective-permute-start | bytes 3145736 | tf_op jit(solution)/shard_map/ppermute | solution.py:504
  565.3 48.0 %collective-permute-start.27 = (bf16[256,2048]{1,0:T(8,128)(2,1)}, bf16[256,2048]{1,0:T(8,128)(2,1)}, u32[]{:S(2)}, u32[]{:S(2)}) collective-permute-start(bf16[256,2048]{1,0:T(8,128)(2,1)} %get-tuple-element.138), channel_id=1, source_target_pairs={{0,4},{4,0},{8,12},{12,8},{16,20},{20,16},{24,28},{28,24},{1,5},{5... | collective-permute-start | bytes 3145736 | tf_op jit(solution)/shard_map/ppermute | solution.py:500
  587.5 25.8 %collective-permute-start.26 = (bf16[256,2048]{1,0:T(8,128)(2,1)}, bf16[256,2048]{1,0:T(8,128)(2,1)}, u32[]{:S(2)}, u32[]{:S(2)}) collective-permute-start(bf16[256,2048]{1,0:T(8,128)(2,1)} %add_convert_fusion.2), channel_id=1, source_target_pairs={{0,8},{4,12},{8,16},{12,20},{16,24},{20,28},{24,0},{28,4},{1,9},{5... | collective-permute-start | bytes 3145736 | tf_op jit(solution)/shard_map/ppermute | solution.py:504
  611.7 37.1 %collective-permute-start.29 = (bf16[256,2048]{1,0:T(8,128)(2,1)}, bf16[256,2048]{1,0:T(8,128)(2,1)}, u32[]{:S(2)}, u32[]{:S(2)}) collective-permute-start(bf16[256,2048]{1,0:T(8,128)(2,1)} %copy-done.71), channel_id=1, source_target_pairs={{0,4},{4,0},{8,12},{12,8},{16,20},{20,16},{24,28},{28,24},{1,5},{5... | collective-permute-start | bytes 3145736 | tf_op jit(solution)/shard_map/ppermute | solution.py:500
  616.8 32.0 %collective-permute-start.28 = (bf16[256,2048]{1,0:T(8,128)(2,1)}, bf16[256,2048]{1,0:T(8,128)(2,1)}, u32[]{:S(2)}, u32[]{:S(2)}) collective-permute-start(bf16[256,2048]{1,0:T(8,128)(2,1)} %add_convert_fusion.1), channel_id=1, source_target_pairs={{0,8},{4,12},{8,16},{12,20},{16,24},{20,28},{24,0},{28,4},{1,9},{5... | collective-permute-start | bytes 3145736 | tf_op jit(solution)/shard_map/ppermute | solution.py:504
  634.9 12.3 %all-to-all-start.1 = ((f32[8,2,256]{2,1,0:T(2,128)}), f32[8,2,256]{2,1,0:T(2,128)S(1)}, u32[]{:S(2)}, u32[]{:S(2)}) async-start(f32[8,2,256]{2,1,0:T(2,128)} %scatter_fusion.1), calls=%async_computation.1 | async-start | bytes 32768 | tf_op jit(solution)/shard_map/all_to_all | solution.py:736
  640.6 391.5 %reduce-scatter.15.cloned.1.call-start = ((), (), s32[]{:S(2)}) async-start(), calls=%async_computation.16 | async-start | bytes 5242880 | tf_op jit(solution)/shard_map/reduce_scatter | solution.py:718
  654.0 32.1 %collective-permute-start.31 = (bf16[256,2048]{1,0:T(8,128)(2,1)}, bf16[256,2048]{1,0:T(8,128)(2,1)}, u32[]{:S(2)}, u32[]{:S(2)}) collective-permute-start(bf16[256,2048]{1,0:T(8,128)(2,1)} %fusion.48), channel_id=1, source_target_pairs={{0,2},{1,3},{2,0},{3,1},{4,6},{5,7},{6,4},{7,5},{8,10},{9,11},{10,... | collective-permute-start | bytes 3145736 | tf_op jit(solution)/shard_map/ppermute | solution.py:475
  654.0 45.8 %collective-permute-start.30 = (bf16[256,2048]{1,0:T(8,128)(2,1)}, bf16[256,2048]{1,0:T(8,128)(2,1)}, u32[]{:S(2)}, u32[]{:S(2)}) collective-permute-start(bf16[256,2048]{1,0:T(8,128)(2,1)} %fusion.48), channel_id=1, source_target_pairs={{0,1},{1,0},{2,3},{3,2},{4,5},{5,4},{6,7},{7,6},{8,9},{9,8},{10,11... | collective-permute-start | bytes 3145736 | tf_op jit(solution)/shard_map/ppermute | solution.py:471
  686.2 13.7 %collective-permute-start.32 = (bf16[256,2048]{1,0:T(8,128)(2,1)}, bf16[256,2048]{1,0:T(8,128)(2,1)}, u32[]{:S(2)}, u32[]{:S(2)}) collective-permute-start(bf16[256,2048]{1,0:T(8,128)(2,1)} %collective-permute-done.31), channel_id=1, source_target_pairs={{0,1},{1,0},{2,3},{3,2},{4,5},{5,4},{6,7},{7,6},{8,9},{9,8},{10,11... | collective-permute-start | bytes 3145736 | tf_op jit(solution)/shard_map/ppermute | solution.py:471
  698.3 333.8 %reduce-scatter.17.cloned.1.call-start = ((), (), s32[]{:S(2)}) async-start(), calls=%async_computation.17 | async-start | bytes 5242880 | tf_op jit(solution)/shard_map/reduce_scatter | solution.py:718
  763.0 27.5 %collective-permute-start.36 = (bf16[4,64,2176]{2,1,0:T(8,128)(2,1)S(1)}, bf16[4,64,2176]{2,1,0:T(8,128)(2,1)}, u32[]{:S(2)}, u32[]{:S(2)}) collective-permute-start(bf16[4,64,2176]{2,1,0:T(8,128)(2,1)S(1)} %get-tuple-element.277), channel_id=1, source_target_pairs={{0,4},{4,0},{8,12},{12,8},{16,20},{20,16},{24,28},{28,24},{1,5},{5... | collective-permute-start | bytes 3342344 | tf_op jit(solution)/shard_map/ppermute | solution.py:500
  763.5 50.8 %collective-permute-start.38 = (bf16[4,64,2176]{2,1,0:T(8,128)(2,1)}, bf16[4,64,2176]{2,1,0:T(8,128)(2,1)}, u32[]{:S(2)}, u32[]{:S(2)}) collective-permute-start(bf16[4,64,2176]{2,1,0:T(8,128)(2,1)} %get-tuple-element.279), channel_id=1, source_target_pairs={{0,4},{4,0},{8,12},{12,8},{16,20},{20,16},{24,28},{28,24},{1,5},{5... | collective-permute-start | bytes 3342344 | tf_op jit(solution)/shard_map/ppermute | solution.py:500
  793.3 28.3 %collective-permute-start.37 = (bf16[4,64,2176]{2,1,0:T(8,128)(2,1)}, bf16[4,64,2176]{2,1,0:T(8,128)(2,1)}, u32[]{:S(2)}, u32[]{:S(2)}) collective-permute-start(bf16[4,64,2176]{2,1,0:T(8,128)(2,1)} %fusion.11), channel_id=1, source_target_pairs={{0,8},{4,12},{8,16},{12,20},{16,24},{20,28},{24,0},{28,4},{1,9},{5... | collective-permute-start | bytes 3342344 | tf_op jit(solution)/shard_map/ppermute | solution.py:504
  793.9 45.3 %collective-permute-start.12 = (bf16[256,2048]{1,0:T(8,128)(2,1)}, bf16[256,2048]{1,0:T(8,128)(2,1)}, u32[]{:S(2)}, u32[]{:S(2)}) collective-permute-start(bf16[256,2048]{1,0:T(8,128)(2,1)} %get-tuple-element.108), channel_id=1, source_target_pairs={{0,4},{4,0},{8,12},{12,8},{16,20},{20,16},{24,28},{28,24},{1,5},{5... | collective-permute-start | bytes 3145736 | tf_op jit(solution)/shard_map/ppermute | solution.py:500
  794.6 66.1 %collective-permute-start.40 = (bf16[4,64,2176]{2,1,0:T(8,128)(2,1)}, bf16[4,64,2176]{2,1,0:T(8,128)(2,1)}, u32[]{:S(2)}, u32[]{:S(2)}) collective-permute-start(bf16[4,64,2176]{2,1,0:T(8,128)(2,1)} %get-tuple-element.278), channel_id=1, source_target_pairs={{0,4},{4,0},{8,12},{12,8},{16,20},{20,16},{24,28},{28,24},{1,5},{5... | collective-permute-start | bytes 3342344 | tf_op jit(solution)/shard_map/ppermute | solution.py:500
  825.0 36.3 %collective-permute-start.39 = (bf16[4,64,2176]{2,1,0:T(8,128)(2,1)}, bf16[4,64,2176]{2,1,0:T(8,128)(2,1)}, u32[]{:S(2)}, u32[]{:S(2)}) collective-permute-start(bf16[4,64,2176]{2,1,0:T(8,128)(2,1)} %fusion.10), channel_id=1, source_target_pairs={{0,8},{4,12},{8,16},{12,20},{16,24},{20,28},{24,0},{28,4},{1,9},{5... | collective-permute-start | bytes 3342344 | tf_op jit(solution)/shard_map/ppermute | solution.py:504
  825.0 125.9 %collective-permute-start.18 = (bf16[256,2048]{1,0:T(8,128)(2,1)}, bf16[256,2048]{1,0:T(8,128)(2,1)}, u32[]{:S(2)}, u32[]{:S(2)}) collective-permute-start(bf16[256,2048]{1,0:T(8,128)(2,1)} %get-tuple-element.124), channel_id=1, source_target_pairs={{0,4},{4,0},{8,12},{12,8},{16,20},{20,16},{24,28},{28,24},{1,5},{5... | collective-permute-start | bytes 3145736 | tf_op jit(solution)/shard_map/ppermute | solution.py:500
  825.7 156.2 %collective-permute-start.20 = (bf16[256,2048]{1,0:T(8,128)(2,1)}, bf16[256,2048]{1,0:T(8,128)(2,1)}, u32[]{:S(2)}, u32[]{:S(2)}) collective-permute-start(bf16[256,2048]{1,0:T(8,128)(2,1)} %get-tuple-element.126), channel_id=1, source_target_pairs={{0,4},{4,0},{8,12},{12,8},{16,20},{20,16},{24,28},{28,24},{1,5},{5... | collective-permute-start | bytes 3145736 | tf_op jit(solution)/shard_map/ppermute | solution.py:500
  843.0 107.8 %collective-permute-start.13 = (bf16[256,2048]{1,0:T(8,128)(2,1)}, bf16[256,2048]{1,0:T(8,128)(2,1)}, u32[]{:S(2)}, u32[]{:S(2)}) collective-permute-start(bf16[256,2048]{1,0:T(8,128)(2,1)} %add_convert_fusion.7), channel_id=1, source_target_pairs={{0,8},{4,12},{8,16},{12,20},{16,24},{20,28},{24,0},{28,4},{1,9},{5... | collective-permute-start | bytes 3145736 | tf_op jit(solution)/shard_map/ppermute | solution.py:504
  860.7 68.3 %collective-permute-start.42 = (bf16[4,64,2176]{2,1,0:T(8,128)(2,1)S(1)}, bf16[4,64,2176]{2,1,0:T(8,128)(2,1)S(1)}, u32[]{:S(2)}, u32[]{:S(2)}) collective-permute-start(bf16[4,64,2176]{2,1,0:T(8,128)(2,1)S(1)} %copy-done.99), channel_id=1, source_target_pairs={{0,4},{4,0},{8,12},{12,8},{16,20},{20,16},{24,28},{28,24},{1,5},{5... | collective-permute-start | bytes 3342344 | tf_op jit(solution)/shard_map/ppermute | solution.py:500
  863.8 65.2 %collective-permute-start.41 = (bf16[4,64,2176]{2,1,0:T(8,128)(2,1)S(1)}, bf16[4,64,2176]{2,1,0:T(8,128)(2,1)S(1)}, u32[]{:S(2)}, u32[]{:S(2)}) collective-permute-start(bf16[4,64,2176]{2,1,0:T(8,128)(2,1)S(1)} %fusion.8), channel_id=1, source_target_pairs={{0,8},{4,12},{8,16},{12,20},{16,24},{20,28},{24,0},{28,4},{1,9},{5... | collective-permute-start | bytes 3342344 | tf_op jit(solution)/shard_map/ppermute | solution.py:504
  931.6 16.6 %all-to-all-start.2 = ((bf16[4,64,1664]{2,1,0:T(8,128)(2,1)}), bf16[4,64,1664]{2,1,0:T(8,128)(2,1)}, u32[]{:S(2)}, u32[]{:S(2)}) async-start(bf16[4,64,1664]{2,1,0:T(8,128)(2,1)} %slice.117), calls=%async_computation.2 | async-start | bytes 1703936 | tf_op jit(solution)/shard_map/all_to_all | solution.py:788
  939.0 17.3 %collective-permute-start.34 = (bf16[256,2048]{1,0:T(8,128)(2,1)}, bf16[256,2048]{1,0:T(8,128)(2,1)}, u32[]{:S(2)}, u32[]{:S(2)}) collective-permute-start(bf16[256,2048]{1,0:T(8,128)(2,1)} %get-tuple-element.282), channel_id=1, source_target_pairs={{0,1},{1,0},{2,3},{3,2},{4,5},{5,4},{6,7},{7,6},{8,9},{9,8},{10,11... | collective-permute-start | bytes 3145736 | tf_op jit(solution)/shard_map/ppermute | solution.py:471
  950.5 28.4 %collective-permute-start.44 = (bf16[64,8320]{1,0:T(8,128)(2,1)S(1)}, bf16[64,8320]{1,0:T(8,128)(2,1)}, u32[]{:S(2)}, u32[]{:S(2)}) collective-permute-start(bf16[64,8320]{1,0:T(8,128)(2,1)S(1)} %pad_maximum_fusion.3.refs_0_), channel_id=1, source_target_pairs={{0,8},{4,12},{8,16},{12,20},{16,24},{20,28},{24,0},{28,4},{1,9},{5... | collective-permute-start | bytes 3194888 | tf_op jit(solution)/shard_map/ppermute | solution.py:504
  953.9 47.5 %collective-permute-start.19 = (bf16[256,2048]{1,0:T(8,128)(2,1)}, bf16[256,2048]{1,0:T(8,128)(2,1)}, u32[]{:S(2)}, u32[]{:S(2)}) collective-permute-start(bf16[256,2048]{1,0:T(8,128)(2,1)} %add_convert_fusion.6), channel_id=1, source_target_pairs={{0,8},{4,12},{8,16},{12,20},{16,24},{20,28},{24,0},{28,4},{1,9},{5... | collective-permute-start | bytes 3145736 | tf_op jit(solution)/shard_map/ppermute | solution.py:504
  955.3 85.7 %collective-permute-start.22 = (bf16[256,2048]{1,0:T(8,128)(2,1)}, bf16[256,2048]{1,0:T(8,128)(2,1)}, u32[]{:S(2)}, u32[]{:S(2)}) collective-permute-start(bf16[256,2048]{1,0:T(8,128)(2,1)} %copy-done.70), channel_id=1, source_target_pairs={{0,4},{4,0},{8,12},{12,8},{16,20},{20,16},{24,28},{28,24},{1,5},{5... | collective-permute-start | bytes 3145736 | tf_op jit(solution)/shard_map/ppermute | solution.py:500
  956.3 79.8 %collective-permute-start.33 = (bf16[256,2048]{1,0:T(8,128)(2,1)}, bf16[256,2048]{1,0:T(8,128)(2,1)}, u32[]{:S(2)}, u32[]{:S(2)}) collective-permute-start(bf16[256,2048]{1,0:T(8,128)(2,1)} %get-tuple-element.281), channel_id=1, source_target_pairs={{0,1},{1,0},{2,3},{3,2},{4,5},{5,4},{6,7},{7,6},{8,9},{9,8},{10,11... | collective-permute-start | bytes 3145736 | tf_op jit(solution)/shard_map/ppermute | solution.py:471
  978.9 45.3 %collective-permute-start.46 = (bf16[64,8320]{1,0:T(8,128)(2,1)}, bf16[64,8320]{1,0:T(8,128)(2,1)}, u32[]{:S(2)}, u32[]{:S(2)}) collective-permute-start(bf16[64,8320]{1,0:T(8,128)(2,1)} %collective-permute-done.44.refs_2_), channel_id=1, source_target_pairs={{0,8},{4,12},{8,16},{12,20},{16,24},{20,28},{24,0},{28,4},{1,9},{5... | collective-permute-start | bytes 3194888 | tf_op jit(solution)/shard_map/ppermute | solution.py:504
  981.8 54.3 %collective-permute-start.35 = (bf16[256,2048]{1,0:T(8,128)(2,1)}, bf16[256,2048]{1,0:T(8,128)(2,1)}, u32[]{:S(2)}, u32[]{:S(2)}) collective-permute-start(bf16[256,2048]{1,0:T(8,128)(2,1)} %add_convert_fusion), channel_id=1, source_target_pairs={{0,2},{1,3},{2,0},{3,1},{4,6},{5,7},{6,4},{7,5},{8,10},{9,11},{10,... | collective-permute-start | bytes 3145736 | tf_op jit(solution)/shard_map/ppermute | solution.py:475
  1004.5 64.3 %collective-permute-start.21 = (bf16[256,2048]{1,0:T(8,128)(2,1)}, bf16[256,2048]{1,0:T(8,128)(2,1)}, u32[]{:S(2)}, u32[]{:S(2)}) collective-permute-start(bf16[256,2048]{1,0:T(8,128)(2,1)} %add_convert_fusion.5), channel_id=1, source_target_pairs={{0,8},{4,12},{8,16},{12,20},{16,24},{20,28},{24,0},{28,4},{1,9},{5... | collective-permute-start | bytes 3145736 | tf_op jit(solution)/shard_map/ppermute | solution.py:504
  1024.2 43.9 %collective-permute-start.48 = (bf16[64,8320]{1,0:T(8,128)(2,1)}, bf16[64,8320]{1,0:T(8,128)(2,1)}, u32[]{:S(2)}, u32[]{:S(2)}) collective-permute-start(bf16[64,8320]{1,0:T(8,128)(2,1)} %collective-permute-done.46.refs_4_), channel_id=1, source_target_pairs={{0,8},{4,12},{8,16},{12,20},{16,24},{20,28},{24,0},{28,4},{1,9},{5... | collective-permute-start | bytes 3194888 | tf_op jit(solution)/shard_map/ppermute | solution.py:504
  1038.9 35.0 %collective-permute-start.43 = (bf16[64,8320]{1,0:T(8,128)(2,1)S(1)}, bf16[64,8320]{1,0:T(8,128)(2,1)S(1)}, u32[]{:S(2)}, u32[]{:S(2)}) collective-permute-start(bf16[64,8320]{1,0:T(8,128)(2,1)S(1)} %pad_maximum_fusion.3.refs_0_), channel_id=1, source_target_pairs={{0,4},{4,0},{8,12},{12,8},{16,20},{20,16},{24,28},{28,24},{1,5},{5... | collective-permute-start | bytes 3194888 | tf_op jit(solution)/shard_map/ppermute | solution.py:500
  1039.6 48.6 %collective-permute-start.45 = (bf16[64,8320]{1,0:T(8,128)(2,1)}, bf16[64,8320]{1,0:T(8,128)(2,1)S(1)}, u32[]{:S(2)}, u32[]{:S(2)}) collective-permute-start(bf16[64,8320]{1,0:T(8,128)(2,1)} %collective-permute-done.44.refs_2_), channel_id=1, source_target_pairs={{0,4},{4,0},{8,12},{12,8},{16,20},{20,16},{24,28},{28,24},{1,5},{5... | collective-permute-start | bytes 3194888 | tf_op jit(solution)/shard_map/ppermute | solution.py:500
  1041.0 70.1 %collective-permute-start.47 = (bf16[64,8320]{1,0:T(8,128)(2,1)}, bf16[64,8320]{1,0:T(8,128)(2,1)S(1)}, u32[]{:S(2)}, u32[]{:S(2)}) collective-permute-start(bf16[64,8320]{1,0:T(8,128)(2,1)} %collective-permute-done.46.refs_4_), channel_id=1, source_target_pairs={{0,4},{4,0},{8,12},{12,8},{16,20},{20,16},{24,28},{28,24},{1,5},{5... | collective-permute-start | bytes 3194888 | tf_op jit(solution)/shard_map/ppermute | solution.py:500
  1068.1 62.2 %collective-permute-start.49 = (bf16[64,8320]{1,0:T(8,128)(2,1)}, bf16[64,8320]{1,0:T(8,128)(2,1)}, u32[]{:S(2)}, u32[]{:S(2)}) collective-permute-start(bf16[64,8320]{1,0:T(8,128)(2,1)} %collective-permute-done.48.refs_6_), channel_id=1, source_target_pairs={{0,4},{4,0},{8,12},{12,8},{16,20},{20,16},{24,28},{28,24},{1,5},{5... | collective-permute-start | bytes 3194888 | tf_op jit(solution)/shard_map/ppermute | solution.py:500
  (122 other events, 1216.7 us)
Sparse Core Ops, SparseCore 0:
  10.8 134.3 all-gather.11
  146.7 78.9 all-gather.9
  227.3 58.2 all-gather.5
  287.0 58.2 all-gather.7
  455.3 44.7 reduce-scatter.10
  524.7 44.7 reduce-scatter.12
  572.6 44.5 reduce-scatter.6
  620.4 61.4 reduce-scatter.8
  698.5 42.4 reduce-scatter.14
  839.3 44.5 reduce-scatter.16

commit v3 on v2

--- a/solution.py
+++ b/solution.py
@@ -17,6 +17,7 @@
 BF = jnp.bfloat16
 F32 = jnp.float32
 QCHUNK = 256
+VMEM = 58 << 20
 
 
 def rms_scale(values):
@@ -39,7 +40,7 @@
     return lax.dot_general(left, right, (((0,), (0,)), ((), ())), preferred_element_type=F32)
 
 
-def params(mib):
+def params(mib=40):
     return pltpu.CompilerParams(vmem_limit_bytes=mib << 20)
 
 
@@ -51,6 +52,10 @@
 
 def after(value, *others):
     return lax.optimization_barrier((value,) + others)[0]
+
+
+def together(*values):
+    return lax.optimization_barrier(values)
 
 
 def pack_columns(q_ref, k_ref, v_ref, out_ref):
@@ -70,9 +75,97 @@
         in_specs=[spec, spec, spec],
         out_specs=pl.BlockSpec((1, rows, 3 * part), lambda s: (s, 0, 0)),
         out_shape=jax.ShapeDtypeStruct((shards, rows, 3 * part), BF),
-        compiler_params=params(32),
+        compiler_params=params(),
         cost_estimate=cost(0, 12 * rows * width),
     )(w_query, w_key, w_value)
+
+
+def pack_part(place_ref, q_ref, k_ref, v_ref, out_ref):
+    pack_columns(q_ref, k_ref, v_ref, out_ref)
+
+
+def packed_part(place, w_query, w_key, w_value, shards, part):
+    width = w_query.shape[1] // shards
+    spec = pl.BlockSpec((part, width), lambda s, n: (n[0], 2 * n[1] + s))
+    return pl.pallas_call(
+        pack_part,
+        grid_spec=pltpu.PrefetchScalarGridSpec(
+            num_scalar_prefetch=1,
+            grid=(2,),
+            in_specs=[spec, spec, spec],
+            out_specs=pl.BlockSpec((1, part, 3 * width), lambda s, n: (s, 0, 0)),
+        ),
+        out_shape=jax.ShapeDtypeStruct((2, part, 3 * width), BF),
+        compiler_params=params(),
+        cost_estimate=cost(0, 24 * part * width),
+    )(place, w_query, w_key, w_value)
+
+
+def project_body(parts, order_ref, shard_ref, gain_ref, packed_ref, near_ref, *refs):
+    token_refs, far_refs = refs[:4], refs[4 : 4 + parts]
+    input_ref, columns_ref, qkv_ref, sem = refs[4 + parts :]
+    rows = near_ref.shape[0]
+    count = token_refs[0].shape[0]
+    part = rows // parts
+
+    def place(start, size):
+        return columns_ref.at[pl.ds(pl.multiple_of(start, 16), size)]
+
+    copies = [
+        pltpu.make_async_copy(packed_ref.at[shard_ref[0]], place(shard_ref[0] * rows, rows), sem.at[0]),
+        pltpu.make_async_copy(near_ref, place(shard_ref[1] * rows, rows), sem.at[1]),
+    ]
+    for i in range(parts):
+        for m in range(2):
+            start = shard_ref[2 + m] * rows + order_ref[i] * part
+            copies.append(
+                pltpu.make_async_copy(
+                    far_refs[i].at[m, pl.ds(0, part)], place(start, part), sem.at[2 + 2 * i + m]
+                )
+            )
+    for copy in copies:
+        copy.start()
+    for i in range(4):
+        x = token_refs[i][...].astype(F32)
+        input_ref[i * count : (i + 1) * count, :] = (x * rms_scale(x) * gain_ref[...]).astype(BF)
+    for copy in copies:
+        copy.wait()
+
+    def step(i, carry):
+        r = pl.ds(pl.multiple_of(i * count, count), count)
+        qkv_ref[r, :] = dot(input_ref[r, :], columns_ref[...])
+        return carry
+
+    lax.fori_loop(0, 4, step, 0)
+
+
+def project(order, shards, gain, packed, near, token_blocks, fars):
+    count, width = token_blocks[0].shape
+    columns = near.shape[1]
+    length = count * len(token_blocks)
+    anywhere = pl.BlockSpec(memory_space=pl.ANY)
+    whole = lambda *shape: pl.BlockSpec(shape, lambda i, a, b: (0, 0))
+    return pl.pallas_call(
+        functools.partial(project_body, len(fars)),
+        grid_spec=pltpu.PrefetchScalarGridSpec(
+            num_scalar_prefetch=2,
+            grid=(1,),
+            in_specs=[whole(1, width), anywhere, anywhere]
+            + [whole(count, width)] * 4
+            + [anywhere] * len(fars),
+            out_specs=[whole(length, width), whole(width, columns), whole(length, columns)],
+            scratch_shapes=[pltpu.SemaphoreType.DMA((2 + 2 * len(fars),))],
+        ),
+        out_shape=[
+            jax.ShapeDtypeStruct((length, width), BF),
+            jax.ShapeDtypeStruct((width, columns), BF),
+            jax.ShapeDtypeStruct((length, columns), F32),
+        ],
+        compiler_params=params(56),
+        cost_estimate=cost(
+            2 * length * width * columns, 4 * length * width + 4 * width * columns + 4 * length * columns
+        ),
+    )(order, shards, gain, packed, near, *token_blocks, *fars)
 
 
 def turned(values, cosine, sine):
@@ -116,13 +209,9 @@
     gk_ref,
     segc_ref,
     segr_ref,
-    grad_ref,
-    gains_ref,
-    kb_ref,
-    vb_ref,
-    dk_acc,
-    dv_acc,
+    *refs,
 ):
+    grad_ref, gains_ref, kb_ref, vb_ref, dk_acc, dv_acc = refs[-6:]
     length = qkv_ref.shape[0]
     scale = HD**-0.5
 
@@ -183,28 +272,30 @@
         out_specs=pl.BlockSpec((length, HD), lambda h: (0, h)),
         out_shape=jax.ShapeDtypeStruct((length, heads * HD), BF),
         scratch_shapes=[pltpu.VMEM((length, HD), BF)] * 2,
-        compiler_params=params(40),
+        compiler_params=params(),
         cost_estimate=cost(16 * heads * length * length * HD, qkv.size * 5, heads * length * length),
     )(qkv, *attn_args)
 
 
-def attention_backward(qkv, grad_o, attn_args):
+def attention_backward(qkv, grad_o, attn_args, first, heads, held=None):
     length = qkv.shape[0]
-    heads = qkv.shape[1] // (3 * HD)
-    wide = pl.BlockSpec((length, 3 * HD), lambda h: (0, h))
+    wide = pl.BlockSpec((length, 3 * HD), lambda h: (0, first + h))
     return pl.pallas_call(
         attend_backward,
         grid=(heads,),
-        in_specs=[wide, pl.BlockSpec((length, HD), lambda h: (0, h))] + attention_specs(length),
+        in_specs=[wide, pl.BlockSpec((length, HD), lambda h: (0, first + h))]
+        + attention_specs(length)
+        + [pl.BlockSpec(memory_space=pl.ANY)] * (held is not None),
         out_specs=[wide, pl.BlockSpec((8, HD), lambda h: (0, 0))],
         out_shape=[
             jax.ShapeDtypeStruct(qkv.shape, BF),
             jax.ShapeDtypeStruct((8, HD), F32),
         ],
         scratch_shapes=[pltpu.VMEM((length, HD), BF)] * 2 + [pltpu.VMEM((length, HD), F32)] * 2,
+        input_output_aliases={} if held is None else {8: 0},
         compiler_params=params(48),
-        cost_estimate=cost(40 * heads * length * length * HD, qkv.size * 7, heads * length * length),
-    )(qkv, grad_o, *attn_args)
+        cost_estimate=cost(40 * heads * length * length * HD, qkv.size * 3, heads * length * length),
+    )(qkv, grad_o, *attn_args, *(() if held is None else (held,)))
 
 
 def pick_rows(has_input, number_ref, slots_ref, named_ref, router_ref, x_ref, grad_ref, *refs):
@@ -212,19 +303,18 @@
     experts, capacity = slots_ref.shape[1], rows_ref.shape[2]
     count = x_ref.shape[0]
     x = x_ref[...]
-    named = named_ref[0]
     logits = dot(x, router_ref[...])
     lane = lax.broadcasted_iota(jnp.int32, logits.shape, 1)
-    logits = jnp.where(lane < number_ref[2], logits, MASKED)
+    logits = jnp.where(lane < number_ref[1], logits, MASKED)
     exps = jnp.exp(logits - jnp.max(logits, axis=-1, keepdims=True))
     probs = exps / jnp.sum(exps, axis=-1, keepdims=True)
-    chosen = jnp.where(named > 0.0, probs, 0.0)
+    chosen = jnp.where(named_ref[0] > 0.0, probs, 0.0)
     gates = chosen / jnp.sum(chosen, axis=-1, keepdims=True)
-    grad = grad_ref[0].astype(F32)
+    grad = grad_ref[...].astype(F32)
     wanted = lax.broadcasted_iota(jnp.int32, (capacity, count), 0)
     columns = []
     for j in range(experts):
-        gate = jnp.sum(jnp.where(lane == number_ref[1] + j, gates, 0.0), axis=1, keepdims=True)
+        gate = jnp.sum(jnp.where(lane == number_ref[0] + j, gates, 0.0), axis=1, keepdims=True)
         hot = (wanted == slots_ref[0, j : j + 1, :]).astype(BF)
         rows_ref[j, 0] = dot(hot, x).astype(BF)
         grad_rows_ref[j, 0] = dot(hot, (grad * gate).astype(BF)).astype(BF)
@@ -232,7 +322,7 @@
     gates_ref[...] = jnp.concatenate(columns, axis=1)
 
 
-def pick(number, slots, named, router, x, grads, held, place, blocks, capacity):
+def pick(number, slots, named, router, x, grad, held, block, place, blocks, capacity):
     count, width = x.shape
     experts = slots.shape[1]
     lanes = router.shape[1]
@@ -245,25 +335,25 @@
             num_scalar_prefetch=1,
             grid=(1,),
             in_specs=[
-                pl.BlockSpec((1, experts, count), lambda i, n: (n[0], 0, 0)),
-                pl.BlockSpec((1, count, lanes), lambda i, n: (n[0], 0, 0)),
+                pl.BlockSpec((1, experts, count), lambda i, n: (block, 0, 0)),
+                pl.BlockSpec((1, count, lanes), lambda i, n: (block, 0, 0)),
                 pl.BlockSpec((width, lanes), lambda i, n: (0, 0)),
                 pl.BlockSpec((count, width), lambda i, n: (0, 0)),
-                pl.BlockSpec((1, count, width), lambda i, n: (n[0], 0, 0)),
+                pl.BlockSpec((count, width), lambda i, n: (0, 0)),
             ]
             + [whole, whole] * (held is not None),
             out_specs=[out, out, pl.BlockSpec((count, experts), lambda i, n: (0, 0))],
         ),
         out_shape=[shape, shape, jax.ShapeDtypeStruct((count, experts), F32)],
         input_output_aliases={} if held is None else {6: 0, 7: 1},
-        compiler_params=params(40),
+        compiler_params=params(58),
         cost_estimate=cost(
             4 * experts * capacity * count * width, 4 * width * (count + experts * capacity)
         ),
-    )(number, slots, named, router, x, grads, *(held or ()))
-
-
-def merge_rows(blocks, ids_ref, slots_ref, *refs):
+    )(number, slots, named, router, x, grad, *(held or ()))
+
+
+def merge_rows_body(blocks, slots_ref, *refs):
     experts = slots_ref.shape[2]
     rows_refs, out_refs = refs[:experts], refs[experts:]
     capacity = rows_refs[0].shape[0]
@@ -281,62 +371,71 @@
             out_refs[i][...] = total.astype(BF)
 
 
-def merge_results(blocks, ids_ref, slots_ref, grad_ref, *refs):
+def merge_rows(slots, first, rows, blocks):
+    count, experts = slots.shape[1:]
+    capacity = rows[0].shape[0] // blocks
+    width = rows[0].shape[1]
+    return pl.pallas_call(
+        functools.partial(merge_rows_body, blocks),
+        grid=(blocks,),
+        in_specs=[pl.BlockSpec((1, count, experts), lambda b: (first + b, 0, 0))]
+        + [pl.BlockSpec((capacity, width), lambda b: (b, 0))] * experts,
+        out_specs=[pl.BlockSpec((count, width), lambda b: (0, 0))] * blocks,
+        out_shape=[jax.ShapeDtypeStruct((count, width), BF)] * blocks,
+        compiler_params=params(),
+        cost_estimate=cost(
+            2 * blocks * experts * capacity * count * width,
+            2 * blocks * width * (count + experts * capacity),
+        ),
+    )(slots, *rows)
+
+
+def merge_results_body(blocks, slots_ref, *refs):
     experts = slots_ref.shape[2]
-    gates_refs, refs = refs[:blocks], refs[blocks:]
+    gates_refs, grad_refs, refs = refs[:blocks], refs[blocks : 2 * blocks], refs[2 * blocks :]
     rows_refs, out_refs, dgate_ref = refs[:experts], refs[experts:-1], refs[-1]
     capacity = rows_refs[0].shape[0]
     count = out_refs[0].shape[0]
     place = lax.broadcasted_iota(jnp.int32, (count, capacity), 1)
-    grad = grad_ref[0].astype(F32)
-    gates = gates_refs[0][...]
-    for i in range(1, blocks):
-        gates = jnp.where(pl.program_id(0) == i, gates_refs[i][...], gates)
-    total = None
-    dgates = []
-    for j in range(experts):
-        hot = (place == slots_ref[0, :, j : j + 1]).astype(BF)
-        rows = dot(hot, rows_refs[j][...])
-        dgates.append(jnp.sum(rows * grad, axis=1, keepdims=True))
-        gated = rows * gates[:, j : j + 1]
-        total = gated if total is None else total + gated
-    dgate_ref[0] = jnp.concatenate(dgates, axis=1)
     for i in range(blocks):
 
         @pl.when(pl.program_id(0) == i)
         def _(i=i):
+            grad = grad_refs[i][...].astype(F32)
+            total = None
+            dgates = []
+            for j in range(experts):
+                hot = (place == slots_ref[0, :, j : j + 1]).astype(BF)
+                rows = dot(hot, rows_refs[j][...])
+                dgates.append(jnp.sum(rows * grad, axis=1, keepdims=True))
+                gated = rows * gates_refs[i][:, j : j + 1]
+                total = gated if total is None else total + gated
             out_refs[i][...] = total.astype(BF)
-
-
-def merge(ids, slots, rows, gates=None, grads=None):
-    blocks = ids.shape[0]
+            dgate_ref[0] = jnp.concatenate(dgates, axis=1)
+
+
+def merge_results(slots, first, gates, grads, rows):
+    blocks = len(gates)
     count, experts = slots.shape[1:]
     capacity = rows[0].shape[0] // blocks
     width = rows[0].shape[1]
-    small = pl.BlockSpec((1, count, experts), lambda b, n: (n[b], 0, 0))
-    in_specs = [small]
-    operands = [slots]
-    out_specs = [pl.BlockSpec((count, width), lambda b, n: (0, 0))] * blocks
-    out_shape = [jax.ShapeDtypeStruct((count, width), BF)] * blocks
-    if gates is not None:
-        in_specs += [pl.BlockSpec((1, count, width), lambda b, n: (n[b], 0, 0))]
-        in_specs += [pl.BlockSpec((count, experts), lambda b, n: (0, 0))] * blocks
-        operands += [grads] + list(gates)
-        out_specs = out_specs + [pl.BlockSpec((1, count, experts), lambda b, n: (b, 0, 0))]
-        out_shape = out_shape + [jax.ShapeDtypeStruct((blocks, count, experts), F32)]
-    in_specs += [pl.BlockSpec((capacity, width), lambda b, n: (b, 0))] * experts
+    tokens = pl.BlockSpec((count, width), lambda b: (0, 0))
     return pl.pallas_call(
-        functools.partial(merge_rows if gates is None else merge_results, blocks),
-        grid_spec=pltpu.PrefetchScalarGridSpec(
-            num_scalar_prefetch=1, grid=(blocks,), in_specs=in_specs, out_specs=out_specs
-        ),
-        out_shape=out_shape,
-        compiler_params=params(40),
+        functools.partial(merge_results_body, blocks),
+        grid=(blocks,),
+        in_specs=[pl.BlockSpec((1, count, experts), lambda b: (first + b, 0, 0))]
+        + [pl.BlockSpec((count, experts), lambda b: (0, 0))] * blocks
+        + [tokens] * blocks
+        + [pl.BlockSpec((capacity, width), lambda b: (b, 0))] * experts,
+        out_specs=[tokens] * blocks + [pl.BlockSpec((1, count, experts), lambda b: (b, 0, 0))],
+        out_shape=[jax.ShapeDtypeStruct((count, width), BF)] * blocks
+        + [jax.ShapeDtypeStruct((blocks, count, experts), F32)],
+        compiler_params=params(),
         cost_estimate=cost(
             2 * blocks * experts * capacity * count * width,
             2 * blocks * width * (2 * count + experts * capacity),
         ),
-    )(ids, *operands, *rows)
+    )(slots, *gates, *grads, *rows)
 
 
 def expert_body(
@@ -485,10 +584,17 @@
     return [value, near, far, swap_core(far)]
 
 
+def added(*terms):
+    total = terms[0].astype(F32)
+    for term in terms[1:]:
+        total = total + term.astype(F32)
+    return total
+
+
 def shard_reduce(blocks):
-    far = blocks[2].astype(F32) + swap_core(blocks[3].astype(BF)).astype(F32)
-    far = swap_x(far.astype(BF))
-    near = blocks[0].astype(F32) + swap_core(blocks[1].astype(BF)).astype(F32)
+    far = added(blocks[2], swap_core(blocks[3])).astype(BF)
+    far = swap_x(far)
+    near = added(blocks[0], swap_core(blocks[1]))
     return near + far.astype(F32)
 
 
@@ -510,30 +616,54 @@
     return [((z + planes - k) % planes) * 2 + (y ^ w) for k in range(planes) for w in range(2)]
 
 
+def turn_and_cross(value, count):
+    return together(turn_z(value, count), swap_y(value, count))
+
+
 def rep_gather(value, count):
     blocks = []
     held = value
     for k in range(count // 2):
-        if k > 0:
-            held = turn_z(held, count)
-        blocks += [held, swap_y(held, count)]
+        if k < count // 2 - 1:
+            nexts, crossed = together(turn_z(held, count), swap_y(held, count))
+        else:
+            nexts, crossed = None, swap_y(held, count)
+        blocks += [held, crossed]
+        held = nexts
     return blocks
 
 
-def rep_reduce(blocks, count):
-    planes = count // 2
-
-    def pair(k):
-        return blocks[2 * k].astype(F32) + swap_y(blocks[2 * k + 1].astype(BF), count).astype(F32)
-
-    total = pair(1)
-    for k in list(range(2, planes)) + [0]:
-        total = turn_z(total.astype(BF), count).astype(F32) + pair(k)
-    return total
-
-
-def write_sums_body(blocks, shards, ids_ref, wq_ref, wk_ref, wv_ref, gain_ref, *refs):
-    in_refs, (q_ref, k_ref, v_ref, o_ref, extra_ref) = refs[:blocks], refs[blocks:]
+class RepReduce:
+    def __init__(self, blocks, count, *ready):
+        self.blocks, self.count = blocks, count
+        self.order = list(range(2, count // 2)) + [0]
+        self.arrived = (swap_y(after(blocks[3], *ready), count),)
+        self.total = None
+        self.k = 1
+
+    def step(self, *ready):
+        arrived = together(*self.arrived, *ready)[: len(self.arrived)]
+        total = added(self.blocks[2 * self.k], *arrived)
+        if not self.order:
+            return total
+        self.k = self.order.pop(0)
+        self.arrived = together(
+            swap_y(after(self.blocks[2 * self.k + 1], arrived[0]), self.count),
+            turn_z(total.astype(BF), self.count),
+        )
+        return None
+
+
+def rep_reduce(blocks, count, *ready):
+    reduce = RepReduce(blocks, count, *ready)
+    while True:
+        total = reduce.step()
+        if total is not None:
+            return total
+
+
+def write_sums_body(blocks, ids_ref, wq_ref, wk_ref, wv_ref, gain_ref, *refs):
+    in_refs, (q_ref, k_ref, v_ref, o_ref, extra_ref) = refs[:blocks], refs[-5:]
     width = q_ref.shape[1]
     heads = width // HD
     for i in range(blocks):
@@ -556,7 +686,7 @@
             extra_ref[...] = jnp.where(lane == extra.shape[1] - 1, attn, extra)
 
 
-def write_sums(ids, w_query, w_key, w_value, gain, gathered, shards):
+def write_sums(ids, w_query, w_key, w_value, gain, gathered, held=()):
     blocks = len(gathered)
     part, total = gathered[0].shape
     rows, width = w_query.shape
@@ -564,18 +694,20 @@
     extra = pl.BlockSpec((part, HD), lambda b, n: (n[b], 0))
     big = jax.ShapeDtypeStruct((rows, width), F32)
     return pl.pallas_call(
-        functools.partial(write_sums_body, blocks, shards),
+        functools.partial(write_sums_body, blocks),
         grid_spec=pltpu.PrefetchScalarGridSpec(
             num_scalar_prefetch=1,
             grid=(blocks,),
             in_specs=[own, own, own, pl.BlockSpec((part, 1), lambda b, n: (n[b], 0))]
-            + [pl.BlockSpec((part, total), lambda b, n: (0, 0))] * blocks,
+            + [pl.BlockSpec((part, total), lambda b, n: (0, 0))] * blocks
+            + [pl.BlockSpec(memory_space=pl.ANY)] * len(held),
             out_specs=[own, own, own, own, extra],
         ),
         out_shape=[big, big, big, big, jax.ShapeDtypeStruct((rows, HD), F32)],
+        input_output_aliases={5 + blocks + i: i for i in range(len(held))},
         compiler_params=params(52),
-        cost_estimate=cost(0, rows * width * 30),
-    )(ids, w_query, w_key, w_value, gain, *gathered)
+        cost_estimate=cost(0, blocks * part * width * 30),
+    )(ids, w_query, w_key, w_value, gain, *gathered, *held)
 
 
 def on_device(
@@ -610,15 +742,34 @@
     order = rep_order(rep, rep_count)
     order_in = shard_order(position)
     group_size = 4
-    groups = [list(range(s, s + group_size)) for s in range(0, rep_count, group_size)]
-
-    token_blocks = shard_gather(tokens)
-    packed = packed_columns(w_query, w_key, w_value, shard_count)
-    columns = lax.all_to_all(packed, "shard", split_axis=0, concat_axis=0, tiled=True)
-    columns = columns.reshape(width, -1)
-    routes_b = jnp.pad(routes.astype(BF), ((0, 0), (0, HD - TOP)))
-    grads = lax.all_gather(jnp.concatenate([cotangent, routes_b], axis=1), "rep", axis=0, tiled=False)
-
+
+    order_array = jnp.stack(order)
+    order_in_array = jnp.stack(order_in)
+    part = rows // rep_count
+    core = position % 2
+
+    far = packed_part(
+        jnp.stack([rep, 1 - position // 2]), w_query, w_key, w_value, shard_count, part
+    )
+    far = swap_x(far)
+    far_tokens = swap_x(tokens)
+    grad_blocks = [cotangent]
+    grad_held, crossed = turn_and_cross(grad_blocks[0], rep_count)
+    grad_blocks += [crossed, grad_held]
+    full_gate = lax.all_gather(after(w_gate, far, far_tokens, grad_held), "shard", axis=1, tiled=True)
+    far = jnp.stack(
+        [
+            lax.dynamic_index_in_dim(far, core, 0, keepdims=False),
+            swap_core(lax.dynamic_index_in_dim(far, 1 - core, 0, keepdims=False)),
+        ]
+    )
+    routes_b = routes.astype(BF).reshape(2, 16, -1)
+    routes_b = jnp.pad(routes_b, ((0, 0), (0, 0), (0, far.shape[2] - routes_b.shape[2])))
+    full_up = lax.all_gather(after(w_up, far, far_tokens, grad_held), "shard", axis=1, tiled=True)
+    fars = rep_gather(jnp.concatenate([far, routes_b], axis=1), rep_count)
+    packed = packed_columns(after(w_query, fars[1]), w_key, w_value, shard_count)
+    near = swap_core(lax.dynamic_index_in_dim(packed, position ^ 1, 0, keepdims=False))
+    token_blocks = [tokens, swap_core(tokens), far_tokens, swap_core(far_tokens)]
     small = jnp.concatenate(
         [
             w_router,
@@ -631,7 +782,6 @@
     )
     small = jnp.pad(small, ((0, 0), (0, HD - small.shape[1])))
     small = jnp.stack(shard_gather(small))
-    order_in_array = jnp.stack(order_in)
     small = jnp.zeros_like(small).at[order_in_array].set(small)
     head_gains = small[:, : norm_query.shape[0], experts + 2 : experts + 4].astype(F32)
     gain_query = head_gains[:, :, 0].reshape(1, HD)
@@ -641,25 +791,9 @@
     gain_ffn = small[:, experts + 1].astype(F32)
     full_router = small[:, :experts]
 
-    full_gate = lax.all_gather(after(w_gate, columns), "shard", axis=1, tiled=True)
-    full_up = lax.all_gather(after(w_up, columns), "shard", axis=1, tiled=True)
-    full_down = lax.all_gather(after(w_down, columns), "shard", axis=1, tiled=True)
-
-    expert_ids = jnp.arange(experts, dtype=jnp.int32)
-    named_all = jnp.any(
-        grads[:, :, width : width + TOP].astype(jnp.int32)[:, :, :, None] == expert_ids, axis=2
+    input_b, columns, qkv = project(
+        order_array, order_in_array, gain_attn[None, :], packed, near, token_blocks, fars
     )
-    first_expert = rep * local_experts
-    named_mine = lax.dynamic_slice_in_dim(named_all, first_expert, local_experts, axis=2)
-    before = jnp.tril(jnp.ones((rows_count, rows_count), BF), -1)
-    slot_mine = jnp.einsum("ts,bsj->btj", before, named_mine.astype(BF), preferred_element_type=F32)
-    slot_tokens = jnp.where(named_mine, slot_mine.astype(jnp.int32), -1)
-    slot_lanes = jnp.swapaxes(slot_tokens, 1, 2)
-    named_lanes = jnp.pad(named_all.astype(F32), ((0, 0), (0, 0), (0, HD - experts)))
-
-    tokens_all = jnp.concatenate(token_blocks, axis=0).astype(F32)
-    input_b = (tokens_all * rms_scale(tokens_all) * gain_attn).astype(BF)
-    qkv = dot(input_b, columns)
     places = jnp.concatenate([p * rows_count + jnp.arange(rows_count, dtype=jnp.int32) for p in order_in])
     inverse = THETA ** (-jnp.arange(HD // 2, dtype=F32) * 2.0 / HD)
     angles = places.astype(F32)[:, None] * inverse[None, :]
@@ -671,66 +805,154 @@
     )
     attn_args = (cosine, sine, gain_query, gain_key, segment_all[:, None], segment_all[None, :])
     mixed_b = attention_forward(qkv, attn_args)
+    planes = rep_count // 2
+    for k in range(1, planes - 1):
+        grad_held, crossed = turn_and_cross(after(grad_held, fars[-1]), rep_count)
+        grad_blocks += [crossed, grad_held]
+        if k == 1:
+            mixed_b = after(mixed_b, grad_held)
     projected = dot(mixed_b, w_out).astype(BF)
     projected = [projected[i * rows_count : (i + 1) * rows_count] for i in range(shard_count)]
     tokens_f = tokens.astype(F32)
-    hidden_state = tokens_f + shard_reduce(projected)
+    attended = shard_reduce(projected)
+    full_down = lax.all_gather(
+        after(w_down, attended, grad_held), "shard", axis=1, tiled=True
+    )
+    hidden_state = tokens_f + attended
 
     scale_mid = rms_scale(hidden_state)
     normed_mid = hidden_state * scale_mid
     mid_b = (normed_mid * gain_ffn).astype(BF)
-    mid_blocks = rep_gather(mid_b, rep_count)
+    expert_ids = jnp.arange(experts, dtype=jnp.int32)
+    first_expert = rep * local_experts
+    before = jnp.tril(jnp.ones((rows_count, rows_count), BF), -1)
+
+    route_all = jnp.stack([block[:, part:, : rows_count * TOP // 32] for block in fars])
+    route_all = route_all.reshape(rep_count, rows_count, TOP).astype(jnp.int32)
+    named_all = jnp.any(route_all[:, :, :, None] == expert_ids, axis=2)
+    named_mine = lax.dynamic_slice_in_dim(named_all, first_expert, local_experts, axis=2)
+    slots = jnp.einsum("ts,bsj->btj", before, named_mine.astype(BF), preferred_element_type=F32)
+    slots = jnp.where(named_mine, slots.astype(jnp.int32), -1)
+    slot_lanes = jnp.swapaxes(slots, 1, 2)
+    named_lanes = jnp.pad(named_all.astype(F32), ((0, 0), (0, 0), (0, HD - experts)))
+
     router_lanes = jnp.pad(full_router, ((0, 0), (0, HD - experts)))
-    expert_rows, grad_rows, kept, result_parts, grad_parts, dgate_parts = [], [], [], [], [], []
-    for group in groups:
-        held, gates = None, []
-        for place, b in enumerate(group):
-            number = jnp.stack([order[b], first_expert, jnp.int32(experts)])
-            x, dy, gate = pick(
+    number = jnp.stack([first_expert, jnp.int32(experts)])
+    picked, groups = [], []
+    mid_b = after(mid_b, grad_held, slots, slot_lanes, named_lanes)
+
+    def pick_next(block):
+        b = len(picked)
+        place = b % group_size
+        held = picked[-1][:2] if place else None
+        picked.append(
+            pick(
                 number,
                 slot_lanes,
                 named_lanes,
                 router_lanes,
-                mid_blocks[b],
-                grads,
+                block,
+                grad_blocks[b],
                 held,
+                b,
                 place,
-                len(group),
+                group_size,
                 capacity,
             )
-            held = (x, dy)
-            gates.append(gate)
-        x, dy = [a.reshape(local_experts, len(group) * capacity, width) for a in held]
-        done = [expert(j, x, dy, full_gate, full_up, full_down) for j in range(local_experts)]
-        ids = jnp.stack([order[b] for b in group])
-        grad_parts += merge(ids, slot_tokens, [d[1] for d in done])
-        *parts, dgate = merge(ids, slot_tokens, [d[0] for d in done], gates, grads)
+        )
+        if place == group_size - 1:
+            x, dy = [
+                a.reshape(local_experts, group_size * capacity, width) for a in picked[-1][:2]
+            ]
+            groups.append((x, dy, []))
+
+    def run_expert(group, j, *others):
+        x, dy, done = groups[group]
+        done.append(expert(j, after(x, *others), dy, full_gate, full_up, full_down))
+        return done[-1][0]
+
+    def merge_grads(group):
+        return merge_rows(slots, group * group_size, [d[1] for d in groups[group][2]], group_size)
+
+    def merge_group(group, *ready):
+        members = slice(group * group_size, (group + 1) * group_size)
+        *parts, dgate = merge_results(
+            after(slots, *ready),
+            group * group_size,
+            [p[2] for p in picked[members]],
+            grad_blocks[members],
+            [d[0] for d in groups[group][2]],
+        )
+        return parts, dgate
+
+    held, crossed, ready = mid_b, None, ()
+    for k in range(planes):
+        held = after(held, *ready)
+        if k < planes - 1:
+            nexts, crossing = turn_and_cross(held, rep_count)
+        else:
+            nexts, crossing = None, swap_y(held, rep_count)
+        if k > 0:
+            pick_next(crossed)
+        pick_next(held)
+        ready = (picked[-1][0],)
+        held, crossed = nexts, crossing
+    grad_blocks.append(swap_y(after(grad_held, crossed), rep_count))
+    grad_parts, result_parts, dgate_parts = [], [], []
+    last = rep_count // group_size - 1
+    ready = ()
+    for g in range(last):
+        for j in range(local_experts):
+            ready = (run_expert(g, j, *ready),)
+        grad_parts += merge_grads(g)
+        ready = (grad_parts[-1],)
+    cross_first = swap_y(grad_parts[3], rep_count)
+    cross_zero = swap_y(after(grad_parts[1], grad_parts[3]), rep_count)
+    pick_next(after(crossed, *ready))
+    y = run_expert(last, 0)
+    cross_first, cross_zero = together(cross_first, cross_zero, y)[:2]
+    total = turn_z(added(grad_parts[2], cross_first).astype(BF), rep_count)
+    for j in range(1, local_experts):
+        y = run_expert(last, j, cross_first, cross_zero)
+    total = after(total, y)
+    grad_parts += merge_grads(last)
+    arrived = swap_y(grad_parts[5], rep_count)
+    for g in range(last + 1):
+        parts, dgate = merge_group(g, grad_parts[-1])
         result_parts += parts
         dgate_parts.append(dgate)
-        expert_rows.append(x)
-        grad_rows.append(dy)
-        kept.append(done)
-    grad_mid_moe = rep_reduce(grad_parts, rep_count)
-    expert_sum = rep_reduce(result_parts, rep_count)
-    output = (hidden_state + expert_sum).astype(BF)
 
     def owned_part(grad):
         return lax.psum_scatter(grad, "shard", scatter_dimension=0, tiled=True)
 
-    sums_gate, sums_up, sums_down = [], [], []
-    for j in range(local_experts):
-        down, = weight_grads([k[j][2] for k in kept], [grad_rows], None, j)
-        gate, up = weight_grads(
-            expert_rows, [[k[j][3] for k in kept], [k[j][4] for k in kept]], j, None
+    def wide_grads(j, *others):
+        return weight_grads(
+            [after(g[0], *others) for g in groups],
+            [[g[2][j][3] for g in groups], [g[2][j][4] for g in groups]],
+            j,
+            None,
         )
-        sums_down.append(owned_part(down))
-        sums_gate.append(owned_part(gate))
-        sums_up.append(owned_part(up))
-    grad_gate = jnp.stack(sums_gate).astype(F32)
-    grad_up = jnp.stack(sums_up).astype(F32)
-    grad_down = jnp.stack(sums_down).astype(F32)
-
-    order_array = jnp.stack(order)
+
+    def down_grads(j, *others):
+        return weight_grads(
+            [after(g[2][j][2], *others) for g in groups], [[g[1] for g in groups]], None, j
+        )[0]
+
+    arrived = after(arrived, *result_parts, *dgate_parts)
+    made = []
+    for k in range(2, planes):
+        total = added(grad_parts[2 * k], arrived, total).astype(BF)
+        if k < planes - 1:
+            total, arrived = together(
+                turn_z(total, rep_count), swap_y(after(grad_parts[2 * k + 3], arrived), rep_count)
+            )
+            if not made:
+                made.append(wide_grads(0, grad_parts[-1], *result_parts))
+                total, arrived = together(total, arrived, *made[0])[:2]
+        else:
+            total = turn_z(total, rep_count)
+    grad_mid_moe = added(grad_parts[0], cross_zero, total)
+
     dgates = jnp.swapaxes(jnp.concatenate(dgate_parts), 1, 2)
     dgates = jnp.zeros_like(dgates).at[order_array].set(dgates)
     dgates = lax.all_to_all(dgates, "rep", split_axis=0, concat_axis=0, tiled=True)
@@ -754,12 +976,19 @@
     grad_state = grad_out + norm_back(grad_mid * gain_ffn, normed_mid, scale_mid)
     grad_state_b = grad_state.astype(BF)
 
-    grad_state_all = jnp.concatenate(shard_gather(grad_state_b), axis=0)
+    state_blocks = shard_gather(grad_state_b)
+    while len(made) < local_experts:
+        made.append(wide_grads(len(made), grad_state_b))
+    grad_state_all = jnp.concatenate(state_blocks, axis=0)
+    grad_state_all = after(grad_state_all, *made[-1])
     grad_mixed = dot_t(grad_state_all, w_out).astype(BF)
+    heads = qkv.shape[1] // (3 * HD)
+    grad_qkv, grad_head_gains = attention_backward(qkv, grad_mixed, attn_args, 0, heads)
+    grad_columns = t_dot(input_b, grad_qkv).astype(BF)
     grad_out_proj = t_dot(mixed_b, grad_state_all).astype(BF)
-    grad_qkv, grad_head_gains = attention_backward(qkv, grad_mixed, attn_args)
-    grad_columns = t_dot(input_b, grad_qkv).astype(BF)
-    grad_input = dot_t(grad_qkv, columns).astype(BF)
+    expert_sum = rep_reduce(result_parts, rep_count, grad_mid_moe)
+    output = (hidden_state + expert_sum).astype(BF)
+    grad_input = dot_t(after(grad_qkv, grad_columns), columns).astype(BF)
     grad_input = shard_reduce(
         [grad_input[i * rows_count : (i + 1) * rows_count] for i in range(shard_count)]
     )
@@ -767,8 +996,9 @@
     tokens_grad = (
         grad_state + norm_back(grad_input * gain_attn, normed_in, rms_scale(tokens_f))
     ).astype(BF)
-
-    part = rows // rep_count
+    sums_gate = [owned_part(after(m[0], state_blocks[2])) for m in made]
+    sums_up = [owned_part(after(m[1], state_blocks[2])) for m in made]
+
     piece = HD // shard_count
     head_columns = jnp.pad(
         grad_head_gains[:2].reshape(2, shard_count, piece), ((0, 0), (0, 0), (0, rows - piece))
@@ -783,21 +1013,33 @@
     extra_parts = extras.reshape(shard_count, rep_count, part, -1)
     to_sum = jnp.concatenate([column_parts, extra_parts, out_columns], axis=3)
     to_sum = [lax.dynamic_index_in_dim(to_sum, r, axis=1, keepdims=False) for r in order]
-    part_sum = rep_reduce(to_sum, rep_count).astype(BF)
+    half = shard_count // 2
+    halves = [
+        RepReduce([a[h : h + half] for a in to_sum], rep_count) for h in (0, half)
+    ]
+    sums_down = []
+    part_sum = [None, None]
+    while None in part_sum:
+        if len(sums_down) < local_experts:
+            sums_down.append(owned_part(down_grads(len(sums_down), halves[0].arrived[0])))
+        part_sum = [h.step() for h in halves]
+    part_sum = jnp.concatenate(part_sum, axis=0).astype(BF)
+    while len(sums_down) < local_experts:
+        sums_down.append(owned_part(down_grads(len(sums_down), part_sum)))
+    grad_gate = jnp.stack(sums_gate).astype(F32)
+    grad_up = jnp.stack(sums_up).astype(F32)
+    grad_down = jnp.stack(sums_down).astype(F32)
     split = grad_columns.shape[1] + HD
     mine = lax.all_to_all(part_sum[:, :, :split], "shard", split_axis=0, concat_axis=0, tiled=True)
     wide = jnp.swapaxes(mine[:, :, : split - HD], 0, 1).reshape(part, -1)
     extra = jnp.sum(mine[:, :, split - HD :].astype(F32), axis=0).astype(BF)
     out_part = jnp.swapaxes(part_sum[:, :, split:], 0, 1).reshape(part, -1)
     gathered = rep_gather(jnp.concatenate([wide, out_part, extra], axis=1), rep_count)
+    gain_rows = norm_attn.astype(F32)[:, None]
+    most = rep_count - 3
+    held = write_sums(order_array[:most], w_query, w_key, w_value, gain_rows, gathered[:most])
     sum_query, sum_key, sum_value, sum_out, extra = write_sums(
-        order_array,
-        w_query,
-        w_key,
-        w_value,
-        norm_attn.astype(F32)[:, None],
-        gathered,
-        shard_count,
+        order_array[most:], w_query, w_key, w_value, gain_rows, gathered[most:], held
     )
     return (
         output,

time: 1160 us -> 962 us (0.83)
  waiting for transfers between devices: 500 us -> 361 us
  blocking collectives: 74.9 us -> 0 us
  Pallas kernels: 276 us -> 311 us
  local copies, waits for them, and re-layouts: 113 us -> 83.6 us
  starting transfers between devices: 41.8 us -> 66.2 us
  matrix products: 47.8 us -> 30.3 us
    ppermute x5 -> x6, waiting for transfers between devices: 101 us -> 11.6 us  [swap_x(): return lax.ppermute(value, 'shard', [(i, i ^ 2) for i in range(4)])]
    ppermute x20 -> x32, waiting for transfers between devices: 213 us -> 137 us  [swap_y(): return lax.ppermute(value, 'rep', [(i, i ^ 1) for i in range(count)])]
    all_to_all x1 -> x0, blocking collectives: 74.9 us -> none  [on_device(): lax.all_to_all(packed, 'shard', split_axis=0, concat_axis=0, tiled=True)]
    unnamed x255 -> x269, local copies, waits for them, and re-layouts: 82.5 us -> 49.8 us
    ppermute x15 -> x24, waiting for transfers between devices: 167 us -> 195 us  [turn_z(): return lax.ppermute(value, 'rep', ring_next(count))]
    pallas_call x5 -> x8, Pallas kernels: 39 us -> 59.3 us  [the longest x1 18.2 us: project(): pl.pallas_call(functools.partial(project_body, len(fars)), grid_spec=pltp...]
    pallas_call x8, Pallas kernels: 29.3 us -> 43.2 us  [pick(): pl.pallas_call(functools.partial(pick_rows, held is not None), grid_spec=...]
    dot_general x3 -> x2, matrix products: 16.3 us -> 3.97 us  [dot(): return jnp.dot(left, right, preferred_element_type=F32)]
  transfers between devices with their start and end apart: 62 -> 85, of which waited for: 26 -> 36; matrix products, arithmetic and copies ran while one was open for 14% -> 14% of each run, Pallas kernels for 17% -> 33%
where the time goes in v3:
time: 962 us; the launch traced here: 954 us
  waiting for transfers between devices  361 us (38%)
  Pallas kernels  311 us (32%)
  other arithmetic  87.1 us (9%)
  local copies, waits for them, and re-layouts  83.6 us (9%)
  starting transfers between devices  66.2 us (7%)
  matrix products  30.3 us (3%)
  between operations  15.7 us (2%)
    ppermute x24, waiting for transfers between devices, turn_z(): return lax.ppermute(value, 'rep', ring_next(count))  195 us
    ppermute x32, waiting for transfers between devices, swap_y(): return lax.ppermute(value, 'rep', [(i, i ^ 1) for i in range(count)])  137 us
    pallas_call x4, Pallas kernels, expert(): pl.pallas_call(functools.partial(expert_body, rows // 2), grid=(2,), in_s...  100 us
    pallas_call x4, Pallas kernels, weight_grads(): pl.pallas_call(functools.partial(weight_grads_body, groups, count), grid=...  55.3 us
    unnamed x269, local copies, waits for them, and re-layouts  49.8 us
    pallas_call x8, Pallas kernels, pick(): pl.pallas_call(functools.partial(pick_rows, held is not None), grid_spec=...  43.2 us
    pallas_call x1, Pallas kernels, attention_backward(): pl.pallas_call(attend_backward, grid=(heads,), in_specs=[wide, pl.BlockSp...  32.6 us
    ppermute x32, starting transfers between devices, swap_y(): return lax.ppermute(value, 'rep', [(i, i ^ 1) for i in range(count)])  31.7 us
  transfers between devices with their start and end apart: 85, of which 36 were waited for; matrix products, arithmetic and copies ran while one was open for 14% of the time, Pallas kernels for 33%

profile of v3, /device:TPU:0, one launch (start us, length us, event | category | flops | bytes accessed | tf_op | source)
XLA Modules:
  0.0 954.5 jit_solution(14538478954806258063)
XLA Ops:
  20.1 15.6 %collective-permute-done.16.grad_ref.refs_6_ = bf16[256,2048]{1,0:T(8,128)(2,1)S(1)} collective-permute-done((bf16[256,2048]{1,0:T(8,128)(2,1)}, bf16[256,2048]{1,0:T(8,128)(2,1)S(1)}, u32[]{:S(2)}, u32[]{:S(2)}) %collective-permute-start.16) | collective-permute-done | bytes 1048608 | tf_op jit(solution)/shard_map/ppermute | solution.py:610
  35.7 9.1 collective-permute-done.3
  55.5 11.7 %collective-permute-done.5.refs_6_ = bf16[2,80,1536]{2,1,0:T(8,128)(2,1)} collective-permute-done((bf16[2,80,1536]{2,1,0:T(8,128)(2,1)}, bf16[2,80,1536]{2,1,0:T(8,128)(2,1)}, u32[]{:S(2)}, u32[]{:S(2)}) %collective-permute-start.5) | collective-permute-done | bytes 491552 | tf_op jit(solution)/shard_map/ppermute | solution.py:610
  104.8 8.0 collective-permute-done.15.refs_11_
  114.9 18.2 %shard_map.265 = (bf16[1024,2048]{1,0:T(8,128)(2,1)}, bf16[2048,1536]{1,0:T(8,128)(2,1)}, f32[1024,1536]{1,0:T(8,128)}) custom-call(s32[8]{0:T(128)} %stack.173.order_ref, s32[4]{0:T(128)} %pad_add_fusion.1.shard_ref, f32[1,2048]{1,0:T(1,128)} %bitcast.254, bf16[4,512,1536]{2,1,0:T(8,128)(2,1)} %copy-done.9, ...), custom_call_target="tpu_custom_call" | custom-call | flops 6442450944 | bytes 27262976 | tf_op jit(solution)/shard_map/pallas_call | solution.py:148
  135.9 18.5 %shard_map.266 = bf16[1024,512]{1,0:T(8,128)(2,1)S(1)} custom-call(f32[1024,1536]{1,0:T(8,128)S(1)} %copy-done.71, f32[1024,128]{1,0:T(8,128)S(1)} %copy-done.42, f32[1024,128]{1,0:T(8,128)S(1)} %copy-done.38, f32[1,128]{1,0:T(1,128)S(1)} %reshape_squeeze.6.gq_ref, f32[1,128]{1,0:T(1,128)S(1)} %reshape_squeeze.7.gk_ref, s32[1024,1]{1,0:T(8,128)S(1)} %copy-done.40, ...), custom_call_target="tpu_custom_call" | custom-call | flops 8589934592 | bytes 7864320 | tf_op jit(solution)/shard_map/pallas_call | solution.py:268
  162.9 21.6 %collective-permute-done.23.grad_ref.refs_6_ = bf16[256,2048]{1,0:T(8,128)(2,1)} collective-permute-done((bf16[256,2048]{1,0:T(8,128)(2,1)S(1)}, bf16[256,2048]{1,0:T(8,128)(2,1)}, u32[]{:S(2)}, u32[]{:S(2)}) %collective-permute-start.23) | collective-permute-done | bytes 1048608 | tf_op jit(solution)/shard_map/ppermute | solution.py:610
  207.6 5.5 shard_map.267
  213.1 17.4 %collective-permute-done.25.x_ref = bf16[256,2048]{1,0:T(8,128)(2,1)} collective-permute-done((bf16[256,2048]{1,0:T(8,128)(2,1)}, bf16[256,2048]{1,0:T(8,128)(2,1)}, u32[]{:S(2)}, u32[]{:S(2)}) %collective-permute-start.25) | collective-permute-done | bytes 1048608 | tf_op jit(solution)/shard_map/ppermute | solution.py:610
  231.9 5.5 shard_map.268
  237.3 5.4 shard_map.269
  242.7 13.4 %collective-permute-done.27.x_ref = bf16[256,2048]{1,0:T(8,128)(2,1)S(1)} collective-permute-done((bf16[256,2048]{1,0:T(8,128)(2,1)}, bf16[256,2048]{1,0:T(8,128)(2,1)S(1)}, u32[]{:S(2)}, u32[]{:S(2)}) %collective-permute-start.27) | collective-permute-done | bytes 1048608 | tf_op jit(solution)/shard_map/ppermute | solution.py:610
  258.2 5.4 shard_map.270
  263.6 18.3 %collective-permute-done.29.x_ref = bf16[256,2048]{1,0:T(8,128)(2,1)S(1)} collective-permute-done((bf16[256,2048]{1,0:T(8,128)(2,1)}, bf16[256,2048]{1,0:T(8,128)(2,1)S(1)}, u32[]{:S(2)}, u32[]{:S(2)}) %collective-permute-start.29) | collective-permute-done | bytes 1048608 | tf_op jit(solution)/shard_map/ppermute | solution.py:610
  283.5 5.4 shard_map.271
  288.9 5.4 shard_map.275
  294.3 5.4 shard_map.276
  299.7 5.2 collective-permute-done.31.x_ref
  306.6 25.1 %shard_map.272 = (bf16[576,2048]{1,0:T(8,128)(2,1)}, bf16[576,2048]{1,0:T(8,128)(2,1)}, bf16[576,1024]{1,0:T(8,128)(2,1)}, bf16[576,1024]{1,0:T(8,128)(2,1)}, bf16[576,1024]{1,0:T(8,128)(2,1)}) custom-call(bf16[2,576,2048]{2,1,0:T(8,128)(2,1)} %bitcast.230, bf16[2,576,2048]{2,1,0:T(8,128)(2,1)} %bitcast.234, ...), custom_call_target="tpu_custom_call" | custom-call | flops 14495514624 | bytes 25559040 | tf_op jit(solution)/shard_map/pallas_call | solution.py:505
  331.7 25.0 %shard_map.273 = (bf16[576,2048]{1,0:T(8,128)(2,1)}, bf16[576,2048]{1,0:T(8,128)(2,1)}, bf16[576,1024]{1,0:T(8,128)(2,1)}, bf16[576,1024]{1,0:T(8,128)(2,1)}, bf16[576,1024]{1,0:T(8,128)(2,1)}) custom-call(bf16[2,576,2048]{2,1,0:T(8,128)(2,1)} %bitcast.231, bf16[2,576,2048]{2,1,0:T(8,128)(2,1)} %bitcast.235, ...), custom_call_target="tpu_custom_call" | custom-call | flops 14495514624 | bytes 25559040 | tf_op jit(solution)/shard_map/pallas_call | solution.py:505
  358.4 4.7 shard_map.274
  367.2 5.4 shard_map.277
  372.6 25.3 %shard_map.278 = (bf16[576,2048]{1,0:T(8,128)(2,1)}, bf16[576,2048]{1,0:T(8,128)(2,1)}, bf16[576,1024]{1,0:T(8,128)(2,1)}, bf16[576,1024]{1,0:T(8,128)(2,1)}, bf16[576,1024]{1,0:T(8,128)(2,1)}) custom-call(bf16[2,576,2048]{2,1,0:T(8,128)(2,1)} %bitcast.222, bf16[2,576,2048]{2,1,0:T(8,128)(2,1)} %bitcast.226, ...), custom_call_target="tpu_custom_call" | custom-call | flops 14495514624 | bytes 25559040 | tf_op jit(solution)/shard_map/pallas_call | solution.py:505
  397.9 10.3 %collective-permute-done.34 = bf16[256,2048]{1,0:T(8,128)(2,1)S(1)} collective-permute-done((bf16[256,2048]{1,0:T(8,128)(2,1)}, bf16[256,2048]{1,0:T(8,128)(2,1)S(1)}, u32[]{:S(2)}, u32[]{:S(2)}) %collective-permute-start.34) | collective-permute-done | bytes 1048608 | tf_op jit(solution)/shard_map/ppermute | solution.py:606
  411.8 25.0 %shard_map.279 = (bf16[576,2048]{1,0:T(8,128)(2,1)}, bf16[576,2048]{1,0:T(8,128)(2,1)}, bf16[576,1024]{1,0:T(8,128)(2,1)}, bf16[576,1024]{1,0:T(8,128)(2,1)}, bf16[576,1024]{1,0:T(8,128)(2,1)}) custom-call(bf16[2,576,2048]{2,1,0:T(8,128)(2,1)} %bitcast.223, bf16[2,576,2048]{2,1,0:T(8,128)(2,1)} %bitcast.227, ...), custom_call_target="tpu_custom_call" | custom-call | flops 14495514624 | bytes 25559040 | tf_op jit(solution)/shard_map/pallas_call | solution.py:505
  438.5 4.4 shard_map.280
  452.7 7.1 shard_map.281
  461.7 8.6 shard_map.282
  470.4 3.4 add_convert_fusion.6
  475.8 16.6 %shard_map.283 = (bf16[2048,1024]{1,0:T(8,128)(2,1)}, bf16[2048,1024]{1,0:T(8,128)(2,1)}) custom-call(bf16[2,576,2048]{2,1,0:T(8,128)(2,1)} %bitcast.232, bf16[2,576,2048]{2,1,0:T(8,128)(2,1)} %bitcast.224, bf16[576,1024]{1,0:T(8,128)(2,1)S(1)} %copy-done.78, bf16[576,1024]{1,0:T(8,128)(2,1)S(1)} %copy-done.80, bf16[576,1024]{1,0:T(8,128)(2,1)S(1)} %copy-done.79, ...), custom_call_target="tpu_custom_call" | custom-call | flops 9663676416 | bytes 17825792 | tf_op jit(solution)/shard_map/pallas_call | solution.py:555
  506.9 6.2 all-to-all-start
  513.1 8.6 all-to-all-done
  528.5 16.5 %shard_map.284 = (bf16[2048,1024]{1,0:T(8,128)(2,1)}, bf16[2048,1024]{1,0:T(8,128)(2,1)}) custom-call(bf16[2,576,2048]{2,1,0:T(8,128)(2,1)} %bitcast.233, bf16[2,576,2048]{2,1,0:T(8,128)(2,1)} %bitcast.225, bf16[576,1024]{1,0:T(8,128)(2,1)S(1)} %copy-done.74, bf16[576,1024]{1,0:T(8,128)(2,1)S(1)} %copy-done.76, bf16[576,1024]{1,0:T(8,128)(2,1)S(1)} %copy-done.75, ...), custom_call_target="tpu_custom_call" | custom-call | flops 9663676416 | bytes 17825792 | tf_op jit(solution)/shard_map/pallas_call | solution.py:555
  563.3 32.6 %shard_map.285 = (bf16[1024,1536]{1,0:T(8,128)(2,1)S(1)}, f32[8,128]{1,0:T(8,128)S(1)}) custom-call(f32[1024,1536]{1,0:T(8,128)} %get-tuple-element.195.qkv_ref, bf16[1024,512]{1,0:T(8,128)(2,1)S(1)} %convolution_convert_fusion.5.do_ref, f32[1024,128]{1,0:T(8,128)S(1)} %copy-done.43, f32[1024,128]{1,0:T(8,128)S(1)} %copy-done.39, f32[1,128]{1,0:T(1,128)S(1)} %copy-done.57, ...), custom_call_target="tpu_custom_call" | custom-call | flops 21474836480 | bytes 4718592 | tf_op jit(solution)/shard_map/pallas_call | solution.py:283
  600.0 10.1 %convolution_convert_fusion = bf16[2048,1536]{1,0:T(8,128)(2,1)S(1)} fusion(bf16[1024,2048]{1,0:T(8,128)(2,1)} %get-tuple-element.311, bf16[1024,1536]{1,0:T(8,128)(2,1)} %copy-done.72), kind=kOutput, calls=%fused_computation.3 | convolution fusion | flops 6445596672 | bytes 13631488 | tf_op jit(solution)/shard_map/dot_general | solution.py:40
  616.8 14.3 %collective-permute-done.53 = bf16[2,64,2176]{2,1,0:T(8,128)(2,1)} collective-permute-done((bf16[2,64,2176]{2,1,0:T(8,128)(2,1)S(1)}, bf16[2,64,2176]{2,1,0:T(8,128)(2,1)}, u32[]{:S(2)}, u32[]{:S(2)}) %collective-permute-start.53) | collective-permute-done | bytes 557088 | tf_op jit(solution)/shard_map/ppermute | solution.py:606
  631.1 11.3 %shard_map.288 = bf16[1024,2048]{1,0:T(8,128)(2,1)} custom-call(bf16[576,1024]{1,0:T(8,128)(2,1)S(1)} %copy-done.67, bf16[576,1024]{1,0:T(8,128)(2,1)S(1)} %copy-done.68, bf16[2,576,2048]{2,1,0:T(8,128)(2,1)} %bitcast.236, bf16[2,576,2048]{2,1,0:T(8,128)(2,1)} %bitcast.228), custom_call_target="tpu_custom_call" | custom-call | flops 4831838208 | bytes 11272192 | tf_op jit(solution)/shard_map/pallas_call | solution.py:555
  643.0 13.8 %collective-permute-done.60 = bf16[2,64,2176]{2,1,0:T(8,128)(2,1)} collective-permute-done((bf16[2,64,2176]{2,1,0:T(8,128)(2,1)}, bf16[2,64,2176]{2,1,0:T(8,128)(2,1)}, u32[]{:S(2)}, u32[]{:S(2)}) %collective-permute-start.60) | collective-permute-done | bytes 557088 | tf_op jit(solution)/shard_map/ppermute | solution.py:606
  661.5 11.2 %collective-permute-done.61 = bf16[2,64,2176]{2,1,0:T(8,128)(2,1)} collective-permute-done((bf16[2,64,2176]{2,1,0:T(8,128)(2,1)}, bf16[2,64,2176]{2,1,0:T(8,128)(2,1)}, u32[]{:S(2)}, u32[]{:S(2)}) %collective-permute-start.61) | collective-permute-done | bytes 557088 | tf_op jit(solution)/shard_map/ppermute | solution.py:606
  679.6 5.1 collective-permute-done.54
  684.6 10.6 %collective-permute-done.55 = bf16[2,64,2176]{2,1,0:T(8,128)(2,1)} collective-permute-done((bf16[2,64,2176]{2,1,0:T(8,128)(2,1)}, bf16[2,64,2176]{2,1,0:T(8,128)(2,1)}, u32[]{:S(2)}, u32[]{:S(2)}) %collective-permute-start.55) | collective-permute-done | bytes 557088 | tf_op jit(solution)/shard_map/ppermute | solution.py:610
  697.0 6.7 collective-permute-done.64
  703.7 3.3 fusion.9
  708.8 10.3 %collective-permute-done.40 = bf16[256,2048]{1,0:T(8,128)(2,1)} collective-permute-done((bf16[256,2048]{1,0:T(8,128)(2,1)}, bf16[256,2048]{1,0:T(8,128)(2,1)}, u32[]{:S(2)}, u32[]{:S(2)}) %collective-permute-start.40) | collective-permute-done | bytes 1048608 | tf_op jit(solution)/shard_map/ppermute | solution.py:606
  721.2 9.8 %collective-permute-done.56 = bf16[2,64,2176]{2,1,0:T(8,128)(2,1)} collective-permute-done((bf16[2,64,2176]{2,1,0:T(8,128)(2,1)}, bf16[2,64,2176]{2,1,0:T(8,128)(2,1)}, u32[]{:S(2)}, u32[]{:S(2)}) %collective-permute-start.56) | collective-permute-done | bytes 557088 | tf_op jit(solution)/shard_map/ppermute | solution.py:606
  731.9 11.0 %collective-permute-done.65 = bf16[2,64,2176]{2,1,0:T(8,128)(2,1)} collective-permute-done((bf16[2,64,2176]{2,1,0:T(8,128)(2,1)}, bf16[2,64,2176]{2,1,0:T(8,128)(2,1)}, u32[]{:S(2)}, u32[]{:S(2)}) %collective-permute-start.65) | collective-permute-done | bytes 557088 | tf_op jit(solution)/shard_map/ppermute | solution.py:606
  745.8 19.4 %collective-permute-done.41 = bf16[256,2048]{1,0:T(8,128)(2,1)S(1)} collective-permute-done((bf16[256,2048]{1,0:T(8,128)(2,1)}, bf16[256,2048]{1,0:T(8,128)(2,1)S(1)}, u32[]{:S(2)}, u32[]{:S(2)}) %collective-permute-start.41) | collective-permute-done | bytes 1048608 | tf_op jit(solution)/shard_map/ppermute | solution.py:606
  765.6 11.6 %collective-permute-done.58 = bf16[2,64,2176]{2,1,0:T(8,128)(2,1)S(1)} collective-permute-done((bf16[2,64,2176]{2,1,0:T(8,128)(2,1)S(1)}, bf16[2,64,2176]{2,1,0:T(8,128)(2,1)S(1)}, u32[]{:S(2)}, u32[]{:S(2)}) %collective-permute-start.58) | collective-permute-done | bytes 557088 | tf_op jit(solution)/shard_map/ppermute | solution.py:606
  780.3 4.2 all-to-all-start.1
  784.6 3.6 add_convert_fusion.3
  788.5 10.9 %shard_map.289 = bf16[1024,2048]{1,0:T(8,128)(2,1)} custom-call(bf16[576,1024]{1,0:T(8,128)(2,1)S(1)} %copy-done.65, bf16[576,1024]{1,0:T(8,128)(2,1)S(1)} %copy-done.66, bf16[2,576,2048]{2,1,0:T(8,128)(2,1)} %bitcast.237, bf16[2,576,2048]{2,1,0:T(8,128)(2,1)} %bitcast.229), custom_call_target="tpu_custom_call" | custom-call | flops 4831838208 | bytes 11272192 | tf_op jit(solution)/shard_map/pallas_call | solution.py:555
  803.6 8.9 convolution_convert_fusion.1
  816.5 21.9 %collective-permute-done.67.refs_2_ = bf16[64,8320]{1,0:T(8,128)(2,1)S(1)} collective-permute-done((bf16[64,8320]{1,0:T(8,128)(2,1)S(1)}, bf16[64,8320]{1,0:T(8,128)(2,1)S(1)}, u32[]{:S(2)}, u32[]{:S(2)}) %collective-permute-start.67) | collective-permute-done | bytes 1064992 | tf_op jit(solution)/shard_map/ppermute | solution.py:610
  838.5 3.8 add_convert_fusion.2
  844.0 22.8 %collective-permute-done.69.refs_4_ = bf16[64,8320]{1,0:T(8,128)(2,1)} collective-permute-done((bf16[64,8320]{1,0:T(8,128)(2,1)S(1)}, bf16[64,8320]{1,0:T(8,128)(2,1)}, u32[]{:S(2)}, u32[]{:S(2)}) %collective-permute-start.69) | collective-permute-done | bytes 1064992 | tf_op jit(solution)/shard_map/ppermute | solution.py:610
  868.5 5.3 collective-permute-done.70.refs_3_
  878.9 10.4 %collective-permute-done.46 = bf16[256,2048]{1,0:T(8,128)(2,1)} collective-permute-done((bf16[256,2048]{1,0:T(8,128)(2,1)}, bf16[256,2048]{1,0:T(8,128)(2,1)}, u32[]{:S(2)}, u32[]{:S(2)}) %collective-permute-start.46) | collective-permute-done | bytes 1048608 | tf_op jit(solution)/shard_map/ppermute | solution.py:610
  892.4 18.3 %collective-permute-done.71.refs_1_ = bf16[64,8320]{1,0:T(8,128)(2,1)} collective-permute-done((bf16[64,8320]{1,0:T(8,128)(2,1)}, bf16[64,8320]{1,0:T(8,128)(2,1)}, u32[]{:S(2)}, u32[]{:S(2)}) %collective-permute-start.71) | collective-permute-done | bytes 1064992 | tf_op jit(solution)/shard_map/ppermute | solution.py:610
  910.9 5.4 fusion.6
  916.3 9.0 shard_map.286
  925.3 3.8 maximum_convert_fusion
  929.2 3.8 maximum_convert_fusion.1
  935.0 6.5 shard_map.287
  943.9 3.8 maximum_convert_fusion.2
  (555 shorter events, 228.1 us)
Async XLA Ops:
  7.2 299.4 %all-gather.4.cloned.1.call-start = ((), (), s32[]{:S(2)}) async-start(), calls=%async_computation.8 | async-start | bytes 10485760 | tf_op jit(solution)/shard_map/all_gather | solution.py:759
  7.2 28.5 %collective-permute-start.16 = (bf16[256,2048]{1,0:T(8,128)(2,1)}, bf16[256,2048]{1,0:T(8,128)(2,1)S(1)}, u32[]{:S(2)}, u32[]{:S(2)}) collective-permute-start(bf16[256,2048]{1,0:T(8,128)(2,1)} %refs_4_.1), channel_id=1, source_target_pairs={{0,8},{4,12},{8,16},{12,20},{16,24},{20,28},{24,0},{28,4},{1,9},{5... | collective-permute-start | bytes 3145736 | tf_op jit(solution)/shard_map/ppermute | solution.py:610
  10.3 25.4 %collective-permute-start.17 = (bf16[256,2048]{1,0:T(8,128)(2,1)}, bf16[256,2048]{1,0:T(8,128)(2,1)}, u32[]{:S(2)}, u32[]{:S(2)}) collective-permute-start(bf16[256,2048]{1,0:T(8,128)(2,1)} %refs_4_.1), channel_id=1, source_target_pairs={{0,4},{4,0},{8,12},{12,8},{16,20},{20,16},{24,28},{28,24},{1,5},{5... | collective-permute-start | bytes 3145736 | tf_op jit(solution)/shard_map/ppermute | solution.py:606
  11.8 33.7 %collective-permute-start.9 = (bf16[256,2048]{1,0:T(8,128)(2,1)}, bf16[256,2048]{1,0:T(8,128)(2,1)}, u32[]{:S(2)}, u32[]{:S(2)}) collective-permute-start(bf16[256,2048]{1,0:T(8,128)(2,1)} %refs_0_.1), channel_id=1, source_target_pairs={{0,2},{1,3},{2,0},{3,1},{4,6},{5,7},{6,4},{7,5},{8,10},{9,11},{10,... | collective-permute-start | bytes 3145736 | tf_op jit(solution)/shard_map/ppermute | solution.py:574
  19.5 25.3 %collective-permute-start.3 = (bf16[2,64,1536]{2,1,0:T(8,128)(2,1)S(1)}, bf16[2,64,1536]{2,1,0:T(8,128)(2,1)S(1)}, u32[]{:S(2)}, u32[]{:S(2)}) collective-permute-start(bf16[2,64,1536]{2,1,0:T(8,128)(2,1)S(1)} %shard_map.263), channel_id=1, source_target_pairs={{0,2},{1,3},{2,0},{3,1},{4,6},{5,7},{6,4},{7,5},{8,10},{9,11},{10,... | collective-permute-start | bytes 1179656 | tf_op jit(solution)/shard_map/ppermute | solution.py:574
  45.6 261.0 %all-gather.6.cloned.1.call-start = ((), (), s32[]{:S(2)}) async-start(), calls=%async_computation.9 | async-start | bytes 10485760 | tf_op jit(solution)/shard_map/all_gather | solution.py:768
  46.3 260.2 %all-gather.8.cloned.1.call-start = ((), (), s32[]{:S(2)}) async-start(), calls=%async_computation.10 | async-start | bytes 10485760 | tf_op jit(solution)/shard_map/all_gather | solution.py:818
  53.9 28.4 %collective-permute-start.1 = (bf16[512,128]{0,1:T(8,128)(2,1)S(1)}, bf16[512,128]{0,1:T(8,128)(2,1)S(1)}, u32[]{:S(2)}, u32[]{:S(2)}) collective-permute-start(bf16[512,128]{0,1:T(8,128)(2,1)S(1)} %get-tuple-element.499), channel_id=1, source_target_pairs={{0,2},{1,3},{2,0},{3,1},{4,6},{5,7},{6,4},{7,5},{8,10},{9,11},{10,... | collective-permute-start | bytes 393224 | tf_op jit(solution)/shard_map/ppermute | solution.py:574
  55.4 28.7 %collective-permute-start = (bf16[512,128]{0,1:T(8,128)(2,1)S(1)}, bf16[512,128]{0,1:T(8,128)(2,1)}, u32[]{:S(2)}, u32[]{:S(2)}) collective-permute-start(bf16[512,128]{0,1:T(8,128)(2,1)S(1)} %get-tuple-element.499), channel_id=1, source_target_pairs={{0,1},{1,0},{2,3},{3,2},{4,5},{5,4},{6,7},{7,6},{8,9},{9,8},{10,11... | collective-permute-start | bytes 393224 | tf_op jit(solution)/shard_map/ppermute | solution.py:570
  79.2 35.6 %collective-permute-start.7 = (bf16[512,1536]{1,0:T(8,128)(2,1)}, bf16[512,1536]{1,0:T(8,128)(2,1)}, u32[]{:S(2)}, u32[]{:S(2)}) collective-permute-start(bf16[512,1536]{1,0:T(8,128)(2,1)} %dynamic-slice_bitcast_fusion), channel_id=1, source_target_pairs={{0,1},{1,0},{2,3},{3,2},{4,5},{5,4},{6,7},{7,6},{8,9},{9,8},{10,11... | collective-permute-start | bytes 4718600 | tf_op jit(solution)/shard_map/ppermute | solution.py:570
  83.0 31.9 %collective-permute-start.8 = (bf16[256,2048]{1,0:T(8,128)(2,1)}, bf16[256,2048]{1,0:T(8,128)(2,1)}, u32[]{:S(2)}, u32[]{:S(2)}) collective-permute-start(bf16[256,2048]{1,0:T(8,128)(2,1)} %refs_0_.1), channel_id=1, source_target_pairs={{0,1},{1,0},{2,3},{3,2},{4,5},{5,4},{6,7},{7,6},{8,9},{9,8},{10,11... | collective-permute-start | bytes 3145736 | tf_op jit(solution)/shard_map/ppermute | solution.py:570
  83.1 31.8 %collective-permute-start.10 = (bf16[256,2048]{1,0:T(8,128)(2,1)}, bf16[256,2048]{1,0:T(8,128)(2,1)}, u32[]{:S(2)}, u32[]{:S(2)}) collective-permute-start(bf16[256,2048]{1,0:T(8,128)(2,1)} %collective-permute-done.9.refs_2_), channel_id=1, source_target_pairs={{0,1},{1,0},{2,3},{3,2},{4,5},{5,4},{6,7},{7,6},{8,9},{9,8},{10,11... | collective-permute-start | bytes 3145736 | tf_op jit(solution)/shard_map/ppermute | solution.py:570
  112.7 41.7 %collective-permute-start.18 = (bf16[256,2048]{1,0:T(8,128)(2,1)S(1)}, bf16[256,2048]{1,0:T(8,128)(2,1)S(1)}, u32[]{:S(2)}, u32[]{:S(2)}) collective-permute-start(bf16[256,2048]{1,0:T(8,128)(2,1)S(1)} %collective-permute-done.16.grad_ref.refs_6_), channel_id=1, source_target_pairs={{0,8},{4,12},{8,16},{12,20},{16,24},{20,28},{24,0},{28,4},{1,9},{5... | collective-permute-start | bytes 3145736 | tf_op jit(solution)/shard_map/ppermute | solution.py:610
  114.4 40.1 %collective-permute-start.19 = (bf16[256,2048]{1,0:T(8,128)(2,1)S(1)}, bf16[256,2048]{1,0:T(8,128)(2,1)S(1)}, u32[]{:S(2)}, u32[]{:S(2)}) collective-permute-start(bf16[256,2048]{1,0:T(8,128)(2,1)S(1)} %collective-permute-done.16.grad_ref.refs_6_), channel_id=1, source_target_pairs={{0,4},{4,0},{8,12},{12,8},{16,20},{20,16},{24,28},{28,24},{1,5},{5... | collective-permute-start | bytes 3145736 | tf_op jit(solution)/shard_map/ppermute | solution.py:606
  157.1 27.5 %collective-permute-start.23 = (bf16[256,2048]{1,0:T(8,128)(2,1)S(1)}, bf16[256,2048]{1,0:T(8,128)(2,1)}, u32[]{:S(2)}, u32[]{:S(2)}) collective-permute-start(bf16[256,2048]{1,0:T(8,128)(2,1)S(1)} %collective-permute-done.18.grad_ref.refs_4_), channel_id=1, source_target_pairs={{0,8},{4,12},{8,16},{12,20},{16,24},{20,28},{24,0},{28,4},{1,9},{5... | collective-permute-start | bytes 3145736 | tf_op jit(solution)/shard_map/ppermute | solution.py:610
  159.2 25.3 %collective-permute-start.24 = (bf16[256,2048]{1,0:T(8,128)(2,1)S(1)}, bf16[256,2048]{1,0:T(8,128)(2,1)}, u32[]{:S(2)}, u32[]{:S(2)}) collective-permute-start(bf16[256,2048]{1,0:T(8,128)(2,1)S(1)} %collective-permute-done.18.grad_ref.refs_4_), channel_id=1, source_target_pairs={{0,4},{4,0},{8,12},{12,8},{16,20},{20,16},{24,28},{28,24},{1,5},{5... | collective-permute-start | bytes 3145736 | tf_op jit(solution)/shard_map/ppermute | solution.py:606
  160.9 23.6 %collective-permute-start.20 = (bf16[256,2048]{1,0:T(8,128)(2,1)S(1)}, bf16[256,2048]{1,0:T(8,128)(2,1)S(1)}, u32[]{:S(2)}, u32[]{:S(2)}) collective-permute-start(bf16[256,2048]{1,0:T(8,128)(2,1)S(1)} %get-tuple-element.491), channel_id=1, source_target_pairs={{0,1},{1,0},{2,3},{3,2},{4,5},{5,4},{6,7},{7,6},{8,9},{9,8},{10,11... | collective-permute-start | bytes 3145736 | tf_op jit(solution)/shard_map/ppermute | solution.py:570
  161.3 25.6 %collective-permute-start.22 = (bf16[256,2048]{1,0:T(8,128)(2,1)S(1)}, bf16[256,2048]{1,0:T(8,128)(2,1)S(1)}, u32[]{:S(2)}, u32[]{:S(2)}) collective-permute-start(bf16[256,2048]{1,0:T(8,128)(2,1)S(1)} %add_convert_fusion.8), channel_id=1, source_target_pairs={{0,2},{1,3},{2,0},{3,1},{4,6},{5,7},{6,4},{7,5},{8,10},{9,11},{10,... | collective-permute-start | bytes 3145736 | tf_op jit(solution)/shard_map/ppermute | solution.py:574
  203.3 27.2 %collective-permute-start.25 = (bf16[256,2048]{1,0:T(8,128)(2,1)}, bf16[256,2048]{1,0:T(8,128)(2,1)}, u32[]{:S(2)}, u32[]{:S(2)}) collective-permute-start(bf16[256,2048]{1,0:T(8,128)(2,1)} %multiply_convert_fusion.x_ref), channel_id=1, source_target_pairs={{0,8},{4,12},{8,16},{12,20},{16,24},{20,28},{24,0},{28,4},{1,9},{5... | collective-permute-start | bytes 3145736 | tf_op jit(solution)/shard_map/ppermute | solution.py:610
  204.3 26.2 %collective-permute-start.26 = (bf16[256,2048]{1,0:T(8,128)(2,1)}, bf16[256,2048]{1,0:T(8,128)(2,1)}, u32[]{:S(2)}, u32[]{:S(2)}) collective-permute-start(bf16[256,2048]{1,0:T(8,128)(2,1)} %multiply_convert_fusion.x_ref), channel_id=1, source_target_pairs={{0,4},{4,0},{8,12},{12,8},{16,20},{20,16},{24,28},{28,24},{1,5},{5... | collective-permute-start | bytes 3145736 | tf_op jit(solution)/shard_map/ppermute | solution.py:606
  230.5 25.7 %collective-permute-start.27 = (bf16[256,2048]{1,0:T(8,128)(2,1)}, bf16[256,2048]{1,0:T(8,128)(2,1)S(1)}, u32[]{:S(2)}, u32[]{:S(2)}) collective-permute-start(bf16[256,2048]{1,0:T(8,128)(2,1)} %collective-permute-done.25.x_ref), channel_id=1, source_target_pairs={{0,8},{4,12},{8,16},{12,20},{16,24},{20,28},{24,0},{28,4},{1,9},{5... | collective-permute-start | bytes 3145736 | tf_op jit(solution)/shard_map/ppermute | solution.py:610
  230.5 25.7 %collective-permute-start.28 = (bf16[256,2048]{1,0:T(8,128)(2,1)}, bf16[256,2048]{1,0:T(8,128)(2,1)S(1)}, u32[]{:S(2)}, u32[]{:S(2)}) collective-permute-start(bf16[256,2048]{1,0:T(8,128)(2,1)} %collective-permute-done.25.x_ref), channel_id=1, source_target_pairs={{0,4},{4,0},{8,12},{12,8},{16,20},{20,16},{24,28},{28,24},{1,5},{5... | collective-permute-start | bytes 3145736 | tf_op jit(solution)/shard_map/ppermute | solution.py:606
  257.1 24.8 %collective-permute-start.29 = (bf16[256,2048]{1,0:T(8,128)(2,1)}, bf16[256,2048]{1,0:T(8,128)(2,1)S(1)}, u32[]{:S(2)}, u32[]{:S(2)}) collective-permute-start(bf16[256,2048]{1,0:T(8,128)(2,1)} %copy-done.106), channel_id=1, source_target_pairs={{0,8},{4,12},{8,16},{12,20},{16,24},{20,28},{24,0},{28,4},{1,9},{5... | collective-permute-start | bytes 3145736 | tf_op jit(solution)/shard_map/ppermute | solution.py:610
  257.1 24.8 %collective-permute-start.30 = (bf16[256,2048]{1,0:T(8,128)(2,1)}, bf16[256,2048]{1,0:T(8,128)(2,1)}, u32[]{:S(2)}, u32[]{:S(2)}) collective-permute-start(bf16[256,2048]{1,0:T(8,128)(2,1)} %copy-done.106), channel_id=1, source_target_pairs={{0,4},{4,0},{8,12},{12,8},{16,20},{20,16},{24,28},{28,24},{1,5},{5... | collective-permute-start | bytes 3145736 | tf_op jit(solution)/shard_map/ppermute | solution.py:606
  281.9 22.9 %collective-permute-start.31 = (bf16[256,2048]{1,0:T(8,128)(2,1)S(1)}, bf16[256,2048]{1,0:T(8,128)(2,1)}, u32[]{:S(2)}, u32[]{:S(2)}) collective-permute-start(bf16[256,2048]{1,0:T(8,128)(2,1)S(1)} %collective-permute-done.29.x_ref), channel_id=1, source_target_pairs={{0,4},{4,0},{8,12},{12,8},{16,20},{20,16},{24,28},{28,24},{1,5},{5... | collective-permute-start | bytes 3145736 | tf_op jit(solution)/shard_map/ppermute | solution.py:606
  304.8 62.3 %collective-permute-start.32 = (bf16[256,2048]{1,0:T(8,128)(2,1)}, bf16[256,2048]{1,0:T(8,128)(2,1)}, u32[]{:S(2)}, u32[]{:S(2)}) collective-permute-start(bf16[256,2048]{1,0:T(8,128)(2,1)} %collective-permute-done.23.grad_ref.refs_6_), channel_id=1, source_target_pairs={{0,4},{4,0},{8,12},{12,8},{16,20},{20,16},{24,28},{28,24},{1,5},{5... | collective-permute-start | bytes 3145736 | tf_op jit(solution)/shard_map/ppermute | solution.py:606
  365.1 32.7 %collective-permute-start.33 = (bf16[256,2048]{1,0:T(8,128)(2,1)}, bf16[256,2048]{1,0:T(8,128)(2,1)}, u32[]{:S(2)}, u32[]{:S(2)}) collective-permute-start(bf16[256,2048]{1,0:T(8,128)(2,1)} %get-tuple-element.229), channel_id=1, source_target_pairs={{0,4},{4,0},{8,12},{12,8},{16,20},{20,16},{24,28},{28,24},{1,5},{5... | collective-permute-start | bytes 3145736 | tf_op jit(solution)/shard_map/ppermute | solution.py:606
  365.4 42.8 %collective-permute-start.34 = (bf16[256,2048]{1,0:T(8,128)(2,1)}, bf16[256,2048]{1,0:T(8,128)(2,1)S(1)}, u32[]{:S(2)}, u32[]{:S(2)}) collective-permute-start(bf16[256,2048]{1,0:T(8,128)(2,1)} %get-tuple-element.243), channel_id=1, source_target_pairs={{0,4},{4,0},{8,12},{12,8},{16,20},{20,16},{24,28},{28,24},{1,5},{5... | collective-permute-start | bytes 3145736 | tf_op jit(solution)/shard_map/ppermute | solution.py:606
  411.8 58.5 %collective-permute-start.36 = (bf16[256,2048]{1,0:T(8,128)(2,1)}, bf16[256,2048]{1,0:T(8,128)(2,1)}, u32[]{:S(2)}, u32[]{:S(2)}) collective-permute-start(bf16[256,2048]{1,0:T(8,128)(2,1)} %add_convert_fusion.7), channel_id=1, source_target_pairs={{0,8},{4,12},{8,16},{12,20},{16,24},{20,28},{24,0},{28,4},{1,9},{5... | collective-permute-start | bytes 3145736 | tf_op jit(solution)/shard_map/ppermute | solution.py:610
  445.9 24.4 %collective-permute-start.35 = (bf16[256,2048]{1,0:T(8,128)(2,1)}, bf16[256,2048]{1,0:T(8,128)(2,1)}, u32[]{:S(2)}, u32[]{:S(2)}) collective-permute-start(bf16[256,2048]{1,0:T(8,128)(2,1)} %get-tuple-element.269), channel_id=1, source_target_pairs={{0,4},{4,0},{8,12},{12,8},{16,20},{20,16},{24,28},{28,24},{1,5},{5... | collective-permute-start | bytes 3145736 | tf_op jit(solution)/shard_map/ppermute | solution.py:606
  473.9 21.1 %collective-permute-start.37 = (bf16[256,2048]{1,0:T(8,128)(2,1)S(1)}, bf16[256,2048]{1,0:T(8,128)(2,1)S(1)}, u32[]{:S(2)}, u32[]{:S(2)}) collective-permute-start(bf16[256,2048]{1,0:T(8,128)(2,1)S(1)} %add_convert_fusion.6), channel_id=1, source_target_pairs={{0,8},{4,12},{8,16},{12,20},{16,24},{20,28},{24,0},{28,4},{1,9},{5... | collective-permute-start | bytes 3145736 | tf_op jit(solution)/shard_map/ppermute | solution.py:610
  473.9 21.0 %collective-permute-start.38 = (bf16[256,2048]{1,0:T(8,128)(2,1)S(1)}, bf16[256,2048]{1,0:T(8,128)(2,1)S(1)}, u32[]{:S(2)}, u32[]{:S(2)}) collective-permute-start(bf16[256,2048]{1,0:T(8,128)(2,1)S(1)} %copy-done.64), channel_id=1, source_target_pairs={{0,4},{4,0},{8,12},{12,8},{16,20},{20,16},{24,28},{28,24},{1,5},{5... | collective-permute-start | bytes 3145736 | tf_op jit(solution)/shard_map/ppermute | solution.py:606
  500.0 21.8 %collective-permute-start.39 = (bf16[256,2048]{1,0:T(8,128)(2,1)}, bf16[256,2048]{1,0:T(8,128)(2,1)}, u32[]{:S(2)}, u32[]{:S(2)}) collective-permute-start(bf16[256,2048]{1,0:T(8,128)(2,1)} %add_convert_fusion.5), channel_id=1, source_target_pairs={{0,8},{4,12},{8,16},{12,20},{16,24},{20,28},{24,0},{28,4},{1,9},{5... | collective-permute-start | bytes 3145736 | tf_op jit(solution)/shard_map/ppermute | solution.py:610
  513.1 412.2 %reduce-scatter.9.cloned.1.call-start = ((), (), s32[]{:S(2)}) async-start(), calls=%async_computation.12 | async-start | bytes 5242880 | tf_op jit(solution)/shard_map/reduce_scatter | solution.py:926
  546.0 379.4 %reduce-scatter.7.cloned.1.call-start = ((), (), s32[]{:S(2)}) async-start(), calls=%async_computation.11 | async-start | bytes 5242880 | tf_op jit(solution)/shard_map/reduce_scatter | solution.py:926
  546.5 382.6 %reduce-scatter.13.cloned.1.call-start = ((), (), s32[]{:S(2)}) async-start(), calls=%async_computation.14 | async-start | bytes 5242880 | tf_op jit(solution)/shard_map/reduce_scatter | solution.py:926
  547.1 382.0 %reduce-scatter.11.cloned.1.call-start = ((), (), s32[]{:S(2)}) async-start(), calls=%async_computation.13 | async-start | bytes 5242880 | tf_op jit(solution)/shard_map/reduce_scatter | solution.py:926
  547.9 396.1 %reduce-scatter.15.cloned.1.call-start = ((), (), s32[]{:S(2)}) async-start(), calls=%async_computation.15 | async-start | bytes 5242880 | tf_op jit(solution)/shard_map/reduce_scatter | solution.py:926
  660.1 24.5 %collective-permute-start.54 = (bf16[2,64,2176]{2,1,0:T(8,128)(2,1)}, bf16[2,64,2176]{2,1,0:T(8,128)(2,1)}, u32[]{:S(2)}, u32[]{:S(2)}) collective-permute-start(bf16[2,64,2176]{2,1,0:T(8,128)(2,1)} %get-tuple-element.315), channel_id=1, source_target_pairs={{0,4},{4,0},{8,12},{12,8},{16,20},{20,16},{24,28},{28,24},{1,5},{5... | collective-permute-start | bytes 1671176 | tf_op jit(solution)/shard_map/ppermute | solution.py:606
  679.3 24.4 %collective-permute-start.64 = (bf16[2,64,2176]{2,1,0:T(8,128)(2,1)}, bf16[2,64,2176]{2,1,0:T(8,128)(2,1)}, u32[]{:S(2)}, u32[]{:S(2)}) collective-permute-start(bf16[2,64,2176]{2,1,0:T(8,128)(2,1)} %get-tuple-element.479), channel_id=1, source_target_pairs={{0,8},{4,12},{8,16},{12,20},{16,24},{20,28},{24,0},{28,4},{1,9},{5... | collective-permute-start | bytes 1671176 | tf_op jit(solution)/shard_map/ppermute | solution.py:610
  679.3 39.7 %collective-permute-start.40 = (bf16[256,2048]{1,0:T(8,128)(2,1)}, bf16[256,2048]{1,0:T(8,128)(2,1)}, u32[]{:S(2)}, u32[]{:S(2)}) collective-permute-start(bf16[256,2048]{1,0:T(8,128)(2,1)} %get-tuple-element.291), channel_id=1, source_target_pairs={{0,4},{4,0},{8,12},{12,8},{16,20},{20,16},{24,28},{28,24},{1,5},{5... | collective-permute-start | bytes 3145736 | tf_op jit(solution)/shard_map/ppermute | solution.py:606
  695.2 35.8 %collective-permute-start.56 = (bf16[2,64,2176]{2,1,0:T(8,128)(2,1)}, bf16[2,64,2176]{2,1,0:T(8,128)(2,1)}, u32[]{:S(2)}, u32[]{:S(2)}) collective-permute-start(bf16[2,64,2176]{2,1,0:T(8,128)(2,1)} %get-tuple-element.317), channel_id=1, source_target_pairs={{0,4},{4,0},{8,12},{12,8},{16,20},{20,16},{24,28},{28,24},{1,5},{5... | collective-permute-start | bytes 1671176 | tf_op jit(solution)/shard_map/ppermute | solution.py:606
  707.0 24.4 %collective-permute-start.57 = (bf16[2,64,2176]{2,1,0:T(8,128)(2,1)}, bf16[2,64,2176]{2,1,0:T(8,128)(2,1)}, u32[]{:S(2)}, u32[]{:S(2)}) collective-permute-start(bf16[2,64,2176]{2,1,0:T(8,128)(2,1)} %get-tuple-element.478), channel_id=1, source_target_pairs={{0,8},{4,12},{8,16},{12,20},{16,24},{20,28},{24,0},{28,4},{1,9},{5... | collective-permute-start | bytes 1671176 | tf_op jit(solution)/shard_map/ppermute | solution.py:610
  707.0 35.9 %collective-permute-start.65 = (bf16[2,64,2176]{2,1,0:T(8,128)(2,1)}, bf16[2,64,2176]{2,1,0:T(8,128)(2,1)}, u32[]{:S(2)}, u32[]{:S(2)}) collective-permute-start(bf16[2,64,2176]{2,1,0:T(8,128)(2,1)} %get-tuple-element.329), channel_id=1, source_target_pairs={{0,4},{4,0},{8,12},{12,8},{16,20},{20,16},{24,28},{28,24},{1,5},{5... | collective-permute-start | bytes 1671176 | tf_op jit(solution)/shard_map/ppermute | solution.py:606
  708.7 34.2 %collective-permute-start.66 = (bf16[2,64,2176]{2,1,0:T(8,128)(2,1)}, bf16[2,64,2176]{2,1,0:T(8,128)(2,1)}, u32[]{:S(2)}, u32[]{:S(2)}) collective-permute-start(bf16[2,64,2176]{2,1,0:T(8,128)(2,1)} %get-tuple-element.477), channel_id=1, source_target_pairs={{0,8},{4,12},{8,16},{12,20},{16,24},{20,28},{24,0},{28,4},{1,9},{5... | collective-permute-start | bytes 1671176 | tf_op jit(solution)/shard_map/ppermute | solution.py:610
  719.0 46.2 %collective-permute-start.41 = (bf16[256,2048]{1,0:T(8,128)(2,1)}, bf16[256,2048]{1,0:T(8,128)(2,1)S(1)}, u32[]{:S(2)}, u32[]{:S(2)}) collective-permute-start(bf16[256,2048]{1,0:T(8,128)(2,1)} %copy-done.62), channel_id=1, source_target_pairs={{0,4},{4,0},{8,12},{12,8},{16,20},{20,16},{24,28},{28,24},{1,5},{5... | collective-permute-start | bytes 3145736 | tf_op jit(solution)/shard_map/ppermute | solution.py:606
  731.0 34.3 %collective-permute-start.42 = (bf16[256,2048]{1,0:T(8,128)(2,1)S(1)}, bf16[256,2048]{1,0:T(8,128)(2,1)S(1)}, u32[]{:S(2)}, u32[]{:S(2)}) collective-permute-start(bf16[256,2048]{1,0:T(8,128)(2,1)S(1)} %add_convert_fusion.4), channel_id=1, source_target_pairs={{0,8},{4,12},{8,16},{12,20},{16,24},{20,28},{24,0},{28,4},{1,9},{5... | collective-permute-start | bytes 3145736 | tf_op jit(solution)/shard_map/ppermute | solution.py:610
  731.3 45.9 %collective-permute-start.58 = (bf16[2,64,2176]{2,1,0:T(8,128)(2,1)S(1)}, bf16[2,64,2176]{2,1,0:T(8,128)(2,1)S(1)}, u32[]{:S(2)}, u32[]{:S(2)}) collective-permute-start(bf16[2,64,2176]{2,1,0:T(8,128)(2,1)S(1)} %copy-done.110), channel_id=1, source_target_pairs={{0,4},{4,0},{8,12},{12,8},{16,20},{20,16},{24,28},{28,24},{1,5},{5... | collective-permute-start | bytes 1671176 | tf_op jit(solution)/shard_map/ppermute | solution.py:606
  745.2 32.0 %collective-permute-start.59 = (bf16[2,64,2176]{2,1,0:T(8,128)(2,1)S(1)}, bf16[2,64,2176]{2,1,0:T(8,128)(2,1)S(1)}, u32[]{:S(2)}, u32[]{:S(2)}) collective-permute-start(bf16[2,64,2176]{2,1,0:T(8,128)(2,1)S(1)} %get-tuple-element.476), channel_id=1, source_target_pairs={{0,8},{4,12},{8,16},{12,20},{16,24},{20,28},{24,0},{28,4},{1,9},{5... | collective-permute-start | bytes 1671176 | tf_op jit(solution)/shard_map/ppermute | solution.py:610
  765.3 48.4 %collective-permute-start.43 = (bf16[256,2048]{1,0:T(8,128)(2,1)}, bf16[256,2048]{1,0:T(8,128)(2,1)}, u32[]{:S(2)}, u32[]{:S(2)}) collective-permute-start(bf16[256,2048]{1,0:T(8,128)(2,1)} %get-tuple-element.294), channel_id=1, source_target_pairs={{0,4},{4,0},{8,12},{12,8},{16,20},{20,16},{24,28},{28,24},{1,5},{5... | collective-permute-start | bytes 3145736 | tf_op jit(solution)/shard_map/ppermute | solution.py:606
  784.5 159.4 %reduce-scatter.17.cloned.1.call-start = ((), (), s32[]{:S(2)}) async-start(), calls=%async_computation.16 | async-start | bytes 5242880 | tf_op jit(solution)/shard_map/reduce_scatter | solution.py:926
  788.1 28.1 %collective-permute-start.44 = (bf16[256,2048]{1,0:T(8,128)(2,1)}, bf16[256,2048]{1,0:T(8,128)(2,1)}, u32[]{:S(2)}, u32[]{:S(2)}) collective-permute-start(bf16[256,2048]{1,0:T(8,128)(2,1)} %add_convert_fusion.3), channel_id=1, source_target_pairs={{0,8},{4,12},{8,16},{12,20},{16,24},{20,28},{24,0},{28,4},{1,9},{5... | collective-permute-start | bytes 3145736 | tf_op jit(solution)/shard_map/ppermute | solution.py:610
  802.8 35.6 %collective-permute-start.67 = (bf16[64,8320]{1,0:T(8,128)(2,1)S(1)}, bf16[64,8320]{1,0:T(8,128)(2,1)S(1)}, u32[]{:S(2)}, u32[]{:S(2)}) collective-permute-start(bf16[64,8320]{1,0:T(8,128)(2,1)S(1)} %pad_maximum_fusion.2.refs_0_), channel_id=1, source_target_pairs={{0,8},{4,12},{8,16},{12,20},{16,24},{20,28},{24,0},{28,4},{1,9},{5... | collective-permute-start | bytes 3194888 | tf_op jit(solution)/shard_map/ppermute | solution.py:610
  802.9 35.5 %collective-permute-start.68 = (bf16[64,8320]{1,0:T(8,128)(2,1)S(1)}, bf16[64,8320]{1,0:T(8,128)(2,1)S(1)}, u32[]{:S(2)}, u32[]{:S(2)}) collective-permute-start(bf16[64,8320]{1,0:T(8,128)(2,1)S(1)} %pad_maximum_fusion.2.refs_0_), channel_id=1, source_target_pairs={{0,4},{4,0},{8,12},{12,8},{16,20},{20,16},{24,28},{28,24},{1,5},{5... | collective-permute-start | bytes 3194888 | tf_op jit(solution)/shard_map/ppermute | solution.py:606
  813.7 28.6 %collective-permute-start.51 = (bf16[256,2048]{1,0:T(8,128)(2,1)S(1)}, bf16[256,2048]{1,0:T(8,128)(2,1)S(1)}, u32[]{:S(2)}, u32[]{:S(2)}) collective-permute-start(bf16[256,2048]{1,0:T(8,128)(2,1)S(1)} %get-tuple-element.490), channel_id=1, source_target_pairs={{0,1},{1,0},{2,3},{3,2},{4,5},{5,4},{6,7},{7,6},{8,9},{9,8},{10,11... | collective-permute-start | bytes 3145736 | tf_op jit(solution)/shard_map/ppermute | solution.py:570
  813.7 75.6 %collective-permute-start.50 = (bf16[256,2048]{1,0:T(8,128)(2,1)}, bf16[256,2048]{1,0:T(8,128)(2,1)}, u32[]{:S(2)}, u32[]{:S(2)}) collective-permute-start(bf16[256,2048]{1,0:T(8,128)(2,1)} %get-tuple-element.489), channel_id=1, source_target_pairs={{0,1},{1,0},{2,3},{3,2},{4,5},{5,4},{6,7},{7,6},{8,9},{9,8},{10,11... | collective-permute-start | bytes 3145736 | tf_op jit(solution)/shard_map/ppermute | solution.py:570
  816.3 58.8 %collective-permute-start.45 = (bf16[256,2048]{1,0:T(8,128)(2,1)S(1)}, bf16[256,2048]{1,0:T(8,128)(2,1)S(1)}, u32[]{:S(2)}, u32[]{:S(2)}) collective-permute-start(bf16[256,2048]{1,0:T(8,128)(2,1)S(1)} %copy-done.61), channel_id=1, source_target_pairs={{0,4},{4,0},{8,12},{12,8},{16,20},{20,16},{24,28},{28,24},{1,5},{5... | collective-permute-start | bytes 3145736 | tf_op jit(solution)/shard_map/ppermute | solution.py:606
  838.4 28.4 %collective-permute-start.69 = (bf16[64,8320]{1,0:T(8,128)(2,1)S(1)}, bf16[64,8320]{1,0:T(8,128)(2,1)}, u32[]{:S(2)}, u32[]{:S(2)}) collective-permute-start(bf16[64,8320]{1,0:T(8,128)(2,1)S(1)} %collective-permute-done.67.refs_2_), channel_id=1, source_target_pairs={{0,8},{4,12},{8,16},{12,20},{16,24},{20,28},{24,0},{28,4},{1,9},{5... | collective-permute-start | bytes 3194888 | tf_op jit(solution)/shard_map/ppermute | solution.py:610
  842.3 47.0 %collective-permute-start.46 = (bf16[256,2048]{1,0:T(8,128)(2,1)}, bf16[256,2048]{1,0:T(8,128)(2,1)}, u32[]{:S(2)}, u32[]{:S(2)}) collective-permute-start(bf16[256,2048]{1,0:T(8,128)(2,1)} %add_convert_fusion.2), channel_id=1, source_target_pairs={{0,8},{4,12},{8,16},{12,20},{16,24},{20,28},{24,0},{28,4},{1,9},{5... | collective-permute-start | bytes 3145736 | tf_op jit(solution)/shard_map/ppermute | solution.py:610
  842.3 31.4 %collective-permute-start.70 = (bf16[64,8320]{1,0:T(8,128)(2,1)S(1)}, bf16[64,8320]{1,0:T(8,128)(2,1)S(1)}, u32[]{:S(2)}, u32[]{:S(2)}) collective-permute-start(bf16[64,8320]{1,0:T(8,128)(2,1)S(1)} %collective-permute-done.67.refs_2_), channel_id=1, source_target_pairs={{0,4},{4,0},{8,12},{12,8},{16,20},{20,16},{24,28},{28,24},{1,5},{5... | collective-permute-start | bytes 3194888 | tf_op jit(solution)/shard_map/ppermute | solution.py:606
  866.8 22.6 %collective-permute-start.52 = (bf16[256,2048]{1,0:T(8,128)(2,1)}, bf16[256,2048]{1,0:T(8,128)(2,1)}, u32[]{:S(2)}, u32[]{:S(2)}) collective-permute-start(bf16[256,2048]{1,0:T(8,128)(2,1)} %add_convert_fusion), channel_id=1, source_target_pairs={{0,2},{1,3},{2,0},{3,1},{4,6},{5,7},{6,4},{7,5},{8,10},{9,11},{10,... | collective-permute-start | bytes 3145736 | tf_op jit(solution)/shard_map/ppermute | solution.py:574
  873.8 36.9 %collective-permute-start.71 = (bf16[64,8320]{1,0:T(8,128)(2,1)}, bf16[64,8320]{1,0:T(8,128)(2,1)}, u32[]{:S(2)}, u32[]{:S(2)}) collective-permute-start(bf16[64,8320]{1,0:T(8,128)(2,1)} %collective-permute-done.69.refs_4_), channel_id=1, source_target_pairs={{0,8},{4,12},{8,16},{12,20},{16,24},{20,28},{24,0},{28,4},{1,9},{5... | collective-permute-start | bytes 3194888 | tf_op jit(solution)/shard_map/ppermute | solution.py:610
  876.0 34.6 %collective-permute-start.72 = (bf16[64,8320]{1,0:T(8,128)(2,1)}, bf16[64,8320]{1,0:T(8,128)(2,1)}, u32[]{:S(2)}, u32[]{:S(2)}) collective-permute-start(bf16[64,8320]{1,0:T(8,128)(2,1)} %collective-permute-done.69.refs_4_), channel_id=1, source_target_pairs={{0,4},{4,0},{8,12},{12,8},{16,20},{20,16},{24,28},{28,24},{1,5},{5... | collective-permute-start | bytes 3194888 | tf_op jit(solution)/shard_map/ppermute | solution.py:606
  910.6 24.4 %collective-permute-start.73 = (bf16[64,8320]{1,0:T(8,128)(2,1)}, bf16[64,8320]{1,0:T(8,128)(2,1)}, u32[]{:S(2)}, u32[]{:S(2)}) collective-permute-start(bf16[64,8320]{1,0:T(8,128)(2,1)} %collective-permute-done.71.refs_1_), channel_id=1, source_target_pairs={{0,4},{4,0},{8,12},{12,8},{16,20},{20,16},{24,28},{28,24},{1,5},{5... | collective-permute-start | bytes 3194888 | tf_op jit(solution)/shard_map/ppermute | solution.py:606
  (150 other events, 2122.6 us)
Sparse Core Ops, SparseCore 0:
  45.7 59.9 all-gather.3
  107.2 58.1 all-gather.5
  189.6 57.7 all-gather.7
  546.1 40.8 reduce-scatter.8
  590.1 44.5 reduce-scatter.6
  637.0 44.5 reduce-scatter.12
  684.3 44.5 reduce-scatter.10
  731.4 44.4 reduce-scatter.14
  799.6 45.0 reduce-scatter.16

commit v4 on v3

--- a/solution.py
+++ b/solution.py
@@ -96,7 +96,7 @@
             out_specs=pl.BlockSpec((1, part, 3 * width), lambda s, n: (s, 0, 0)),
         ),
         out_shape=jax.ShapeDtypeStruct((2, part, 3 * width), BF),
-        compiler_params=params(),
+        compiler_params=params(58),
         cost_estimate=cost(0, 24 * part * width),
     )(place, w_query, w_key, w_value)
 
@@ -296,6 +296,49 @@
         compiler_params=params(48),
         cost_estimate=cost(40 * heads * length * length * HD, qkv.size * 3, heads * length * length),
     )(qkv, grad_o, *attn_args, *(() if held is None else (held,)))
+
+
+def read_names_body(experts, local, first_ref, *refs):
+    name_refs, (lanes_ref, slots_ref, named_ref) = refs[:-3], refs[-3:]
+    count = lanes_ref.shape[2]
+    row = lax.broadcasted_iota(jnp.int32, (count, count), 0)
+    column = lax.broadcasted_iota(jnp.int32, (count, count), 1)
+    earlier = (row < column).astype(BF)
+    expert_row = lax.broadcasted_iota(jnp.int32, (experts, count), 0)
+    for b, ref in enumerate(name_refs):
+        named = ref[0, ref.shape[1] - experts :, :]
+        slots = jnp.where(named > 0, dot(named, earlier), -1.0)
+        mine = [
+            jnp.sum(jnp.where(expert_row == first_ref[0] + j, slots, 0.0), axis=0, keepdims=True)
+            for j in range(local)
+        ]
+        mine = jnp.concatenate(mine, axis=0)
+        lanes_ref[b] = mine.astype(jnp.int32)
+        filled = jnp.concatenate([mine, jnp.zeros((HD - local, count), F32)], axis=0)
+        slots_ref[b] = filled.T.astype(jnp.int32)
+        filled = jnp.concatenate([named.astype(F32), jnp.zeros((HD - experts, count), F32)], axis=0)
+        named_ref[b] = filled.T
+
+
+def read_names(first, blocks, experts, local, count):
+    number, height = len(blocks), blocks[0].shape[1]
+    whole = lambda *shape: pl.BlockSpec(shape, lambda i, n: (0, 0, 0))
+    return pl.pallas_call(
+        functools.partial(read_names_body, experts, local),
+        grid_spec=pltpu.PrefetchScalarGridSpec(
+            num_scalar_prefetch=1,
+            grid=(1,),
+            in_specs=[whole(1, height, count)] * number,
+            out_specs=[whole(number, local, count), whole(number, count, HD), whole(number, count, HD)],
+        ),
+        out_shape=[
+            jax.ShapeDtypeStruct((number, local, count), jnp.int32),
+            jax.ShapeDtypeStruct((number, count, HD), jnp.int32),
+            jax.ShapeDtypeStruct((number, count, HD), F32),
+        ],
+        compiler_params=params(),
+        cost_estimate=cost(2 * number * experts * count * count, 10 * number * count * HD),
+    )(first, *blocks)
 
 
 def pick_rows(has_input, number_ref, slots_ref, named_ref, router_ref, x_ref, grad_ref, *refs):
@@ -354,7 +397,7 @@
 
 
 def merge_rows_body(blocks, slots_ref, *refs):
-    experts = slots_ref.shape[2]
+    experts = len(refs) - blocks
     rows_refs, out_refs = refs[:experts], refs[experts:]
     capacity = rows_refs[0].shape[0]
     count = out_refs[0].shape[0]
@@ -372,14 +415,15 @@
 
 
 def merge_rows(slots, first, rows, blocks):
-    count, experts = slots.shape[1:]
-    capacity = rows[0].shape[0] // blocks
-    width = rows[0].shape[1]
+    count, lanes = slots.shape[1:]
+    experts = rows.shape[0]
+    capacity = rows.shape[1] // blocks
+    width = rows.shape[2]
     return pl.pallas_call(
         functools.partial(merge_rows_body, blocks),
         grid=(blocks,),
-        in_specs=[pl.BlockSpec((1, count, experts), lambda b: (first + b, 0, 0))]
-        + [pl.BlockSpec((capacity, width), lambda b: (b, 0))] * experts,
+        in_specs=[pl.BlockSpec((1, count, lanes), lambda b: (first + b, 0, 0))]
+        + [pl.BlockSpec((None, capacity, width), lambda b, j=j: (j, b, 0)) for j in range(experts)],
         out_specs=[pl.BlockSpec((count, width), lambda b: (0, 0))] * blocks,
         out_shape=[jax.ShapeDtypeStruct((count, width), BF)] * blocks,
         compiler_params=params(),
@@ -387,11 +431,11 @@
             2 * blocks * experts * capacity * count * width,
             2 * blocks * width * (count + experts * capacity),
         ),
-    )(slots, *rows)
+    )(slots, *[rows] * experts)
 
 
 def merge_results_body(blocks, slots_ref, *refs):
-    experts = slots_ref.shape[2]
+    experts = len(refs) - 3 * blocks - 1
     gates_refs, grad_refs, refs = refs[:blocks], refs[blocks : 2 * blocks], refs[2 * blocks :]
     rows_refs, out_refs, dgate_ref = refs[:experts], refs[experts:-1], refs[-1]
     capacity = rows_refs[0].shape[0]
@@ -416,17 +460,18 @@
 
 def merge_results(slots, first, gates, grads, rows):
     blocks = len(gates)
-    count, experts = slots.shape[1:]
-    capacity = rows[0].shape[0] // blocks
-    width = rows[0].shape[1]
+    count, lanes = slots.shape[1:]
+    experts = rows.shape[0]
+    capacity = rows.shape[1] // blocks
+    width = rows.shape[2]
     tokens = pl.BlockSpec((count, width), lambda b: (0, 0))
     return pl.pallas_call(
         functools.partial(merge_results_body, blocks),
         grid=(blocks,),
-        in_specs=[pl.BlockSpec((1, count, experts), lambda b: (first + b, 0, 0))]
+        in_specs=[pl.BlockSpec((1, count, lanes), lambda b: (first + b, 0, 0))]
         + [pl.BlockSpec((count, experts), lambda b: (0, 0))] * blocks
         + [tokens] * blocks
-        + [pl.BlockSpec((capacity, width), lambda b: (b, 0))] * experts,
+        + [pl.BlockSpec((None, capacity, width), lambda b, j=j: (j, b, 0)) for j in range(experts)],
         out_specs=[tokens] * blocks + [pl.BlockSpec((1, count, experts), lambda b: (b, 0, 0))],
         out_shape=[jax.ShapeDtypeStruct((count, width), BF)] * blocks
         + [jax.ShapeDtypeStruct((blocks, count, experts), F32)],
@@ -435,7 +480,7 @@
             2 * blocks * experts * capacity * count * width,
             2 * blocks * width * (2 * count + experts * capacity),
         ),
-    )(slots, *gates, *grads, *rows)
+    )(slots, *gates, *grads, *[rows] * experts)
 
 
 def expert_body(
@@ -453,19 +498,19 @@
     y_acc,
     dx_acc,
 ):
-    f = pl.program_id(0)
-    last = pl.num_programs(0) - 1
+    f = pl.program_id(1)
+    last = pl.num_programs(1) - 1
 
     def step(i, carry):
         r = pl.ds(pl.multiple_of(i * sub, sub), sub)
         x = x_ref[r, :]
         gate = dot(x, wg_ref[...])
         up = dot(x, wu_ref[...])
+        grad_hidden = dot_t(dy_ref[r, :], wd_ref[...])
         sigmoid = 1.0 / (1.0 + jnp.exp(-gate))
         activated = gate * sigmoid
         hidden = (activated * up).astype(BF)
         h_ref[r, :] = hidden
-        grad_hidden = dot_t(dy_ref[r, :], wd_ref[...])
         grad_gate = (grad_hidden * up * sigmoid * (1.0 + gate * (1.0 - sigmoid))).astype(BF)
         grad_up = (grad_hidden * activated).astype(BF)
         dg_ref[r, :] = grad_gate
@@ -493,33 +538,32 @@
     lax.fori_loop(0, x_ref.shape[0] // sub, step, 0)
 
 
-def expert(j, x, dy, w_gate, w_up, w_down):
-    _, rows, width = x.shape
+def run_experts(x, dy, w_gate, w_up, w_down):
+    experts, rows, width = x.shape
     hidden = w_gate.shape[2]
     tile = hidden // 2
-    rows_in = pl.BlockSpec((None, rows, width), lambda f: (j, 0, 0))
-    rows_out = pl.BlockSpec((rows, width), lambda f: (0, 0))
-    part = pl.BlockSpec((rows, tile), lambda f: (0, f))
-    wide = jax.ShapeDtypeStruct((rows, width), BF)
-    thin = jax.ShapeDtypeStruct((rows, hidden), BF)
+    whole = pl.BlockSpec((None, rows, width), lambda j, f: (j, 0, 0))
+    part = pl.BlockSpec((None, rows, tile), lambda j, f: (j, 0, f))
+    wide = jax.ShapeDtypeStruct((experts, rows, width), BF)
+    thin = jax.ShapeDtypeStruct((experts, rows, hidden), BF)
     return pl.pallas_call(
         functools.partial(expert_body, rows // 2),
-        grid=(2,),
+        grid=(experts, 2),
         in_specs=[
-            rows_in,
-            rows_in,
-            pl.BlockSpec((None, width, tile), lambda f: (j, 0, f)),
-            pl.BlockSpec((None, width, tile), lambda f: (j, 0, f)),
-            pl.BlockSpec((None, tile, width), lambda f: (j, f, 0)),
+            whole,
+            whole,
+            pl.BlockSpec((None, width, tile), lambda j, f: (j, 0, f)),
+            pl.BlockSpec((None, width, tile), lambda j, f: (j, 0, f)),
+            pl.BlockSpec((None, tile, width), lambda j, f: (j, f, 0)),
         ],
-        out_specs=[rows_out, rows_out, part, part, part],
+        out_specs=[whole, whole, part, part, part],
         out_shape=[wide, wide, thin, thin, thin],
         scratch_shapes=[pltpu.VMEM((rows, width), F32)] * 2,
-        compiler_params=params(58),
+        compiler_params=params(60),
         cost_estimate=cost(
-            12 * rows * width * hidden,
-            8 * rows * width + 6 * rows * hidden + 6 * width * hidden,
-            rows * hidden,
+            12 * experts * rows * width * hidden,
+            experts * (8 * rows * width + 6 * rows * hidden + 6 * width * hidden),
+            experts * rows * hidden,
         ),
     )(x, dy, w_gate, w_up, w_down)
 
@@ -620,10 +664,11 @@
     return together(turn_z(value, count), swap_y(value, count))
 
 
-def rep_gather(value, count):
+def rep_gather(value, count, ties=None):
     blocks = []
     held = value
     for k in range(count // 2):
+        held = after(held, *(ties or {}).get(k, ()))
         if k < count // 2 - 1:
             nexts, crossed = together(turn_z(held, count), swap_y(held, count))
         else:
@@ -647,9 +692,10 @@
         if not self.order:
             return total
         self.k = self.order.pop(0)
+        self.sent = total.astype(BF)
         self.arrived = together(
             swap_y(after(self.blocks[2 * self.k + 1], arrived[0]), self.count),
-            turn_z(total.astype(BF), self.count),
+            turn_z(self.sent, self.count),
         )
         return None
 
@@ -763,10 +809,14 @@
             swap_core(lax.dynamic_index_in_dim(far, 1 - core, 0, keepdims=False)),
         ]
     )
-    routes_b = routes.astype(BF).reshape(2, 16, -1)
-    routes_b = jnp.pad(routes_b, ((0, 0), (0, 0), (0, far.shape[2] - routes_b.shape[2])))
-    full_up = lax.all_gather(after(w_up, far, far_tokens, grad_held), "shard", axis=1, tiled=True)
-    fars = rep_gather(jnp.concatenate([far, routes_b], axis=1), rep_count)
+    expert_ids = jnp.arange(experts, dtype=jnp.int32)
+    named_own = jnp.any(routes[:, :, None] == expert_ids, axis=1)
+    names = jnp.pad(named_own.T.astype(BF), ((0, 0), (0, far.shape[2] - rows_count)))
+    names = jnp.stack([names, names])
+    full_up = lax.all_gather(
+        after(w_up, far, far_tokens, grad_held), "shard", axis=1, tiled=True
+    )
+    fars = rep_gather(jnp.concatenate([far, names], axis=1), rep_count)
     packed = packed_columns(after(w_query, fars[1]), w_key, w_value, shard_count)
     near = swap_core(lax.dynamic_index_in_dim(packed, position ^ 1, 0, keepdims=False))
     token_blocks = [tokens, swap_core(tokens), far_tokens, swap_core(far_tokens)]
@@ -823,19 +873,10 @@
     scale_mid = rms_scale(hidden_state)
     normed_mid = hidden_state * scale_mid
     mid_b = (normed_mid * gain_ffn).astype(BF)
-    expert_ids = jnp.arange(experts, dtype=jnp.int32)
     first_expert = rep * local_experts
-    before = jnp.tril(jnp.ones((rows_count, rows_count), BF), -1)
-
-    route_all = jnp.stack([block[:, part:, : rows_count * TOP // 32] for block in fars])
-    route_all = route_all.reshape(rep_count, rows_count, TOP).astype(jnp.int32)
-    named_all = jnp.any(route_all[:, :, :, None] == expert_ids, axis=2)
-    named_mine = lax.dynamic_slice_in_dim(named_all, first_expert, local_experts, axis=2)
-    slots = jnp.einsum("ts,bsj->btj", before, named_mine.astype(BF), preferred_element_type=F32)
-    slots = jnp.where(named_mine, slots.astype(jnp.int32), -1)
-    slot_lanes = jnp.swapaxes(slots, 1, 2)
-    named_lanes = jnp.pad(named_all.astype(F32), ((0, 0), (0, 0), (0, HD - experts)))
-
+    slot_lanes, slots, named_lanes = read_names(
+        first_expert[None], fars, experts, local_experts, rows_count
+    )
     router_lanes = jnp.pad(full_router, ((0, 0), (0, HD - experts)))
     number = jnp.stack([first_expert, jnp.int32(experts)])
     picked, groups = [], []
@@ -864,15 +905,16 @@
             x, dy = [
                 a.reshape(local_experts, group_size * capacity, width) for a in picked[-1][:2]
             ]
-            groups.append((x, dy, []))
-
-    def run_expert(group, j, *others):
-        x, dy, done = groups[group]
-        done.append(expert(j, after(x, *others), dy, full_gate, full_up, full_down))
-        return done[-1][0]
+            groups.append((x, dy))
+
+    def run_group(group, *others):
+        x, dy = groups[group]
+        done = run_experts(after(x, *others), dy, full_gate, full_up, full_down)
+        groups[group] = (x, dy, done)
+        return done[0]
 
     def merge_grads(group):
-        return merge_rows(slots, group * group_size, [d[1] for d in groups[group][2]], group_size)
+        return merge_rows(slots, group * group_size, groups[group][2][1], group_size)
 
     def merge_group(group, *ready):
         members = slice(group * group_size, (group + 1) * group_size)
@@ -881,7 +923,7 @@
             group * group_size,
             [p[2] for p in picked[members]],
             grad_blocks[members],
-            [d[0] for d in groups[group][2]],
+            groups[group][2][0],
         )
         return parts, dgate
 
@@ -902,19 +944,15 @@
     last = rep_count // group_size - 1
     ready = ()
     for g in range(last):
-        for j in range(local_experts):
-            ready = (run_expert(g, j, *ready),)
+        run_group(g, *ready)
         grad_parts += merge_grads(g)
         ready = (grad_parts[-1],)
     cross_first = swap_y(grad_parts[3], rep_count)
-    cross_zero = swap_y(after(grad_parts[1], grad_parts[3]), rep_count)
+    cross_zero = swap_y(grad_parts[1], rep_count)
     pick_next(after(crossed, *ready))
-    y = run_expert(last, 0)
-    cross_first, cross_zero = together(cross_first, cross_zero, y)[:2]
+    y = run_group(last)
+    cross_first, cross_zero, y = together(cross_first, cross_zero, y)
     total = turn_z(added(grad_parts[2], cross_first).astype(BF), rep_count)
-    for j in range(1, local_experts):
-        y = run_expert(last, j, cross_first, cross_zero)
-    total = after(total, y)
     grad_parts += merge_grads(last)
     arrived = swap_y(grad_parts[5], rep_count)
     for g in range(last + 1):
@@ -928,14 +966,14 @@
     def wide_grads(j, *others):
         return weight_grads(
             [after(g[0], *others) for g in groups],
-            [[g[2][j][3] for g in groups], [g[2][j][4] for g in groups]],
+            [[g[2][3] for g in groups], [g[2][4] for g in groups]],
             j,
-            None,
+            j,
         )
 
     def down_grads(j, *others):
         return weight_grads(
-            [after(g[2][j][2], *others) for g in groups], [[g[1] for g in groups]], None, j
+            [after(g[2][2], *others) for g in groups], [[g[1] for g in groups]], j, j
         )[0]
 
     arrived = after(arrived, *result_parts, *dgate_parts)
@@ -950,14 +988,19 @@
                 made.append(wide_grads(0, grad_parts[-1], *result_parts))
                 total, arrived = together(total, arrived, *made[0])[:2]
         else:
+            sent = total
             total = turn_z(total, rep_count)
+            while len(made) < local_experts:
+                made.append(wide_grads(len(made), sent))
+                total = together(total, *made[-1])[0]
+    results_sum = RepReduce(result_parts, rep_count, arrived)
+    total = after(total, *results_sum.arrived)
     grad_mid_moe = added(grad_parts[0], cross_zero, total)
 
     dgates = jnp.swapaxes(jnp.concatenate(dgate_parts), 1, 2)
     dgates = jnp.zeros_like(dgates).at[order_array].set(dgates)
     dgates = lax.all_to_all(dgates, "rep", split_axis=0, concat_axis=0, tiled=True)
     dgates = dgates.reshape(experts, rows_count).T
-    named_own = jnp.any(routes[:, :, None] == expert_ids, axis=1)
     logits = dot(mid_b, full_router)
     exps = jnp.exp(logits - jnp.max(logits, axis=-1, keepdims=True))
     probs_own = exps / jnp.sum(exps, axis=-1, keepdims=True)
@@ -976,18 +1019,20 @@
     grad_state = grad_out + norm_back(grad_mid * gain_ffn, normed_mid, scale_mid)
     grad_state_b = grad_state.astype(BF)
 
-    state_blocks = shard_gather(grad_state_b)
-    while len(made) < local_experts:
-        made.append(wide_grads(len(made), grad_state_b))
+    far_state = swap_x(grad_state_b)
+    while len(results_sum.order) > 2:
+        results_sum.step()
+    downs = [down_grads(j, grad_state_b) for j in range(local_experts)]
+    far_state = together(far_state, *results_sum.arrived, *downs)[0]
+    state_blocks = [grad_state_b, swap_core(grad_state_b), far_state, swap_core(far_state)]
     grad_state_all = jnp.concatenate(state_blocks, axis=0)
-    grad_state_all = after(grad_state_all, *made[-1])
     grad_mixed = dot_t(grad_state_all, w_out).astype(BF)
     heads = qkv.shape[1] // (3 * HD)
+    results_sum.step()
     grad_qkv, grad_head_gains = attention_backward(qkv, grad_mixed, attn_args, 0, heads)
+    grad_qkv, *results_sum.arrived = together(grad_qkv, *results_sum.arrived)
     grad_columns = t_dot(input_b, grad_qkv).astype(BF)
     grad_out_proj = t_dot(mixed_b, grad_state_all).astype(BF)
-    expert_sum = rep_reduce(result_parts, rep_count, grad_mid_moe)
-    output = (hidden_state + expert_sum).astype(BF)
     grad_input = dot_t(after(grad_qkv, grad_columns), columns).astype(BF)
     grad_input = shard_reduce(
         [grad_input[i * rows_count : (i + 1) * rows_count] for i in range(shard_count)]
@@ -996,8 +1041,8 @@
     tokens_grad = (
         grad_state + norm_back(grad_input * gain_attn, normed_in, rms_scale(tokens_f))
     ).astype(BF)
-    sums_gate = [owned_part(after(m[0], state_blocks[2])) for m in made]
-    sums_up = [owned_part(after(m[1], state_blocks[2])) for m in made]
+    sums_gate = [owned_part(after(m[0], grad_mixed)) for m in made]
+    sums_up = [owned_part(after(m[1], grad_mixed)) for m in made]
 
     piece = HD // shard_count
     head_columns = jnp.pad(
@@ -1013,19 +1058,16 @@
     extra_parts = extras.reshape(shard_count, rep_count, part, -1)
     to_sum = jnp.concatenate([column_parts, extra_parts, out_columns], axis=3)
     to_sum = [lax.dynamic_index_in_dim(to_sum, r, axis=1, keepdims=False) for r in order]
-    half = shard_count // 2
-    halves = [
-        RepReduce([a[h : h + half] for a in to_sum], rep_count) for h in (0, half)
-    ]
-    sums_down = []
-    part_sum = [None, None]
-    while None in part_sum:
-        if len(sums_down) < local_experts:
-            sums_down.append(owned_part(down_grads(len(sums_down), halves[0].arrived[0])))
-        part_sum = [h.step() for h in halves]
-    part_sum = jnp.concatenate(part_sum, axis=0).astype(BF)
-    while len(sums_down) < local_experts:
-        sums_down.append(owned_part(down_grads(len(sums_down), part_sum)))
+    sums = RepReduce(to_sum, rep_count)
+    expert_sum = None
+    while expert_sum is None:
+        expert_sum = results_sum.step()
+    sums_down = [owned_part(after(d, grad_mixed)) for d in downs]
+    part_sum = None
+    while part_sum is None:
+        part_sum = sums.step()
+    part_sum = part_sum.astype(BF)
+    output = (hidden_state + expert_sum).astype(BF)
     grad_gate = jnp.stack(sums_gate).astype(F32)
     grad_up = jnp.stack(sums_up).astype(F32)
     grad_down = jnp.stack(sums_down).astype(F32)
@@ -1034,9 +1076,13 @@
     wide = jnp.swapaxes(mine[:, :, : split - HD], 0, 1).reshape(part, -1)
     extra = jnp.sum(mine[:, :, split - HD :].astype(F32), axis=0).astype(BF)
     out_part = jnp.swapaxes(part_sum[:, :, split:], 0, 1).reshape(part, -1)
-    gathered = rep_gather(jnp.concatenate([wide, out_part, extra], axis=1), rep_count)
+    gathered = rep_gather(
+        jnp.concatenate([wide, out_part, extra], axis=1),
+        rep_count,
+        {2: (grad_gate, grad_up, output), 3: (grad_down, tokens_grad)},
+    )
     gain_rows = norm_attn.astype(F32)[:, None]
-    most = rep_count - 3
+    most = rep_count - 1
     held = write_sums(order_array[:most], w_query, w_key, w_value, gain_rows, gathered[:most])
     sum_query, sum_key, sum_value, sum_out, extra = write_sums(
         order_array[most:], w_query, w_key, w_value, gain_rows, gathered[most:], held

time: 962 us -> 917 us (0.953)
  waiting for transfers between devices: 361 us -> 329 us
    ppermute x32 -> x28, waiting for transfers between devices: 137 us -> 49.6 us  [swap_y(): return lax.ppermute(value, 'rep', [(i, i ^ 1) for i in range(count)])]
    ppermute x24 -> x21, waiting for transfers between devices: 195 us -> 227 us  [turn_z(): return lax.ppermute(value, 'rep', ring_next(count))]
    ppermute x6, waiting for transfers between devices: 11.6 us -> 29.5 us  [swap_x(): return lax.ppermute(value, 'shard', [(i, i ^ 2) for i in range(4)])]
    all_to_all x1, waiting for transfers between devices: 0.01 us -> 15.4 us  [on_device(): lax.all_to_all(part_sum[:, :, :split], 'shard', split_axis=0, concat_axis...]
    pallas_call x4 -> x3, Pallas kernels: 100 us -> 93.7 us  [the longest x2 92 us: run_experts(): pl.pallas_call(functools.partial(expert_body, rows // 2), grid=(experts,...]
    unnamed x269 -> x194, local copies, waits for them, and re-layouts: 49.8 us -> 47.3 us
    ppermute x32 -> x28, starting transfers between devices: 31.7 us -> 31.2 us  [swap_y(): return lax.ppermute(value, 'rep', [(i, i ^ 1) for i in range(count)])]
  transfers between devices with their start and end apart: 85 -> 78, of which waited for: 36 -> 24; matrix products, arithmetic and copies ran while one was open for 14% -> 15% of each run, Pallas kernels for 33% -> 34%
where the time goes in v4:
time: 917 us; the launch traced here: 910 us
  waiting for transfers between devices  329 us (36%)
  Pallas kernels  308 us (34%)
  other arithmetic  79.2 us (9%)
  local copies, waits for them, and re-layouts  74.9 us (8%)
  starting transfers between devices  68 us (7%)
  matrix products  36.1 us (4%)
  between operations  15.3 us (2%)
    ppermute x21, waiting for transfers between devices, turn_z(): return lax.ppermute(value, 'rep', ring_next(count))  227 us
    pallas_call x2, Pallas kernels, run_experts(): pl.pallas_call(functools.partial(expert_body, rows // 2), grid=(experts,...  92 us
    pallas_call x4, Pallas kernels, weight_grads(): pl.pallas_call(functools.partial(weight_grads_body, groups, count), grid=...  56.8 us
    ppermute x28, waiting for transfers between devices, swap_y(): return lax.ppermute(value, 'rep', [(i, i ^ 1) for i in range(count)])  49.6 us
    unnamed x194, local copies, waits for them, and re-layouts  47.3 us
    pallas_call x8, Pallas kernels, pick(): pl.pallas_call(functools.partial(pick_rows, held is not None), grid_spec=...  43.6 us
    pallas_call x1, Pallas kernels, attention_backward(): pl.pallas_call(attend_backward, grid=(heads,), in_specs=[wide, pl.BlockSp...  32.8 us
    ppermute x28, starting transfers between devices, swap_y(): return lax.ppermute(value, 'rep', [(i, i ^ 1) for i in range(count)])  31.2 us
  transfers between devices with their start and end apart: 78, of which 24 were waited for; matrix products, arithmetic and copies ran while one was open for 15% of the time, Pallas kernels for 34%

profile of v4, /device:TPU:0, one launch (start us, length us, event | category | flops | bytes accessed | tf_op | source)
XLA Modules:
  0.0 910.4 jit_solution(2390702260860713384)
XLA Ops:
  7.2 3.1 collective-permute-start.16
  16.9 18.8 %collective-permute-done.16.grad_ref.refs_6_ = bf16[256,2048]{1,0:T(8,128)(2,1)S(1)} collective-permute-done((bf16[256,2048]{1,0:T(8,128)(2,1)}, bf16[256,2048]{1,0:T(8,128)(2,1)S(1)}, u32[]{:S(2)}, u32[]{:S(2)}) %collective-permute-start.16) | collective-permute-done | bytes 1048608 | tf_op jit(solution)/shard_map/ppermute | solution.py:654
  35.7 9.1 collective-permute-done.3
  56.0 10.9 %collective-permute-done.5.refs_6_.refs_2_ = bf16[2,80,1536]{2,1,0:T(8,128)(2,1)} collective-permute-done((bf16[2,80,1536]{2,1,0:T(8,128)(2,1)}, bf16[2,80,1536]{2,1,0:T(8,128)(2,1)}, u32[]{:S(2)}, u32[]{:S(2)}) %collective-permute-start.5) | collective-permute-done | bytes 491552 | tf_op jit(solution)/shard_map/ppermute | solution.py:654
  78.8 3.1 fusion.19
  103.9 9.3 %collective-permute-done.15.refs_11_.refs_7_ = bf16[2,80,1536]{2,1,0:T(8,128)(2,1)} collective-permute-done((bf16[2,80,1536]{2,1,0:T(8,128)(2,1)}, bf16[2,80,1536]{2,1,0:T(8,128)(2,1)}, u32[]{:S(2)}, u32[]{:S(2)}) %collective-permute-start.15) | collective-permute-done | bytes 491552 | tf_op jit(solution)/shard_map/ppermute | solution.py:650
  114.3 18.2 %shard_map.265 = (bf16[1024,2048]{1,0:T(8,128)(2,1)}, bf16[2048,1536]{1,0:T(8,128)(2,1)}, f32[1024,1536]{1,0:T(8,128)}) custom-call(s32[8]{0:T(128)} %stack.153.order_ref, s32[4]{0:T(128)} %pad_add_fusion.1.shard_ref, f32[1,2048]{1,0:T(1,128)} %bitcast.182, bf16[4,512,1536]{2,1,0:T(8,128)(2,1)} %copy-done.10, ...), custom_call_target="tpu_custom_call" | custom-call | flops 6442450944 | bytes 27262976 | tf_op jit(solution)/shard_map/pallas_call | solution.py:148
  135.3 18.5 %shard_map.266 = bf16[1024,512]{1,0:T(8,128)(2,1)S(1)} custom-call(f32[1024,1536]{1,0:T(8,128)S(1)} %copy-done.53, f32[1024,128]{1,0:T(8,128)S(1)} %copy-done.39, f32[1024,128]{1,0:T(8,128)S(1)} %copy-done.35, f32[1,128]{1,0:T(1,128)S(1)} %reshape_squeeze.6.gq_ref, f32[1,128]{1,0:T(1,128)S(1)} %reshape_squeeze.7.gk_ref, s32[1024,1]{1,0:T(8,128)S(1)} %copy-done.37, ...), custom_call_target="tpu_custom_call" | custom-call | flops 8589934592 | bytes 7864320 | tf_op jit(solution)/shard_map/pallas_call | solution.py:268
  162.5 21.8 %collective-permute-done.23.grad_ref.refs_6_ = bf16[256,2048]{1,0:T(8,128)(2,1)} collective-permute-done((bf16[256,2048]{1,0:T(8,128)(2,1)S(1)}, bf16[256,2048]{1,0:T(8,128)(2,1)}, u32[]{:S(2)}, u32[]{:S(2)}) %collective-permute-start.23) | collective-permute-done | bytes 1048608 | tf_op jit(solution)/shard_map/ppermute | solution.py:654
  196.5 5.8 shard_map.268
  202.3 16.8 %collective-permute-done.25.x_ref = bf16[256,2048]{1,0:T(8,128)(2,1)S(1)} collective-permute-done((bf16[256,2048]{1,0:T(8,128)(2,1)S(1)}, bf16[256,2048]{1,0:T(8,128)(2,1)S(1)}, u32[]{:S(2)}, u32[]{:S(2)}) %collective-permute-start.25) | collective-permute-done | bytes 1048608 | tf_op jit(solution)/shard_map/ppermute | solution.py:654
  221.3 5.4 shard_map.269
  226.6 5.4 shard_map.270
  232.0 12.9 %collective-permute-done.27.x_ref = bf16[256,2048]{1,0:T(8,128)(2,1)S(1)} collective-permute-done((bf16[256,2048]{1,0:T(8,128)(2,1)S(1)}, bf16[256,2048]{1,0:T(8,128)(2,1)S(1)}, u32[]{:S(2)}, u32[]{:S(2)}) %collective-permute-start.27) | collective-permute-done | bytes 1048608 | tf_op jit(solution)/shard_map/ppermute | solution.py:654
  246.4 5.4 shard_map.271
  251.8 18.0 %collective-permute-done.29.x_ref = bf16[256,2048]{1,0:T(8,128)(2,1)} collective-permute-done((bf16[256,2048]{1,0:T(8,128)(2,1)S(1)}, bf16[256,2048]{1,0:T(8,128)(2,1)}, u32[]{:S(2)}, u32[]{:S(2)}) %collective-permute-start.29) | collective-permute-done | bytes 1048608 | tf_op jit(solution)/shard_map/ppermute | solution.py:654
  271.5 5.4 shard_map.272
  276.9 5.4 shard_map.275
  282.3 5.4 shard_map.276
  287.7 5.2 collective-permute-done.31.x_ref
  294.7 50.4 %shard_map.273 = (bf16[2,576,2048]{2,1,0:T(8,128)(2,1)}, bf16[2,576,2048]{2,1,0:T(8,128)(2,1)}, bf16[2,576,1024]{2,1,0:T(8,128)(2,1)}, bf16[2,576,1024]{2,1,0:T(8,128)(2,1)}, bf16[2,576,1024]{2,1,0:T(8,128)(2,1)}) custom-call(bf16[2,576,2048]{2,1,0:T(8,128)(2,1)} %bitcast.162, bf16[2,576,2048]{2,1,0:T(8,128)(2,1)} %bitcast.156, ...), custom_call_target="tpu_custom_call" | custom-call | flops 28991029248 | bytes 51118080 | tf_op jit(solution)/shard_map/pallas_call | solution.py:549
  347.5 4.8 shard_map.274
  354.6 5.4 shard_map.277
  361.7 41.6 %shard_map.278 = (bf16[2,576,2048]{2,1,0:T(8,128)(2,1)}, bf16[2,576,2048]{2,1,0:T(8,128)(2,1)}, bf16[2,576,1024]{2,1,0:T(8,128)(2,1)}, bf16[2,576,1024]{2,1,0:T(8,128)(2,1)}, bf16[2,576,1024]{2,1,0:T(8,128)(2,1)}) custom-call(bf16[2,576,2048]{2,1,0:T(8,128)(2,1)} %bitcast.159, bf16[2,576,2048]{2,1,0:T(8,128)(2,1)} %bitcast.153, ...), custom_call_target="tpu_custom_call" | custom-call | flops 28991029248 | bytes 51118080 | tf_op jit(solution)/shard_map/pallas_call | solution.py:549
  405.7 4.6 shard_map.279
  415.9 7.3 shard_map.280
  426.1 8.6 shard_map.281
  442.5 6.3 all-to-all-start
  450.9 3.6 add_convert_fusion.6
  457.6 17.7 %shard_map.282 = (bf16[2048,1024]{1,0:T(8,128)(2,1)}, bf16[2048,1024]{1,0:T(8,128)(2,1)}) custom-call(bf16[2,576,2048]{2,1,0:T(8,128)(2,1)} %bitcast.163, bf16[2,576,2048]{2,1,0:T(8,128)(2,1)} %bitcast.160, bf16[2,576,1024]{2,1,0:T(8,128)(2,1)S(1)} %copy-done.55, bf16[2,576,1024]{2,1,0:T(8,128)(2,1)S(1)} %copy-done.57, ...), custom_call_target="tpu_custom_call" | custom-call | flops 9663676416 | bytes 17825792 | tf_op jit(solution)/shard_map/pallas_call | solution.py:599
  482.0 17.3 %shard_map.283 = (bf16[2048,1024]{1,0:T(8,128)(2,1)}, bf16[2048,1024]{1,0:T(8,128)(2,1)}) custom-call(bf16[2,576,2048]{2,1,0:T(8,128)(2,1)} %bitcast.164, bf16[2,576,2048]{2,1,0:T(8,128)(2,1)} %bitcast.161, bf16[2,576,1024]{2,1,0:T(8,128)(2,1)S(1)} %copy-done.56, bf16[2,576,1024]{2,1,0:T(8,128)(2,1)S(1)} %copy-done.58, ...), custom_call_target="tpu_custom_call" | custom-call | flops 9663676416 | bytes 17825792 | tf_op jit(solution)/shard_map/pallas_call | solution.py:599
  500.3 4.2 multiply_reduce_fusion
  508.0 10.9 %shard_map.285 = bf16[1024,2048]{1,0:T(8,128)(2,1)} custom-call(bf16[2,576,1024]{2,1,0:T(8,128)(2,1)S(1)} %copy-done.11, bf16[2,576,1024]{2,1,0:T(8,128)(2,1)S(1)} %copy-done.13, bf16[2,576,2048]{2,1,0:T(8,128)(2,1)} %bitcast.157, bf16[2,576,2048]{2,1,0:T(8,128)(2,1)} %bitcast.154), custom_call_target="tpu_custom_call" | custom-call | flops 4831838208 | bytes 11272192 | tf_op jit(solution)/shard_map/pallas_call | solution.py:599
  522.2 10.9 %shard_map.284 = bf16[1024,2048]{1,0:T(8,128)(2,1)} custom-call(bf16[2,576,1024]{2,1,0:T(8,128)(2,1)S(1)} %copy-done.12, bf16[2,576,1024]{2,1,0:T(8,128)(2,1)S(1)} %copy-done.14, bf16[2,576,2048]{2,1,0:T(8,128)(2,1)} %bitcast.158, bf16[2,576,2048]{2,1,0:T(8,128)(2,1)} %bitcast.155), custom_call_target="tpu_custom_call" | custom-call | flops 4831838208 | bytes 11272192 | tf_op jit(solution)/shard_map/pallas_call | solution.py:599
  533.1 2.9 collective-permute-done.43
  537.0 5.2 convolution_convert_fusion.5.do_ref
  544.2 2.9 add_convert_fusion.4
  551.8 22.6 %collective-permute-done.45 = bf16[256,2048]{1,0:T(8,128)(2,1)} collective-permute-done((bf16[256,2048]{1,0:T(8,128)(2,1)}, bf16[256,2048]{1,0:T(8,128)(2,1)}, u32[]{:S(2)}, u32[]{:S(2)}) %collective-permute-start.45) | collective-permute-done | bytes 1048608 | tf_op jit(solution)/shard_map/ppermute | solution.py:654
  574.4 3.4 add_convert_fusion.3
  579.4 32.8 %shard_map.286 = (bf16[1024,1536]{1,0:T(8,128)(2,1)S(1)}, f32[8,128]{1,0:T(8,128)S(1)}) custom-call(f32[1024,1536]{1,0:T(8,128)} %get-tuple-element.183.qkv_ref, bf16[1024,512]{1,0:T(8,128)(2,1)S(1)} %copy-done.62, f32[1024,128]{1,0:T(8,128)S(1)} %copy-done.40, f32[1024,128]{1,0:T(8,128)S(1)} %copy-done.36, f32[1,128]{1,0:T(1,128)S(1)} %reshape_squeeze.6.gq_ref, ...), custom_call_target="tpu_custom_call" | custom-call | flops 21474836480 | bytes 4718592 | tf_op jit(solution)/shard_map/pallas_call | solution.py:283
  614.2 6.2 convolution_convert_fusion.3
  625.1 9.4 %convolution_convert_fusion = bf16[2048,1536]{1,0:T(8,128)(2,1)S(1)} fusion(bf16[1024,2048]{1,0:T(8,128)(2,1)} %get-tuple-element.301, bf16[1024,1536]{1,0:T(8,128)(2,1)S(1)} %copy-done.60), kind=kOutput, calls=%fused_computation.3 | convolution fusion | flops 6445596672 | bytes 13631488 | tf_op jit(solution)/shard_map/dot_general | solution.py:40
  641.2 25.2 %collective-permute-done.53 = bf16[4,64,2176]{2,1,0:T(8,128)(2,1)} collective-permute-done((bf16[4,64,2176]{2,1,0:T(8,128)(2,1)}, bf16[4,64,2176]{2,1,0:T(8,128)(2,1)}, u32[]{:S(2)}, u32[]{:S(2)}) %collective-permute-start.53) | collective-permute-done | bytes 1114144 | tf_op jit(solution)/shard_map/ppermute | solution.py:650
  666.4 2.9 fusion.6
  670.6 25.4 %collective-permute-done.55 = bf16[4,64,2176]{2,1,0:T(8,128)(2,1)} collective-permute-done((bf16[4,64,2176]{2,1,0:T(8,128)(2,1)}, bf16[4,64,2176]{2,1,0:T(8,128)(2,1)}, u32[]{:S(2)}, u32[]{:S(2)}) %collective-permute-start.55) | collective-permute-done | bytes 1114144 | tf_op jit(solution)/shard_map/ppermute | solution.py:654
  696.0 3.3 fusion.5
  700.1 25.3 %collective-permute-done.57 = bf16[4,64,2176]{2,1,0:T(8,128)(2,1)} collective-permute-done((bf16[4,64,2176]{2,1,0:T(8,128)(2,1)}, bf16[4,64,2176]{2,1,0:T(8,128)(2,1)}, u32[]{:S(2)}, u32[]{:S(2)}) %collective-permute-start.57) | collective-permute-done | bytes 1114144 | tf_op jit(solution)/shard_map/ppermute | solution.py:654
  729.0 9.0 convolution_convert_fusion.1
  741.5 3.2 add_convert_fusion.2
  746.1 9.5 %collective-permute-done.59 = bf16[4,64,2176]{2,1,0:T(8,128)(2,1)S(1)} collective-permute-done((bf16[4,64,2176]{2,1,0:T(8,128)(2,1)S(1)}, bf16[4,64,2176]{2,1,0:T(8,128)(2,1)S(1)}, u32[]{:S(2)}, u32[]{:S(2)}) %collective-permute-start.59) | collective-permute-done | bytes 1114144 | tf_op jit(solution)/shard_map/ppermute | solution.py:654
  759.2 4.2 all-to-all-start.1
  763.5 2.9 add_convert_fusion
  769.5 15.4 %all-to-all-done.1 = bf16[4,64,1664]{2,1,0:T(8,128)(2,1)} async-done(((bf16[4,64,1664]{2,1,0:T(8,128)(2,1)}), bf16[4,64,1664]{2,1,0:T(8,128)(2,1)}, u32[]{:S(2)}, u32[]{:S(2)}) %all-to-all-start.1) | async-done | bytes 852000 | tf_op jit(solution)/shard_map/all_to_all | solution.py:1075
  789.0 18.3 %collective-permute-done.52 = bf16[256,2048]{1,0:T(8,128)(2,1)} collective-permute-done((bf16[256,2048]{1,0:T(8,128)(2,1)}, bf16[256,2048]{1,0:T(8,128)(2,1)}, u32[]{:S(2)}, u32[]{:S(2)}) %collective-permute-start.52) | collective-permute-done | bytes 1048608 | tf_op jit(solution)/shard_map/ppermute | solution.py:618
  809.9 4.5 collective-permute-done.60.refs_2_
  816.9 5.0 fusion.13
  821.9 20.0 %collective-permute-done.62.refs_4_ = bf16[64,8320]{1,0:T(8,128)(2,1)} collective-permute-done((bf16[64,8320]{1,0:T(8,128)(2,1)S(1)}, bf16[64,8320]{1,0:T(8,128)(2,1)}, u32[]{:S(2)}, u32[]{:S(2)}) %collective-permute-start.62) | collective-permute-done | bytes 1064992 | tf_op jit(solution)/shard_map/ppermute | solution.py:654
  841.9 3.8 maximum_convert_fusion.1
  845.8 3.8 maximum_convert_fusion
  850.7 3.9 maximum_convert_fusion.2
  854.6 20.7 %collective-permute-done.64.refs_6_ = bf16[64,8320]{1,0:T(8,128)(2,1)} collective-permute-done((bf16[64,8320]{1,0:T(8,128)(2,1)}, bf16[64,8320]{1,0:T(8,128)(2,1)}, u32[]{:S(2)}, u32[]{:S(2)}) %collective-permute-start.64) | collective-permute-done | bytes 1064992 | tf_op jit(solution)/shard_map/ppermute | solution.py:654
  876.5 12.0 %shard_map.287 = (f32[512,2048]{1,0:T(8,128)}, f32[512,2048]{1,0:T(8,128)}, f32[512,2048]{1,0:T(8,128)}, f32[512,2048]{1,0:T(8,128)}, f32[512,128]{1,0:T(8,128)S(1)}) custom-call(s32[7]{0:T(128)S(1)} %stack.196.ids_ref, bf16[512,2048]{1,0:T(8,128)(2,1)} %wq_ref.3, bf16[512,2048]{1,0:T(8,128)(2,1)} %wk_ref.3, bf16[512,2048]{1,0:T(8,128)(2,1)} %wv_ref.3, ...), custom_call_target="tpu_custom_call" | custom-call | bytes 27525120 | tf_op jit(solution)/shard_map/pallas_call | solution.py:742
  888.5 9.8 %collective-permute-done.66.refs_0_ = bf16[64,8320]{1,0:T(8,128)(2,1)} collective-permute-done((bf16[64,8320]{1,0:T(8,128)(2,1)}, bf16[64,8320]{1,0:T(8,128)(2,1)}, u32[]{:S(2)}, u32[]{:S(2)}) %collective-permute-start.66) | collective-permute-done | bytes 1064992 | tf_op jit(solution)/shard_map/ppermute | solution.py:650
  898.3 3.0 shard_map.288
  (428 shorter events, 180.7 us)
Async XLA Ops:
  7.2 287.5 %all-gather.4.cloned.1.call-start = ((), (), s32[]{:S(2)}) async-start(), calls=%async_computation.8 | async-start | bytes 10485760 | tf_op jit(solution)/shard_map/all_gather | solution.py:805
  7.2 28.5 %collective-permute-start.16 = (bf16[256,2048]{1,0:T(8,128)(2,1)}, bf16[256,2048]{1,0:T(8,128)(2,1)S(1)}, u32[]{:S(2)}, u32[]{:S(2)}) collective-permute-start(bf16[256,2048]{1,0:T(8,128)(2,1)} %refs_4_.1), channel_id=1, source_target_pairs={{0,8},{4,12},{8,16},{12,20},{16,24},{20,28},{24,0},{28,4},{1,9},{5... | collective-permute-start | bytes 3145736 | tf_op jit(solution)/shard_map/ppermute | solution.py:654
  10.3 25.4 %collective-permute-start.17 = (bf16[256,2048]{1,0:T(8,128)(2,1)}, bf16[256,2048]{1,0:T(8,128)(2,1)}, u32[]{:S(2)}, u32[]{:S(2)}) collective-permute-start(bf16[256,2048]{1,0:T(8,128)(2,1)} %refs_4_.1), channel_id=1, source_target_pairs={{0,4},{4,0},{8,12},{12,8},{16,20},{20,16},{24,28},{28,24},{1,5},{5... | collective-permute-start | bytes 3145736 | tf_op jit(solution)/shard_map/ppermute | solution.py:650
  11.8 33.0 %collective-permute-start.9 = (bf16[256,2048]{1,0:T(8,128)(2,1)}, bf16[256,2048]{1,0:T(8,128)(2,1)}, u32[]{:S(2)}, u32[]{:S(2)}) collective-permute-start(bf16[256,2048]{1,0:T(8,128)(2,1)} %refs_0_.1), channel_id=1, source_target_pairs={{0,2},{1,3},{2,0},{3,1},{4,6},{5,7},{6,4},{7,5},{8,10},{9,11},{10,... | collective-permute-start | bytes 3145736 | tf_op jit(solution)/shard_map/ppermute | solution.py:618
  16.3 28.5 %collective-permute-start.3 = (bf16[2,64,1536]{2,1,0:T(8,128)(2,1)}, bf16[2,64,1536]{2,1,0:T(8,128)(2,1)S(1)}, u32[]{:S(2)}, u32[]{:S(2)}) collective-permute-start(bf16[2,64,1536]{2,1,0:T(8,128)(2,1)} %shard_map.263), channel_id=1, source_target_pairs={{0,2},{1,3},{2,0},{3,1},{4,6},{5,7},{6,4},{7,5},{8,10},{9,11},{10,... | collective-permute-start | bytes 1179656 | tf_op jit(solution)/shard_map/ppermute | solution.py:618
  44.8 249.9 %all-gather.6.cloned.1.call-start = ((), (), s32[]{:S(2)}) async-start(), calls=%async_computation.9 | async-start | bytes 10485760 | tf_op jit(solution)/shard_map/all_gather | solution.py:816
  45.6 249.1 %all-gather.8.cloned.1.call-start = ((), (), s32[]{:S(2)}) async-start(), calls=%async_computation.10 | async-start | bytes 10485760 | tf_op jit(solution)/shard_map/all_gather | solution.py:868
  54.3 27.6 %collective-permute-start.1 = (bf16[512,128]{0,1:T(8,128)(2,1)S(1)}, bf16[512,128]{0,1:T(8,128)(2,1)}, u32[]{:S(2)}, u32[]{:S(2)}) collective-permute-start(bf16[512,128]{0,1:T(8,128)(2,1)S(1)} %get-tuple-element.450), channel_id=1, source_target_pairs={{0,2},{1,3},{2,0},{3,1},{4,6},{5,7},{6,4},{7,5},{8,10},{9,11},{10,... | collective-permute-start | bytes 393224 | tf_op jit(solution)/shard_map/ppermute | solution.py:618
  55.9 27.3 %collective-permute-start = (bf16[512,128]{0,1:T(8,128)(2,1)S(1)}, bf16[512,128]{0,1:T(8,128)(2,1)}, u32[]{:S(2)}, u32[]{:S(2)}) collective-permute-start(bf16[512,128]{0,1:T(8,128)(2,1)S(1)} %get-tuple-element.450), channel_id=1, source_target_pairs={{0,1},{1,0},{2,3},{3,2},{4,5},{5,4},{6,7},{7,6},{8,9},{9,8},{10,11... | collective-permute-start | bytes 393224 | tf_op jit(solution)/shard_map/ppermute | solution.py:614
  78.8 35.5 %collective-permute-start.7 = (bf16[512,1536]{1,0:T(8,128)(2,1)}, bf16[512,1536]{1,0:T(8,128)(2,1)}, u32[]{:S(2)}, u32[]{:S(2)}) collective-permute-start(bf16[512,1536]{1,0:T(8,128)(2,1)} %dynamic-slice_bitcast_fusion), channel_id=1, source_target_pairs={{0,1},{1,0},{2,3},{3,2},{4,5},{5,4},{6,7},{7,6},{8,9},{9,8},{10,11... | collective-permute-start | bytes 4718600 | tf_op jit(solution)/shard_map/ppermute | solution.py:614
  82.5 31.7 %collective-permute-start.8 = (bf16[256,2048]{1,0:T(8,128)(2,1)}, bf16[256,2048]{1,0:T(8,128)(2,1)}, u32[]{:S(2)}, u32[]{:S(2)}) collective-permute-start(bf16[256,2048]{1,0:T(8,128)(2,1)} %refs_0_.1), channel_id=1, source_target_pairs={{0,1},{1,0},{2,3},{3,2},{4,5},{5,4},{6,7},{7,6},{8,9},{9,8},{10,11... | collective-permute-start | bytes 3145736 | tf_op jit(solution)/shard_map/ppermute | solution.py:614
  82.7 31.6 %collective-permute-start.10 = (bf16[256,2048]{1,0:T(8,128)(2,1)}, bf16[256,2048]{1,0:T(8,128)(2,1)}, u32[]{:S(2)}, u32[]{:S(2)}) collective-permute-start(bf16[256,2048]{1,0:T(8,128)(2,1)} %collective-permute-done.9.refs_2_), channel_id=1, source_target_pairs={{0,1},{1,0},{2,3},{3,2},{4,5},{5,4},{6,7},{7,6},{8,9},{9,8},{10,11... | collective-permute-start | bytes 3145736 | tf_op jit(solution)/shard_map/ppermute | solution.py:614
  113.2 40.7 %collective-permute-start.18 = (bf16[256,2048]{1,0:T(8,128)(2,1)S(1)}, bf16[256,2048]{1,0:T(8,128)(2,1)S(1)}, u32[]{:S(2)}, u32[]{:S(2)}) collective-permute-start(bf16[256,2048]{1,0:T(8,128)(2,1)S(1)} %collective-permute-done.16.grad_ref.refs_6_), channel_id=1, source_target_pairs={{0,8},{4,12},{8,16},{12,20},{16,24},{20,28},{24,0},{28,4},{1,9},{5... | collective-permute-start | bytes 3145736 | tf_op jit(solution)/shard_map/ppermute | solution.py:654
  113.7 40.2 %collective-permute-start.19 = (bf16[256,2048]{1,0:T(8,128)(2,1)S(1)}, bf16[256,2048]{1,0:T(8,128)(2,1)S(1)}, u32[]{:S(2)}, u32[]{:S(2)}) collective-permute-start(bf16[256,2048]{1,0:T(8,128)(2,1)S(1)} %collective-permute-done.16.grad_ref.refs_6_), channel_id=1, source_target_pairs={{0,4},{4,0},{8,12},{12,8},{16,20},{20,16},{24,28},{28,24},{1,5},{5... | collective-permute-start | bytes 3145736 | tf_op jit(solution)/shard_map/ppermute | solution.py:650
  156.5 27.8 %collective-permute-start.23 = (bf16[256,2048]{1,0:T(8,128)(2,1)S(1)}, bf16[256,2048]{1,0:T(8,128)(2,1)}, u32[]{:S(2)}, u32[]{:S(2)}) collective-permute-start(bf16[256,2048]{1,0:T(8,128)(2,1)S(1)} %collective-permute-done.18.grad_ref.refs_4_), channel_id=1, source_target_pairs={{0,8},{4,12},{8,16},{12,20},{16,24},{20,28},{24,0},{28,4},{1,9},{5... | collective-permute-start | bytes 3145736 | tf_op jit(solution)/shard_map/ppermute | solution.py:654
  158.9 25.4 %collective-permute-start.24 = (bf16[256,2048]{1,0:T(8,128)(2,1)S(1)}, bf16[256,2048]{1,0:T(8,128)(2,1)}, u32[]{:S(2)}, u32[]{:S(2)}) collective-permute-start(bf16[256,2048]{1,0:T(8,128)(2,1)S(1)} %collective-permute-done.18.grad_ref.refs_4_), channel_id=1, source_target_pairs={{0,4},{4,0},{8,12},{12,8},{16,20},{20,16},{24,28},{28,24},{1,5},{5... | collective-permute-start | bytes 3145736 | tf_op jit(solution)/shard_map/ppermute | solution.py:650
  160.4 23.9 %collective-permute-start.20 = (bf16[256,2048]{1,0:T(8,128)(2,1)S(1)}, bf16[256,2048]{1,0:T(8,128)(2,1)S(1)}, u32[]{:S(2)}, u32[]{:S(2)}) collective-permute-start(bf16[256,2048]{1,0:T(8,128)(2,1)S(1)} %get-tuple-element.442), channel_id=1, source_target_pairs={{0,1},{1,0},{2,3},{3,2},{4,5},{5,4},{6,7},{7,6},{8,9},{9,8},{10,11... | collective-permute-start | bytes 3145736 | tf_op jit(solution)/shard_map/ppermute | solution.py:614
  160.8 25.6 %collective-permute-start.22 = (bf16[256,2048]{1,0:T(8,128)(2,1)S(1)}, bf16[256,2048]{1,0:T(8,128)(2,1)S(1)}, u32[]{:S(2)}, u32[]{:S(2)}) collective-permute-start(bf16[256,2048]{1,0:T(8,128)(2,1)S(1)} %add_convert_fusion.8), channel_id=1, source_target_pairs={{0,2},{1,3},{2,0},{3,1},{4,6},{5,7},{6,4},{7,5},{8,10},{9,11},{10,... | collective-permute-start | bytes 3145736 | tf_op jit(solution)/shard_map/ppermute | solution.py:618
  192.5 26.6 %collective-permute-start.25 = (bf16[256,2048]{1,0:T(8,128)(2,1)S(1)}, bf16[256,2048]{1,0:T(8,128)(2,1)S(1)}, u32[]{:S(2)}, u32[]{:S(2)}) collective-permute-start(bf16[256,2048]{1,0:T(8,128)(2,1)S(1)} %multiply_convert_fusion.x_ref), channel_id=1, source_target_pairs={{0,8},{4,12},{8,16},{12,20},{16,24},{20,28},{24,0},{28,4},{1,9},{5... | collective-permute-start | bytes 3145736 | tf_op jit(solution)/shard_map/ppermute | solution.py:654
  193.8 25.4 %collective-permute-start.26 = (bf16[256,2048]{1,0:T(8,128)(2,1)S(1)}, bf16[256,2048]{1,0:T(8,128)(2,1)}, u32[]{:S(2)}, u32[]{:S(2)}) collective-permute-start(bf16[256,2048]{1,0:T(8,128)(2,1)S(1)} %multiply_convert_fusion.x_ref), channel_id=1, source_target_pairs={{0,4},{4,0},{8,12},{12,8},{16,20},{20,16},{24,28},{28,24},{1,5},{5... | collective-permute-start | bytes 3145736 | tf_op jit(solution)/shard_map/ppermute | solution.py:650
  219.2 25.7 %collective-permute-start.27 = (bf16[256,2048]{1,0:T(8,128)(2,1)S(1)}, bf16[256,2048]{1,0:T(8,128)(2,1)S(1)}, u32[]{:S(2)}, u32[]{:S(2)}) collective-permute-start(bf16[256,2048]{1,0:T(8,128)(2,1)S(1)} %collective-permute-done.25.x_ref), channel_id=1, source_target_pairs={{0,8},{4,12},{8,16},{12,20},{16,24},{20,28},{24,0},{28,4},{1,9},{5... | collective-permute-start | bytes 3145736 | tf_op jit(solution)/shard_map/ppermute | solution.py:654
  219.9 25.0 %collective-permute-start.28 = (bf16[256,2048]{1,0:T(8,128)(2,1)S(1)}, bf16[256,2048]{1,0:T(8,128)(2,1)}, u32[]{:S(2)}, u32[]{:S(2)}) collective-permute-start(bf16[256,2048]{1,0:T(8,128)(2,1)S(1)} %collective-permute-done.25.x_ref), channel_id=1, source_target_pairs={{0,4},{4,0},{8,12},{12,8},{16,20},{20,16},{24,28},{28,24},{1,5},{5... | collective-permute-start | bytes 3145736 | tf_op jit(solution)/shard_map/ppermute | solution.py:650
  244.9 24.9 %collective-permute-start.29 = (bf16[256,2048]{1,0:T(8,128)(2,1)S(1)}, bf16[256,2048]{1,0:T(8,128)(2,1)}, u32[]{:S(2)}, u32[]{:S(2)}) collective-permute-start(bf16[256,2048]{1,0:T(8,128)(2,1)S(1)} %collective-permute-done.27.x_ref), channel_id=1, source_target_pairs={{0,8},{4,12},{8,16},{12,20},{16,24},{20,28},{24,0},{28,4},{1,9},{5... | collective-permute-start | bytes 3145736 | tf_op jit(solution)/shard_map/ppermute | solution.py:654
  244.9 24.9 %collective-permute-start.30 = (bf16[256,2048]{1,0:T(8,128)(2,1)S(1)}, bf16[256,2048]{1,0:T(8,128)(2,1)}, u32[]{:S(2)}, u32[]{:S(2)}) collective-permute-start(bf16[256,2048]{1,0:T(8,128)(2,1)S(1)} %collective-permute-done.27.x_ref), channel_id=1, source_target_pairs={{0,4},{4,0},{8,12},{12,8},{16,20},{20,16},{24,28},{28,24},{1,5},{5... | collective-permute-start | bytes 3145736 | tf_op jit(solution)/shard_map/ppermute | solution.py:650
  269.8 23.2 %collective-permute-start.31 = (bf16[256,2048]{1,0:T(8,128)(2,1)}, bf16[256,2048]{1,0:T(8,128)(2,1)}, u32[]{:S(2)}, u32[]{:S(2)}) collective-permute-start(bf16[256,2048]{1,0:T(8,128)(2,1)} %collective-permute-done.29.x_ref), channel_id=1, source_target_pairs={{0,4},{4,0},{8,12},{12,8},{16,20},{20,16},{24,28},{28,24},{1,5},{5... | collective-permute-start | bytes 3145736 | tf_op jit(solution)/shard_map/ppermute | solution.py:650
  293.0 61.6 %collective-permute-start.32 = (bf16[256,2048]{1,0:T(8,128)(2,1)}, bf16[256,2048]{1,0:T(8,128)(2,1)}, u32[]{:S(2)}, u32[]{:S(2)}) collective-permute-start(bf16[256,2048]{1,0:T(8,128)(2,1)} %collective-permute-done.23.grad_ref.refs_6_), channel_id=1, source_target_pairs={{0,4},{4,0},{8,12},{12,8},{16,20},{20,16},{24,28},{28,24},{1,5},{5... | collective-permute-start | bytes 3145736 | tf_op jit(solution)/shard_map/ppermute | solution.py:650
  354.3 58.2 %collective-permute-start.33 = (bf16[256,2048]{1,0:T(8,128)(2,1)}, bf16[256,2048]{1,0:T(8,128)(2,1)}, u32[]{:S(2)}, u32[]{:S(2)}) collective-permute-start(bf16[256,2048]{1,0:T(8,128)(2,1)} %get-tuple-element.217), channel_id=1, source_target_pairs={{0,4},{4,0},{8,12},{12,8},{16,20},{20,16},{24,28},{28,24},{1,5},{5... | collective-permute-start | bytes 3145736 | tf_op jit(solution)/shard_map/ppermute | solution.py:650
  360.0 52.5 %collective-permute-start.34 = (bf16[256,2048]{1,0:T(8,128)(2,1)}, bf16[256,2048]{1,0:T(8,128)(2,1)}, u32[]{:S(2)}, u32[]{:S(2)}) collective-permute-start(bf16[256,2048]{1,0:T(8,128)(2,1)} %get-tuple-element.240), channel_id=1, source_target_pairs={{0,4},{4,0},{8,12},{12,8},{16,20},{20,16},{24,28},{28,24},{1,5},{5... | collective-permute-start | bytes 3145736 | tf_op jit(solution)/shard_map/ppermute | solution.py:650
  412.2 36.6 %collective-permute-start.35 = (bf16[256,2048]{1,0:T(8,128)(2,1)}, bf16[256,2048]{1,0:T(8,128)(2,1)}, u32[]{:S(2)}, u32[]{:S(2)}) collective-permute-start(bf16[256,2048]{1,0:T(8,128)(2,1)} %get-tuple-element.245), channel_id=1, source_target_pairs={{0,4},{4,0},{8,12},{12,8},{16,20},{20,16},{24,28},{28,24},{1,5},{5... | collective-permute-start | bytes 3145736 | tf_op jit(solution)/shard_map/ppermute | solution.py:650
  415.3 35.5 %collective-permute-start.36 = (bf16[256,2048]{1,0:T(8,128)(2,1)}, bf16[256,2048]{1,0:T(8,128)(2,1)}, u32[]{:S(2)}, u32[]{:S(2)}) collective-permute-start(bf16[256,2048]{1,0:T(8,128)(2,1)} %add_convert_fusion.7), channel_id=1, source_target_pairs={{0,8},{4,12},{8,16},{12,20},{16,24},{20,28},{24,0},{28,4},{1,9},{5... | collective-permute-start | bytes 3145736 | tf_op jit(solution)/shard_map/ppermute | solution.py:654
  442.5 32.8 %all-to-all-start = ((f32[8,2,256]{2,1,0:T(2,128)}), f32[8,2,256]{2,1,0:T(2,128)S(1)}, u32[]{:S(2)}, u32[]{:S(2)}) async-start(f32[8,2,256]{2,1,0:T(2,128)} %scatter_fusion.1), calls=%async_computation | async-start | bytes 32768 | tf_op jit(solution)/shard_map/all_to_all | solution.py:1002
  448.8 393.2 %reduce-scatter.11.cloned.1.call-start = ((), (), s32[]{:S(2)}) async-start(), calls=%async_computation.13 | async-start | bytes 5242880 | tf_op jit(solution)/shard_map/reduce_scatter | solution.py:964
  448.8 26.6 %collective-permute-start.38 = (bf16[256,2048]{1,0:T(8,128)(2,1)}, bf16[256,2048]{1,0:T(8,128)(2,1)}, u32[]{:S(2)}, u32[]{:S(2)}) collective-permute-start(bf16[256,2048]{1,0:T(8,128)(2,1)} %copy-done.52), channel_id=1, source_target_pairs={{0,4},{4,0},{8,12},{12,8},{16,20},{20,16},{24,28},{28,24},{1,5},{5... | collective-permute-start | bytes 3145736 | tf_op jit(solution)/shard_map/ppermute | solution.py:650
  475.4 24.9 %collective-permute-start.40 = (bf16[256,2048]{1,0:T(8,128)(2,1)}, bf16[256,2048]{1,0:T(8,128)(2,1)}, u32[]{:S(2)}, u32[]{:S(2)}) collective-permute-start(bf16[256,2048]{1,0:T(8,128)(2,1)} %copy-done.51), channel_id=1, source_target_pairs={{0,4},{4,0},{8,12},{12,8},{16,20},{20,16},{24,28},{28,24},{1,5},{5... | collective-permute-start | bytes 3145736 | tf_op jit(solution)/shard_map/ppermute | solution.py:650
  506.2 27.0 %collective-permute-start.42 = (bf16[256,2048]{1,0:T(8,128)(2,1)}, bf16[256,2048]{1,0:T(8,128)(2,1)}, u32[]{:S(2)}, u32[]{:S(2)}) collective-permute-start(bf16[256,2048]{1,0:T(8,128)(2,1)} %fusion.31), channel_id=1, source_target_pairs={{0,2},{1,3},{2,0},{3,1},{4,6},{5,7},{6,4},{7,5},{8,10},{9,11},{10,... | collective-permute-start | bytes 3145736 | tf_op jit(solution)/shard_map/ppermute | solution.py:618
  506.8 26.4 %collective-permute-start.41 = (bf16[256,2048]{1,0:T(8,128)(2,1)}, bf16[256,2048]{1,0:T(8,128)(2,1)}, u32[]{:S(2)}, u32[]{:S(2)}) collective-permute-start(bf16[256,2048]{1,0:T(8,128)(2,1)} %fusion.31), channel_id=1, source_target_pairs={{0,1},{1,0},{2,3},{3,2},{4,5},{5,4},{6,7},{7,6},{8,9},{9,8},{10,11... | collective-permute-start | bytes 3145736 | tf_op jit(solution)/shard_map/ppermute | solution.py:614
  542.2 299.7 %reduce-scatter.13.cloned.1.call-start = ((), (), s32[]{:S(2)}) async-start(), calls=%async_computation.14 | async-start | bytes 5242880 | tf_op jit(solution)/shard_map/reduce_scatter | solution.py:964
  542.8 303.0 %reduce-scatter.7.cloned.1.call-start = ((), (), s32[]{:S(2)}) async-start(), calls=%async_computation.11 | async-start | bytes 5242880 | tf_op jit(solution)/shard_map/reduce_scatter | solution.py:964
  543.4 302.4 %reduce-scatter.9.cloned.1.call-start = ((), (), s32[]{:S(2)}) async-start(), calls=%async_computation.12 | async-start | bytes 5242880 | tf_op jit(solution)/shard_map/reduce_scatter | solution.py:964
  544.1 306.6 %reduce-scatter.15.cloned.1.call-start = ((), (), s32[]{:S(2)}) async-start(), calls=%async_computation.15 | async-start | bytes 5242880 | tf_op jit(solution)/shard_map/reduce_scatter | solution.py:964
  547.1 27.3 %collective-permute-start.45 = (bf16[256,2048]{1,0:T(8,128)(2,1)}, bf16[256,2048]{1,0:T(8,128)(2,1)}, u32[]{:S(2)}, u32[]{:S(2)}) collective-permute-start(bf16[256,2048]{1,0:T(8,128)(2,1)} %add_convert_fusion.4), channel_id=1, source_target_pairs={{0,8},{4,12},{8,16},{12,20},{16,24},{20,28},{24,0},{28,4},{1,9},{5... | collective-permute-start | bytes 3145736 | tf_op jit(solution)/shard_map/ppermute | solution.py:654
  548.6 25.9 %collective-permute-start.44 = (bf16[256,2048]{1,0:T(8,128)(2,1)}, bf16[256,2048]{1,0:T(8,128)(2,1)}, u32[]{:S(2)}, u32[]{:S(2)}) collective-permute-start(bf16[256,2048]{1,0:T(8,128)(2,1)} %get-tuple-element.287), channel_id=1, source_target_pairs={{0,4},{4,0},{8,12},{12,8},{16,20},{20,16},{24,28},{28,24},{1,5},{5... | collective-permute-start | bytes 3145736 | tf_op jit(solution)/shard_map/ppermute | solution.py:650
  577.9 46.6 %collective-permute-start.47 = (bf16[256,2048]{1,0:T(8,128)(2,1)}, bf16[256,2048]{1,0:T(8,128)(2,1)}, u32[]{:S(2)}, u32[]{:S(2)}) collective-permute-start(bf16[256,2048]{1,0:T(8,128)(2,1)} %add_convert_fusion.3), channel_id=1, source_target_pairs={{0,8},{4,12},{8,16},{12,20},{16,24},{20,28},{24,0},{28,4},{1,9},{5... | collective-permute-start | bytes 3145736 | tf_op jit(solution)/shard_map/ppermute | solution.py:654
  577.9 46.6 %collective-permute-start.46 = (bf16[256,2048]{1,0:T(8,128)(2,1)}, bf16[256,2048]{1,0:T(8,128)(2,1)}, u32[]{:S(2)}, u32[]{:S(2)}) collective-permute-start(bf16[256,2048]{1,0:T(8,128)(2,1)} %get-tuple-element.289), channel_id=1, source_target_pairs={{0,4},{4,0},{8,12},{12,8},{16,20},{20,16},{24,28},{28,24},{1,5},{5... | collective-permute-start | bytes 3145736 | tf_op jit(solution)/shard_map/ppermute | solution.py:650
  614.1 236.6 %reduce-scatter.17.cloned.1.call-start = ((), (), s32[]{:S(2)}) async-start(), calls=%async_computation.16 | async-start | bytes 5242880 | tf_op jit(solution)/shard_map/reduce_scatter | solution.py:964
  640.6 25.8 %collective-permute-start.53 = (bf16[4,64,2176]{2,1,0:T(8,128)(2,1)}, bf16[4,64,2176]{2,1,0:T(8,128)(2,1)}, u32[]{:S(2)}, u32[]{:S(2)}) collective-permute-start(bf16[4,64,2176]{2,1,0:T(8,128)(2,1)} %get-tuple-element.436), channel_id=1, source_target_pairs={{0,4},{4,0},{8,12},{12,8},{16,20},{20,16},{24,28},{28,24},{1,5},{5... | collective-permute-start | bytes 3342344 | tf_op jit(solution)/shard_map/ppermute | solution.py:650
  669.3 26.7 %collective-permute-start.55 = (bf16[4,64,2176]{2,1,0:T(8,128)(2,1)}, bf16[4,64,2176]{2,1,0:T(8,128)(2,1)}, u32[]{:S(2)}, u32[]{:S(2)}) collective-permute-start(bf16[4,64,2176]{2,1,0:T(8,128)(2,1)} %fusion.6), channel_id=1, source_target_pairs={{0,8},{4,12},{8,16},{12,20},{16,24},{20,28},{24,0},{28,4},{1,9},{5... | collective-permute-start | bytes 3342344 | tf_op jit(solution)/shard_map/ppermute | solution.py:654
  670.1 25.9 %collective-permute-start.54 = (bf16[4,64,2176]{2,1,0:T(8,128)(2,1)}, bf16[4,64,2176]{2,1,0:T(8,128)(2,1)}, u32[]{:S(2)}, u32[]{:S(2)}) collective-permute-start(bf16[4,64,2176]{2,1,0:T(8,128)(2,1)} %get-tuple-element.305), channel_id=1, source_target_pairs={{0,4},{4,0},{8,12},{12,8},{16,20},{20,16},{24,28},{28,24},{1,5},{5... | collective-permute-start | bytes 3342344 | tf_op jit(solution)/shard_map/ppermute | solution.py:650
  699.3 26.1 %collective-permute-start.57 = (bf16[4,64,2176]{2,1,0:T(8,128)(2,1)}, bf16[4,64,2176]{2,1,0:T(8,128)(2,1)}, u32[]{:S(2)}, u32[]{:S(2)}) collective-permute-start(bf16[4,64,2176]{2,1,0:T(8,128)(2,1)} %fusion.5), channel_id=1, source_target_pairs={{0,8},{4,12},{8,16},{12,20},{16,24},{20,28},{24,0},{28,4},{1,9},{5... | collective-permute-start | bytes 3342344 | tf_op jit(solution)/shard_map/ppermute | solution.py:654
  699.3 26.1 %collective-permute-start.56 = (bf16[4,64,2176]{2,1,0:T(8,128)(2,1)}, bf16[4,64,2176]{2,1,0:T(8,128)(2,1)}, u32[]{:S(2)}, u32[]{:S(2)}) collective-permute-start(bf16[4,64,2176]{2,1,0:T(8,128)(2,1)} %get-tuple-element.307), channel_id=1, source_target_pairs={{0,4},{4,0},{8,12},{12,8},{16,20},{20,16},{24,28},{28,24},{1,5},{5... | collective-permute-start | bytes 3342344 | tf_op jit(solution)/shard_map/ppermute | solution.py:650
  727.7 27.8 %collective-permute-start.59 = (bf16[4,64,2176]{2,1,0:T(8,128)(2,1)S(1)}, bf16[4,64,2176]{2,1,0:T(8,128)(2,1)S(1)}, u32[]{:S(2)}, u32[]{:S(2)}) collective-permute-start(bf16[4,64,2176]{2,1,0:T(8,128)(2,1)S(1)} %fusion.3), channel_id=1, source_target_pairs={{0,8},{4,12},{8,16},{12,20},{16,24},{20,28},{24,0},{28,4},{1,9},{5... | collective-permute-start | bytes 3342344 | tf_op jit(solution)/shard_map/ppermute | solution.py:654
  728.0 27.6 %collective-permute-start.58 = (bf16[4,64,2176]{2,1,0:T(8,128)(2,1)S(1)}, bf16[4,64,2176]{2,1,0:T(8,128)(2,1)S(1)}, u32[]{:S(2)}, u32[]{:S(2)}) collective-permute-start(bf16[4,64,2176]{2,1,0:T(8,128)(2,1)S(1)} %copy-done.78), channel_id=1, source_target_pairs={{0,4},{4,0},{8,12},{12,8},{16,20},{20,16},{24,28},{28,24},{1,5},{5... | collective-permute-start | bytes 3342344 | tf_op jit(solution)/shard_map/ppermute | solution.py:650
  744.7 42.6 %collective-permute-start.49 = (bf16[256,2048]{1,0:T(8,128)(2,1)}, bf16[256,2048]{1,0:T(8,128)(2,1)}, u32[]{:S(2)}, u32[]{:S(2)}) collective-permute-start(bf16[256,2048]{1,0:T(8,128)(2,1)} %add_convert_fusion.2), channel_id=1, source_target_pairs={{0,8},{4,12},{8,16},{12,20},{16,24},{20,28},{24,0},{28,4},{1,9},{5... | collective-permute-start | bytes 3145736 | tf_op jit(solution)/shard_map/ppermute | solution.py:654
  744.7 44.3 %collective-permute-start.48 = (bf16[256,2048]{1,0:T(8,128)(2,1)}, bf16[256,2048]{1,0:T(8,128)(2,1)}, u32[]{:S(2)}, u32[]{:S(2)}) collective-permute-start(bf16[256,2048]{1,0:T(8,128)(2,1)} %get-tuple-element.296), channel_id=1, source_target_pairs={{0,4},{4,0},{8,12},{12,8},{16,20},{20,16},{24,28},{28,24},{1,5},{5... | collective-permute-start | bytes 3145736 | tf_op jit(solution)/shard_map/ppermute | solution.py:650
  755.6 33.4 %collective-permute-start.50 = (bf16[256,2048]{1,0:T(8,128)(2,1)}, bf16[256,2048]{1,0:T(8,128)(2,1)}, u32[]{:S(2)}, u32[]{:S(2)}) collective-permute-start(bf16[256,2048]{1,0:T(8,128)(2,1)} %get-tuple-element.440), channel_id=1, source_target_pairs={{0,1},{1,0},{2,3},{3,2},{4,5},{5,4},{6,7},{7,6},{8,9},{9,8},{10,11... | collective-permute-start | bytes 3145736 | tf_op jit(solution)/shard_map/ppermute | solution.py:614
  759.2 25.7 %all-to-all-start.1 = ((bf16[4,64,1664]{2,1,0:T(8,128)(2,1)}), bf16[4,64,1664]{2,1,0:T(8,128)(2,1)}, u32[]{:S(2)}, u32[]{:S(2)}) async-start(bf16[4,64,1664]{2,1,0:T(8,128)(2,1)} %slice.114), calls=%async_computation.1 | async-start | bytes 1703936 | tf_op jit(solution)/shard_map/all_to_all | solution.py:1075
  766.4 40.9 %collective-permute-start.52 = (bf16[256,2048]{1,0:T(8,128)(2,1)}, bf16[256,2048]{1,0:T(8,128)(2,1)}, u32[]{:S(2)}, u32[]{:S(2)}) collective-permute-start(bf16[256,2048]{1,0:T(8,128)(2,1)} %add_convert_fusion), channel_id=1, source_target_pairs={{0,2},{1,3},{2,0},{3,1},{4,6},{5,7},{6,4},{7,5},{8,10},{9,11},{10,... | collective-permute-start | bytes 3145736 | tf_op jit(solution)/shard_map/ppermute | solution.py:618
  787.2 27.2 %collective-permute-start.60 = (bf16[64,8320]{1,0:T(8,128)(2,1)S(1)}, bf16[64,8320]{1,0:T(8,128)(2,1)S(1)}, u32[]{:S(2)}, u32[]{:S(2)}) collective-permute-start(bf16[64,8320]{1,0:T(8,128)(2,1)S(1)} %pad_maximum_fusion.2.refs_0_), channel_id=1, source_target_pairs={{0,8},{4,12},{8,16},{12,20},{16,24},{20,28},{24,0},{28,4},{1,9},{5... | collective-permute-start | bytes 3194888 | tf_op jit(solution)/shard_map/ppermute | solution.py:654
  787.3 27.2 %collective-permute-start.61 = (bf16[64,8320]{1,0:T(8,128)(2,1)S(1)}, bf16[64,8320]{1,0:T(8,128)(2,1)S(1)}, u32[]{:S(2)}, u32[]{:S(2)}) collective-permute-start(bf16[64,8320]{1,0:T(8,128)(2,1)S(1)} %pad_maximum_fusion.2.refs_0_), channel_id=1, source_target_pairs={{0,4},{4,0},{8,12},{12,8},{16,20},{20,16},{24,28},{28,24},{1,5},{5... | collective-permute-start | bytes 3194888 | tf_op jit(solution)/shard_map/ppermute | solution.py:650
  815.5 26.4 %collective-permute-start.62 = (bf16[64,8320]{1,0:T(8,128)(2,1)S(1)}, bf16[64,8320]{1,0:T(8,128)(2,1)}, u32[]{:S(2)}, u32[]{:S(2)}) collective-permute-start(bf16[64,8320]{1,0:T(8,128)(2,1)S(1)} %collective-permute-done.60.refs_2_), channel_id=1, source_target_pairs={{0,8},{4,12},{8,16},{12,20},{16,24},{20,28},{24,0},{28,4},{1,9},{5... | collective-permute-start | bytes 3194888 | tf_op jit(solution)/shard_map/ppermute | solution.py:654
  815.5 26.4 %collective-permute-start.63 = (bf16[64,8320]{1,0:T(8,128)(2,1)S(1)}, bf16[64,8320]{1,0:T(8,128)(2,1)}, u32[]{:S(2)}, u32[]{:S(2)}) collective-permute-start(bf16[64,8320]{1,0:T(8,128)(2,1)S(1)} %collective-permute-done.60.refs_2_), channel_id=1, source_target_pairs={{0,4},{4,0},{8,12},{12,8},{16,20},{20,16},{24,28},{28,24},{1,5},{5... | collective-permute-start | bytes 3194888 | tf_op jit(solution)/shard_map/ppermute | solution.py:650
  849.6 25.7 %collective-permute-start.64 = (bf16[64,8320]{1,0:T(8,128)(2,1)}, bf16[64,8320]{1,0:T(8,128)(2,1)}, u32[]{:S(2)}, u32[]{:S(2)}) collective-permute-start(bf16[64,8320]{1,0:T(8,128)(2,1)} %collective-permute-done.62.refs_4_), channel_id=1, source_target_pairs={{0,8},{4,12},{8,16},{12,20},{16,24},{20,28},{24,0},{28,4},{1,9},{5... | collective-permute-start | bytes 3194888 | tf_op jit(solution)/shard_map/ppermute | solution.py:654
  849.6 25.7 %collective-permute-start.65 = (bf16[64,8320]{1,0:T(8,128)(2,1)}, bf16[64,8320]{1,0:T(8,128)(2,1)}, u32[]{:S(2)}, u32[]{:S(2)}) collective-permute-start(bf16[64,8320]{1,0:T(8,128)(2,1)} %collective-permute-done.62.refs_4_), channel_id=1, source_target_pairs={{0,4},{4,0},{8,12},{12,8},{16,20},{20,16},{24,28},{28,24},{1,5},{5... | collective-permute-start | bytes 3194888 | tf_op jit(solution)/shard_map/ppermute | solution.py:650
  875.3 23.0 %collective-permute-start.66 = (bf16[64,8320]{1,0:T(8,128)(2,1)}, bf16[64,8320]{1,0:T(8,128)(2,1)}, u32[]{:S(2)}, u32[]{:S(2)}) collective-permute-start(bf16[64,8320]{1,0:T(8,128)(2,1)} %collective-permute-done.64.refs_6_), channel_id=1, source_target_pairs={{0,4},{4,0},{8,12},{12,8},{16,20},{20,16},{24,28},{28,24},{1,5},{5... | collective-permute-start | bytes 3194888 | tf_op jit(solution)/shard_map/ppermute | solution.py:650
  (108 other events, 1402.3 us)
Sparse Core Ops, SparseCore 0:
  45.0 60.3 all-gather.3
  106.9 58.2 all-gather.5
  189.1 58.0 all-gather.7
  542.3 43.5 reduce-scatter.10
  589.0 44.5 reduce-scatter.12
  636.5 44.5 reduce-scatter.6
  684.4 44.5 reduce-scatter.8
  732.0 53.6 reduce-scatter.14
  788.9 48.2 reduce-scatter.16

commit v5 on v4

--- a/solution.py
+++ b/solution.py
@@ -293,7 +293,7 @@
         ],
         scratch_shapes=[pltpu.VMEM((length, HD), BF)] * 2 + [pltpu.VMEM((length, HD), F32)] * 2,
         input_output_aliases={} if held is None else {8: 0},
-        compiler_params=params(48),
+        compiler_params=params(58),
         cost_estimate=cost(40 * heads * length * length * HD, qkv.size * 3, heads * length * length),
     )(qkv, grad_o, *attn_args, *(() if held is None else (held,)))
 
@@ -664,6 +664,11 @@
     return together(turn_z(value, count), swap_y(value, count))
 
 
+def last_crossing(held, before, count):
+    half = held.shape[0] // 2
+    return jnp.concatenate(together(swap_y(held[:half], count), turn_z(before[half:], count)), axis=0)
+
+
 def rep_gather(value, count, ties=None):
     blocks = []
     held = value
@@ -672,23 +677,35 @@
         if k < count // 2 - 1:
             nexts, crossed = together(turn_z(held, count), swap_y(held, count))
         else:
-            nexts, crossed = None, swap_y(held, count)
+            nexts, crossed = None, last_crossing(held, blocks[-1], count)
         blocks += [held, crossed]
         held = nexts
     return blocks
 
 
 class RepReduce:
-    def __init__(self, blocks, count, *ready):
-        self.blocks, self.count = blocks, count
+    def __init__(self, blocks, count, *ready, split=False):
+        self.blocks, self.count = list(blocks), count
         self.order = list(range(2, count // 2)) + [0]
-        self.arrived = (swap_y(after(blocks[3], *ready), count),)
+        self.half = blocks[3].shape[0] // 2 if split else None
+        first = after(blocks[3], *ready)
+        if split:
+            self.arrived = together(
+                swap_y(first[: self.half], count), turn_z(first[self.half :], count)
+            )
+        else:
+            self.arrived = (swap_y(first, count),)
         self.total = None
         self.k = 1
 
     def step(self, *ready):
         arrived = together(*self.arrived, *ready)[: len(self.arrived)]
-        total = added(self.blocks[2 * self.k], *arrived)
+        if self.half is not None and self.k == 1:
+            half, (near, far) = self.half, arrived
+            total = self.blocks[2].at[:half].add(near)
+            self.blocks[5] = self.blocks[5].at[half:].add(far)
+        else:
+            total = added(self.blocks[2 * self.k], *arrived)
         if not self.order:
             return total
         self.k = self.order.pop(0)
@@ -927,17 +944,18 @@
         )
         return parts, dgate
 
-    held, crossed, ready = mid_b, None, ()
+    held, crossed = mid_b, None
     for k in range(planes):
-        held = after(held, *ready)
+        if k > 0:
+            held, x = together(held, picked[-1][0])
+            picked[-1] = (x,) + picked[-1][1:]
         if k < planes - 1:
             nexts, crossing = turn_and_cross(held, rep_count)
         else:
-            nexts, crossing = None, swap_y(held, rep_count)
+            nexts, crossing = None, last_crossing(held, crossed, rep_count)
         if k > 0:
             pick_next(crossed)
         pick_next(held)
-        ready = (picked[-1][0],)
         held, crossed = nexts, crossing
     grad_blocks.append(swap_y(after(grad_held, crossed), rep_count))
     grad_parts, result_parts, dgate_parts = [], [], []
@@ -977,9 +995,13 @@
         )[0]
 
     arrived = after(arrived, *result_parts, *dgate_parts)
+    dgates = jnp.swapaxes(jnp.concatenate(dgate_parts), 1, 2)
+    dgates = jnp.zeros_like(dgates).at[order_array].set(dgates)
     made = []
     for k in range(2, planes):
         total = added(grad_parts[2 * k], arrived, total).astype(BF)
+        if k == 2:
+            total, dgates = together(total, dgates)
         if k < planes - 1:
             total, arrived = together(
                 turn_z(total, rep_count), swap_y(after(grad_parts[2 * k + 3], arrived), rep_count)
@@ -997,8 +1019,6 @@
     total = after(total, *results_sum.arrived)
     grad_mid_moe = added(grad_parts[0], cross_zero, total)
 
-    dgates = jnp.swapaxes(jnp.concatenate(dgate_parts), 1, 2)
-    dgates = jnp.zeros_like(dgates).at[order_array].set(dgates)
     dgates = lax.all_to_all(dgates, "rep", split_axis=0, concat_axis=0, tiled=True)
     dgates = dgates.reshape(experts, rows_count).T
     logits = dot(mid_b, full_router)
@@ -1023,7 +1043,8 @@
     while len(results_sum.order) > 2:
         results_sum.step()
     downs = [down_grads(j, grad_state_b) for j in range(local_experts)]
-    far_state = together(far_state, *results_sum.arrived, *downs)[0]
+    far_state, *both = together(far_state, *results_sum.arrived, *downs)
+    results_sum.arrived, downs = tuple(both[:2]), both[2:]
     state_blocks = [grad_state_b, swap_core(grad_state_b), far_state, swap_core(far_state)]
     grad_state_all = jnp.concatenate(state_blocks, axis=0)
     grad_mixed = dot_t(grad_state_all, w_out).astype(BF)
@@ -1058,7 +1079,7 @@
     extra_parts = extras.reshape(shard_count, rep_count, part, -1)
     to_sum = jnp.concatenate([column_parts, extra_parts, out_columns], axis=3)
     to_sum = [lax.dynamic_index_in_dim(to_sum, r, axis=1, keepdims=False) for r in order]
-    sums = RepReduce(to_sum, rep_count)
+    sums = RepReduce(to_sum, rep_count, split=True)
     expert_sum = None
     while expert_sum is None:
         expert_sum = results_sum.step()

time: 917 us -> 877 us (0.956)
  waiting for transfers between devices: 329 us -> 291 us
  local copies, waits for them, and re-layouts: 74.9 us -> 88 us
    ppermute x21 -> x25, waiting for transfers between devices: 227 us -> 176 us  [turn_z(): return lax.ppermute(value, 'rep', ring_next(count))]
    reduce_scatter x6, waiting for transfers between devices: 0.01 us -> 17 us  [owned_part(): return lax.psum_scatter(grad, 'shard', scatter_dimension=0, tiled=True)]
    ppermute x6, waiting for transfers between devices: 29.5 us -> 44.5 us  [swap_x(): return lax.ppermute(value, 'shard', [(i, i ^ 2) for i in range(4)])]
    slice x0 -> x7, local copies, waits for them, and re-layouts: none -> 9.79 us  [the longest x3 4.37 us: last_crossing(): held[:half]]
    ppermute x28, waiting for transfers between devices: 49.6 us -> 40 us  [swap_y(): return lax.ppermute(value, 'rep', [(i, i ^ 1) for i in range(count)])]
    ppermute x21 -> x25, starting transfers between devices: 16.5 us -> 19 us  [turn_z(): return lax.ppermute(value, 'rep', ring_next(count))]
    unnamed x194 -> x208, local copies, waits for them, and re-layouts: 47.3 us -> 49.6 us
  transfers between devices with their start and end apart: 78 -> 82, of which waited for: 24 -> 28; matrix products, arithmetic and copies ran while one was open for 15% -> 17% of each run, Pallas kernels for 34% -> 34%
where the time goes in v5:
time: 877 us; the launch traced here: 871 us
  Pallas kernels  300 us (34%)
  waiting for transfers between devices  291 us (33%)
  local copies, waits for them, and re-layouts  88 us (10%)
  other arithmetic  77.7 us (9%)
  starting transfers between devices  61.5 us (7%)
  matrix products  37.2 us (4%)
  between operations  15.8 us (2%)
    ppermute x25, waiting for transfers between devices, turn_z(): return lax.ppermute(value, 'rep', ring_next(count))  176 us
    pallas_call x2, Pallas kernels, run_experts(): pl.pallas_call(functools.partial(expert_body, rows // 2), grid=(experts,...  83.6 us
    pallas_call x4, Pallas kernels, weight_grads(): pl.pallas_call(functools.partial(weight_grads_body, groups, count), grid=...  56.6 us
    unnamed x208, local copies, waits for them, and re-layouts  49.6 us
    ppermute x6, waiting for transfers between devices, swap_x(): return lax.ppermute(value, 'shard', [(i, i ^ 2) for i in range(4)])  44.5 us
    pallas_call x8, Pallas kernels, pick(): pl.pallas_call(functools.partial(pick_rows, held is not None), grid_spec=...  43.8 us
    ppermute x28, waiting for transfers between devices, swap_y(): return lax.ppermute(value, 'rep', [(i, i ^ 1) for i in range(count)])  40 us
    pallas_call x1, Pallas kernels, attention_backward(): pl.pallas_call(attend_backward, grid=(heads,), in_specs=[wide, pl.BlockSp...  34 us
  transfers between devices with their start and end apart: 82, of which 28 were waited for; matrix products, arithmetic and copies ran while one was open for 17% of the time, Pallas kernels for 34%

profile of v5, /device:TPU:0, one launch (start us, length us, event | category | flops | bytes accessed | tf_op | source)
XLA Modules:
  0.0 871.4 jit_solution(4992933726383490229)
XLA Ops:
  7.2 3.1 collective-permute-start.17
  17.0 18.7 %collective-permute-done.17.grad_ref.refs_6_ = bf16[256,2048]{1,0:T(8,128)(2,1)S(1)} collective-permute-done((bf16[256,2048]{1,0:T(8,128)(2,1)}, bf16[256,2048]{1,0:T(8,128)(2,1)S(1)}, u32[]{:S(2)}, u32[]{:S(2)}) %collective-permute-start.17) | collective-permute-done | bytes 1048608 | tf_op jit(solution)/shard_map/ppermute | solution.py:654
  35.7 9.2 %collective-permute-done.3 = bf16[2,64,1536]{2,1,0:T(8,128)(2,1)} collective-permute-done((bf16[2,64,1536]{2,1,0:T(8,128)(2,1)}, bf16[2,64,1536]{2,1,0:T(8,128)(2,1)}, u32[]{:S(2)}, u32[]{:S(2)}) %collective-permute-start.3) | collective-permute-done | bytes 393248 | tf_op jit(solution)/shard_map/ppermute | solution.py:618
  53.2 3.1 fusion.20
  56.3 10.4 %collective-permute-done.5.refs_6_.refs_2_ = bf16[2,80,1536]{2,1,0:T(8,128)(2,1)} collective-permute-done((bf16[2,80,1536]{2,1,0:T(8,128)(2,1)}, bf16[2,80,1536]{2,1,0:T(8,128)(2,1)}, u32[]{:S(2)}, u32[]{:S(2)}) %collective-permute-start.5) | collective-permute-done | bytes 491552 | tf_op jit(solution)/shard_map/ppermute | solution.py:654
  91.9 2.7 scatter_fusion
  105.3 5.0 collective-permute-done.16
  112.4 18.2 %shard_map.265 = (bf16[1024,2048]{1,0:T(8,128)(2,1)}, bf16[2048,1536]{1,0:T(8,128)(2,1)}, f32[1024,1536]{1,0:T(8,128)}) custom-call(s32[8]{0:T(128)} %stack.153.order_ref, s32[4]{0:T(128)} %pad_add_fusion.1.shard_ref, f32[1,2048]{1,0:T(1,128)} %bitcast.193, bf16[4,512,1536]{2,1,0:T(8,128)(2,1)} %copy-done.10, ...), custom_call_target="tpu_custom_call" | custom-call | flops 6442450944 | bytes 27262976 | tf_op jit(solution)/shard_map/pallas_call | solution.py:148
  130.7 2.8 copy-done.56
  133.5 18.6 %shard_map.266 = bf16[1024,512]{1,0:T(8,128)(2,1)S(1)} custom-call(f32[1024,1536]{1,0:T(8,128)S(1)} %copy-done.56, f32[1024,128]{1,0:T(8,128)S(1)} %copy-done.39, f32[1024,128]{1,0:T(8,128)S(1)} %copy-done.38, f32[1,128]{1,0:T(1,128)S(1)} %reshape_squeeze.6.gq_ref, f32[1,128]{1,0:T(1,128)S(1)} %reshape_squeeze.7.gk_ref, s32[1024,1]{1,0:T(8,128)S(1)} %copy-done.40, ...), custom_call_target="tpu_custom_call" | custom-call | flops 8589934592 | bytes 7864320 | tf_op jit(solution)/shard_map/pallas_call | solution.py:268
  158.9 23.5 %collective-permute-done.24.grad_ref.refs_6_ = bf16[256,2048]{1,0:T(8,128)(2,1)} collective-permute-done((bf16[256,2048]{1,0:T(8,128)(2,1)S(1)}, bf16[256,2048]{1,0:T(8,128)(2,1)}, u32[]{:S(2)}, u32[]{:S(2)}) %collective-permute-start.24) | collective-permute-done | bytes 1048608 | tf_op jit(solution)/shard_map/ppermute | solution.py:654
  192.7 5.8 shard_map.268
  198.6 16.7 %collective-permute-done.26.x_ref = bf16[256,2048]{1,0:T(8,128)(2,1)S(1)} collective-permute-done((bf16[256,2048]{1,0:T(8,128)(2,1)S(1)}, bf16[256,2048]{1,0:T(8,128)(2,1)S(1)}, u32[]{:S(2)}, u32[]{:S(2)}) %collective-permute-start.26) | collective-permute-done | bytes 1048608 | tf_op jit(solution)/shard_map/ppermute | solution.py:654
  218.2 5.4 shard_map.269
  223.6 5.4 shard_map.270
  229.1 12.0 %collective-permute-done.28.x_ref = bf16[256,2048]{1,0:T(8,128)(2,1)} collective-permute-done((bf16[256,2048]{1,0:T(8,128)(2,1)S(1)}, bf16[256,2048]{1,0:T(8,128)(2,1)}, u32[]{:S(2)}, u32[]{:S(2)}) %collective-permute-start.28) | collective-permute-done | bytes 1048608 | tf_op jit(solution)/shard_map/ppermute | solution.py:654
  243.4 5.4 shard_map.271
  248.8 17.9 %collective-permute-done.30.x_ref = bf16[256,2048]{1,0:T(8,128)(2,1)S(1)} collective-permute-done((bf16[256,2048]{1,0:T(8,128)(2,1)}, bf16[256,2048]{1,0:T(8,128)(2,1)S(1)}, u32[]{:S(2)}, u32[]{:S(2)}) %collective-permute-start.30) | collective-permute-done | bytes 1048608 | tf_op jit(solution)/shard_map/ppermute | solution.py:654
  270.6 5.4 shard_map.272
  276.0 5.4 shard_map.275
  281.4 5.5 shard_map.276
  291.6 41.9 %shard_map.273 = (bf16[2,576,2048]{2,1,0:T(8,128)(2,1)}, bf16[2,576,2048]{2,1,0:T(8,128)(2,1)}, bf16[2,576,1024]{2,1,0:T(8,128)(2,1)}, bf16[2,576,1024]{2,1,0:T(8,128)(2,1)}, bf16[2,576,1024]{2,1,0:T(8,128)(2,1)}) custom-call(bf16[2,576,2048]{2,1,0:T(8,128)(2,1)} %bitcast.173, bf16[2,576,2048]{2,1,0:T(8,128)(2,1)} %bitcast.167, ...), custom_call_target="tpu_custom_call" | custom-call | flops 28991029248 | bytes 51118080 | tf_op jit(solution)/shard_map/pallas_call | solution.py:549
  335.8 4.7 shard_map.274
  343.7 5.4 shard_map.277
  350.0 41.6 %shard_map.278 = (bf16[2,576,2048]{2,1,0:T(8,128)(2,1)}, bf16[2,576,2048]{2,1,0:T(8,128)(2,1)}, bf16[2,576,1024]{2,1,0:T(8,128)(2,1)}, bf16[2,576,1024]{2,1,0:T(8,128)(2,1)}, bf16[2,576,1024]{2,1,0:T(8,128)(2,1)}) custom-call(bf16[2,576,2048]{2,1,0:T(8,128)(2,1)} %bitcast.170, bf16[2,576,2048]{2,1,0:T(8,128)(2,1)} %bitcast.164, ...), custom_call_target="tpu_custom_call" | custom-call | flops 28991029248 | bytes 51118080 | tf_op jit(solution)/shard_map/pallas_call | solution.py:549
  394.0 4.8 shard_map.279
  402.0 2.7 add_convert_fusion.7
  405.3 7.3 shard_map.280
  415.5 8.6 shard_map.281
  432.8 3.4 add_convert_fusion.6
  438.2 4.9 all-to-all-start
  446.5 17.5 %shard_map.282 = (bf16[2048,1024]{1,0:T(8,128)(2,1)}, bf16[2048,1024]{1,0:T(8,128)(2,1)}) custom-call(bf16[2,576,2048]{2,1,0:T(8,128)(2,1)} %bitcast.174, bf16[2,576,2048]{2,1,0:T(8,128)(2,1)} %bitcast.171, bf16[2,576,1024]{2,1,0:T(8,128)(2,1)S(1)} %copy-done.58, bf16[2,576,1024]{2,1,0:T(8,128)(2,1)S(1)} %copy-done.60, ...), custom_call_target="tpu_custom_call" | custom-call | flops 9663676416 | bytes 17825792 | tf_op jit(solution)/shard_map/pallas_call | solution.py:599
  464.0 2.8 fusion.16
  474.7 17.3 %shard_map.283 = (bf16[2048,1024]{1,0:T(8,128)(2,1)}, bf16[2048,1024]{1,0:T(8,128)(2,1)}) custom-call(bf16[2,576,2048]{2,1,0:T(8,128)(2,1)} %bitcast.175, bf16[2,576,2048]{2,1,0:T(8,128)(2,1)} %bitcast.172, bf16[2,576,1024]{2,1,0:T(8,128)(2,1)S(1)} %copy-done.59, bf16[2,576,1024]{2,1,0:T(8,128)(2,1)S(1)} %copy-done.61, ...), custom_call_target="tpu_custom_call" | custom-call | flops 9663676416 | bytes 17825792 | tf_op jit(solution)/shard_map/pallas_call | solution.py:599
  494.3 4.2 multiply_reduce_fusion
  503.6 10.9 %shard_map.285 = bf16[1024,2048]{1,0:T(8,128)(2,1)} custom-call(bf16[2,576,1024]{2,1,0:T(8,128)(2,1)S(1)} %copy-done.11, bf16[2,576,1024]{2,1,0:T(8,128)(2,1)S(1)} %copy-done.13, bf16[2,576,2048]{2,1,0:T(8,128)(2,1)} %bitcast.168, bf16[2,576,2048]{2,1,0:T(8,128)(2,1)} %bitcast.165), custom_call_target="tpu_custom_call" | custom-call | flops 4831838208 | bytes 11272192 | tf_op jit(solution)/shard_map/pallas_call | solution.py:599
  517.8 10.9 %shard_map.284 = bf16[1024,2048]{1,0:T(8,128)(2,1)} custom-call(bf16[2,576,1024]{2,1,0:T(8,128)(2,1)S(1)} %copy-done.12, bf16[2,576,1024]{2,1,0:T(8,128)(2,1)S(1)} %copy-done.14, bf16[2,576,2048]{2,1,0:T(8,128)(2,1)} %bitcast.169, bf16[2,576,2048]{2,1,0:T(8,128)(2,1)} %bitcast.166), custom_call_target="tpu_custom_call" | custom-call | flops 4831838208 | bytes 11272192 | tf_op jit(solution)/shard_map/pallas_call | solution.py:599
  532.7 5.2 convolution_convert_fusion.5.do_ref
  541.4 3.8 add_convert_fusion.3
  547.8 34.0 %shard_map.286 = (bf16[1024,1536]{1,0:T(8,128)(2,1)}, f32[8,128]{1,0:T(8,128)}) custom-call(f32[1024,1536]{1,0:T(8,128)} %get-tuple-element.228.qkv_ref, bf16[1024,512]{1,0:T(8,128)(2,1)} %convolution_convert_fusion.5.do_ref, f32[1024,128]{1,0:T(8,128)} %pad_maximum_fusion.7.cos_ref, f32[1024,128]{1,0:T(8,128)} %pad_maximum_fusion.8.sin_ref, ...), custom_call_target="tpu_custom_call" | custom-call | flops 21474836480 | bytes 4718592 | tf_op jit(solution)/shard_map/pallas_call | solution.py:283
  585.6 4.9 convolution_convert_fusion.3
  592.1 11.0 %convolution_convert_fusion = bf16[2048,1536]{1,0:T(8,128)(2,1)S(1)} fusion(bf16[1024,2048]{1,0:T(8,128)(2,1)} %get-tuple-element.357, bf16[1024,1536]{1,0:T(8,128)(2,1)} %get-tuple-element.358), kind=kOutput, calls=%fused_computation.3 | convolution fusion | flops 6445596672 | bytes 13631488 | tf_op jit(solution)/shard_map/dot_general | solution.py:40
  610.9 14.2 %collective-permute-done.55 = bf16[2,64,2176]{2,1,0:T(8,128)(2,1)} collective-permute-done((bf16[2,64,2176]{2,1,0:T(8,128)(2,1)}, bf16[2,64,2176]{2,1,0:T(8,128)(2,1)}, u32[]{:S(2)}, u32[]{:S(2)}) %collective-permute-start.55) | collective-permute-done | bytes 557088 | tf_op jit(solution)/shard_map/ppermute | solution.py:650
  626.9 2.8 fusion.14
  631.5 23.9 %collective-permute-done.57 = bf16[4,64,2176]{2,1,0:T(8,128)(2,1)} collective-permute-done((bf16[4,64,2176]{2,1,0:T(8,128)(2,1)}, bf16[4,64,2176]{2,1,0:T(8,128)(2,1)}, u32[]{:S(2)}, u32[]{:S(2)}) %collective-permute-start.57) | collective-permute-done | bytes 1114144 | tf_op jit(solution)/shard_map/ppermute | solution.py:650
  655.4 3.3 collective-permute-done.58
  658.7 3.3 fusion.5
  662.3 25.9 %collective-permute-done.60 = bf16[4,64,2176]{2,1,0:T(8,128)(2,1)} collective-permute-done((bf16[4,64,2176]{2,1,0:T(8,128)(2,1)}, bf16[4,64,2176]{2,1,0:T(8,128)(2,1)}, u32[]{:S(2)}, u32[]{:S(2)}) %collective-permute-start.60) | collective-permute-done | bytes 1114144 | tf_op jit(solution)/shard_map/ppermute | solution.py:654
  688.2 3.0 fusion.3
  691.4 9.1 %convolution_convert_fusion.1 = bf16[1024,2048]{1,0:T(8,128)(2,1)S(1)} fusion(bf16[1024,1536]{1,0:T(8,128)(2,1)S(1)} %copy-done.99, bf16[2048,1536]{1,0:T(8,128)(2,1)} %get-tuple-element.359), kind=kOutput, calls=%fused_computation.5 | convolution fusion | flops 6444548096 | bytes 13631488 | tf_op jit(solution)/shard_map/dot_general | solution.py:36
  703.2 3.1 add_convert_fusion.2
  708.2 12.4 %collective-permute-done.62 = bf16[4,64,2176]{2,1,0:T(8,128)(2,1)S(1)} collective-permute-done((bf16[4,64,2176]{2,1,0:T(8,128)(2,1)S(1)}, bf16[4,64,2176]{2,1,0:T(8,128)(2,1)S(1)}, u32[]{:S(2)}, u32[]{:S(2)}) %collective-permute-start.62) | collective-permute-done | bytes 1114144 | tf_op jit(solution)/shard_map/ppermute | solution.py:654
  724.3 4.2 all-to-all-start.1
  728.5 2.9 add_convert_fusion
  734.4 7.0 all-to-all-done.1
  743.9 34.3 %collective-permute-done.54 = bf16[256,2048]{1,0:T(8,128)(2,1)} collective-permute-done((bf16[256,2048]{1,0:T(8,128)(2,1)}, bf16[256,2048]{1,0:T(8,128)(2,1)}, u32[]{:S(2)}, u32[]{:S(2)}) %collective-permute-start.54) | collective-permute-done | bytes 1048608 | tf_op jit(solution)/shard_map/ppermute | solution.py:618
  782.0 5.0 fusion.12
  787.0 21.0 %collective-permute-done.65.refs_4_ = bf16[64,8320]{1,0:T(8,128)(2,1)} collective-permute-done((bf16[64,8320]{1,0:T(8,128)(2,1)S(1)}, bf16[64,8320]{1,0:T(8,128)(2,1)}, u32[]{:S(2)}, u32[]{:S(2)}) %collective-permute-start.65) | collective-permute-done | bytes 1064992 | tf_op jit(solution)/shard_map/ppermute | solution.py:654
  808.0 3.8 maximum_convert_fusion.1
  811.8 3.8 maximum_convert_fusion
  815.6 17.0 %reduce-scatter.17.cloned.1.call-done = bf16[256,2048]{1,0:T(8,128)(2,1)} async-done(((bf16[1024,2048]{1,0:T(8,128)(2,1)}), bf16[256,2048]{1,0:T(8,128)(2,1)}) %reduce-scatter.17.cloned.1.call-update) | async-done | bytes 1048592 | tf_op jit(solution)/shard_map/reduce_scatter | solution.py:982
  832.6 3.8 maximum_convert_fusion.2
  836.5 4.7 collective-permute-done.67.refs_6_
  845.2 12.0 %shard_map.287 = (f32[512,2048]{1,0:T(8,128)}, f32[512,2048]{1,0:T(8,128)}, f32[512,2048]{1,0:T(8,128)}, f32[512,2048]{1,0:T(8,128)}, f32[512,128]{1,0:T(8,128)S(1)}) custom-call(s32[7]{0:T(128)S(1)} %stack.196.ids_ref, bf16[512,2048]{1,0:T(8,128)(2,1)} %wq_ref.3, bf16[512,2048]{1,0:T(8,128)(2,1)} %wk_ref.3, bf16[512,2048]{1,0:T(8,128)(2,1)} %wv_ref.3, ...), custom_call_target="tpu_custom_call" | custom-call | bytes 27525120 | tf_op jit(solution)/shard_map/pallas_call | solution.py:759
  (459 shorter events, 187.0 us)
Async XLA Ops:
  7.2 284.4 %all-gather.4.cloned.1.call-start = ((), (), s32[]{:S(2)}) async-start(), calls=%async_computation.8 | async-start | bytes 10485760 | tf_op jit(solution)/shard_map/all_gather | solution.py:822
  7.2 28.5 %collective-permute-start.17 = (bf16[256,2048]{1,0:T(8,128)(2,1)}, bf16[256,2048]{1,0:T(8,128)(2,1)S(1)}, u32[]{:S(2)}, u32[]{:S(2)}) collective-permute-start(bf16[256,2048]{1,0:T(8,128)(2,1)} %refs_4_.1), channel_id=1, source_target_pairs={{0,8},{4,12},{8,16},{12,20},{16,24},{20,28},{24,0},{28,4},{1,9},{5... | collective-permute-start | bytes 3145736 | tf_op jit(solution)/shard_map/ppermute | solution.py:654
  10.3 25.4 %collective-permute-start.18 = (bf16[256,2048]{1,0:T(8,128)(2,1)}, bf16[256,2048]{1,0:T(8,128)(2,1)}, u32[]{:S(2)}, u32[]{:S(2)}) collective-permute-start(bf16[256,2048]{1,0:T(8,128)(2,1)} %refs_4_.1), channel_id=1, source_target_pairs={{0,4},{4,0},{8,12},{12,8},{16,20},{20,16},{24,28},{28,24},{1,5},{5... | collective-permute-start | bytes 3145736 | tf_op jit(solution)/shard_map/ppermute | solution.py:650
  11.8 33.1 %collective-permute-start.9 = (bf16[256,2048]{1,0:T(8,128)(2,1)}, bf16[256,2048]{1,0:T(8,128)(2,1)}, u32[]{:S(2)}, u32[]{:S(2)}) collective-permute-start(bf16[256,2048]{1,0:T(8,128)(2,1)} %refs_0_.1), channel_id=1, source_target_pairs={{0,2},{1,3},{2,0},{3,1},{4,6},{5,7},{6,4},{7,5},{8,10},{9,11},{10,... | collective-permute-start | bytes 3145736 | tf_op jit(solution)/shard_map/ppermute | solution.py:618
  16.4 28.5 %collective-permute-start.3 = (bf16[2,64,1536]{2,1,0:T(8,128)(2,1)}, bf16[2,64,1536]{2,1,0:T(8,128)(2,1)}, u32[]{:S(2)}, u32[]{:S(2)}) collective-permute-start(bf16[2,64,1536]{2,1,0:T(8,128)(2,1)} %shard_map.263), channel_id=1, source_target_pairs={{0,2},{1,3},{2,0},{3,1},{4,6},{5,7},{6,4},{7,5},{8,10},{9,11},{10,... | collective-permute-start | bytes 1179656 | tf_op jit(solution)/shard_map/ppermute | solution.py:618
  45.0 246.6 %all-gather.6.cloned.1.call-start = ((), (), s32[]{:S(2)}) async-start(), calls=%async_computation.9 | async-start | bytes 10485760 | tf_op jit(solution)/shard_map/all_gather | solution.py:833
  45.7 245.9 %all-gather.8.cloned.1.call-start = ((), (), s32[]{:S(2)}) async-start(), calls=%async_computation.10 | async-start | bytes 10485760 | tf_op jit(solution)/shard_map/all_gather | solution.py:885
  45.9 33.8 %collective-permute-start.1 = (bf16[512,128]{0,1:T(8,128)(2,1)S(1)}, bf16[512,128]{0,1:T(8,128)(2,1)}, u32[]{:S(2)}, u32[]{:S(2)}) collective-permute-start(bf16[512,128]{0,1:T(8,128)(2,1)S(1)} %get-tuple-element.517), channel_id=1, source_target_pairs={{0,2},{1,3},{2,0},{3,1},{4,6},{5,7},{6,4},{7,5},{8,10},{9,11},{10,... | collective-permute-start | bytes 393224 | tf_op jit(solution)/shard_map/ppermute | solution.py:618
  47.5 39.1 %collective-permute-start = (bf16[512,128]{0,1:T(8,128)(2,1)S(1)}, bf16[512,128]{0,1:T(8,128)(2,1)}, u32[]{:S(2)}, u32[]{:S(2)}) collective-permute-start(bf16[512,128]{0,1:T(8,128)(2,1)S(1)} %get-tuple-element.517), channel_id=1, source_target_pairs={{0,1},{1,0},{2,3},{3,2},{4,5},{5,4},{6,7},{7,6},{8,9},{9,8},{10,11... | collective-permute-start | bytes 393224 | tf_op jit(solution)/shard_map/ppermute | solution.py:614
  78.6 33.8 %collective-permute-start.7 = (bf16[512,1536]{1,0:T(8,128)(2,1)}, bf16[512,1536]{1,0:T(8,128)(2,1)}, u32[]{:S(2)}, u32[]{:S(2)}) collective-permute-start(bf16[512,1536]{1,0:T(8,128)(2,1)} %dynamic-slice_bitcast_fusion), channel_id=1, source_target_pairs={{0,1},{1,0},{2,3},{3,2},{4,5},{5,4},{6,7},{7,6},{8,9},{9,8},{10,11... | collective-permute-start | bytes 4718600 | tf_op jit(solution)/shard_map/ppermute | solution.py:614
  86.6 25.8 %collective-permute-start.8 = (bf16[256,2048]{1,0:T(8,128)(2,1)}, bf16[256,2048]{1,0:T(8,128)(2,1)}, u32[]{:S(2)}, u32[]{:S(2)}) collective-permute-start(bf16[256,2048]{1,0:T(8,128)(2,1)} %refs_0_.1), channel_id=1, source_target_pairs={{0,1},{1,0},{2,3},{3,2},{4,5},{5,4},{6,7},{7,6},{8,9},{9,8},{10,11... | collective-permute-start | bytes 3145736 | tf_op jit(solution)/shard_map/ppermute | solution.py:614
  86.6 25.8 %collective-permute-start.10 = (bf16[256,2048]{1,0:T(8,128)(2,1)}, bf16[256,2048]{1,0:T(8,128)(2,1)}, u32[]{:S(2)}, u32[]{:S(2)}) collective-permute-start(bf16[256,2048]{1,0:T(8,128)(2,1)} %collective-permute-done.9.refs_2_), channel_id=1, source_target_pairs={{0,1},{1,0},{2,3},{3,2},{4,5},{5,4},{6,7},{7,6},{8,9},{9,8},{10,11... | collective-permute-start | bytes 3145736 | tf_op jit(solution)/shard_map/ppermute | solution.py:614
  111.3 40.8 %collective-permute-start.19 = (bf16[256,2048]{1,0:T(8,128)(2,1)S(1)}, bf16[256,2048]{1,0:T(8,128)(2,1)S(1)}, u32[]{:S(2)}, u32[]{:S(2)}) collective-permute-start(bf16[256,2048]{1,0:T(8,128)(2,1)S(1)} %collective-permute-done.17.grad_ref.refs_6_), channel_id=1, source_target_pairs={{0,8},{4,12},{8,16},{12,20},{16,24},{20,28},{24,0},{28,4},{1,9},{5... | collective-permute-start | bytes 3145736 | tf_op jit(solution)/shard_map/ppermute | solution.py:654
  111.8 40.2 %collective-permute-start.20 = (bf16[256,2048]{1,0:T(8,128)(2,1)S(1)}, bf16[256,2048]{1,0:T(8,128)(2,1)S(1)}, u32[]{:S(2)}, u32[]{:S(2)}) collective-permute-start(bf16[256,2048]{1,0:T(8,128)(2,1)S(1)} %collective-permute-done.17.grad_ref.refs_6_), channel_id=1, source_target_pairs={{0,4},{4,0},{8,12},{12,8},{16,20},{20,16},{24,28},{28,24},{1,5},{5... | collective-permute-start | bytes 3145736 | tf_op jit(solution)/shard_map/ppermute | solution.py:650
  154.8 27.6 %collective-permute-start.24 = (bf16[256,2048]{1,0:T(8,128)(2,1)S(1)}, bf16[256,2048]{1,0:T(8,128)(2,1)}, u32[]{:S(2)}, u32[]{:S(2)}) collective-permute-start(bf16[256,2048]{1,0:T(8,128)(2,1)S(1)} %collective-permute-done.19.grad_ref.refs_4_), channel_id=1, source_target_pairs={{0,8},{4,12},{8,16},{12,20},{16,24},{20,28},{24,0},{28,4},{1,9},{5... | collective-permute-start | bytes 3145736 | tf_op jit(solution)/shard_map/ppermute | solution.py:654
  156.3 26.2 %collective-permute-start.25 = (bf16[256,2048]{1,0:T(8,128)(2,1)S(1)}, bf16[256,2048]{1,0:T(8,128)(2,1)}, u32[]{:S(2)}, u32[]{:S(2)}) collective-permute-start(bf16[256,2048]{1,0:T(8,128)(2,1)S(1)} %collective-permute-done.19.grad_ref.refs_4_), channel_id=1, source_target_pairs={{0,4},{4,0},{8,12},{12,8},{16,20},{20,16},{24,28},{28,24},{1,5},{5... | collective-permute-start | bytes 3145736 | tf_op jit(solution)/shard_map/ppermute | solution.py:650
  157.3 25.2 %collective-permute-start.21 = (bf16[256,2048]{1,0:T(8,128)(2,1)S(1)}, bf16[256,2048]{1,0:T(8,128)(2,1)S(1)}, u32[]{:S(2)}, u32[]{:S(2)}) collective-permute-start(bf16[256,2048]{1,0:T(8,128)(2,1)S(1)} %get-tuple-element.507), channel_id=1, source_target_pairs={{0,1},{1,0},{2,3},{3,2},{4,5},{5,4},{6,7},{7,6},{8,9},{9,8},{10,11... | collective-permute-start | bytes 3145736 | tf_op jit(solution)/shard_map/ppermute | solution.py:614
  158.2 25.3 %collective-permute-start.23 = (bf16[256,2048]{1,0:T(8,128)(2,1)S(1)}, bf16[256,2048]{1,0:T(8,128)(2,1)S(1)}, u32[]{:S(2)}, u32[]{:S(2)}) collective-permute-start(bf16[256,2048]{1,0:T(8,128)(2,1)S(1)} %add_convert_fusion.8), channel_id=1, source_target_pairs={{0,2},{1,3},{2,0},{3,1},{4,6},{5,7},{6,4},{7,5},{8,10},{9,11},{10,... | collective-permute-start | bytes 3145736 | tf_op jit(solution)/shard_map/ppermute | solution.py:618
  189.1 26.2 %collective-permute-start.26 = (bf16[256,2048]{1,0:T(8,128)(2,1)S(1)}, bf16[256,2048]{1,0:T(8,128)(2,1)S(1)}, u32[]{:S(2)}, u32[]{:S(2)}) collective-permute-start(bf16[256,2048]{1,0:T(8,128)(2,1)S(1)} %multiply_convert_fusion.x_ref), channel_id=1, source_target_pairs={{0,8},{4,12},{8,16},{12,20},{16,24},{20,28},{24,0},{28,4},{1,9},{5... | collective-permute-start | bytes 3145736 | tf_op jit(solution)/shard_map/ppermute | solution.py:654
  190.8 24.6 %collective-permute-start.27 = (bf16[256,2048]{1,0:T(8,128)(2,1)S(1)}, bf16[256,2048]{1,0:T(8,128)(2,1)}, u32[]{:S(2)}, u32[]{:S(2)}) collective-permute-start(bf16[256,2048]{1,0:T(8,128)(2,1)S(1)} %multiply_convert_fusion.x_ref), channel_id=1, source_target_pairs={{0,4},{4,0},{8,12},{12,8},{16,20},{20,16},{24,28},{28,24},{1,5},{5... | collective-permute-start | bytes 3145736 | tf_op jit(solution)/shard_map/ppermute | solution.py:650
  215.4 25.6 %collective-permute-start.28 = (bf16[256,2048]{1,0:T(8,128)(2,1)S(1)}, bf16[256,2048]{1,0:T(8,128)(2,1)}, u32[]{:S(2)}, u32[]{:S(2)}) collective-permute-start(bf16[256,2048]{1,0:T(8,128)(2,1)S(1)} %collective-permute-done.26.x_ref), channel_id=1, source_target_pairs={{0,8},{4,12},{8,16},{12,20},{16,24},{20,28},{24,0},{28,4},{1,9},{5... | collective-permute-start | bytes 3145736 | tf_op jit(solution)/shard_map/ppermute | solution.py:654
  217.7 23.3 %collective-permute-start.29 = (bf16[256,2048]{1,0:T(8,128)(2,1)S(1)}, bf16[256,2048]{1,0:T(8,128)(2,1)S(1)}, u32[]{:S(2)}, u32[]{:S(2)}) collective-permute-start(bf16[256,2048]{1,0:T(8,128)(2,1)S(1)} %collective-permute-done.26.x_ref), channel_id=1, source_target_pairs={{0,4},{4,0},{8,12},{12,8},{16,20},{20,16},{24,28},{28,24},{1,5},{5... | collective-permute-start | bytes 3145736 | tf_op jit(solution)/shard_map/ppermute | solution.py:650
  242.0 24.7 %collective-permute-start.30 = (bf16[256,2048]{1,0:T(8,128)(2,1)}, bf16[256,2048]{1,0:T(8,128)(2,1)S(1)}, u32[]{:S(2)}, u32[]{:S(2)}) collective-permute-start(bf16[256,2048]{1,0:T(8,128)(2,1)} %collective-permute-done.28.x_ref), channel_id=1, source_target_pairs={{0,8},{4,12},{8,16},{12,20},{16,24},{20,28},{24,0},{28,4},{1,9},{5... | collective-permute-start | bytes 3145736 | tf_op jit(solution)/shard_map/ppermute | solution.py:654
  242.6 24.1 %collective-permute-start.31 = (bf16[256,2048]{1,0:T(8,128)(2,1)}, bf16[256,2048]{1,0:T(8,128)(2,1)S(1)}, u32[]{:S(2)}, u32[]{:S(2)}) collective-permute-start(bf16[256,2048]{1,0:T(8,128)(2,1)} %collective-permute-done.28.x_ref), channel_id=1, source_target_pairs={{0,4},{4,0},{8,12},{12,8},{16,20},{20,16},{24,28},{28,24},{1,5},{5... | collective-permute-start | bytes 3145736 | tf_op jit(solution)/shard_map/ppermute | solution.py:650
  268.5 18.4 %collective-permute-start.32 = (bf16[128,2048]{1,0:T(8,128)(2,1)}, bf16[128,2048]{1,0:T(8,128)(2,1)}, u32[]{:S(2)}, u32[]{:S(2)}) collective-permute-start(bf16[128,2048]{1,0:T(8,128)(2,1)} %slice.153), channel_id=1, source_target_pairs={{0,4},{4,0},{8,12},{12,8},{16,20},{20,16},{24,28},{28,24},{1,5},{5... | collective-permute-start | bytes 1572872 | tf_op jit(solution)/shard_map/ppermute | solution.py:650
  290.7 53.0 %collective-permute-start.34 = (bf16[256,2048]{1,0:T(8,128)(2,1)}, bf16[256,2048]{1,0:T(8,128)(2,1)}, u32[]{:S(2)}, u32[]{:S(2)}) collective-permute-start(bf16[256,2048]{1,0:T(8,128)(2,1)} %collective-permute-done.24.grad_ref.refs_6_), channel_id=1, source_target_pairs={{0,4},{4,0},{8,12},{12,8},{16,20},{20,16},{24,28},{28,24},{1,5},{5... | collective-permute-start | bytes 3145736 | tf_op jit(solution)/shard_map/ppermute | solution.py:650
  342.6 59.3 %collective-permute-start.35 = (bf16[256,2048]{1,0:T(8,128)(2,1)}, bf16[256,2048]{1,0:T(8,128)(2,1)}, u32[]{:S(2)}, u32[]{:S(2)}) collective-permute-start(bf16[256,2048]{1,0:T(8,128)(2,1)} %get-tuple-element.267), channel_id=1, source_target_pairs={{0,4},{4,0},{8,12},{12,8},{16,20},{20,16},{24,28},{28,24},{1,5},{5... | collective-permute-start | bytes 3145736 | tf_op jit(solution)/shard_map/ppermute | solution.py:650
  349.1 52.8 %collective-permute-start.36 = (bf16[256,2048]{1,0:T(8,128)(2,1)}, bf16[256,2048]{1,0:T(8,128)(2,1)}, u32[]{:S(2)}, u32[]{:S(2)}) collective-permute-start(bf16[256,2048]{1,0:T(8,128)(2,1)} %get-tuple-element.290), channel_id=1, source_target_pairs={{0,4},{4,0},{8,12},{12,8},{16,20},{20,16},{24,28},{28,24},{1,5},{5... | collective-permute-start | bytes 3145736 | tf_op jit(solution)/shard_map/ppermute | solution.py:650
  400.7 31.3 %collective-permute-start.37 = (bf16[256,2048]{1,0:T(8,128)(2,1)}, bf16[256,2048]{1,0:T(8,128)(2,1)}, u32[]{:S(2)}, u32[]{:S(2)}) collective-permute-start(bf16[256,2048]{1,0:T(8,128)(2,1)} %get-tuple-element.295), channel_id=1, source_target_pairs={{0,4},{4,0},{8,12},{12,8},{16,20},{20,16},{24,28},{28,24},{1,5},{5... | collective-permute-start | bytes 3145736 | tf_op jit(solution)/shard_map/ppermute | solution.py:650
  404.7 28.1 %collective-permute-start.38 = (bf16[256,2048]{1,0:T(8,128)(2,1)}, bf16[256,2048]{1,0:T(8,128)(2,1)}, u32[]{:S(2)}, u32[]{:S(2)}) collective-permute-start(bf16[256,2048]{1,0:T(8,128)(2,1)} %add_convert_fusion.7), channel_id=1, source_target_pairs={{0,8},{4,12},{8,16},{12,20},{16,24},{20,28},{24,0},{28,4},{1,9},{5... | collective-permute-start | bytes 3145736 | tf_op jit(solution)/shard_map/ppermute | solution.py:654
  432.0 34.9 %collective-permute-start.40 = (bf16[256,2048]{1,0:T(8,128)(2,1)}, bf16[256,2048]{1,0:T(8,128)(2,1)}, u32[]{:S(2)}, u32[]{:S(2)}) collective-permute-start(bf16[256,2048]{1,0:T(8,128)(2,1)} %copy-done.54), channel_id=1, source_target_pairs={{0,4},{4,0},{8,12},{12,8},{16,20},{20,16},{24,28},{28,24},{1,5},{5... | collective-permute-start | bytes 3145736 | tf_op jit(solution)/shard_map/ppermute | solution.py:650
  436.3 30.6 %collective-permute-start.39 = (bf16[256,2048]{1,0:T(8,128)(2,1)}, bf16[256,2048]{1,0:T(8,128)(2,1)}, u32[]{:S(2)}, u32[]{:S(2)}) collective-permute-start(bf16[256,2048]{1,0:T(8,128)(2,1)} %add_convert_fusion.6), channel_id=1, source_target_pairs={{0,8},{4,12},{8,16},{12,20},{16,24},{20,28},{24,0},{28,4},{1,9},{5... | collective-permute-start | bytes 3145736 | tf_op jit(solution)/shard_map/ppermute | solution.py:654
  438.2 25.7 %all-to-all-start = ((f32[8,2,256]{2,1,0:T(2,128)}), f32[8,2,256]{2,1,0:T(2,128)S(1)}, u32[]{:S(2)}, u32[]{:S(2)}) async-start(f32[8,2,256]{2,1,0:T(2,128)} %scatter_fusion.1), calls=%async_computation | async-start | bytes 32768 | tf_op jit(solution)/shard_map/all_to_all | solution.py:1022
  443.1 364.9 %reduce-scatter.11.cloned.1.call-start = ((), (), s32[]{:S(2)}) async-start(), calls=%async_computation.13 | async-start | bytes 5242880 | tf_op jit(solution)/shard_map/reduce_scatter | solution.py:982
  466.9 25.1 %collective-permute-start.42 = (bf16[256,2048]{1,0:T(8,128)(2,1)}, bf16[256,2048]{1,0:T(8,128)(2,1)S(1)}, u32[]{:S(2)}, u32[]{:S(2)}) collective-permute-start(bf16[256,2048]{1,0:T(8,128)(2,1)} %copy-done.55), channel_id=1, source_target_pairs={{0,4},{4,0},{8,12},{12,8},{16,20},{20,16},{24,28},{28,24},{1,5},{5... | collective-permute-start | bytes 3145736 | tf_op jit(solution)/shard_map/ppermute | solution.py:650
  471.5 21.9 %collective-permute-start.41 = (bf16[256,2048]{1,0:T(8,128)(2,1)S(1)}, bf16[256,2048]{1,0:T(8,128)(2,1)S(1)}, u32[]{:S(2)}, u32[]{:S(2)}) collective-permute-start(bf16[256,2048]{1,0:T(8,128)(2,1)S(1)} %add_convert_fusion.5), channel_id=1, source_target_pairs={{0,8},{4,12},{8,16},{12,20},{16,24},{20,28},{24,0},{28,4},{1,9},{5... | collective-permute-start | bytes 3145736 | tf_op jit(solution)/shard_map/ppermute | solution.py:654
  498.5 30.2 %collective-permute-start.46 = (bf16[256,2048]{1,0:T(8,128)(2,1)}, bf16[256,2048]{1,0:T(8,128)(2,1)}, u32[]{:S(2)}, u32[]{:S(2)}) collective-permute-start(bf16[256,2048]{1,0:T(8,128)(2,1)} %add_convert_fusion.4), channel_id=1, source_target_pairs={{0,8},{4,12},{8,16},{12,20},{16,24},{20,28},{24,0},{28,4},{1,9},{5... | collective-permute-start | bytes 3145736 | tf_op jit(solution)/shard_map/ppermute | solution.py:654
  500.1 28.6 %collective-permute-start.45 = (bf16[256,2048]{1,0:T(8,128)(2,1)}, bf16[256,2048]{1,0:T(8,128)(2,1)}, u32[]{:S(2)}, u32[]{:S(2)}) collective-permute-start(bf16[256,2048]{1,0:T(8,128)(2,1)} %get-tuple-element.333), channel_id=1, source_target_pairs={{0,4},{4,0},{8,12},{12,8},{16,20},{20,16},{24,28},{28,24},{1,5},{5... | collective-permute-start | bytes 3145736 | tf_op jit(solution)/shard_map/ppermute | solution.py:650
  502.2 26.5 %collective-permute-start.44 = (bf16[256,2048]{1,0:T(8,128)(2,1)}, bf16[256,2048]{1,0:T(8,128)(2,1)}, u32[]{:S(2)}, u32[]{:S(2)}) collective-permute-start(bf16[256,2048]{1,0:T(8,128)(2,1)} %fusion.32), channel_id=1, source_target_pairs={{0,2},{1,3},{2,0},{3,1},{4,6},{5,7},{6,4},{7,5},{8,10},{9,11},{10,... | collective-permute-start | bytes 3145736 | tf_op jit(solution)/shard_map/ppermute | solution.py:618
  503.5 25.7 %collective-permute-start.43 = (bf16[256,2048]{1,0:T(8,128)(2,1)}, bf16[256,2048]{1,0:T(8,128)(2,1)}, u32[]{:S(2)}, u32[]{:S(2)}) collective-permute-start(bf16[256,2048]{1,0:T(8,128)(2,1)} %fusion.32), channel_id=1, source_target_pairs={{0,1},{1,0},{2,3},{3,2},{4,5},{5,4},{6,7},{7,6},{8,9},{9,8},{10,11... | collective-permute-start | bytes 3145736 | tf_op jit(solution)/shard_map/ppermute | solution.py:614
  537.9 270.1 %reduce-scatter.13.cloned.1.call-start = ((), (), s32[]{:S(2)}) async-start(), calls=%async_computation.14 | async-start | bytes 5242880 | tf_op jit(solution)/shard_map/reduce_scatter | solution.py:982
  538.5 273.3 %reduce-scatter.7.cloned.1.call-start = ((), (), s32[]{:S(2)}) async-start(), calls=%async_computation.11 | async-start | bytes 5242880 | tf_op jit(solution)/shard_map/reduce_scatter | solution.py:982
  539.1 272.7 %reduce-scatter.9.cloned.1.call-start = ((), (), s32[]{:S(2)}) async-start(), calls=%async_computation.12 | async-start | bytes 5242880 | tf_op jit(solution)/shard_map/reduce_scatter | solution.py:982
  539.8 275.8 %reduce-scatter.15.cloned.1.call-start = ((), (), s32[]{:S(2)}) async-start(), calls=%async_computation.15 | async-start | bytes 5242880 | tf_op jit(solution)/shard_map/reduce_scatter | solution.py:982
  545.2 46.8 %collective-permute-start.49 = (bf16[256,2048]{1,0:T(8,128)(2,1)}, bf16[256,2048]{1,0:T(8,128)(2,1)}, u32[]{:S(2)}, u32[]{:S(2)}) collective-permute-start(bf16[256,2048]{1,0:T(8,128)(2,1)} %add_convert_fusion.3), channel_id=1, source_target_pairs={{0,8},{4,12},{8,16},{12,20},{16,24},{20,28},{24,0},{28,4},{1,9},{5... | collective-permute-start | bytes 3145736 | tf_op jit(solution)/shard_map/ppermute | solution.py:654
  546.3 45.7 %collective-permute-start.48 = (bf16[256,2048]{1,0:T(8,128)(2,1)}, bf16[256,2048]{1,0:T(8,128)(2,1)}, u32[]{:S(2)}, u32[]{:S(2)}) collective-permute-start(bf16[256,2048]{1,0:T(8,128)(2,1)} %get-tuple-element.345), channel_id=1, source_target_pairs={{0,4},{4,0},{8,12},{12,8},{16,20},{20,16},{24,28},{28,24},{1,5},{5... | collective-permute-start | bytes 3145736 | tf_op jit(solution)/shard_map/ppermute | solution.py:650
  592.0 240.6 %reduce-scatter.17.cloned.1.call-start = ((), (), s32[]{:S(2)}) async-start(), calls=%async_computation.16 | async-start | bytes 5242880 | tf_op jit(solution)/shard_map/reduce_scatter | solution.py:982
  629.8 25.7 %collective-permute-start.57 = (bf16[4,64,2176]{2,1,0:T(8,128)(2,1)}, bf16[4,64,2176]{2,1,0:T(8,128)(2,1)}, u32[]{:S(2)}, u32[]{:S(2)}) collective-permute-start(bf16[4,64,2176]{2,1,0:T(8,128)(2,1)} %get-tuple-element.363), channel_id=1, source_target_pairs={{0,4},{4,0},{8,12},{12,8},{16,20},{20,16},{24,28},{28,24},{1,5},{5... | collective-permute-start | bytes 3342344 | tf_op jit(solution)/shard_map/ppermute | solution.py:650
  631.5 27.2 %collective-permute-start.58 = (bf16[4,64,2176]{2,1,0:T(8,128)(2,1)}, bf16[4,64,2176]{2,1,0:T(8,128)(2,1)}, u32[]{:S(2)}, u32[]{:S(2)}) collective-permute-start(bf16[4,64,2176]{2,1,0:T(8,128)(2,1)} %get-tuple-element.498), channel_id=1, source_target_pairs={{0,8},{4,12},{8,16},{12,20},{16,24},{20,28},{24,0},{28,4},{1,9},{5... | collective-permute-start | bytes 3342344 | tf_op jit(solution)/shard_map/ppermute | solution.py:654
  662.0 26.2 %collective-permute-start.60 = (bf16[4,64,2176]{2,1,0:T(8,128)(2,1)}, bf16[4,64,2176]{2,1,0:T(8,128)(2,1)}, u32[]{:S(2)}, u32[]{:S(2)}) collective-permute-start(bf16[4,64,2176]{2,1,0:T(8,128)(2,1)} %fusion.5), channel_id=1, source_target_pairs={{0,8},{4,12},{8,16},{12,20},{16,24},{20,28},{24,0},{28,4},{1,9},{5... | collective-permute-start | bytes 3342344 | tf_op jit(solution)/shard_map/ppermute | solution.py:654
  662.0 26.2 %collective-permute-start.59 = (bf16[4,64,2176]{2,1,0:T(8,128)(2,1)}, bf16[4,64,2176]{2,1,0:T(8,128)(2,1)}, u32[]{:S(2)}, u32[]{:S(2)}) collective-permute-start(bf16[4,64,2176]{2,1,0:T(8,128)(2,1)} %get-tuple-element.365), channel_id=1, source_target_pairs={{0,4},{4,0},{8,12},{12,8},{16,20},{20,16},{24,28},{28,24},{1,5},{5... | collective-permute-start | bytes 3342344 | tf_op jit(solution)/shard_map/ppermute | solution.py:650
  691.3 29.4 %collective-permute-start.62 = (bf16[4,64,2176]{2,1,0:T(8,128)(2,1)S(1)}, bf16[4,64,2176]{2,1,0:T(8,128)(2,1)S(1)}, u32[]{:S(2)}, u32[]{:S(2)}) collective-permute-start(bf16[4,64,2176]{2,1,0:T(8,128)(2,1)S(1)} %fusion.3), channel_id=1, source_target_pairs={{0,8},{4,12},{8,16},{12,20},{16,24},{20,28},{24,0},{28,4},{1,9},{5... | collective-permute-start | bytes 3342344 | tf_op jit(solution)/shard_map/ppermute | solution.py:654
  691.3 29.3 %collective-permute-start.61 = (bf16[4,64,2176]{2,1,0:T(8,128)(2,1)S(1)}, bf16[4,64,2176]{2,1,0:T(8,128)(2,1)S(1)}, u32[]{:S(2)}, u32[]{:S(2)}) collective-permute-start(bf16[4,64,2176]{2,1,0:T(8,128)(2,1)S(1)} %copy-done.80), channel_id=1, source_target_pairs={{0,4},{4,0},{8,12},{12,8},{16,20},{20,16},{24,28},{28,24},{1,5},{5... | collective-permute-start | bytes 3342344 | tf_op jit(solution)/shard_map/ppermute | solution.py:650
  703.2 25.3 %collective-permute-start.53 = (bf16[256,2048]{1,0:T(8,128)(2,1)}, bf16[256,2048]{1,0:T(8,128)(2,1)}, u32[]{:S(2)}, u32[]{:S(2)}) collective-permute-start(bf16[256,2048]{1,0:T(8,128)(2,1)} %get-tuple-element.506), channel_id=1, source_target_pairs={{0,1},{1,0},{2,3},{3,2},{4,5},{5,4},{6,7},{7,6},{8,9},{9,8},{10,11... | collective-permute-start | bytes 3145736 | tf_op jit(solution)/shard_map/ppermute | solution.py:614
  706.2 37.6 %collective-permute-start.51 = (bf16[256,2048]{1,0:T(8,128)(2,1)}, bf16[256,2048]{1,0:T(8,128)(2,1)}, u32[]{:S(2)}, u32[]{:S(2)}) collective-permute-start(bf16[256,2048]{1,0:T(8,128)(2,1)} %add_convert_fusion.2), channel_id=1, source_target_pairs={{0,8},{4,12},{8,16},{12,20},{16,24},{20,28},{24,0},{28,4},{1,9},{5... | collective-permute-start | bytes 3145736 | tf_op jit(solution)/shard_map/ppermute | solution.py:654
  706.2 37.7 %collective-permute-start.50 = (bf16[256,2048]{1,0:T(8,128)(2,1)}, bf16[256,2048]{1,0:T(8,128)(2,1)}, u32[]{:S(2)}, u32[]{:S(2)}) collective-permute-start(bf16[256,2048]{1,0:T(8,128)(2,1)} %get-tuple-element.352), channel_id=1, source_target_pairs={{0,4},{4,0},{8,12},{12,8},{16,20},{20,16},{24,28},{28,24},{1,5},{5... | collective-permute-start | bytes 3145736 | tf_op jit(solution)/shard_map/ppermute | solution.py:650
  720.6 23.3 %collective-permute-start.52 = (bf16[256,2048]{1,0:T(8,128)(2,1)}, bf16[256,2048]{1,0:T(8,128)(2,1)}, u32[]{:S(2)}, u32[]{:S(2)}) collective-permute-start(bf16[256,2048]{1,0:T(8,128)(2,1)} %get-tuple-element.505), channel_id=1, source_target_pairs={{0,1},{1,0},{2,3},{3,2},{4,5},{5,4},{6,7},{7,6},{8,9},{9,8},{10,11... | collective-permute-start | bytes 3145736 | tf_op jit(solution)/shard_map/ppermute | solution.py:614
  731.4 46.8 %collective-permute-start.54 = (bf16[256,2048]{1,0:T(8,128)(2,1)}, bf16[256,2048]{1,0:T(8,128)(2,1)}, u32[]{:S(2)}, u32[]{:S(2)}) collective-permute-start(bf16[256,2048]{1,0:T(8,128)(2,1)} %add_convert_fusion), channel_id=1, source_target_pairs={{0,2},{1,3},{2,0},{3,1},{4,6},{5,7},{6,4},{7,5},{8,10},{9,11},{10,... | collective-permute-start | bytes 3145736 | tf_op jit(solution)/shard_map/ppermute | solution.py:618
  743.7 37.1 %collective-permute-start.63 = (bf16[64,8320]{1,0:T(8,128)(2,1)S(1)}, bf16[64,8320]{1,0:T(8,128)(2,1)S(1)}, u32[]{:S(2)}, u32[]{:S(2)}) collective-permute-start(bf16[64,8320]{1,0:T(8,128)(2,1)S(1)} %pad_maximum_fusion.2.refs_0_), channel_id=1, source_target_pairs={{0,8},{4,12},{8,16},{12,20},{16,24},{20,28},{24,0},{28,4},{1,9},{5... | collective-permute-start | bytes 3194888 | tf_op jit(solution)/shard_map/ppermute | solution.py:654
  743.8 37.1 %collective-permute-start.64 = (bf16[64,8320]{1,0:T(8,128)(2,1)S(1)}, bf16[64,8320]{1,0:T(8,128)(2,1)S(1)}, u32[]{:S(2)}, u32[]{:S(2)}) collective-permute-start(bf16[64,8320]{1,0:T(8,128)(2,1)S(1)} %pad_maximum_fusion.2.refs_0_), channel_id=1, source_target_pairs={{0,4},{4,0},{8,12},{12,8},{16,20},{20,16},{24,28},{28,24},{1,5},{5... | collective-permute-start | bytes 3194888 | tf_op jit(solution)/shard_map/ppermute | solution.py:650
  781.9 26.0 %collective-permute-start.65 = (bf16[64,8320]{1,0:T(8,128)(2,1)S(1)}, bf16[64,8320]{1,0:T(8,128)(2,1)}, u32[]{:S(2)}, u32[]{:S(2)}) collective-permute-start(bf16[64,8320]{1,0:T(8,128)(2,1)S(1)} %collective-permute-done.63.refs_2_), channel_id=1, source_target_pairs={{0,8},{4,12},{8,16},{12,20},{16,24},{20,28},{24,0},{28,4},{1,9},{5... | collective-permute-start | bytes 3194888 | tf_op jit(solution)/shard_map/ppermute | solution.py:654
  781.9 26.0 %collective-permute-start.66 = (bf16[64,8320]{1,0:T(8,128)(2,1)S(1)}, bf16[64,8320]{1,0:T(8,128)(2,1)}, u32[]{:S(2)}, u32[]{:S(2)}) collective-permute-start(bf16[64,8320]{1,0:T(8,128)(2,1)S(1)} %collective-permute-done.63.refs_2_), channel_id=1, source_target_pairs={{0,4},{4,0},{8,12},{12,8},{16,20},{20,16},{24,28},{28,24},{1,5},{5... | collective-permute-start | bytes 3194888 | tf_op jit(solution)/shard_map/ppermute | solution.py:650
  815.6 25.5 %collective-permute-start.67 = (bf16[64,8320]{1,0:T(8,128)(2,1)}, bf16[64,8320]{1,0:T(8,128)(2,1)}, u32[]{:S(2)}, u32[]{:S(2)}) collective-permute-start(bf16[64,8320]{1,0:T(8,128)(2,1)} %collective-permute-done.65.refs_4_), channel_id=1, source_target_pairs={{0,8},{4,12},{8,16},{12,20},{16,24},{20,28},{24,0},{28,4},{1,9},{5... | collective-permute-start | bytes 3194888 | tf_op jit(solution)/shard_map/ppermute | solution.py:654
  815.6 25.5 %collective-permute-start.68 = (bf16[64,8320]{1,0:T(8,128)(2,1)}, bf16[64,8320]{1,0:T(8,128)(2,1)}, u32[]{:S(2)}, u32[]{:S(2)}) collective-permute-start(bf16[64,8320]{1,0:T(8,128)(2,1)} %collective-permute-done.65.refs_4_), channel_id=1, source_target_pairs={{0,4},{4,0},{8,12},{12,8},{16,20},{20,16},{24,28},{28,24},{1,5},{5... | collective-permute-start | bytes 3194888 | tf_op jit(solution)/shard_map/ppermute | solution.py:650
  (118 other events, 1624.5 us)
Sparse Core Ops, SparseCore 0:
  45.1 57.5 all-gather.3
  104.2 58.2 all-gather.5
  186.2 58.3 all-gather.7
  538.0 43.9 reduce-scatter.10
  585.2 44.5 reduce-scatter.12
  632.7 44.4 reduce-scatter.6
  680.5 44.5 reduce-scatter.8
  728.1 58.9 reduce-scatter.14
  790.4 42.1 reduce-scatter.16

commit v6 on v5

--- a/solution.py
+++ b/solution.py
@@ -272,7 +272,7 @@
         out_specs=pl.BlockSpec((length, HD), lambda h: (0, h)),
         out_shape=jax.ShapeDtypeStruct((length, heads * HD), BF),
         scratch_shapes=[pltpu.VMEM((length, HD), BF)] * 2,
-        compiler_params=params(),
+        compiler_params=params(58),
         cost_estimate=cost(16 * heads * length * length * HD, qkv.size * 5, heads * length * length),
     )(qkv, *attn_args)
 
@@ -426,7 +426,7 @@
         + [pl.BlockSpec((None, capacity, width), lambda b, j=j: (j, b, 0)) for j in range(experts)],
         out_specs=[pl.BlockSpec((count, width), lambda b: (0, 0))] * blocks,
         out_shape=[jax.ShapeDtypeStruct((count, width), BF)] * blocks,
-        compiler_params=params(),
+        compiler_params=params(58),
         cost_estimate=cost(
             2 * blocks * experts * capacity * count * width,
             2 * blocks * width * (count + experts * capacity),
@@ -475,7 +475,7 @@
         out_specs=[tokens] * blocks + [pl.BlockSpec((1, count, experts), lambda b: (b, 0, 0))],
         out_shape=[jax.ShapeDtypeStruct((count, width), BF)] * blocks
         + [jax.ShapeDtypeStruct((blocks, count, experts), F32)],
-        compiler_params=params(),
+        compiler_params=params(58),
         cost_estimate=cost(
             2 * blocks * experts * capacity * count * width,
             2 * blocks * width * (2 * count + experts * capacity),
@@ -602,7 +602,7 @@
         in_specs=[tiled(a, left_index, tile) for a in lefts] + [fixed(a, right_index) for a in flat],
         out_specs=[pl.BlockSpec((tile, wide), lambda d: (d, 0))] * count,
         out_shape=[jax.ShapeDtypeStruct((tall, wide), BF)] * count,
-        compiler_params=params(48),
+        compiler_params=params(58),
         cost_estimate=cost(
             2 * count * total_rows * tall * wide,
             2 * total_rows * (tall + count * wide) + 2 * count * tall * wide,

time: 877 us -> 869 us (level)
  local copies, waits for them, and re-layouts: 88 us -> 60.5 us
  Pallas kernels: 300 us -> 323 us
  waiting for transfers between devices: 291 us -> 277 us
  starting transfers between devices: 61.5 us -> 74.3 us
    unnamed x208 -> x138, local copies, waits for them, and re-layouts: 49.6 us -> 25.8 us
    ppermute x25, waiting for transfers between devices: 176 us -> 162 us  [turn_z(): return lax.ppermute(value, 'rep', ring_next(count))]
    ppermute x6, waiting for transfers between devices: 44.5 us -> 32.7 us  [swap_x(): return lax.ppermute(value, 'shard', [(i, i ^ 2) for i in range(4)])]
    reduce_scatter x6, waiting for transfers between devices: 17 us -> 26.2 us  [owned_part(): return lax.psum_scatter(grad, 'shard', scatter_dimension=0, tiled=True)]
  transfers between devices with their start and end apart: 82 -> 82, of which waited for: 28 -> 28; matrix products, arithmetic and copies ran while one was open for 17% -> 16% of each run, Pallas kernels for 34% -> 37%
where the time goes in v6:
time: 869 us; the launch traced here: 863 us
  Pallas kernels  323 us (37%)
  waiting for transfers between devices  277 us (32%)
  other arithmetic  76 us (9%)
  starting transfers between devices  74.3 us (9%)
  local copies, waits for them, and re-layouts  60.5 us (7%)
  matrix products  37.1 us (4%)
  between operations  15.2 us (2%)
    ppermute x25, waiting for transfers between devices, turn_z(): return lax.ppermute(value, 'rep', ring_next(count))  162 us
    pallas_call x2, Pallas kernels, run_experts(): pl.pallas_call(functools.partial(expert_body, rows // 2), grid=(experts,...  92.1 us
    pallas_call x4, Pallas kernels, weight_grads(): pl.pallas_call(functools.partial(weight_grads_body, groups, count), grid=...  58.3 us
    pallas_call x8, Pallas kernels, pick(): pl.pallas_call(functools.partial(pick_rows, held is not None), grid_spec=...  43.7 us
    ppermute x28, waiting for transfers between devices, swap_y(): return lax.ppermute(value, 'rep', [(i, i ^ 1) for i in range(count)])  41.7 us
    pallas_call x1, Pallas kernels, attention_backward(): pl.pallas_call(attend_backward, grid=(heads,), in_specs=[wide, pl.BlockSp...  34.2 us
    ppermute x6, waiting for transfers between devices, swap_x(): return lax.ppermute(value, 'shard', [(i, i ^ 2) for i in range(4)])  32.7 us
    ppermute x28, starting transfers between devices, swap_y(): return lax.ppermute(value, 'rep', [(i, i ^ 1) for i in range(count)])  30.8 us
  transfers between devices with their start and end apart: 82, of which 28 were waited for; matrix products, arithmetic and copies ran while one was open for 16% of the time, Pallas kernels for 37%

profile of v6, /device:TPU:0, one launch (start us, length us, event | category | flops | bytes accessed | tf_op | source)
XLA Modules:
  0.0 862.9 jit_solution(15483706336126764580)
XLA Ops:
  7.2 3.1 collective-permute-start.17
  17.0 18.7 %collective-permute-done.17.grad_ref.refs_6_ = bf16[256,2048]{1,0:T(8,128)(2,1)S(1)} collective-permute-done((bf16[256,2048]{1,0:T(8,128)(2,1)}, bf16[256,2048]{1,0:T(8,128)(2,1)S(1)}, u32[]{:S(2)}, u32[]{:S(2)}) %collective-permute-start.17) | collective-permute-done | bytes 1048608 | tf_op jit(solution)/shard_map/ppermute | solution.py:654
  35.7 9.2 %collective-permute-done.3 = bf16[2,64,1536]{2,1,0:T(8,128)(2,1)} collective-permute-done((bf16[2,64,1536]{2,1,0:T(8,128)(2,1)}, bf16[2,64,1536]{2,1,0:T(8,128)(2,1)}, u32[]{:S(2)}, u32[]{:S(2)}) %collective-permute-start.3) | collective-permute-done | bytes 393248 | tf_op jit(solution)/shard_map/ppermute | solution.py:618
  52.5 3.1 fusion.20
  55.6 10.1 %collective-permute-done.5.refs_6_.refs_2_ = bf16[2,80,1536]{2,1,0:T(8,128)(2,1)S(1)} collective-permute-done((bf16[2,80,1536]{2,1,0:T(8,128)(2,1)S(1)}, bf16[2,80,1536]{2,1,0:T(8,128)(2,1)S(1)}, u32[]{:S(2)}, u32[]{:S(2)}) %collective-permute-start.5) | collective-permute-done | bytes 491552 | tf_op jit(solution)/shard_map/ppermute | solution.py:654
  92.0 2.7 scatter_fusion
  104.4 3.7 collective-permute-done.16
  110.0 19.0 %shard_map.265 = (bf16[1024,2048]{1,0:T(8,128)(2,1)}, bf16[2048,1536]{1,0:T(8,128)(2,1)}, f32[1024,1536]{1,0:T(8,128)}) custom-call(s32[8]{0:T(128)} %stack.153.order_ref, s32[4]{0:T(128)} %pad_add_fusion.1.shard_ref, f32[1,2048]{1,0:T(1,128)} %bitcast.190, bf16[4,512,1536]{2,1,0:T(8,128)(2,1)} %copy-done.6, ...), custom_call_target="tpu_custom_call" | custom-call | flops 6442450944 | bytes 27262976 | tf_op jit(solution)/shard_map/pallas_call | solution.py:148
  129.0 20.9 %shard_map.266 = bf16[1024,512]{1,0:T(8,128)(2,1)} custom-call(f32[1024,1536]{1,0:T(8,128)} %get-tuple-element.228.qkv_ref, f32[1024,128]{1,0:T(8,128)} %pad_maximum_fusion.7.cos_ref, f32[1024,128]{1,0:T(8,128)} %pad_maximum_fusion.8.sin_ref, f32[1,128]{1,0:T(1,128)} %reshape_squeeze.6.gq_ref, f32[1,128]{1,0:T(1,128)} %reshape_squeeze.7.gk_ref, ...), custom_call_target="tpu_custom_call" | custom-call | flops 8589934592 | bytes 7864320 | tf_op jit(solution)/shard_map/pallas_call | solution.py:268
  150.0 4.3 convolution_convert_fusion.2
  157.9 24.6 %collective-permute-done.24.grad_ref.refs_6_ = bf16[256,2048]{1,0:T(8,128)(2,1)} collective-permute-done((bf16[256,2048]{1,0:T(8,128)(2,1)S(1)}, bf16[256,2048]{1,0:T(8,128)(2,1)}, u32[]{:S(2)}, u32[]{:S(2)}) %collective-permute-start.24) | collective-permute-done | bytes 1048608 | tf_op jit(solution)/shard_map/ppermute | solution.py:654
  197.0 5.6 shard_map.268
  202.6 16.8 %collective-permute-done.26.x_ref = bf16[256,2048]{1,0:T(8,128)(2,1)S(1)} collective-permute-done((bf16[256,2048]{1,0:T(8,128)(2,1)S(1)}, bf16[256,2048]{1,0:T(8,128)(2,1)S(1)}, u32[]{:S(2)}, u32[]{:S(2)}) %collective-permute-start.26) | collective-permute-done | bytes 1048608 | tf_op jit(solution)/shard_map/ppermute | solution.py:654
  222.2 5.4 shard_map.269
  227.6 5.4 shard_map.270
  233.1 11.8 %collective-permute-done.28.x_ref = bf16[256,2048]{1,0:T(8,128)(2,1)} collective-permute-done((bf16[256,2048]{1,0:T(8,128)(2,1)S(1)}, bf16[256,2048]{1,0:T(8,128)(2,1)}, u32[]{:S(2)}, u32[]{:S(2)}) %collective-permute-start.28) | collective-permute-done | bytes 1048608 | tf_op jit(solution)/shard_map/ppermute | solution.py:654
  247.9 5.4 shard_map.271
  253.4 17.3 %collective-permute-done.30.x_ref = bf16[256,2048]{1,0:T(8,128)(2,1)S(1)} collective-permute-done((bf16[256,2048]{1,0:T(8,128)(2,1)}, bf16[256,2048]{1,0:T(8,128)(2,1)S(1)}, u32[]{:S(2)}, u32[]{:S(2)}) %collective-permute-start.30) | collective-permute-done | bytes 1048608 | tf_op jit(solution)/shard_map/ppermute | solution.py:654
  275.7 5.4 shard_map.272
  281.1 5.5 shard_map.275
  286.6 5.5 shard_map.276
  294.8 50.4 %shard_map.273 = (bf16[2,576,2048]{2,1,0:T(8,128)(2,1)}, bf16[2,576,2048]{2,1,0:T(8,128)(2,1)}, bf16[2,576,1024]{2,1,0:T(8,128)(2,1)}, bf16[2,576,1024]{2,1,0:T(8,128)(2,1)}, bf16[2,576,1024]{2,1,0:T(8,128)(2,1)}) custom-call(bf16[2,576,2048]{2,1,0:T(8,128)(2,1)} %bitcast.170, bf16[2,576,2048]{2,1,0:T(8,128)(2,1)} %bitcast.164, ...), custom_call_target="tpu_custom_call" | custom-call | flops 28991029248 | bytes 51118080 | tf_op jit(solution)/shard_map/pallas_call | solution.py:549
  345.3 7.3 shard_map.274
  354.6 5.4 shard_map.277
  360.1 41.6 %shard_map.278 = (bf16[2,576,2048]{2,1,0:T(8,128)(2,1)}, bf16[2,576,2048]{2,1,0:T(8,128)(2,1)}, bf16[2,576,1024]{2,1,0:T(8,128)(2,1)}, bf16[2,576,1024]{2,1,0:T(8,128)(2,1)}, bf16[2,576,1024]{2,1,0:T(8,128)(2,1)}) custom-call(bf16[2,576,2048]{2,1,0:T(8,128)(2,1)} %bitcast.167, bf16[2,576,2048]{2,1,0:T(8,128)(2,1)} %bitcast.161, ...), custom_call_target="tpu_custom_call" | custom-call | flops 28991029248 | bytes 51118080 | tf_op jit(solution)/shard_map/pallas_call | solution.py:549
  401.7 7.5 shard_map.279
  414.4 9.8 %shard_map.280 = (bf16[256,2048]{1,0:T(8,128)(2,1)}, bf16[256,2048]{1,0:T(8,128)(2,1)}, bf16[256,2048]{1,0:T(8,128)(2,1)}, bf16[256,2048]{1,0:T(8,128)(2,1)}, f32[4,256,2]{2,1,0:T(8,128)}) custom-call(s32[8,256,128]{2,1,0:T(8,128)} %copy-done.5, f32[256,2]{1,0:T(8,128)} %get-tuple-element.282.refs_0_, f32[256,2]{1,0:T(8,128)} %get-tuple-element.283.refs_1_, ...), custom_call_target="tpu_custom_call" | custom-call | flops 1207959552 | bytes 13107200 | tf_op jit(solution)/shard_map/pallas_call | solution.py:468
  424.2 9.8 %shard_map.281 = (bf16[256,2048]{1,0:T(8,128)(2,1)}, bf16[256,2048]{1,0:T(8,128)(2,1)}, bf16[256,2048]{1,0:T(8,128)(2,1)}, bf16[256,2048]{1,0:T(8,128)(2,1)}, f32[4,256,2]{2,1,0:T(8,128)}) custom-call(s32[8,256,128]{2,1,0:T(8,128)} %copy-done.5, f32[256,2]{1,0:T(8,128)} %get-tuple-element.298.refs_0_, f32[256,2]{1,0:T(8,128)} %get-tuple-element.299.refs_1_, ...), custom_call_target="tpu_custom_call" | custom-call | flops 1207959552 | bytes 13107200 | tf_op jit(solution)/shard_map/pallas_call | solution.py:468
  438.1 3.4 add_convert_fusion.6
  443.6 5.4 all-to-all-start
  449.1 18.5 %shard_map.282 = (bf16[2048,1024]{1,0:T(8,128)(2,1)}, bf16[2048,1024]{1,0:T(8,128)(2,1)}) custom-call(bf16[2,576,2048]{2,1,0:T(8,128)(2,1)} %bitcast.171, bf16[2,576,2048]{2,1,0:T(8,128)(2,1)} %bitcast.168, bf16[2,576,1024]{2,1,0:T(8,128)(2,1)} %get-tuple-element.317.refs_2_, bf16[2,576,1024]{2,1,0:T(8,128)(2,1)} %get-tuple-element.318.refs_3_, ...), custom_call_target="tpu_custom_call" | custom-call | flops 9663676416 | bytes 17825792 | tf_op jit(solution)/shard_map/pallas_call | solution.py:599
  471.5 3.4 add_convert_fusion.5
  476.4 18.0 %shard_map.283 = (bf16[2048,1024]{1,0:T(8,128)(2,1)}, bf16[2048,1024]{1,0:T(8,128)(2,1)}) custom-call(bf16[2,576,2048]{2,1,0:T(8,128)(2,1)} %bitcast.172, bf16[2,576,2048]{2,1,0:T(8,128)(2,1)} %bitcast.169, bf16[2,576,1024]{2,1,0:T(8,128)(2,1)} %get-tuple-element.317.refs_2_, bf16[2,576,1024]{2,1,0:T(8,128)(2,1)} %get-tuple-element.318.refs_3_, ...), custom_call_target="tpu_custom_call" | custom-call | flops 9663676416 | bytes 17825792 | tf_op jit(solution)/shard_map/pallas_call | solution.py:599
  495.8 4.3 multiply_reduce_fusion
  504.2 10.9 %shard_map.285 = bf16[1024,2048]{1,0:T(8,128)(2,1)} custom-call(bf16[2,576,1024]{2,1,0:T(8,128)(2,1)} %get-tuple-element.337.refs_0_, bf16[2,576,1024]{2,1,0:T(8,128)(2,1)} %get-tuple-element.339.refs_1_, bf16[2,576,2048]{2,1,0:T(8,128)(2,1)} %bitcast.165, bf16[2,576,2048]{2,1,0:T(8,128)(2,1)} %bitcast.162), custom_call_target="tpu_custom_call" | custom-call | flops 4831838208 | bytes 11272192 | tf_op jit(solution)/shard_map/pallas_call | solution.py:599
  515.1 10.9 %shard_map.284 = bf16[1024,2048]{1,0:T(8,128)(2,1)} custom-call(bf16[2,576,1024]{2,1,0:T(8,128)(2,1)} %get-tuple-element.337.refs_0_, bf16[2,576,1024]{2,1,0:T(8,128)(2,1)} %get-tuple-element.339.refs_1_, bf16[2,576,2048]{2,1,0:T(8,128)(2,1)} %bitcast.166, bf16[2,576,2048]{2,1,0:T(8,128)(2,1)} %bitcast.163), custom_call_target="tpu_custom_call" | custom-call | flops 4831838208 | bytes 11272192 | tf_op jit(solution)/shard_map/pallas_call | solution.py:599
  530.1 5.3 convolution_convert_fusion.5.do_ref
  538.1 3.4 add_convert_fusion.3
  544.4 34.2 %shard_map.286 = (bf16[1024,1536]{1,0:T(8,128)(2,1)}, f32[8,128]{1,0:T(8,128)}) custom-call(f32[1024,1536]{1,0:T(8,128)} %get-tuple-element.228.qkv_ref, bf16[1024,512]{1,0:T(8,128)(2,1)} %convolution_convert_fusion.5.do_ref, f32[1024,128]{1,0:T(8,128)} %pad_maximum_fusion.7.cos_ref, f32[1024,128]{1,0:T(8,128)} %pad_maximum_fusion.8.sin_ref, ...), custom_call_target="tpu_custom_call" | custom-call | flops 21474836480 | bytes 4718592 | tf_op jit(solution)/shard_map/pallas_call | solution.py:283
  579.9 4.9 convolution_convert_fusion.3
  586.5 10.4 %convolution_convert_fusion = bf16[2048,1536]{1,0:T(8,128)(2,1)S(1)} fusion(bf16[1024,2048]{1,0:T(8,128)(2,1)} %get-tuple-element.357, bf16[1024,1536]{1,0:T(8,128)(2,1)} %get-tuple-element.358), kind=kOutput, calls=%fused_computation.3 | convolution fusion | flops 6445596672 | bytes 13631488 | tf_op jit(solution)/shard_map/dot_general | solution.py:40
  605.4 12.7 %collective-permute-done.55 = bf16[2,64,2176]{2,1,0:T(8,128)(2,1)} collective-permute-done((bf16[2,64,2176]{2,1,0:T(8,128)(2,1)}, bf16[2,64,2176]{2,1,0:T(8,128)(2,1)}, u32[]{:S(2)}, u32[]{:S(2)}) %collective-permute-start.55) | collective-permute-done | bytes 557088 | tf_op jit(solution)/shard_map/ppermute | solution.py:650
  618.0 2.6 collective-permute-done.56
  620.7 2.8 fusion.14
  624.4 24.7 %collective-permute-done.57 = bf16[4,64,2176]{2,1,0:T(8,128)(2,1)} collective-permute-done((bf16[4,64,2176]{2,1,0:T(8,128)(2,1)}, bf16[4,64,2176]{2,1,0:T(8,128)(2,1)}, u32[]{:S(2)}, u32[]{:S(2)}) %collective-permute-start.57) | collective-permute-done | bytes 1114144 | tf_op jit(solution)/shard_map/ppermute | solution.py:650
  650.9 3.3 fusion.5
  656.0 23.9 %collective-permute-done.60 = bf16[4,64,2176]{2,1,0:T(8,128)(2,1)} collective-permute-done((bf16[4,64,2176]{2,1,0:T(8,128)(2,1)}, bf16[4,64,2176]{2,1,0:T(8,128)(2,1)}, u32[]{:S(2)}, u32[]{:S(2)}) %collective-permute-start.60) | collective-permute-done | bytes 1114144 | tf_op jit(solution)/shard_map/ppermute | solution.py:654
  682.2 3.0 collective-permute-start.61
  685.2 9.7 %convolution_convert_fusion.1 = bf16[1024,2048]{1,0:T(8,128)(2,1)S(1)} fusion(bf16[1024,1536]{1,0:T(8,128)(2,1)S(1)} %copy-done.64, bf16[2048,1536]{1,0:T(8,128)(2,1)} %get-tuple-element.359), kind=kOutput, calls=%fused_computation.5 | convolution fusion | flops 6444548096 | bytes 13631488 | tf_op jit(solution)/shard_map/dot_general | solution.py:36
  698.0 3.1 add_convert_fusion.2
  701.1 6.5 collective-permute-done.62
  712.9 5.8 all-to-all-start.1
  718.6 2.9 add_convert_fusion
  721.5 2.8 collective-permute-start.54
  724.4 8.0 all-to-all-done.1
  736.8 22.8 %collective-permute-done.54 = bf16[256,2048]{1,0:T(8,128)(2,1)} collective-permute-done((bf16[256,2048]{1,0:T(8,128)(2,1)}, bf16[256,2048]{1,0:T(8,128)(2,1)}, u32[]{:S(2)}, u32[]{:S(2)}) %collective-permute-start.54) | collective-permute-done | bytes 1048608 | tf_op jit(solution)/shard_map/ppermute | solution.py:618
  759.6 2.6 fusion.8
  765.1 5.0 fusion.12
  770.1 20.0 %collective-permute-done.65.refs_4_ = bf16[64,8320]{1,0:T(8,128)(2,1)} collective-permute-done((bf16[64,8320]{1,0:T(8,128)(2,1)S(1)}, bf16[64,8320]{1,0:T(8,128)(2,1)}, u32[]{:S(2)}, u32[]{:S(2)}) %collective-permute-start.65) | collective-permute-done | bytes 1064992 | tf_op jit(solution)/shard_map/ppermute | solution.py:654
  790.1 4.0 maximum_convert_fusion.1
  794.1 3.8 maximum_convert_fusion
  799.0 26.1 %reduce-scatter.17.cloned.1.call-done = bf16[256,2048]{1,0:T(8,128)(2,1)} async-done(((bf16[1024,2048]{1,0:T(8,128)(2,1)}), bf16[256,2048]{1,0:T(8,128)(2,1)}) %reduce-scatter.17.cloned.1.call-update) | async-done | bytes 1048592 | tf_op jit(solution)/shard_map/reduce_scatter | solution.py:982
  825.1 3.8 maximum_convert_fusion.2
  836.0 12.0 %shard_map.287 = (f32[512,2048]{1,0:T(8,128)}, f32[512,2048]{1,0:T(8,128)}, f32[512,2048]{1,0:T(8,128)}, f32[512,2048]{1,0:T(8,128)}, f32[512,128]{1,0:T(8,128)S(1)}) custom-call(s32[7]{0:T(128)S(1)} %stack.196.ids_ref, bf16[512,2048]{1,0:T(8,128)(2,1)} %wq_ref.3, bf16[512,2048]{1,0:T(8,128)(2,1)} %wk_ref.3, bf16[512,2048]{1,0:T(8,128)(2,1)} %wv_ref.3, ...), custom_call_target="tpu_custom_call" | custom-call | bytes 27525120 | tf_op jit(solution)/shard_map/pallas_call | solution.py:759
  (389 shorter events, 167.2 us)
Async XLA Ops:
  7.2 287.6 %all-gather.4.cloned.1.call-start = ((), (), s32[]{:S(2)}) async-start(), calls=%async_computation.8 | async-start | bytes 10485760 | tf_op jit(solution)/shard_map/all_gather | solution.py:822
  7.2 28.5 %collective-permute-start.17 = (bf16[256,2048]{1,0:T(8,128)(2,1)}, bf16[256,2048]{1,0:T(8,128)(2,1)S(1)}, u32[]{:S(2)}, u32[]{:S(2)}) collective-permute-start(bf16[256,2048]{1,0:T(8,128)(2,1)} %refs_4_.1), channel_id=1, source_target_pairs={{0,8},{4,12},{8,16},{12,20},{16,24},{20,28},{24,0},{28,4},{1,9},{5... | collective-permute-start | bytes 3145736 | tf_op jit(solution)/shard_map/ppermute | solution.py:654
  10.3 25.4 %collective-permute-start.18 = (bf16[256,2048]{1,0:T(8,128)(2,1)}, bf16[256,2048]{1,0:T(8,128)(2,1)}, u32[]{:S(2)}, u32[]{:S(2)}) collective-permute-start(bf16[256,2048]{1,0:T(8,128)(2,1)} %refs_4_.1), channel_id=1, source_target_pairs={{0,4},{4,0},{8,12},{12,8},{16,20},{20,16},{24,28},{28,24},{1,5},{5... | collective-permute-start | bytes 3145736 | tf_op jit(solution)/shard_map/ppermute | solution.py:650
  11.8 33.1 %collective-permute-start.9 = (bf16[256,2048]{1,0:T(8,128)(2,1)}, bf16[256,2048]{1,0:T(8,128)(2,1)}, u32[]{:S(2)}, u32[]{:S(2)}) collective-permute-start(bf16[256,2048]{1,0:T(8,128)(2,1)} %refs_0_.1), channel_id=1, source_target_pairs={{0,2},{1,3},{2,0},{3,1},{4,6},{5,7},{6,4},{7,5},{8,10},{9,11},{10,... | collective-permute-start | bytes 3145736 | tf_op jit(solution)/shard_map/ppermute | solution.py:618
  16.4 28.5 %collective-permute-start.3 = (bf16[2,64,1536]{2,1,0:T(8,128)(2,1)}, bf16[2,64,1536]{2,1,0:T(8,128)(2,1)}, u32[]{:S(2)}, u32[]{:S(2)}) collective-permute-start(bf16[2,64,1536]{2,1,0:T(8,128)(2,1)} %shard_map.263), channel_id=1, source_target_pairs={{0,2},{1,3},{2,0},{3,1},{4,6},{5,7},{6,4},{7,5},{8,10},{9,11},{10,... | collective-permute-start | bytes 1179656 | tf_op jit(solution)/shard_map/ppermute | solution.py:618
  45.0 249.8 %all-gather.6.cloned.1.call-start = ((), (), s32[]{:S(2)}) async-start(), calls=%async_computation.9 | async-start | bytes 10485760 | tf_op jit(solution)/shard_map/all_gather | solution.py:833
  45.7 249.1 %all-gather.8.cloned.1.call-start = ((), (), s32[]{:S(2)}) async-start(), calls=%async_computation.10 | async-start | bytes 10485760 | tf_op jit(solution)/shard_map/all_gather | solution.py:885
  46.0 32.9 %collective-permute-start.1 = (bf16[512,128]{0,1:T(8,128)(2,1)S(1)}, bf16[512,128]{0,1:T(8,128)(2,1)}, u32[]{:S(2)}, u32[]{:S(2)}) collective-permute-start(bf16[512,128]{0,1:T(8,128)(2,1)S(1)} %get-tuple-element.517), channel_id=1, source_target_pairs={{0,2},{1,3},{2,0},{3,1},{4,6},{5,7},{6,4},{7,5},{8,10},{9,11},{10,... | collective-permute-start | bytes 393224 | tf_op jit(solution)/shard_map/ppermute | solution.py:618
  47.5 39.1 %collective-permute-start = (bf16[512,128]{0,1:T(8,128)(2,1)S(1)}, bf16[512,128]{0,1:T(8,128)(2,1)}, u32[]{:S(2)}, u32[]{:S(2)}) collective-permute-start(bf16[512,128]{0,1:T(8,128)(2,1)S(1)} %get-tuple-element.517), channel_id=1, source_target_pairs={{0,1},{1,0},{2,3},{3,2},{4,5},{5,4},{6,7},{7,6},{8,9},{9,8},{10,11... | collective-permute-start | bytes 393224 | tf_op jit(solution)/shard_map/ppermute | solution.py:614
  77.7 32.2 %collective-permute-start.7 = (bf16[512,1536]{1,0:T(8,128)(2,1)}, bf16[512,1536]{1,0:T(8,128)(2,1)}, u32[]{:S(2)}, u32[]{:S(2)}) collective-permute-start(bf16[512,1536]{1,0:T(8,128)(2,1)} %dynamic-slice_bitcast_fusion), channel_id=1, source_target_pairs={{0,1},{1,0},{2,3},{3,2},{4,5},{5,4},{6,7},{7,6},{8,9},{9,8},{10,11... | collective-permute-start | bytes 4718600 | tf_op jit(solution)/shard_map/ppermute | solution.py:614
  86.7 23.3 %collective-permute-start.8 = (bf16[256,2048]{1,0:T(8,128)(2,1)}, bf16[256,2048]{1,0:T(8,128)(2,1)}, u32[]{:S(2)}, u32[]{:S(2)}) collective-permute-start(bf16[256,2048]{1,0:T(8,128)(2,1)} %refs_0_.1), channel_id=1, source_target_pairs={{0,1},{1,0},{2,3},{3,2},{4,5},{5,4},{6,7},{7,6},{8,9},{9,8},{10,11... | collective-permute-start | bytes 3145736 | tf_op jit(solution)/shard_map/ppermute | solution.py:614
  86.7 23.3 %collective-permute-start.10 = (bf16[256,2048]{1,0:T(8,128)(2,1)}, bf16[256,2048]{1,0:T(8,128)(2,1)}, u32[]{:S(2)}, u32[]{:S(2)}) collective-permute-start(bf16[256,2048]{1,0:T(8,128)(2,1)} %collective-permute-done.9.refs_2_), channel_id=1, source_target_pairs={{0,1},{1,0},{2,3},{3,2},{4,5},{5,4},{6,7},{7,6},{8,9},{9,8},{10,11... | collective-permute-start | bytes 3145736 | tf_op jit(solution)/shard_map/ppermute | solution.py:614
  109.1 40.8 %collective-permute-start.19 = (bf16[256,2048]{1,0:T(8,128)(2,1)}, bf16[256,2048]{1,0:T(8,128)(2,1)S(1)}, u32[]{:S(2)}, u32[]{:S(2)}) collective-permute-start(bf16[256,2048]{1,0:T(8,128)(2,1)} %copy-done.36), channel_id=1, source_target_pairs={{0,8},{4,12},{8,16},{12,20},{16,24},{20,28},{24,0},{28,4},{1,9},{5... | collective-permute-start | bytes 3145736 | tf_op jit(solution)/shard_map/ppermute | solution.py:654
  109.2 40.7 %collective-permute-start.20 = (bf16[256,2048]{1,0:T(8,128)(2,1)}, bf16[256,2048]{1,0:T(8,128)(2,1)S(1)}, u32[]{:S(2)}, u32[]{:S(2)}) collective-permute-start(bf16[256,2048]{1,0:T(8,128)(2,1)} %copy-done.36), channel_id=1, source_target_pairs={{0,4},{4,0},{8,12},{12,8},{16,20},{20,16},{24,28},{28,24},{1,5},{5... | collective-permute-start | bytes 3145736 | tf_op jit(solution)/shard_map/ppermute | solution.py:650
  154.6 27.9 %collective-permute-start.24 = (bf16[256,2048]{1,0:T(8,128)(2,1)S(1)}, bf16[256,2048]{1,0:T(8,128)(2,1)}, u32[]{:S(2)}, u32[]{:S(2)}) collective-permute-start(bf16[256,2048]{1,0:T(8,128)(2,1)S(1)} %collective-permute-done.19.grad_ref.refs_4_), channel_id=1, source_target_pairs={{0,8},{4,12},{8,16},{12,20},{16,24},{20,28},{24,0},{28,4},{1,9},{5... | collective-permute-start | bytes 3145736 | tf_op jit(solution)/shard_map/ppermute | solution.py:654
  156.4 26.2 %collective-permute-start.25 = (bf16[256,2048]{1,0:T(8,128)(2,1)S(1)}, bf16[256,2048]{1,0:T(8,128)(2,1)}, u32[]{:S(2)}, u32[]{:S(2)}) collective-permute-start(bf16[256,2048]{1,0:T(8,128)(2,1)S(1)} %collective-permute-done.19.grad_ref.refs_4_), channel_id=1, source_target_pairs={{0,4},{4,0},{8,12},{12,8},{16,20},{20,16},{24,28},{28,24},{1,5},{5... | collective-permute-start | bytes 3145736 | tf_op jit(solution)/shard_map/ppermute | solution.py:650
  156.4 26.1 %collective-permute-start.21 = (bf16[256,2048]{1,0:T(8,128)(2,1)S(1)}, bf16[256,2048]{1,0:T(8,128)(2,1)S(1)}, u32[]{:S(2)}, u32[]{:S(2)}) collective-permute-start(bf16[256,2048]{1,0:T(8,128)(2,1)S(1)} %get-tuple-element.507), channel_id=1, source_target_pairs={{0,1},{1,0},{2,3},{3,2},{4,5},{5,4},{6,7},{7,6},{8,9},{9,8},{10,11... | collective-permute-start | bytes 3145736 | tf_op jit(solution)/shard_map/ppermute | solution.py:614
  157.7 25.6 %collective-permute-start.23 = (bf16[256,2048]{1,0:T(8,128)(2,1)S(1)}, bf16[256,2048]{1,0:T(8,128)(2,1)S(1)}, u32[]{:S(2)}, u32[]{:S(2)}) collective-permute-start(bf16[256,2048]{1,0:T(8,128)(2,1)S(1)} %add_convert_fusion.8), channel_id=1, source_target_pairs={{0,2},{1,3},{2,0},{3,1},{4,6},{5,7},{6,4},{7,5},{8,10},{9,11},{10,... | collective-permute-start | bytes 3145736 | tf_op jit(solution)/shard_map/ppermute | solution.py:618
  193.2 26.2 %collective-permute-start.26 = (bf16[256,2048]{1,0:T(8,128)(2,1)S(1)}, bf16[256,2048]{1,0:T(8,128)(2,1)S(1)}, u32[]{:S(2)}, u32[]{:S(2)}) collective-permute-start(bf16[256,2048]{1,0:T(8,128)(2,1)S(1)} %multiply_convert_fusion.x_ref), channel_id=1, source_target_pairs={{0,8},{4,12},{8,16},{12,20},{16,24},{20,28},{24,0},{28,4},{1,9},{5... | collective-permute-start | bytes 3145736 | tf_op jit(solution)/shard_map/ppermute | solution.py:654
  194.9 24.6 %collective-permute-start.27 = (bf16[256,2048]{1,0:T(8,128)(2,1)S(1)}, bf16[256,2048]{1,0:T(8,128)(2,1)}, u32[]{:S(2)}, u32[]{:S(2)}) collective-permute-start(bf16[256,2048]{1,0:T(8,128)(2,1)S(1)} %multiply_convert_fusion.x_ref), channel_id=1, source_target_pairs={{0,4},{4,0},{8,12},{12,8},{16,20},{20,16},{24,28},{28,24},{1,5},{5... | collective-permute-start | bytes 3145736 | tf_op jit(solution)/shard_map/ppermute | solution.py:650
  219.5 25.4 %collective-permute-start.28 = (bf16[256,2048]{1,0:T(8,128)(2,1)S(1)}, bf16[256,2048]{1,0:T(8,128)(2,1)}, u32[]{:S(2)}, u32[]{:S(2)}) collective-permute-start(bf16[256,2048]{1,0:T(8,128)(2,1)S(1)} %collective-permute-done.26.x_ref), channel_id=1, source_target_pairs={{0,8},{4,12},{8,16},{12,20},{16,24},{20,28},{24,0},{28,4},{1,9},{5... | collective-permute-start | bytes 3145736 | tf_op jit(solution)/shard_map/ppermute | solution.py:654
  221.8 23.3 %collective-permute-start.29 = (bf16[256,2048]{1,0:T(8,128)(2,1)S(1)}, bf16[256,2048]{1,0:T(8,128)(2,1)S(1)}, u32[]{:S(2)}, u32[]{:S(2)}) collective-permute-start(bf16[256,2048]{1,0:T(8,128)(2,1)S(1)} %collective-permute-done.26.x_ref), channel_id=1, source_target_pairs={{0,4},{4,0},{8,12},{12,8},{16,20},{20,16},{24,28},{28,24},{1,5},{5... | collective-permute-start | bytes 3145736 | tf_op jit(solution)/shard_map/ppermute | solution.py:650
  246.2 24.5 %collective-permute-start.30 = (bf16[256,2048]{1,0:T(8,128)(2,1)}, bf16[256,2048]{1,0:T(8,128)(2,1)S(1)}, u32[]{:S(2)}, u32[]{:S(2)}) collective-permute-start(bf16[256,2048]{1,0:T(8,128)(2,1)} %collective-permute-done.28.x_ref), channel_id=1, source_target_pairs={{0,8},{4,12},{8,16},{12,20},{16,24},{20,28},{24,0},{28,4},{1,9},{5... | collective-permute-start | bytes 3145736 | tf_op jit(solution)/shard_map/ppermute | solution.py:654
  246.8 23.9 %collective-permute-start.31 = (bf16[256,2048]{1,0:T(8,128)(2,1)}, bf16[256,2048]{1,0:T(8,128)(2,1)S(1)}, u32[]{:S(2)}, u32[]{:S(2)}) collective-permute-start(bf16[256,2048]{1,0:T(8,128)(2,1)} %collective-permute-done.28.x_ref), channel_id=1, source_target_pairs={{0,4},{4,0},{8,12},{12,8},{16,20},{20,16},{24,28},{28,24},{1,5},{5... | collective-permute-start | bytes 3145736 | tf_op jit(solution)/shard_map/ppermute | solution.py:650
  294.8 59.8 %collective-permute-start.34 = (bf16[256,2048]{1,0:T(8,128)(2,1)}, bf16[256,2048]{1,0:T(8,128)(2,1)}, u32[]{:S(2)}, u32[]{:S(2)}) collective-permute-start(bf16[256,2048]{1,0:T(8,128)(2,1)} %collective-permute-done.24.grad_ref.refs_6_), channel_id=1, source_target_pairs={{0,4},{4,0},{8,12},{12,8},{16,20},{20,16},{24,28},{28,24},{1,5},{5... | collective-permute-start | bytes 3145736 | tf_op jit(solution)/shard_map/ppermute | solution.py:650
  352.6 58.7 %collective-permute-start.35 = (bf16[256,2048]{1,0:T(8,128)(2,1)}, bf16[256,2048]{1,0:T(8,128)(2,1)}, u32[]{:S(2)}, u32[]{:S(2)}) collective-permute-start(bf16[256,2048]{1,0:T(8,128)(2,1)} %get-tuple-element.267), channel_id=1, source_target_pairs={{0,4},{4,0},{8,12},{12,8},{16,20},{20,16},{24,28},{28,24},{1,5},{5... | collective-permute-start | bytes 3145736 | tf_op jit(solution)/shard_map/ppermute | solution.py:650
  360.0 51.3 %collective-permute-start.36 = (bf16[256,2048]{1,0:T(8,128)(2,1)}, bf16[256,2048]{1,0:T(8,128)(2,1)}, u32[]{:S(2)}, u32[]{:S(2)}) collective-permute-start(bf16[256,2048]{1,0:T(8,128)(2,1)} %get-tuple-element.290), channel_id=1, source_target_pairs={{0,4},{4,0},{8,12},{12,8},{16,20},{20,16},{24,28},{28,24},{1,5},{5... | collective-permute-start | bytes 3145736 | tf_op jit(solution)/shard_map/ppermute | solution.py:650
  409.2 28.8 %collective-permute-start.37 = (bf16[256,2048]{1,0:T(8,128)(2,1)}, bf16[256,2048]{1,0:T(8,128)(2,1)}, u32[]{:S(2)}, u32[]{:S(2)}) collective-permute-start(bf16[256,2048]{1,0:T(8,128)(2,1)} %get-tuple-element.295), channel_id=1, source_target_pairs={{0,4},{4,0},{8,12},{12,8},{16,20},{20,16},{24,28},{28,24},{1,5},{5... | collective-permute-start | bytes 3145736 | tf_op jit(solution)/shard_map/ppermute | solution.py:650
  413.9 24.2 %collective-permute-start.38 = (bf16[256,2048]{1,0:T(8,128)(2,1)}, bf16[256,2048]{1,0:T(8,128)(2,1)}, u32[]{:S(2)}, u32[]{:S(2)}) collective-permute-start(bf16[256,2048]{1,0:T(8,128)(2,1)} %add_convert_fusion.7), channel_id=1, source_target_pairs={{0,8},{4,12},{8,16},{12,20},{16,24},{20,28},{24,0},{28,4},{1,9},{5... | collective-permute-start | bytes 3145736 | tf_op jit(solution)/shard_map/ppermute | solution.py:654
  438.0 31.6 %collective-permute-start.40 = (bf16[256,2048]{1,0:T(8,128)(2,1)}, bf16[256,2048]{1,0:T(8,128)(2,1)}, u32[]{:S(2)}, u32[]{:S(2)}) collective-permute-start(bf16[256,2048]{1,0:T(8,128)(2,1)} %get-tuple-element.312), channel_id=1, source_target_pairs={{0,4},{4,0},{8,12},{12,8},{16,20},{20,16},{24,28},{28,24},{1,5},{5... | collective-permute-start | bytes 3145736 | tf_op jit(solution)/shard_map/ppermute | solution.py:650
  441.5 28.1 %collective-permute-start.39 = (bf16[256,2048]{1,0:T(8,128)(2,1)}, bf16[256,2048]{1,0:T(8,128)(2,1)}, u32[]{:S(2)}, u32[]{:S(2)}) collective-permute-start(bf16[256,2048]{1,0:T(8,128)(2,1)} %add_convert_fusion.6), channel_id=1, source_target_pairs={{0,8},{4,12},{8,16},{12,20},{16,24},{20,28},{24,0},{28,4},{1,9},{5... | collective-permute-start | bytes 3145736 | tf_op jit(solution)/shard_map/ppermute | solution.py:654
  443.6 24.0 %all-to-all-start = ((f32[8,2,256]{2,1,0:T(2,128)}), f32[8,2,256]{2,1,0:T(2,128)S(1)}, u32[]{:S(2)}, u32[]{:S(2)}) async-start(f32[8,2,256]{2,1,0:T(2,128)} %scatter_fusion.1), calls=%async_computation | async-start | bytes 32768 | tf_op jit(solution)/shard_map/all_to_all | solution.py:1022
  449.1 341.1 %reduce-scatter.11.cloned.1.call-start = ((), (), s32[]{:S(2)}) async-start(), calls=%async_computation.13 | async-start | bytes 5242880 | tf_op jit(solution)/shard_map/reduce_scatter | solution.py:982
  469.6 24.9 %collective-permute-start.42 = (bf16[256,2048]{1,0:T(8,128)(2,1)}, bf16[256,2048]{1,0:T(8,128)(2,1)S(1)}, u32[]{:S(2)}, u32[]{:S(2)}) collective-permute-start(bf16[256,2048]{1,0:T(8,128)(2,1)} %get-tuple-element.330), channel_id=1, source_target_pairs={{0,4},{4,0},{8,12},{12,8},{16,20},{20,16},{24,28},{28,24},{1,5},{5... | collective-permute-start | bytes 3145736 | tf_op jit(solution)/shard_map/ppermute | solution.py:650
  475.0 20.8 %collective-permute-start.41 = (bf16[256,2048]{1,0:T(8,128)(2,1)}, bf16[256,2048]{1,0:T(8,128)(2,1)}, u32[]{:S(2)}, u32[]{:S(2)}) collective-permute-start(bf16[256,2048]{1,0:T(8,128)(2,1)} %add_convert_fusion.5), channel_id=1, source_target_pairs={{0,8},{4,12},{8,16},{12,20},{16,24},{20,28},{24,0},{28,4},{1,9},{5... | collective-permute-start | bytes 3145736 | tf_op jit(solution)/shard_map/ppermute | solution.py:654
  500.1 26.0 %collective-permute-start.46 = (bf16[256,2048]{1,0:T(8,128)(2,1)S(1)}, bf16[256,2048]{1,0:T(8,128)(2,1)}, u32[]{:S(2)}, u32[]{:S(2)}) collective-permute-start(bf16[256,2048]{1,0:T(8,128)(2,1)S(1)} %add_convert_fusion.4), channel_id=1, source_target_pairs={{0,8},{4,12},{8,16},{12,20},{16,24},{20,28},{24,0},{28,4},{1,9},{5... | collective-permute-start | bytes 3145736 | tf_op jit(solution)/shard_map/ppermute | solution.py:654
  500.7 25.3 %collective-permute-start.45 = (bf16[256,2048]{1,0:T(8,128)(2,1)}, bf16[256,2048]{1,0:T(8,128)(2,1)}, u32[]{:S(2)}, u32[]{:S(2)}) collective-permute-start(bf16[256,2048]{1,0:T(8,128)(2,1)} %get-tuple-element.333), channel_id=1, source_target_pairs={{0,4},{4,0},{8,12},{12,8},{16,20},{20,16},{24,28},{28,24},{1,5},{5... | collective-permute-start | bytes 3145736 | tf_op jit(solution)/shard_map/ppermute | solution.py:650
  502.9 23.1 %collective-permute-start.44 = (bf16[256,2048]{1,0:T(8,128)(2,1)}, bf16[256,2048]{1,0:T(8,128)(2,1)}, u32[]{:S(2)}, u32[]{:S(2)}) collective-permute-start(bf16[256,2048]{1,0:T(8,128)(2,1)} %fusion.32), channel_id=1, source_target_pairs={{0,2},{1,3},{2,0},{3,1},{4,6},{5,7},{6,4},{7,5},{8,10},{9,11},{10,... | collective-permute-start | bytes 3145736 | tf_op jit(solution)/shard_map/ppermute | solution.py:618
  504.2 22.4 %collective-permute-start.43 = (bf16[256,2048]{1,0:T(8,128)(2,1)}, bf16[256,2048]{1,0:T(8,128)(2,1)}, u32[]{:S(2)}, u32[]{:S(2)}) collective-permute-start(bf16[256,2048]{1,0:T(8,128)(2,1)} %fusion.32), channel_id=1, source_target_pairs={{0,1},{1,0},{2,3},{3,2},{4,5},{5,4},{6,7},{7,6},{8,9},{9,8},{10,11... | collective-permute-start | bytes 3145736 | tf_op jit(solution)/shard_map/ppermute | solution.py:614
  535.4 254.7 %reduce-scatter.13.cloned.1.call-start = ((), (), s32[]{:S(2)}) async-start(), calls=%async_computation.14 | async-start | bytes 5242880 | tf_op jit(solution)/shard_map/reduce_scatter | solution.py:982
  536.0 258.1 %reduce-scatter.7.cloned.1.call-start = ((), (), s32[]{:S(2)}) async-start(), calls=%async_computation.11 | async-start | bytes 5242880 | tf_op jit(solution)/shard_map/reduce_scatter | solution.py:982
  536.6 257.5 %reduce-scatter.9.cloned.1.call-start = ((), (), s32[]{:S(2)}) async-start(), calls=%async_computation.12 | async-start | bytes 5242880 | tf_op jit(solution)/shard_map/reduce_scatter | solution.py:982
  537.4 261.6 %reduce-scatter.15.cloned.1.call-start = ((), (), s32[]{:S(2)}) async-start(), calls=%async_computation.15 | async-start | bytes 5242880 | tf_op jit(solution)/shard_map/reduce_scatter | solution.py:982
  541.5 44.9 %collective-permute-start.49 = (bf16[256,2048]{1,0:T(8,128)(2,1)}, bf16[256,2048]{1,0:T(8,128)(2,1)}, u32[]{:S(2)}, u32[]{:S(2)}) collective-permute-start(bf16[256,2048]{1,0:T(8,128)(2,1)} %add_convert_fusion.3), channel_id=1, source_target_pairs={{0,8},{4,12},{8,16},{12,20},{16,24},{20,28},{24,0},{28,4},{1,9},{5... | collective-permute-start | bytes 3145736 | tf_op jit(solution)/shard_map/ppermute | solution.py:654
  543.0 43.4 %collective-permute-start.48 = (bf16[256,2048]{1,0:T(8,128)(2,1)}, bf16[256,2048]{1,0:T(8,128)(2,1)}, u32[]{:S(2)}, u32[]{:S(2)}) collective-permute-start(bf16[256,2048]{1,0:T(8,128)(2,1)} %get-tuple-element.345), channel_id=1, source_target_pairs={{0,4},{4,0},{8,12},{12,8},{16,20},{20,16},{24,28},{28,24},{1,5},{5... | collective-permute-start | bytes 3145736 | tf_op jit(solution)/shard_map/ppermute | solution.py:650
  586.4 238.7 %reduce-scatter.17.cloned.1.call-start = ((), (), s32[]{:S(2)}) async-start(), calls=%async_computation.16 | async-start | bytes 5242880 | tf_op jit(solution)/shard_map/reduce_scatter | solution.py:982
  623.5 25.6 %collective-permute-start.57 = (bf16[4,64,2176]{2,1,0:T(8,128)(2,1)}, bf16[4,64,2176]{2,1,0:T(8,128)(2,1)}, u32[]{:S(2)}, u32[]{:S(2)}) collective-permute-start(bf16[4,64,2176]{2,1,0:T(8,128)(2,1)} %get-tuple-element.363), channel_id=1, source_target_pairs={{0,4},{4,0},{8,12},{12,8},{16,20},{20,16},{24,28},{28,24},{1,5},{5... | collective-permute-start | bytes 3342344 | tf_op jit(solution)/shard_map/ppermute | solution.py:650
  624.4 26.5 %collective-permute-start.58 = (bf16[4,64,2176]{2,1,0:T(8,128)(2,1)}, bf16[4,64,2176]{2,1,0:T(8,128)(2,1)}, u32[]{:S(2)}, u32[]{:S(2)}) collective-permute-start(bf16[4,64,2176]{2,1,0:T(8,128)(2,1)} %get-tuple-element.498), channel_id=1, source_target_pairs={{0,8},{4,12},{8,16},{12,20},{16,24},{20,28},{24,0},{28,4},{1,9},{5... | collective-permute-start | bytes 3342344 | tf_op jit(solution)/shard_map/ppermute | solution.py:654
  654.2 25.6 %collective-permute-start.60 = (bf16[4,64,2176]{2,1,0:T(8,128)(2,1)}, bf16[4,64,2176]{2,1,0:T(8,128)(2,1)}, u32[]{:S(2)}, u32[]{:S(2)}) collective-permute-start(bf16[4,64,2176]{2,1,0:T(8,128)(2,1)} %fusion.5), channel_id=1, source_target_pairs={{0,8},{4,12},{8,16},{12,20},{16,24},{20,28},{24,0},{28,4},{1,9},{5... | collective-permute-start | bytes 3342344 | tf_op jit(solution)/shard_map/ppermute | solution.py:654
  654.2 25.6 %collective-permute-start.59 = (bf16[4,64,2176]{2,1,0:T(8,128)(2,1)}, bf16[4,64,2176]{2,1,0:T(8,128)(2,1)}, u32[]{:S(2)}, u32[]{:S(2)}) collective-permute-start(bf16[4,64,2176]{2,1,0:T(8,128)(2,1)} %get-tuple-element.365), channel_id=1, source_target_pairs={{0,4},{4,0},{8,12},{12,8},{16,20},{20,16},{24,28},{28,24},{1,5},{5... | collective-permute-start | bytes 3342344 | tf_op jit(solution)/shard_map/ppermute | solution.py:650
  682.2 25.5 %collective-permute-start.62 = (bf16[4,64,2176]{2,1,0:T(8,128)(2,1)S(1)}, bf16[4,64,2176]{2,1,0:T(8,128)(2,1)S(1)}, u32[]{:S(2)}, u32[]{:S(2)}) collective-permute-start(bf16[4,64,2176]{2,1,0:T(8,128)(2,1)S(1)} %fusion.3), channel_id=1, source_target_pairs={{0,8},{4,12},{8,16},{12,20},{16,24},{20,28},{24,0},{28,4},{1,9},{5... | collective-permute-start | bytes 3342344 | tf_op jit(solution)/shard_map/ppermute | solution.py:654
  682.2 28.0 %collective-permute-start.61 = (bf16[4,64,2176]{2,1,0:T(8,128)(2,1)S(1)}, bf16[4,64,2176]{2,1,0:T(8,128)(2,1)S(1)}, u32[]{:S(2)}, u32[]{:S(2)}) collective-permute-start(bf16[4,64,2176]{2,1,0:T(8,128)(2,1)S(1)} %get-tuple-element.368), channel_id=1, source_target_pairs={{0,4},{4,0},{8,12},{12,8},{16,20},{20,16},{24,28},{28,24},{1,5},{5... | collective-permute-start | bytes 3342344 | tf_op jit(solution)/shard_map/ppermute | solution.py:650
  698.0 20.6 %collective-permute-start.53 = (bf16[256,2048]{1,0:T(8,128)(2,1)}, bf16[256,2048]{1,0:T(8,128)(2,1)}, u32[]{:S(2)}, u32[]{:S(2)}) collective-permute-start(bf16[256,2048]{1,0:T(8,128)(2,1)} %get-tuple-element.506), channel_id=1, source_target_pairs={{0,1},{1,0},{2,3},{3,2},{4,5},{5,4},{6,7},{7,6},{8,9},{9,8},{10,11... | collective-permute-start | bytes 3145736 | tf_op jit(solution)/shard_map/ppermute | solution.py:614
  701.1 33.9 %collective-permute-start.51 = (bf16[256,2048]{1,0:T(8,128)(2,1)}, bf16[256,2048]{1,0:T(8,128)(2,1)}, u32[]{:S(2)}, u32[]{:S(2)}) collective-permute-start(bf16[256,2048]{1,0:T(8,128)(2,1)} %add_convert_fusion.2), channel_id=1, source_target_pairs={{0,8},{4,12},{8,16},{12,20},{16,24},{20,28},{24,0},{28,4},{1,9},{5... | collective-permute-start | bytes 3145736 | tf_op jit(solution)/shard_map/ppermute | solution.py:654
  701.1 35.6 %collective-permute-start.50 = (bf16[256,2048]{1,0:T(8,128)(2,1)}, bf16[256,2048]{1,0:T(8,128)(2,1)}, u32[]{:S(2)}, u32[]{:S(2)}) collective-permute-start(bf16[256,2048]{1,0:T(8,128)(2,1)} %get-tuple-element.352), channel_id=1, source_target_pairs={{0,4},{4,0},{8,12},{12,8},{16,20},{20,16},{24,28},{28,24},{1,5},{5... | collective-permute-start | bytes 3145736 | tf_op jit(solution)/shard_map/ppermute | solution.py:650
  707.7 29.1 %collective-permute-start.52 = (bf16[256,2048]{1,0:T(8,128)(2,1)}, bf16[256,2048]{1,0:T(8,128)(2,1)}, u32[]{:S(2)}, u32[]{:S(2)}) collective-permute-start(bf16[256,2048]{1,0:T(8,128)(2,1)} %get-tuple-element.505), channel_id=1, source_target_pairs={{0,1},{1,0},{2,3},{3,2},{4,5},{5,4},{6,7},{7,6},{8,9},{9,8},{10,11... | collective-permute-start | bytes 3145736 | tf_op jit(solution)/shard_map/ppermute | solution.py:614
  712.9 19.5 %all-to-all-start.1 = ((bf16[4,64,1664]{2,1,0:T(8,128)(2,1)}), bf16[4,64,1664]{2,1,0:T(8,128)(2,1)}, u32[]{:S(2)}, u32[]{:S(2)}) async-start(bf16[4,64,1664]{2,1,0:T(8,128)(2,1)} %slice.191), calls=%async_computation.1 | async-start | bytes 1703936 | tf_op jit(solution)/shard_map/all_to_all | solution.py:1096
  721.5 38.0 %collective-permute-start.54 = (bf16[256,2048]{1,0:T(8,128)(2,1)}, bf16[256,2048]{1,0:T(8,128)(2,1)}, u32[]{:S(2)}, u32[]{:S(2)}) collective-permute-start(bf16[256,2048]{1,0:T(8,128)(2,1)} %add_convert_fusion), channel_id=1, source_target_pairs={{0,2},{1,3},{2,0},{3,1},{4,6},{5,7},{6,4},{7,5},{8,10},{9,11},{10,... | collective-permute-start | bytes 3145736 | tf_op jit(solution)/shard_map/ppermute | solution.py:618
  734.8 27.4 %collective-permute-start.63 = (bf16[64,8320]{1,0:T(8,128)(2,1)S(1)}, bf16[64,8320]{1,0:T(8,128)(2,1)S(1)}, u32[]{:S(2)}, u32[]{:S(2)}) collective-permute-start(bf16[64,8320]{1,0:T(8,128)(2,1)S(1)} %pad_maximum_fusion.2.refs_0_), channel_id=1, source_target_pairs={{0,8},{4,12},{8,16},{12,20},{16,24},{20,28},{24,0},{28,4},{1,9},{5... | collective-permute-start | bytes 3194888 | tf_op jit(solution)/shard_map/ppermute | solution.py:654
  735.0 27.2 %collective-permute-start.64 = (bf16[64,8320]{1,0:T(8,128)(2,1)S(1)}, bf16[64,8320]{1,0:T(8,128)(2,1)S(1)}, u32[]{:S(2)}, u32[]{:S(2)}) collective-permute-start(bf16[64,8320]{1,0:T(8,128)(2,1)S(1)} %pad_maximum_fusion.2.refs_0_), channel_id=1, source_target_pairs={{0,4},{4,0},{8,12},{12,8},{16,20},{20,16},{24,28},{28,24},{1,5},{5... | collective-permute-start | bytes 3194888 | tf_op jit(solution)/shard_map/ppermute | solution.py:650
  763.2 26.9 %collective-permute-start.65 = (bf16[64,8320]{1,0:T(8,128)(2,1)S(1)}, bf16[64,8320]{1,0:T(8,128)(2,1)}, u32[]{:S(2)}, u32[]{:S(2)}) collective-permute-start(bf16[64,8320]{1,0:T(8,128)(2,1)S(1)} %collective-permute-done.63.refs_2_), channel_id=1, source_target_pairs={{0,8},{4,12},{8,16},{12,20},{16,24},{20,28},{24,0},{28,4},{1,9},{5... | collective-permute-start | bytes 3194888 | tf_op jit(solution)/shard_map/ppermute | solution.py:654
  763.2 26.9 %collective-permute-start.66 = (bf16[64,8320]{1,0:T(8,128)(2,1)S(1)}, bf16[64,8320]{1,0:T(8,128)(2,1)}, u32[]{:S(2)}, u32[]{:S(2)}) collective-permute-start(bf16[64,8320]{1,0:T(8,128)(2,1)S(1)} %collective-permute-done.63.refs_2_), channel_id=1, source_target_pairs={{0,4},{4,0},{8,12},{12,8},{16,20},{20,16},{24,28},{28,24},{1,5},{5... | collective-permute-start | bytes 3194888 | tf_op jit(solution)/shard_map/ppermute | solution.py:650
  797.9 31.0 %collective-permute-start.67 = (bf16[64,8320]{1,0:T(8,128)(2,1)}, bf16[64,8320]{1,0:T(8,128)(2,1)}, u32[]{:S(2)}, u32[]{:S(2)}) collective-permute-start(bf16[64,8320]{1,0:T(8,128)(2,1)} %collective-permute-done.65.refs_4_), channel_id=1, source_target_pairs={{0,8},{4,12},{8,16},{12,20},{16,24},{20,28},{24,0},{28,4},{1,9},{5... | collective-permute-start | bytes 3194888 | tf_op jit(solution)/shard_map/ppermute | solution.py:654
  797.9 31.0 %collective-permute-start.68 = (bf16[64,8320]{1,0:T(8,128)(2,1)}, bf16[64,8320]{1,0:T(8,128)(2,1)}, u32[]{:S(2)}, u32[]{:S(2)}) collective-permute-start(bf16[64,8320]{1,0:T(8,128)(2,1)} %collective-permute-done.65.refs_4_), channel_id=1, source_target_pairs={{0,4},{4,0},{8,12},{12,8},{16,20},{20,16},{24,28},{28,24},{1,5},{5... | collective-permute-start | bytes 3194888 | tf_op jit(solution)/shard_map/ppermute | solution.py:650
  (83 other events, 1028.5 us)
Sparse Core Ops, SparseCore 0:
  45.1 57.5 all-gather.3
  104.2 58.5 all-gather.5
  185.9 58.6 all-gather.7
  535.5 44.6 reduce-scatter.10
  583.4 44.5 reduce-scatter.12
  630.9 44.4 reduce-scatter.6
  678.7 44.4 reduce-scatter.8
  726.3 52.1 reduce-scatter.14
  781.7 43.3 reduce-scatter.16

commit v7 on v6

--- a/solution.py
+++ b/solution.py
@@ -768,7 +768,7 @@
         ),
         out_shape=[big, big, big, big, jax.ShapeDtypeStruct((rows, HD), F32)],
         input_output_aliases={5 + blocks + i: i for i in range(len(held))},
-        compiler_params=params(52),
+        compiler_params=params(58),
         cost_estimate=cost(0, blocks * part * width * 30),
     )(ids, w_query, w_key, w_value, gain, *gathered, *held)
 
@@ -1100,7 +1100,7 @@
     gathered = rep_gather(
         jnp.concatenate([wide, out_part, extra], axis=1),
         rep_count,
-        {2: (grad_gate, grad_up, output), 3: (grad_down, tokens_grad)},
+        {2: (grad_gate, grad_up, output), 3: (tokens_grad,)},
     )
     gain_rows = norm_attn.astype(F32)[:, None]
     most = rep_count - 1

time: 869 us -> 868 us (level)
  starting transfers between devices: 74.3 us -> 64.5 us
    ppermute x25, waiting for transfers between devices: 162 us -> 197 us  [turn_z(): return lax.ppermute(value, 'rep', ring_next(count))]
    reduce_scatter x6, waiting for transfers between devices: 26.2 us -> 0.01 us  [owned_part(): return lax.psum_scatter(grad, 'shard', scatter_dimension=0, tiled=True)]
    unnamed x138 -> x148, local copies, waits for them, and re-layouts: 25.8 us -> 27.5 us
  transfers between devices with their start and end apart: 82 -> 82, of which waited for: 28 -> 26; matrix products, arithmetic and copies ran while one was open for 16% -> 16% of each run, Pallas kernels for 37% -> 37%
where the time goes in v7:
time: 868 us; the launch traced here: 861 us
  Pallas kernels  323 us (37%)
  waiting for transfers between devices  282 us (32%)
  other arithmetic  77.6 us (9%)
  starting transfers between devices  64.5 us (7%)
  local copies, waits for them, and re-layouts  62.4 us (7%)
  matrix products  36.2 us (4%)
  between operations  15.2 us (2%)
    ppermute x25, waiting for transfers between devices, turn_z(): return lax.ppermute(value, 'rep', ring_next(count))  197 us
    pallas_call x2, Pallas kernels, run_experts(): pl.pallas_call(functools.partial(expert_body, rows // 2), grid=(experts,...  92 us
    pallas_call x4, Pallas kernels, weight_grads(): pl.pallas_call(functools.partial(weight_grads_body, groups, count), grid=...  58.3 us
    pallas_call x8, Pallas kernels, pick(): pl.pallas_call(functools.partial(pick_rows, held is not None), grid_spec=...  43.4 us
    ppermute x28, waiting for transfers between devices, swap_y(): return lax.ppermute(value, 'rep', [(i, i ^ 1) for i in range(count)])  38.9 us
    pallas_call x1, Pallas kernels, attention_backward(): pl.pallas_call(attend_backward, grid=(heads,), in_specs=[wide, pl.BlockSp...  34.3 us
    ppermute x6, waiting for transfers between devices, swap_x(): return lax.ppermute(value, 'shard', [(i, i ^ 2) for i in range(4)])  31.1 us
    unnamed x148, local copies, waits for them, and re-layouts  27.5 us
  transfers between devices with their start and end apart: 82, of which 26 were waited for; matrix products, arithmetic and copies ran while one was open for 16% of the time, Pallas kernels for 37%

profile of v7, /device:TPU:0, one launch (start us, length us, event | category | flops | bytes accessed | tf_op | source)
XLA Modules:
  0.0 860.9 jit_solution(12490204668315495441)
XLA Ops:
  7.2 3.1 collective-permute-start.17
  17.0 18.7 %collective-permute-done.17.grad_ref.refs_6_ = bf16[256,2048]{1,0:T(8,128)(2,1)S(1)} collective-permute-done((bf16[256,2048]{1,0:T(8,128)(2,1)}, bf16[256,2048]{1,0:T(8,128)(2,1)S(1)}, u32[]{:S(2)}, u32[]{:S(2)}) %collective-permute-start.17) | collective-permute-done | bytes 1048608 | tf_op jit(solution)/shard_map/ppermute | solution.py:654
  35.7 9.2 %collective-permute-done.3 = bf16[2,64,1536]{2,1,0:T(8,128)(2,1)} collective-permute-done((bf16[2,64,1536]{2,1,0:T(8,128)(2,1)}, bf16[2,64,1536]{2,1,0:T(8,128)(2,1)}, u32[]{:S(2)}, u32[]{:S(2)}) %collective-permute-start.3) | collective-permute-done | bytes 393248 | tf_op jit(solution)/shard_map/ppermute | solution.py:618
  52.5 3.1 fusion.20
  55.6 10.1 %collective-permute-done.5.refs_6_.refs_2_ = bf16[2,80,1536]{2,1,0:T(8,128)(2,1)S(1)} collective-permute-done((bf16[2,80,1536]{2,1,0:T(8,128)(2,1)S(1)}, bf16[2,80,1536]{2,1,0:T(8,128)(2,1)S(1)}, u32[]{:S(2)}, u32[]{:S(2)}) %collective-permute-start.5) | collective-permute-done | bytes 491552 | tf_op jit(solution)/shard_map/ppermute | solution.py:654
  91.9 2.7 scatter_fusion
  104.4 3.7 collective-permute-done.16
  109.9 19.0 %shard_map.265 = (bf16[1024,2048]{1,0:T(8,128)(2,1)}, bf16[2048,1536]{1,0:T(8,128)(2,1)}, f32[1024,1536]{1,0:T(8,128)}) custom-call(s32[8]{0:T(128)} %stack.153.order_ref, s32[4]{0:T(128)} %pad_add_fusion.1.shard_ref, f32[1,2048]{1,0:T(1,128)} %bitcast.190, bf16[4,512,1536]{2,1,0:T(8,128)(2,1)} %copy-done.6, ...), custom_call_target="tpu_custom_call" | custom-call | flops 6442450944 | bytes 27262976 | tf_op jit(solution)/shard_map/pallas_call | solution.py:148
  128.9 20.7 %shard_map.266 = bf16[1024,512]{1,0:T(8,128)(2,1)} custom-call(f32[1024,1536]{1,0:T(8,128)} %get-tuple-element.228.qkv_ref, f32[1024,128]{1,0:T(8,128)} %pad_maximum_fusion.7.cos_ref, f32[1024,128]{1,0:T(8,128)} %pad_maximum_fusion.8.sin_ref, f32[1,128]{1,0:T(1,128)} %reshape_squeeze.6.gq_ref, f32[1,128]{1,0:T(1,128)} %reshape_squeeze.7.gk_ref, ...), custom_call_target="tpu_custom_call" | custom-call | flops 8589934592 | bytes 7864320 | tf_op jit(solution)/shard_map/pallas_call | solution.py:268
  149.6 4.3 convolution_convert_fusion.2
  157.5 24.7 %collective-permute-done.24.grad_ref.refs_6_ = bf16[256,2048]{1,0:T(8,128)(2,1)} collective-permute-done((bf16[256,2048]{1,0:T(8,128)(2,1)S(1)}, bf16[256,2048]{1,0:T(8,128)(2,1)}, u32[]{:S(2)}, u32[]{:S(2)}) %collective-permute-start.24) | collective-permute-done | bytes 1048608 | tf_op jit(solution)/shard_map/ppermute | solution.py:654
  197.1 5.6 shard_map.268
  202.6 17.2 %collective-permute-done.26.x_ref = bf16[256,2048]{1,0:T(8,128)(2,1)S(1)} collective-permute-done((bf16[256,2048]{1,0:T(8,128)(2,1)S(1)}, bf16[256,2048]{1,0:T(8,128)(2,1)S(1)}, u32[]{:S(2)}, u32[]{:S(2)}) %collective-permute-start.26) | collective-permute-done | bytes 1048608 | tf_op jit(solution)/shard_map/ppermute | solution.py:654
  222.2 5.4 shard_map.269
  227.6 5.4 shard_map.270
  232.9 12.7 %collective-permute-done.28.x_ref = bf16[256,2048]{1,0:T(8,128)(2,1)} collective-permute-done((bf16[256,2048]{1,0:T(8,128)(2,1)S(1)}, bf16[256,2048]{1,0:T(8,128)(2,1)}, u32[]{:S(2)}, u32[]{:S(2)}) %collective-permute-start.28) | collective-permute-done | bytes 1048608 | tf_op jit(solution)/shard_map/ppermute | solution.py:654
  248.3 5.4 shard_map.271
  253.8 17.9 %collective-permute-done.30.x_ref = bf16[256,2048]{1,0:T(8,128)(2,1)S(1)} collective-permute-done((bf16[256,2048]{1,0:T(8,128)(2,1)}, bf16[256,2048]{1,0:T(8,128)(2,1)S(1)}, u32[]{:S(2)}, u32[]{:S(2)}) %collective-permute-start.30) | collective-permute-done | bytes 1048608 | tf_op jit(solution)/shard_map/ppermute | solution.py:654
  276.2 5.4 shard_map.272
  281.6 5.5 shard_map.275
  287.1 5.4 shard_map.276
  295.5 50.4 %shard_map.273 = (bf16[2,576,2048]{2,1,0:T(8,128)(2,1)}, bf16[2,576,2048]{2,1,0:T(8,128)(2,1)}, bf16[2,576,1024]{2,1,0:T(8,128)(2,1)}, bf16[2,576,1024]{2,1,0:T(8,128)(2,1)}, bf16[2,576,1024]{2,1,0:T(8,128)(2,1)}) custom-call(bf16[2,576,2048]{2,1,0:T(8,128)(2,1)} %bitcast.169, bf16[2,576,2048]{2,1,0:T(8,128)(2,1)} %bitcast.163, ...), custom_call_target="tpu_custom_call" | custom-call | flops 28991029248 | bytes 51118080 | tf_op jit(solution)/shard_map/pallas_call | solution.py:549
  345.9 7.4 shard_map.274
  355.1 5.4 shard_map.277
  360.7 41.6 %shard_map.278 = (bf16[2,576,2048]{2,1,0:T(8,128)(2,1)}, bf16[2,576,2048]{2,1,0:T(8,128)(2,1)}, bf16[2,576,1024]{2,1,0:T(8,128)(2,1)}, bf16[2,576,1024]{2,1,0:T(8,128)(2,1)}, bf16[2,576,1024]{2,1,0:T(8,128)(2,1)}) custom-call(bf16[2,576,2048]{2,1,0:T(8,128)(2,1)} %bitcast.166, bf16[2,576,2048]{2,1,0:T(8,128)(2,1)} %bitcast.160, ...), custom_call_target="tpu_custom_call" | custom-call | flops 28991029248 | bytes 51118080 | tf_op jit(solution)/shard_map/pallas_call | solution.py:549
  402.3 7.5 shard_map.279
  411.7 2.6 add_convert_fusion.7
  414.8 9.8 %shard_map.280 = (bf16[256,2048]{1,0:T(8,128)(2,1)}, bf16[256,2048]{1,0:T(8,128)(2,1)}, bf16[256,2048]{1,0:T(8,128)(2,1)}, bf16[256,2048]{1,0:T(8,128)(2,1)}, f32[4,256,2]{2,1,0:T(8,128)}) custom-call(s32[8,256,128]{2,1,0:T(8,128)} %copy-done.5, f32[256,2]{1,0:T(8,128)} %get-tuple-element.282.refs_0_, f32[256,2]{1,0:T(8,128)} %get-tuple-element.283.refs_1_, ...), custom_call_target="tpu_custom_call" | custom-call | flops 1207959552 | bytes 13107200 | tf_op jit(solution)/shard_map/pallas_call | solution.py:468
  424.6 9.8 %shard_map.281 = (bf16[256,2048]{1,0:T(8,128)(2,1)}, bf16[256,2048]{1,0:T(8,128)(2,1)}, bf16[256,2048]{1,0:T(8,128)(2,1)}, bf16[256,2048]{1,0:T(8,128)(2,1)}, f32[4,256,2]{2,1,0:T(8,128)}) custom-call(s32[8,256,128]{2,1,0:T(8,128)} %copy-done.5, f32[256,2]{1,0:T(8,128)} %get-tuple-element.298.refs_0_, f32[256,2]{1,0:T(8,128)} %get-tuple-element.299.refs_1_, ...), custom_call_target="tpu_custom_call" | custom-call | flops 1207959552 | bytes 13107200 | tf_op jit(solution)/shard_map/pallas_call | solution.py:468
  438.7 3.4 add_convert_fusion.6
  444.1 5.4 all-to-all-start
  449.6 18.5 %shard_map.282 = (bf16[2048,1024]{1,0:T(8,128)(2,1)}, bf16[2048,1024]{1,0:T(8,128)(2,1)}) custom-call(bf16[2,576,2048]{2,1,0:T(8,128)(2,1)} %bitcast.170, bf16[2,576,2048]{2,1,0:T(8,128)(2,1)} %bitcast.167, bf16[2,576,1024]{2,1,0:T(8,128)(2,1)} %get-tuple-element.317.refs_2_, bf16[2,576,1024]{2,1,0:T(8,128)(2,1)} %get-tuple-element.318.refs_3_, ...), custom_call_target="tpu_custom_call" | custom-call | flops 9663676416 | bytes 17825792 | tf_op jit(solution)/shard_map/pallas_call | solution.py:599
  472.0 3.4 add_convert_fusion.5
  476.9 18.0 %shard_map.283 = (bf16[2048,1024]{1,0:T(8,128)(2,1)}, bf16[2048,1024]{1,0:T(8,128)(2,1)}) custom-call(bf16[2,576,2048]{2,1,0:T(8,128)(2,1)} %bitcast.171, bf16[2,576,2048]{2,1,0:T(8,128)(2,1)} %bitcast.168, bf16[2,576,1024]{2,1,0:T(8,128)(2,1)} %get-tuple-element.317.refs_2_, bf16[2,576,1024]{2,1,0:T(8,128)(2,1)} %get-tuple-element.318.refs_3_, ...), custom_call_target="tpu_custom_call" | custom-call | flops 9663676416 | bytes 17825792 | tf_op jit(solution)/shard_map/pallas_call | solution.py:599
  496.4 4.3 multiply_reduce_fusion
  504.2 10.9 %shard_map.285 = bf16[1024,2048]{1,0:T(8,128)(2,1)} custom-call(bf16[2,576,1024]{2,1,0:T(8,128)(2,1)} %get-tuple-element.337.refs_0_, bf16[2,576,1024]{2,1,0:T(8,128)(2,1)} %get-tuple-element.339.refs_1_, bf16[2,576,2048]{2,1,0:T(8,128)(2,1)} %bitcast.164, bf16[2,576,2048]{2,1,0:T(8,128)(2,1)} %bitcast.161), custom_call_target="tpu_custom_call" | custom-call | flops 4831838208 | bytes 11272192 | tf_op jit(solution)/shard_map/pallas_call | solution.py:599
  515.1 10.9 %shard_map.284 = bf16[1024,2048]{1,0:T(8,128)(2,1)} custom-call(bf16[2,576,1024]{2,1,0:T(8,128)(2,1)} %get-tuple-element.337.refs_0_, bf16[2,576,1024]{2,1,0:T(8,128)(2,1)} %get-tuple-element.339.refs_1_, bf16[2,576,2048]{2,1,0:T(8,128)(2,1)} %bitcast.165, bf16[2,576,2048]{2,1,0:T(8,128)(2,1)} %bitcast.162), custom_call_target="tpu_custom_call" | custom-call | flops 4831838208 | bytes 11272192 | tf_op jit(solution)/shard_map/pallas_call | solution.py:599
  530.0 5.3 convolution_convert_fusion.5.do_ref
  538.0 3.4 add_convert_fusion.3
  544.3 34.3 %shard_map.286 = (bf16[1024,1536]{1,0:T(8,128)(2,1)}, f32[8,128]{1,0:T(8,128)}) custom-call(f32[1024,1536]{1,0:T(8,128)} %get-tuple-element.228.qkv_ref, bf16[1024,512]{1,0:T(8,128)(2,1)} %convolution_convert_fusion.5.do_ref, f32[1024,128]{1,0:T(8,128)} %pad_maximum_fusion.7.cos_ref, f32[1024,128]{1,0:T(8,128)} %pad_maximum_fusion.8.sin_ref, ...), custom_call_target="tpu_custom_call" | custom-call | flops 21474836480 | bytes 4718592 | tf_op jit(solution)/shard_map/pallas_call | solution.py:283
  579.9 4.9 convolution_convert_fusion.3
  586.4 10.0 %convolution_convert_fusion = bf16[2048,1536]{1,0:T(8,128)(2,1)S(1)} fusion(bf16[1024,2048]{1,0:T(8,128)(2,1)} %get-tuple-element.357, bf16[1024,1536]{1,0:T(8,128)(2,1)} %get-tuple-element.358), kind=kOutput, calls=%fused_computation.3 | convolution fusion | flops 6445596672 | bytes 13631488 | tf_op jit(solution)/shard_map/dot_general | solution.py:40
  604.9 13.2 %collective-permute-done.55 = bf16[2,64,2176]{2,1,0:T(8,128)(2,1)} collective-permute-done((bf16[2,64,2176]{2,1,0:T(8,128)(2,1)}, bf16[2,64,2176]{2,1,0:T(8,128)(2,1)}, u32[]{:S(2)}, u32[]{:S(2)}) %collective-permute-start.55) | collective-permute-done | bytes 557088 | tf_op jit(solution)/shard_map/ppermute | solution.py:650
  620.5 2.8 fusion.14
  624.5 24.1 %collective-permute-done.57 = bf16[4,64,2176]{2,1,0:T(8,128)(2,1)} collective-permute-done((bf16[4,64,2176]{2,1,0:T(8,128)(2,1)}, bf16[4,64,2176]{2,1,0:T(8,128)(2,1)}, u32[]{:S(2)}, u32[]{:S(2)}) %collective-permute-start.57) | collective-permute-done | bytes 1114144 | tf_op jit(solution)/shard_map/ppermute | solution.py:650
  648.6 2.8 collective-permute-done.58
  651.4 3.3 fusion.5
  655.6 25.6 %collective-permute-done.60 = bf16[4,64,2176]{2,1,0:T(8,128)(2,1)} collective-permute-done((bf16[4,64,2176]{2,1,0:T(8,128)(2,1)}, bf16[4,64,2176]{2,1,0:T(8,128)(2,1)}, u32[]{:S(2)}, u32[]{:S(2)}) %collective-permute-start.60) | collective-permute-done | bytes 1114144 | tf_op jit(solution)/shard_map/ppermute | solution.py:654
  683.8 9.2 %convolution_convert_fusion.1 = bf16[1024,2048]{1,0:T(8,128)(2,1)S(1)} fusion(bf16[1024,1536]{1,0:T(8,128)(2,1)S(1)} %copy-done.69, bf16[2048,1536]{1,0:T(8,128)(2,1)} %get-tuple-element.359), kind=kOutput, calls=%fused_computation.5 | convolution fusion | flops 6444548096 | bytes 13631488 | tf_op jit(solution)/shard_map/dot_general | solution.py:36
  695.7 3.1 add_convert_fusion.2
  700.7 12.1 %collective-permute-done.62 = bf16[4,64,2176]{2,1,0:T(8,128)(2,1)S(1)} collective-permute-done((bf16[4,64,2176]{2,1,0:T(8,128)(2,1)S(1)}, bf16[4,64,2176]{2,1,0:T(8,128)(2,1)S(1)}, u32[]{:S(2)}, u32[]{:S(2)}) %collective-permute-start.62) | collective-permute-done | bytes 1114144 | tf_op jit(solution)/shard_map/ppermute | solution.py:654
  715.4 4.2 all-to-all-start.1
  719.7 2.9 add_convert_fusion
  724.8 8.0 all-to-all-done.1
  737.0 20.9 %collective-permute-done.54 = bf16[256,2048]{1,0:T(8,128)(2,1)} collective-permute-done((bf16[256,2048]{1,0:T(8,128)(2,1)}, bf16[256,2048]{1,0:T(8,128)(2,1)}, u32[]{:S(2)}, u32[]{:S(2)}) %collective-permute-start.54) | collective-permute-done | bytes 1048608 | tf_op jit(solution)/shard_map/ppermute | solution.py:618
  757.9 2.6 fusion.8
  764.1 5.0 fusion.12
  769.1 20.1 %collective-permute-done.65.refs_4_ = bf16[64,8320]{1,0:T(8,128)(2,1)S(1)} collective-permute-done((bf16[64,8320]{1,0:T(8,128)(2,1)S(1)}, bf16[64,8320]{1,0:T(8,128)(2,1)S(1)}, u32[]{:S(2)}, u32[]{:S(2)}) %collective-permute-start.65) | collective-permute-done | bytes 1064992 | tf_op jit(solution)/shard_map/ppermute | solution.py:654
  790.2 3.9 maximum_convert_fusion.1
  794.2 3.9 maximum_convert_fusion
  798.3 25.4 %collective-permute-done.67.refs_6_ = bf16[64,8320]{1,0:T(8,128)(2,1)S(1)} collective-permute-done((bf16[64,8320]{1,0:T(8,128)(2,1)S(1)}, bf16[64,8320]{1,0:T(8,128)(2,1)S(1)}, u32[]{:S(2)}, u32[]{:S(2)}) %collective-permute-start.67) | collective-permute-done | bytes 1064992 | tf_op jit(solution)/shard_map/ppermute | solution.py:654
  827.4 3.8 maximum_convert_fusion.2
  831.2 12.5 %shard_map.287 = (f32[512,2048]{1,0:T(8,128)}, f32[512,2048]{1,0:T(8,128)}, f32[512,2048]{1,0:T(8,128)}, f32[512,2048]{1,0:T(8,128)}, f32[512,128]{1,0:T(8,128)}) custom-call(s32[7]{0:T(128)} %stack.193.ids_ref, bf16[512,2048]{1,0:T(8,128)(2,1)} %wq_ref.3, bf16[512,2048]{1,0:T(8,128)(2,1)} %wk_ref.3, bf16[512,2048]{1,0:T(8,128)(2,1)} %wv_ref.3, ...), custom_call_target="tpu_custom_call" | custom-call | bytes 27525120 | tf_op jit(solution)/shard_map/pallas_call | solution.py:759
  846.0 3.0 shard_map.288
  (399 shorter events, 160.8 us)
Async XLA Ops:
  7.2 288.3 %all-gather.4.cloned.1.call-start = ((), (), s32[]{:S(2)}) async-start(), calls=%async_computation.8 | async-start | bytes 10485760 | tf_op jit(solution)/shard_map/all_gather | solution.py:822
  7.2 28.5 %collective-permute-start.17 = (bf16[256,2048]{1,0:T(8,128)(2,1)}, bf16[256,2048]{1,0:T(8,128)(2,1)S(1)}, u32[]{:S(2)}, u32[]{:S(2)}) collective-permute-start(bf16[256,2048]{1,0:T(8,128)(2,1)} %refs_4_.1), channel_id=1, source_target_pairs={{0,8},{4,12},{8,16},{12,20},{16,24},{20,28},{24,0},{28,4},{1,9},{5... | collective-permute-start | bytes 3145736 | tf_op jit(solution)/shard_map/ppermute | solution.py:654
  10.3 25.4 %collective-permute-start.18 = (bf16[256,2048]{1,0:T(8,128)(2,1)}, bf16[256,2048]{1,0:T(8,128)(2,1)}, u32[]{:S(2)}, u32[]{:S(2)}) collective-permute-start(bf16[256,2048]{1,0:T(8,128)(2,1)} %refs_4_.1), channel_id=1, source_target_pairs={{0,4},{4,0},{8,12},{12,8},{16,20},{20,16},{24,28},{28,24},{1,5},{5... | collective-permute-start | bytes 3145736 | tf_op jit(solution)/shard_map/ppermute | solution.py:650
  11.8 33.1 %collective-permute-start.9 = (bf16[256,2048]{1,0:T(8,128)(2,1)}, bf16[256,2048]{1,0:T(8,128)(2,1)}, u32[]{:S(2)}, u32[]{:S(2)}) collective-permute-start(bf16[256,2048]{1,0:T(8,128)(2,1)} %refs_0_.1), channel_id=1, source_target_pairs={{0,2},{1,3},{2,0},{3,1},{4,6},{5,7},{6,4},{7,5},{8,10},{9,11},{10,... | collective-permute-start | bytes 3145736 | tf_op jit(solution)/shard_map/ppermute | solution.py:618
  16.4 28.5 %collective-permute-start.3 = (bf16[2,64,1536]{2,1,0:T(8,128)(2,1)}, bf16[2,64,1536]{2,1,0:T(8,128)(2,1)}, u32[]{:S(2)}, u32[]{:S(2)}) collective-permute-start(bf16[2,64,1536]{2,1,0:T(8,128)(2,1)} %shard_map.263), channel_id=1, source_target_pairs={{0,2},{1,3},{2,0},{3,1},{4,6},{5,7},{6,4},{7,5},{8,10},{9,11},{10,... | collective-permute-start | bytes 1179656 | tf_op jit(solution)/shard_map/ppermute | solution.py:618
  45.0 250.5 %all-gather.6.cloned.1.call-start = ((), (), s32[]{:S(2)}) async-start(), calls=%async_computation.9 | async-start | bytes 10485760 | tf_op jit(solution)/shard_map/all_gather | solution.py:833
  45.7 249.7 %all-gather.8.cloned.1.call-start = ((), (), s32[]{:S(2)}) async-start(), calls=%async_computation.10 | async-start | bytes 10485760 | tf_op jit(solution)/shard_map/all_gather | solution.py:885
  46.0 32.9 %collective-permute-start.1 = (bf16[512,128]{0,1:T(8,128)(2,1)S(1)}, bf16[512,128]{0,1:T(8,128)(2,1)}, u32[]{:S(2)}, u32[]{:S(2)}) collective-permute-start(bf16[512,128]{0,1:T(8,128)(2,1)S(1)} %get-tuple-element.517), channel_id=1, source_target_pairs={{0,2},{1,3},{2,0},{3,1},{4,6},{5,7},{6,4},{7,5},{8,10},{9,11},{10,... | collective-permute-start | bytes 393224 | tf_op jit(solution)/shard_map/ppermute | solution.py:618
  47.5 39.1 %collective-permute-start = (bf16[512,128]{0,1:T(8,128)(2,1)S(1)}, bf16[512,128]{0,1:T(8,128)(2,1)}, u32[]{:S(2)}, u32[]{:S(2)}) collective-permute-start(bf16[512,128]{0,1:T(8,128)(2,1)S(1)} %get-tuple-element.517), channel_id=1, source_target_pairs={{0,1},{1,0},{2,3},{3,2},{4,5},{5,4},{6,7},{7,6},{8,9},{9,8},{10,11... | collective-permute-start | bytes 393224 | tf_op jit(solution)/shard_map/ppermute | solution.py:614
  77.7 32.1 %collective-permute-start.7 = (bf16[512,1536]{1,0:T(8,128)(2,1)}, bf16[512,1536]{1,0:T(8,128)(2,1)}, u32[]{:S(2)}, u32[]{:S(2)}) collective-permute-start(bf16[512,1536]{1,0:T(8,128)(2,1)} %dynamic-slice_bitcast_fusion), channel_id=1, source_target_pairs={{0,1},{1,0},{2,3},{3,2},{4,5},{5,4},{6,7},{7,6},{8,9},{9,8},{10,11... | collective-permute-start | bytes 4718600 | tf_op jit(solution)/shard_map/ppermute | solution.py:614
  86.6 23.3 %collective-permute-start.8 = (bf16[256,2048]{1,0:T(8,128)(2,1)}, bf16[256,2048]{1,0:T(8,128)(2,1)}, u32[]{:S(2)}, u32[]{:S(2)}) collective-permute-start(bf16[256,2048]{1,0:T(8,128)(2,1)} %refs_0_.1), channel_id=1, source_target_pairs={{0,1},{1,0},{2,3},{3,2},{4,5},{5,4},{6,7},{7,6},{8,9},{9,8},{10,11... | collective-permute-start | bytes 3145736 | tf_op jit(solution)/shard_map/ppermute | solution.py:614
  86.6 23.3 %collective-permute-start.10 = (bf16[256,2048]{1,0:T(8,128)(2,1)}, bf16[256,2048]{1,0:T(8,128)(2,1)}, u32[]{:S(2)}, u32[]{:S(2)}) collective-permute-start(bf16[256,2048]{1,0:T(8,128)(2,1)} %collective-permute-done.9.refs_2_), channel_id=1, source_target_pairs={{0,1},{1,0},{2,3},{3,2},{4,5},{5,4},{6,7},{7,6},{8,9},{9,8},{10,11... | collective-permute-start | bytes 3145736 | tf_op jit(solution)/shard_map/ppermute | solution.py:614
  109.1 40.5 %collective-permute-start.19 = (bf16[256,2048]{1,0:T(8,128)(2,1)}, bf16[256,2048]{1,0:T(8,128)(2,1)S(1)}, u32[]{:S(2)}, u32[]{:S(2)}) collective-permute-start(bf16[256,2048]{1,0:T(8,128)(2,1)} %copy-done.37), channel_id=1, source_target_pairs={{0,8},{4,12},{8,16},{12,20},{16,24},{20,28},{24,0},{28,4},{1,9},{5... | collective-permute-start | bytes 3145736 | tf_op jit(solution)/shard_map/ppermute | solution.py:654
  109.2 40.4 %collective-permute-start.20 = (bf16[256,2048]{1,0:T(8,128)(2,1)}, bf16[256,2048]{1,0:T(8,128)(2,1)S(1)}, u32[]{:S(2)}, u32[]{:S(2)}) collective-permute-start(bf16[256,2048]{1,0:T(8,128)(2,1)} %copy-done.37), channel_id=1, source_target_pairs={{0,4},{4,0},{8,12},{12,8},{16,20},{20,16},{24,28},{28,24},{1,5},{5... | collective-permute-start | bytes 3145736 | tf_op jit(solution)/shard_map/ppermute | solution.py:650
  154.3 27.9 %collective-permute-start.24 = (bf16[256,2048]{1,0:T(8,128)(2,1)S(1)}, bf16[256,2048]{1,0:T(8,128)(2,1)}, u32[]{:S(2)}, u32[]{:S(2)}) collective-permute-start(bf16[256,2048]{1,0:T(8,128)(2,1)S(1)} %collective-permute-done.19.grad_ref.refs_4_), channel_id=1, source_target_pairs={{0,8},{4,12},{8,16},{12,20},{16,24},{20,28},{24,0},{28,4},{1,9},{5... | collective-permute-start | bytes 3145736 | tf_op jit(solution)/shard_map/ppermute | solution.py:654
  156.1 26.2 %collective-permute-start.25 = (bf16[256,2048]{1,0:T(8,128)(2,1)S(1)}, bf16[256,2048]{1,0:T(8,128)(2,1)}, u32[]{:S(2)}, u32[]{:S(2)}) collective-permute-start(bf16[256,2048]{1,0:T(8,128)(2,1)S(1)} %collective-permute-done.19.grad_ref.refs_4_), channel_id=1, source_target_pairs={{0,4},{4,0},{8,12},{12,8},{16,20},{20,16},{24,28},{28,24},{1,5},{5... | collective-permute-start | bytes 3145736 | tf_op jit(solution)/shard_map/ppermute | solution.py:650
  156.2 26.1 %collective-permute-start.21 = (bf16[256,2048]{1,0:T(8,128)(2,1)S(1)}, bf16[256,2048]{1,0:T(8,128)(2,1)S(1)}, u32[]{:S(2)}, u32[]{:S(2)}) collective-permute-start(bf16[256,2048]{1,0:T(8,128)(2,1)S(1)} %get-tuple-element.507), channel_id=1, source_target_pairs={{0,1},{1,0},{2,3},{3,2},{4,5},{5,4},{6,7},{7,6},{8,9},{9,8},{10,11... | collective-permute-start | bytes 3145736 | tf_op jit(solution)/shard_map/ppermute | solution.py:614
  157.3 25.9 %collective-permute-start.23 = (bf16[256,2048]{1,0:T(8,128)(2,1)S(1)}, bf16[256,2048]{1,0:T(8,128)(2,1)S(1)}, u32[]{:S(2)}, u32[]{:S(2)}) collective-permute-start(bf16[256,2048]{1,0:T(8,128)(2,1)S(1)} %add_convert_fusion.8), channel_id=1, source_target_pairs={{0,2},{1,3},{2,0},{3,1},{4,6},{5,7},{6,4},{7,5},{8,10},{9,11},{10,... | collective-permute-start | bytes 3145736 | tf_op jit(solution)/shard_map/ppermute | solution.py:618
  193.2 26.6 %collective-permute-start.26 = (bf16[256,2048]{1,0:T(8,128)(2,1)S(1)}, bf16[256,2048]{1,0:T(8,128)(2,1)S(1)}, u32[]{:S(2)}, u32[]{:S(2)}) collective-permute-start(bf16[256,2048]{1,0:T(8,128)(2,1)S(1)} %multiply_convert_fusion.x_ref), channel_id=1, source_target_pairs={{0,8},{4,12},{8,16},{12,20},{16,24},{20,28},{24,0},{28,4},{1,9},{5... | collective-permute-start | bytes 3145736 | tf_op jit(solution)/shard_map/ppermute | solution.py:654
  194.7 25.1 %collective-permute-start.27 = (bf16[256,2048]{1,0:T(8,128)(2,1)S(1)}, bf16[256,2048]{1,0:T(8,128)(2,1)}, u32[]{:S(2)}, u32[]{:S(2)}) collective-permute-start(bf16[256,2048]{1,0:T(8,128)(2,1)S(1)} %multiply_convert_fusion.x_ref), channel_id=1, source_target_pairs={{0,4},{4,0},{8,12},{12,8},{16,20},{20,16},{24,28},{28,24},{1,5},{5... | collective-permute-start | bytes 3145736 | tf_op jit(solution)/shard_map/ppermute | solution.py:650
  219.8 25.8 %collective-permute-start.28 = (bf16[256,2048]{1,0:T(8,128)(2,1)S(1)}, bf16[256,2048]{1,0:T(8,128)(2,1)}, u32[]{:S(2)}, u32[]{:S(2)}) collective-permute-start(bf16[256,2048]{1,0:T(8,128)(2,1)S(1)} %collective-permute-done.26.x_ref), channel_id=1, source_target_pairs={{0,8},{4,12},{8,16},{12,20},{16,24},{20,28},{24,0},{28,4},{1,9},{5... | collective-permute-start | bytes 3145736 | tf_op jit(solution)/shard_map/ppermute | solution.py:654
  221.6 24.1 %collective-permute-start.29 = (bf16[256,2048]{1,0:T(8,128)(2,1)S(1)}, bf16[256,2048]{1,0:T(8,128)(2,1)S(1)}, u32[]{:S(2)}, u32[]{:S(2)}) collective-permute-start(bf16[256,2048]{1,0:T(8,128)(2,1)S(1)} %collective-permute-done.26.x_ref), channel_id=1, source_target_pairs={{0,4},{4,0},{8,12},{12,8},{16,20},{20,16},{24,28},{28,24},{1,5},{5... | collective-permute-start | bytes 3145736 | tf_op jit(solution)/shard_map/ppermute | solution.py:650
  246.7 25.0 %collective-permute-start.30 = (bf16[256,2048]{1,0:T(8,128)(2,1)}, bf16[256,2048]{1,0:T(8,128)(2,1)S(1)}, u32[]{:S(2)}, u32[]{:S(2)}) collective-permute-start(bf16[256,2048]{1,0:T(8,128)(2,1)} %collective-permute-done.28.x_ref), channel_id=1, source_target_pairs={{0,8},{4,12},{8,16},{12,20},{16,24},{20,28},{24,0},{28,4},{1,9},{5... | collective-permute-start | bytes 3145736 | tf_op jit(solution)/shard_map/ppermute | solution.py:654
  246.7 25.0 %collective-permute-start.31 = (bf16[256,2048]{1,0:T(8,128)(2,1)}, bf16[256,2048]{1,0:T(8,128)(2,1)S(1)}, u32[]{:S(2)}, u32[]{:S(2)}) collective-permute-start(bf16[256,2048]{1,0:T(8,128)(2,1)} %collective-permute-done.28.x_ref), channel_id=1, source_target_pairs={{0,4},{4,0},{8,12},{12,8},{16,20},{20,16},{24,28},{28,24},{1,5},{5... | collective-permute-start | bytes 3145736 | tf_op jit(solution)/shard_map/ppermute | solution.py:650
  295.2 59.8 %collective-permute-start.34 = (bf16[256,2048]{1,0:T(8,128)(2,1)}, bf16[256,2048]{1,0:T(8,128)(2,1)}, u32[]{:S(2)}, u32[]{:S(2)}) collective-permute-start(bf16[256,2048]{1,0:T(8,128)(2,1)} %collective-permute-done.24.grad_ref.refs_6_), channel_id=1, source_target_pairs={{0,4},{4,0},{8,12},{12,8},{16,20},{20,16},{24,28},{28,24},{1,5},{5... | collective-permute-start | bytes 3145736 | tf_op jit(solution)/shard_map/ppermute | solution.py:650
  353.3 58.4 %collective-permute-start.35 = (bf16[256,2048]{1,0:T(8,128)(2,1)}, bf16[256,2048]{1,0:T(8,128)(2,1)}, u32[]{:S(2)}, u32[]{:S(2)}) collective-permute-start(bf16[256,2048]{1,0:T(8,128)(2,1)} %get-tuple-element.267), channel_id=1, source_target_pairs={{0,4},{4,0},{8,12},{12,8},{16,20},{20,16},{24,28},{28,24},{1,5},{5... | collective-permute-start | bytes 3145736 | tf_op jit(solution)/shard_map/ppermute | solution.py:650
  360.4 51.3 %collective-permute-start.36 = (bf16[256,2048]{1,0:T(8,128)(2,1)}, bf16[256,2048]{1,0:T(8,128)(2,1)}, u32[]{:S(2)}, u32[]{:S(2)}) collective-permute-start(bf16[256,2048]{1,0:T(8,128)(2,1)} %get-tuple-element.290), channel_id=1, source_target_pairs={{0,4},{4,0},{8,12},{12,8},{16,20},{20,16},{24,28},{28,24},{1,5},{5... | collective-permute-start | bytes 3145736 | tf_op jit(solution)/shard_map/ppermute | solution.py:650
  409.8 28.6 %collective-permute-start.37 = (bf16[256,2048]{1,0:T(8,128)(2,1)}, bf16[256,2048]{1,0:T(8,128)(2,1)}, u32[]{:S(2)}, u32[]{:S(2)}) collective-permute-start(bf16[256,2048]{1,0:T(8,128)(2,1)} %get-tuple-element.295), channel_id=1, source_target_pairs={{0,4},{4,0},{8,12},{12,8},{16,20},{20,16},{24,28},{28,24},{1,5},{5... | collective-permute-start | bytes 3145736 | tf_op jit(solution)/shard_map/ppermute | solution.py:650
  414.3 24.4 %collective-permute-start.38 = (bf16[256,2048]{1,0:T(8,128)(2,1)}, bf16[256,2048]{1,0:T(8,128)(2,1)}, u32[]{:S(2)}, u32[]{:S(2)}) collective-permute-start(bf16[256,2048]{1,0:T(8,128)(2,1)} %add_convert_fusion.7), channel_id=1, source_target_pairs={{0,8},{4,12},{8,16},{12,20},{16,24},{20,28},{24,0},{28,4},{1,9},{5... | collective-permute-start | bytes 3145736 | tf_op jit(solution)/shard_map/ppermute | solution.py:654
  438.5 31.6 %collective-permute-start.40 = (bf16[256,2048]{1,0:T(8,128)(2,1)}, bf16[256,2048]{1,0:T(8,128)(2,1)}, u32[]{:S(2)}, u32[]{:S(2)}) collective-permute-start(bf16[256,2048]{1,0:T(8,128)(2,1)} %get-tuple-element.312), channel_id=1, source_target_pairs={{0,4},{4,0},{8,12},{12,8},{16,20},{20,16},{24,28},{28,24},{1,5},{5... | collective-permute-start | bytes 3145736 | tf_op jit(solution)/shard_map/ppermute | solution.py:650
  442.1 27.9 %collective-permute-start.39 = (bf16[256,2048]{1,0:T(8,128)(2,1)}, bf16[256,2048]{1,0:T(8,128)(2,1)}, u32[]{:S(2)}, u32[]{:S(2)}) collective-permute-start(bf16[256,2048]{1,0:T(8,128)(2,1)} %add_convert_fusion.6), channel_id=1, source_target_pairs={{0,8},{4,12},{8,16},{12,20},{16,24},{20,28},{24,0},{28,4},{1,9},{5... | collective-permute-start | bytes 3145736 | tf_op jit(solution)/shard_map/ppermute | solution.py:654
  444.1 24.0 %all-to-all-start = ((f32[8,2,256]{2,1,0:T(2,128)}), f32[8,2,256]{2,1,0:T(2,128)S(1)}, u32[]{:S(2)}, u32[]{:S(2)}) async-start(f32[8,2,256]{2,1,0:T(2,128)} %scatter_fusion.1), calls=%async_computation | async-start | bytes 32768 | tf_op jit(solution)/shard_map/all_to_all | solution.py:1022
  449.6 340.7 %reduce-scatter.11.cloned.1.call-start = ((), (), s32[]{:S(2)}) async-start(), calls=%async_computation.13 | async-start | bytes 5242880 | tf_op jit(solution)/shard_map/reduce_scatter | solution.py:982
  470.0 24.9 %collective-permute-start.42 = (bf16[256,2048]{1,0:T(8,128)(2,1)}, bf16[256,2048]{1,0:T(8,128)(2,1)S(1)}, u32[]{:S(2)}, u32[]{:S(2)}) collective-permute-start(bf16[256,2048]{1,0:T(8,128)(2,1)} %get-tuple-element.330), channel_id=1, source_target_pairs={{0,4},{4,0},{8,12},{12,8},{16,20},{20,16},{24,28},{28,24},{1,5},{5... | collective-permute-start | bytes 3145736 | tf_op jit(solution)/shard_map/ppermute | solution.py:650
  475.4 20.9 %collective-permute-start.41 = (bf16[256,2048]{1,0:T(8,128)(2,1)}, bf16[256,2048]{1,0:T(8,128)(2,1)}, u32[]{:S(2)}, u32[]{:S(2)}) collective-permute-start(bf16[256,2048]{1,0:T(8,128)(2,1)} %add_convert_fusion.5), channel_id=1, source_target_pairs={{0,8},{4,12},{8,16},{12,20},{16,24},{20,28},{24,0},{28,4},{1,9},{5... | collective-permute-start | bytes 3145736 | tf_op jit(solution)/shard_map/ppermute | solution.py:654
  500.7 25.3 %collective-permute-start.46 = (bf16[256,2048]{1,0:T(8,128)(2,1)S(1)}, bf16[256,2048]{1,0:T(8,128)(2,1)}, u32[]{:S(2)}, u32[]{:S(2)}) collective-permute-start(bf16[256,2048]{1,0:T(8,128)(2,1)S(1)} %add_convert_fusion.4), channel_id=1, source_target_pairs={{0,8},{4,12},{8,16},{12,20},{16,24},{20,28},{24,0},{28,4},{1,9},{5... | collective-permute-start | bytes 3145736 | tf_op jit(solution)/shard_map/ppermute | solution.py:654
  501.2 24.8 %collective-permute-start.45 = (bf16[256,2048]{1,0:T(8,128)(2,1)}, bf16[256,2048]{1,0:T(8,128)(2,1)}, u32[]{:S(2)}, u32[]{:S(2)}) collective-permute-start(bf16[256,2048]{1,0:T(8,128)(2,1)} %get-tuple-element.333), channel_id=1, source_target_pairs={{0,4},{4,0},{8,12},{12,8},{16,20},{20,16},{24,28},{28,24},{1,5},{5... | collective-permute-start | bytes 3145736 | tf_op jit(solution)/shard_map/ppermute | solution.py:650
  503.4 22.6 %collective-permute-start.44 = (bf16[256,2048]{1,0:T(8,128)(2,1)}, bf16[256,2048]{1,0:T(8,128)(2,1)}, u32[]{:S(2)}, u32[]{:S(2)}) collective-permute-start(bf16[256,2048]{1,0:T(8,128)(2,1)} %fusion.32), channel_id=1, source_target_pairs={{0,2},{1,3},{2,0},{3,1},{4,6},{5,7},{6,4},{7,5},{8,10},{9,11},{10,... | collective-permute-start | bytes 3145736 | tf_op jit(solution)/shard_map/ppermute | solution.py:618
  504.2 22.4 %collective-permute-start.43 = (bf16[256,2048]{1,0:T(8,128)(2,1)}, bf16[256,2048]{1,0:T(8,128)(2,1)}, u32[]{:S(2)}, u32[]{:S(2)}) collective-permute-start(bf16[256,2048]{1,0:T(8,128)(2,1)} %fusion.32), channel_id=1, source_target_pairs={{0,1},{1,0},{2,3},{3,2},{4,5},{5,4},{6,7},{7,6},{8,9},{9,8},{10,11... | collective-permute-start | bytes 3145736 | tf_op jit(solution)/shard_map/ppermute | solution.py:614
  535.3 254.9 %reduce-scatter.13.cloned.1.call-start = ((), (), s32[]{:S(2)}) async-start(), calls=%async_computation.14 | async-start | bytes 5242880 | tf_op jit(solution)/shard_map/reduce_scatter | solution.py:982
  535.9 258.3 %reduce-scatter.7.cloned.1.call-start = ((), (), s32[]{:S(2)}) async-start(), calls=%async_computation.11 | async-start | bytes 5242880 | tf_op jit(solution)/shard_map/reduce_scatter | solution.py:982
  536.5 257.7 %reduce-scatter.9.cloned.1.call-start = ((), (), s32[]{:S(2)}) async-start(), calls=%async_computation.12 | async-start | bytes 5242880 | tf_op jit(solution)/shard_map/reduce_scatter | solution.py:982
  537.3 290.1 %reduce-scatter.15.cloned.1.call-start = ((), (), s32[]{:S(2)}) async-start(), calls=%async_computation.15 | async-start | bytes 5242880 | tf_op jit(solution)/shard_map/reduce_scatter | solution.py:982
  541.4 45.0 %collective-permute-start.49 = (bf16[256,2048]{1,0:T(8,128)(2,1)}, bf16[256,2048]{1,0:T(8,128)(2,1)}, u32[]{:S(2)}, u32[]{:S(2)}) collective-permute-start(bf16[256,2048]{1,0:T(8,128)(2,1)} %add_convert_fusion.3), channel_id=1, source_target_pairs={{0,8},{4,12},{8,16},{12,20},{16,24},{20,28},{24,0},{28,4},{1,9},{5... | collective-permute-start | bytes 3145736 | tf_op jit(solution)/shard_map/ppermute | solution.py:654
  542.9 43.5 %collective-permute-start.48 = (bf16[256,2048]{1,0:T(8,128)(2,1)}, bf16[256,2048]{1,0:T(8,128)(2,1)}, u32[]{:S(2)}, u32[]{:S(2)}) collective-permute-start(bf16[256,2048]{1,0:T(8,128)(2,1)} %get-tuple-element.345), channel_id=1, source_target_pairs={{0,4},{4,0},{8,12},{12,8},{16,20},{20,16},{24,28},{28,24},{1,5},{5... | collective-permute-start | bytes 3145736 | tf_op jit(solution)/shard_map/ppermute | solution.py:650
  586.4 241.0 %reduce-scatter.17.cloned.1.call-start = ((), (), s32[]{:S(2)}) async-start(), calls=%async_computation.16 | async-start | bytes 5242880 | tf_op jit(solution)/shard_map/reduce_scatter | solution.py:982
  623.3 25.3 %collective-permute-start.57 = (bf16[4,64,2176]{2,1,0:T(8,128)(2,1)}, bf16[4,64,2176]{2,1,0:T(8,128)(2,1)}, u32[]{:S(2)}, u32[]{:S(2)}) collective-permute-start(bf16[4,64,2176]{2,1,0:T(8,128)(2,1)} %get-tuple-element.363), channel_id=1, source_target_pairs={{0,4},{4,0},{8,12},{12,8},{16,20},{20,16},{24,28},{28,24},{1,5},{5... | collective-permute-start | bytes 3342344 | tf_op jit(solution)/shard_map/ppermute | solution.py:650
  624.5 26.9 %collective-permute-start.58 = (bf16[4,64,2176]{2,1,0:T(8,128)(2,1)}, bf16[4,64,2176]{2,1,0:T(8,128)(2,1)}, u32[]{:S(2)}, u32[]{:S(2)}) collective-permute-start(bf16[4,64,2176]{2,1,0:T(8,128)(2,1)} %get-tuple-element.498), channel_id=1, source_target_pairs={{0,8},{4,12},{8,16},{12,20},{16,24},{20,28},{24,0},{28,4},{1,9},{5... | collective-permute-start | bytes 3342344 | tf_op jit(solution)/shard_map/ppermute | solution.py:654
  654.7 26.5 %collective-permute-start.60 = (bf16[4,64,2176]{2,1,0:T(8,128)(2,1)}, bf16[4,64,2176]{2,1,0:T(8,128)(2,1)}, u32[]{:S(2)}, u32[]{:S(2)}) collective-permute-start(bf16[4,64,2176]{2,1,0:T(8,128)(2,1)} %fusion.5), channel_id=1, source_target_pairs={{0,8},{4,12},{8,16},{12,20},{16,24},{20,28},{24,0},{28,4},{1,9},{5... | collective-permute-start | bytes 3342344 | tf_op jit(solution)/shard_map/ppermute | solution.py:654
  654.7 26.5 %collective-permute-start.59 = (bf16[4,64,2176]{2,1,0:T(8,128)(2,1)}, bf16[4,64,2176]{2,1,0:T(8,128)(2,1)}, u32[]{:S(2)}, u32[]{:S(2)}) collective-permute-start(bf16[4,64,2176]{2,1,0:T(8,128)(2,1)} %get-tuple-element.365), channel_id=1, source_target_pairs={{0,4},{4,0},{8,12},{12,8},{16,20},{20,16},{24,28},{28,24},{1,5},{5... | collective-permute-start | bytes 3342344 | tf_op jit(solution)/shard_map/ppermute | solution.py:650
  683.5 29.4 %collective-permute-start.62 = (bf16[4,64,2176]{2,1,0:T(8,128)(2,1)S(1)}, bf16[4,64,2176]{2,1,0:T(8,128)(2,1)S(1)}, u32[]{:S(2)}, u32[]{:S(2)}) collective-permute-start(bf16[4,64,2176]{2,1,0:T(8,128)(2,1)S(1)} %fusion.3), channel_id=1, source_target_pairs={{0,8},{4,12},{8,16},{12,20},{16,24},{20,28},{24,0},{28,4},{1,9},{5... | collective-permute-start | bytes 3342344 | tf_op jit(solution)/shard_map/ppermute | solution.py:654
  683.5 29.3 %collective-permute-start.61 = (bf16[4,64,2176]{2,1,0:T(8,128)(2,1)S(1)}, bf16[4,64,2176]{2,1,0:T(8,128)(2,1)S(1)}, u32[]{:S(2)}, u32[]{:S(2)}) collective-permute-start(bf16[4,64,2176]{2,1,0:T(8,128)(2,1)S(1)} %get-tuple-element.368), channel_id=1, source_target_pairs={{0,4},{4,0},{8,12},{12,8},{16,20},{20,16},{24,28},{28,24},{1,5},{5... | collective-permute-start | bytes 3342344 | tf_op jit(solution)/shard_map/ppermute | solution.py:650
  695.7 24.0 %collective-permute-start.53 = (bf16[256,2048]{1,0:T(8,128)(2,1)}, bf16[256,2048]{1,0:T(8,128)(2,1)}, u32[]{:S(2)}, u32[]{:S(2)}) collective-permute-start(bf16[256,2048]{1,0:T(8,128)(2,1)} %get-tuple-element.506), channel_id=1, source_target_pairs={{0,1},{1,0},{2,3},{3,2},{4,5},{5,4},{6,7},{7,6},{8,9},{9,8},{10,11... | collective-permute-start | bytes 3145736 | tf_op jit(solution)/shard_map/ppermute | solution.py:614
  698.8 36.5 %collective-permute-start.51 = (bf16[256,2048]{1,0:T(8,128)(2,1)}, bf16[256,2048]{1,0:T(8,128)(2,1)}, u32[]{:S(2)}, u32[]{:S(2)}) collective-permute-start(bf16[256,2048]{1,0:T(8,128)(2,1)} %add_convert_fusion.2), channel_id=1, source_target_pairs={{0,8},{4,12},{8,16},{12,20},{16,24},{20,28},{24,0},{28,4},{1,9},{5... | collective-permute-start | bytes 3145736 | tf_op jit(solution)/shard_map/ppermute | solution.py:654
  698.8 38.2 %collective-permute-start.50 = (bf16[256,2048]{1,0:T(8,128)(2,1)}, bf16[256,2048]{1,0:T(8,128)(2,1)}, u32[]{:S(2)}, u32[]{:S(2)}) collective-permute-start(bf16[256,2048]{1,0:T(8,128)(2,1)} %get-tuple-element.352), channel_id=1, source_target_pairs={{0,4},{4,0},{8,12},{12,8},{16,20},{20,16},{24,28},{28,24},{1,5},{5... | collective-permute-start | bytes 3145736 | tf_op jit(solution)/shard_map/ppermute | solution.py:650
  712.8 24.2 %collective-permute-start.52 = (bf16[256,2048]{1,0:T(8,128)(2,1)}, bf16[256,2048]{1,0:T(8,128)(2,1)}, u32[]{:S(2)}, u32[]{:S(2)}) collective-permute-start(bf16[256,2048]{1,0:T(8,128)(2,1)} %get-tuple-element.505), channel_id=1, source_target_pairs={{0,1},{1,0},{2,3},{3,2},{4,5},{5,4},{6,7},{7,6},{8,9},{9,8},{10,11... | collective-permute-start | bytes 3145736 | tf_op jit(solution)/shard_map/ppermute | solution.py:614
  722.6 35.3 %collective-permute-start.54 = (bf16[256,2048]{1,0:T(8,128)(2,1)}, bf16[256,2048]{1,0:T(8,128)(2,1)}, u32[]{:S(2)}, u32[]{:S(2)}) collective-permute-start(bf16[256,2048]{1,0:T(8,128)(2,1)} %add_convert_fusion), channel_id=1, source_target_pairs={{0,2},{1,3},{2,0},{3,1},{4,6},{5,7},{6,4},{7,5},{8,10},{9,11},{10,... | collective-permute-start | bytes 3145736 | tf_op jit(solution)/shard_map/ppermute | solution.py:618
  735.2 27.0 %collective-permute-start.63 = (bf16[64,8320]{1,0:T(8,128)(2,1)S(1)}, bf16[64,8320]{1,0:T(8,128)(2,1)S(1)}, u32[]{:S(2)}, u32[]{:S(2)}) collective-permute-start(bf16[64,8320]{1,0:T(8,128)(2,1)S(1)} %pad_maximum_fusion.2.refs_0_), channel_id=1, source_target_pairs={{0,8},{4,12},{8,16},{12,20},{16,24},{20,28},{24,0},{28,4},{1,9},{5... | collective-permute-start | bytes 3194888 | tf_op jit(solution)/shard_map/ppermute | solution.py:654
  735.4 26.8 %collective-permute-start.64 = (bf16[64,8320]{1,0:T(8,128)(2,1)S(1)}, bf16[64,8320]{1,0:T(8,128)(2,1)S(1)}, u32[]{:S(2)}, u32[]{:S(2)}) collective-permute-start(bf16[64,8320]{1,0:T(8,128)(2,1)S(1)} %pad_maximum_fusion.2.refs_0_), channel_id=1, source_target_pairs={{0,4},{4,0},{8,12},{12,8},{16,20},{20,16},{24,28},{28,24},{1,5},{5... | collective-permute-start | bytes 3194888 | tf_op jit(solution)/shard_map/ppermute | solution.py:650
  763.2 26.1 %collective-permute-start.65 = (bf16[64,8320]{1,0:T(8,128)(2,1)S(1)}, bf16[64,8320]{1,0:T(8,128)(2,1)S(1)}, u32[]{:S(2)}, u32[]{:S(2)}) collective-permute-start(bf16[64,8320]{1,0:T(8,128)(2,1)S(1)} %collective-permute-done.63.refs_2_), channel_id=1, source_target_pairs={{0,8},{4,12},{8,16},{12,20},{16,24},{20,28},{24,0},{28,4},{1,9},{5... | collective-permute-start | bytes 3194888 | tf_op jit(solution)/shard_map/ppermute | solution.py:654
  763.2 27.1 %collective-permute-start.66 = (bf16[64,8320]{1,0:T(8,128)(2,1)S(1)}, bf16[64,8320]{1,0:T(8,128)(2,1)}, u32[]{:S(2)}, u32[]{:S(2)}) collective-permute-start(bf16[64,8320]{1,0:T(8,128)(2,1)S(1)} %collective-permute-done.63.refs_2_), channel_id=1, source_target_pairs={{0,4},{4,0},{8,12},{12,8},{16,20},{20,16},{24,28},{28,24},{1,5},{5... | collective-permute-start | bytes 3194888 | tf_op jit(solution)/shard_map/ppermute | solution.py:650
  798.1 25.6 %collective-permute-start.67 = (bf16[64,8320]{1,0:T(8,128)(2,1)S(1)}, bf16[64,8320]{1,0:T(8,128)(2,1)S(1)}, u32[]{:S(2)}, u32[]{:S(2)}) collective-permute-start(bf16[64,8320]{1,0:T(8,128)(2,1)S(1)} %copy-done.47), channel_id=1, source_target_pairs={{0,8},{4,12},{8,16},{12,20},{16,24},{20,28},{24,0},{28,4},{1,9},{5... | collective-permute-start | bytes 3194888 | tf_op jit(solution)/shard_map/ppermute | solution.py:654
  798.1 25.6 %collective-permute-start.68 = (bf16[64,8320]{1,0:T(8,128)(2,1)S(1)}, bf16[64,8320]{1,0:T(8,128)(2,1)S(1)}, u32[]{:S(2)}, u32[]{:S(2)}) collective-permute-start(bf16[64,8320]{1,0:T(8,128)(2,1)S(1)} %copy-done.47), channel_id=1, source_target_pairs={{0,4},{4,0},{8,12},{12,8},{16,20},{20,16},{24,28},{28,24},{1,5},{5... | collective-permute-start | bytes 3194888 | tf_op jit(solution)/shard_map/ppermute | solution.py:650
  824.6 19.1 %collective-permute-start.69 = (bf16[32,8320]{1,0:T(8,128)(2,1)}, bf16[32,8320]{1,0:T(8,128)(2,1)}, u32[]{:S(2)}, u32[]{:S(2)}) collective-permute-start(bf16[32,8320]{1,0:T(8,128)(2,1)} %slice.167), channel_id=1, source_target_pairs={{0,4},{4,0},{8,12},{12,8},{16,20},{20,16},{24,28},{28,24},{1,5},{5... | collective-permute-start | bytes 1597448 | tf_op jit(solution)/shard_map/ppermute | solution.py:650
  (88 other events, 1077.6 us)
Sparse Core Ops, SparseCore 0:
  45.1 57.5 all-gather.3
  104.2 58.8 all-gather.5
  185.9 58.2 all-gather.7
  535.5 45.1 reduce-scatter.10
  583.8 44.4 reduce-scatter.12
  631.3 44.4 reduce-scatter.6
  679.1 44.4 reduce-scatter.8
  726.7 52.1 reduce-scatter.14
  782.1 43.3 reduce-scatter.16
